TPU v7x, 256 devices: a whole 4x4x8 slice. The times are simulated.
256 devices in a mesh: pages: 64 (over y, z, core), expert: 4 (over x).
Axes of the slice: x: 4, y: 4, z: 8, core: 2. Of those that a mesh axis runs over, the one named last changes fastest.
Arguments:
- old_keys: bfloat16 [512, 128, 2048], P('pages', None, 'expert'), may hold values from -6 to 6
- old_values: bfloat16 [512, 128, 2048], P('pages', None, 'expert'), may hold values from -6 to 6
- keep_lists: int32 [512, 31], P('pages'), may hold values from 0 to 127, as said below
- drop_weights: int32 [512, 128], P('pages'), may hold values from 1 to 8
- request_pages: int32 [64], replicated, may hold values from 4 to 12, as said below
- page_table: int32 [64, 12], replicated, may hold values from 0 to 511, as said below
- new_table: int32 [64, 3], replicated, may hold values from 0 to 255, as said below
- queries: bfloat16 [64, 2, 2048], P(None, None, 'expert'), may hold values from -20 to 20
- new_keys: bfloat16 [64, 2048], P('pages', 'expert'), may hold values from -12 to 12
- new_values: bfloat16 [64, 2048], P('pages', 'expert'), may hold values from -6 to 6
- expert_ids: int32 [64, 2], replicated, may hold values from 0 to 7, all different within a row
- router_logits: float32 [64, 8], P('pages'), may hold values from -6 to 6
- out_weight: bfloat16 [64, 2048, 256], P('pages', 'expert'), may hold values from -0.375 to 0.375
Outputs:
- compact_keys: bfloat16 [256, 128, 2048], P('pages', None, 'expert')
- compact_values: bfloat16 [256, 128, 2048], P('pages', None, 'expert')
- mixed: bfloat16 [64, 2048], P('pages', 'expert')
Inputs may be any that keep to these rules, and one draw needn't show every extreme that they name: `request_pages`: every count is a multiple of 4; the counts sum to 512; one request has 12 pages. `page_table`: the first request_pages[r] entries of row r name that request's old pages in order and later entries are unused; every old page belongs to exactly one request; old page g lies on index g // 8 of pages; no index of pages holds more than 1 old pages whose new pages lie on one index, and some index holds that many. `new_table`: the first request_pages[r] / 4 entries of row r name distinct new slots and later entries are unused; slot s lies on index s // 4 of pages; some index has all 4 of its slots used. `keep_lists`: each row holds 31 distinct positions in increasing order.
All inputs are finite; a program needn't handle non-finite values.
Results may differ from a plain program's by a relative error of at most 0.012.
Values may be sent and summed in bfloat16 or wider, within the bound.
No kernel may reach another device: no remote copies, remote signals or barrier semaphores. Data moves between devices by JAX's collectives and lax.ppermute only.
A program may use at most 64 MiB of HBM per device.

v0:
```python
import math

import jax
import jax.numpy as jnp
from jax import lax
from jax.sharding import PartitionSpec as P

HD = 128
EXPERTS = 8


NEGATIVE = -1e30


def compact_blocks(page_cache, pick_matrix, merge_coef, merge_total):
    kept_rows = jnp.einsum(
        "skt,stc->skc", pick_matrix, page_cache, preferred_element_type=jnp.float32
    )
    merged = (
        jnp.einsum("st,stc->sc", merge_coef, page_cache, preferred_element_type=jnp.float32)
        / merge_total[:, None]
    )
    return jnp.concatenate([kept_rows, merged[:, None, :]], axis=1).astype(jnp.bfloat16)


def local_scores(key_groups, group_req, group_live, queries, bias_row):
    groups, group_len, lane_width = key_groups.shape
    requests = queries.shape[0]
    topk_slots = queries.shape[1]
    head_count = lane_width // HD
    request_ids = jnp.arange(requests, dtype=jnp.int32)
    selected = (group_req[:, None] == request_ids[None, :]) & group_live[:, None]
    group_query = jnp.einsum(
        "gr,rkc->gkc", selected.astype(jnp.bfloat16), queries, preferred_element_type=jnp.float32
    ).astype(jnp.bfloat16)
    scores = jnp.einsum(
        "gkhd,glhd->gkhl",
        group_query.reshape(groups, topk_slots, head_count, HD),
        key_groups.reshape(groups, group_len, head_count, HD),
        preferred_element_type=jnp.float32,
    )
    scores = scores * (1.0 / math.sqrt(HD)) + bias_row[None, None, None, :]
    group_peak = jnp.max(scores, axis=3)
    request_peak = jnp.max(
        jnp.where(selected[:, :, None, None], group_peak[:, None, :, :], NEGATIVE), axis=0
    )
    return (selected, scores, request_peak)


def local_sums(selected, scores, value_groups, global_peak, group_live):
    groups, group_len, lane_width = value_groups.shape
    head_count = lane_width // HD
    topk_slots = scores.shape[1]
    highest = lax.Precision.HIGHEST
    chosen = selected.astype(jnp.float32)
    group_peak = jnp.einsum("gr,rkh->gkh", chosen, global_peak, precision=highest)
    terms = (
        jnp.exp(scores - group_peak[:, :, :, None])
        * group_live.astype(jnp.float32)[:, None, None, None]
    )
    numerator = jnp.einsum(
        "gkhl,glhd->gkhd",
        terms.astype(jnp.bfloat16),
        value_groups.reshape(groups, group_len, head_count, HD),
        preferred_element_type=jnp.float32,
    )
    numerator = numerator.reshape(groups, topk_slots, lane_width)
    request_num = jnp.einsum("gr,gkc->rkc", chosen, numerator, precision=highest)
    request_den = jnp.einsum("gr,gkh->rkh", chosen, jnp.sum(terms, axis=3), precision=highest)
    return (request_num, request_den)


def shards(
    old_keys,
    old_values,
    keep_lists,
    drop_weights,
    request_pages,
    page_table,
    new_table,
    queries,
    new_keys,
    new_values,
    expert_ids,
    router_logits,
    out_weight,
):
    devices = lax.axis_size("pages")
    shard_count = lax.axis_size("expert")
    my_index = lax.axis_index("pages")
    slots, page_len, lane_width = old_keys.shape
    keep_count = keep_lists.shape[1]
    block_rows = keep_count + 1
    per_new = page_len // block_rows
    requests, max_pages = page_table.shape
    max_new = new_table.shape[1]
    new_cap = 2 * (slots // per_new)
    capacity = (2 * slots + devices - 1) // devices
    head_count = lane_width // HD
    request_ids = jnp.arange(requests, dtype=jnp.int32)
    positions = jnp.arange(page_len, dtype=jnp.int32)
    picked = keep_lists[:, :, None] == positions[None, None, :]
    pick_matrix = picked.astype(jnp.bfloat16)
    merge_coef = jnp.where(jnp.any(picked, axis=1), 0.0, drop_weights.astype(jnp.float32))
    merge_total = jnp.sum(merge_coef, axis=1)
    key_blocks = compact_blocks(old_keys, pick_matrix, merge_coef.astype(jnp.bfloat16), merge_total)
    value_blocks = compact_blocks(
        old_values, pick_matrix, merge_coef.astype(jnp.bfloat16), merge_total
    )
    slot_ids = my_index * slots + jnp.arange(slots, dtype=jnp.int32)
    logical = jnp.arange(max_pages, dtype=jnp.int32)
    in_use = logical[None, :] < request_pages[:, None]
    found_at = (page_table[None, :, :] == slot_ids[:, None, None]) & in_use[None, :, :]
    owner_req = jnp.sum(jnp.where(found_at, request_ids[None, :, None], 0), axis=(1, 2))
    page_pos = jnp.sum(jnp.where(found_at, logical[None, None, :], 0), axis=(1, 2))
    fresh_slot = new_table[owner_req, page_pos // per_new]
    target_dev = fresh_slot // new_cap
    target_row = fresh_slot % new_cap * per_new + page_pos % per_new
    slot_order = jnp.arange(slots, dtype=jnp.int32)
    earlier = (target_dev[:, None] == target_dev[None, :]) & (
        slot_order[None, :] < slot_order[:, None]
    )
    send_pos = target_dev * capacity + jnp.sum(earlier, axis=1)
    outbox = send_pos[None, :] == jnp.arange(devices * capacity, dtype=jnp.int32)[:, None]
    outbox_matrix = outbox.astype(jnp.bfloat16)
    send_rows = (jnp.sum(jnp.where(outbox, target_row[None, :] + 1, 0), axis=1) - 1).reshape(
        devices, capacity
    )

    def pack_blocks(blocks):
        packed = jnp.einsum(
            "ps,sec->pec", outbox_matrix, blocks, preferred_element_type=jnp.float32
        )
        return packed.astype(jnp.bfloat16).reshape(devices, capacity, block_rows, lane_width)

    got_keys, got_values, got_rows = (
        lax.all_to_all(pack_blocks(key_blocks), "pages", split_axis=0, concat_axis=0, tiled=True),
        lax.all_to_all(pack_blocks(value_blocks), "pages", split_axis=0, concat_axis=0, tiled=True),
        lax.all_to_all(send_rows, "pages", split_axis=0, concat_axis=0, tiled=True),
    )
    landing = (
        got_rows.reshape(-1)[None, :] == jnp.arange(new_cap * per_new, dtype=jnp.int32)[:, None]
    ).astype(jnp.bfloat16)

    def land_blocks(received):
        flat_rows = received.reshape(devices * capacity, block_rows, lane_width)
        placed = jnp.einsum("qp,pec->qec", landing, flat_rows, preferred_element_type=jnp.float32)
        return placed.astype(jnp.bfloat16).reshape(new_cap, per_new * block_rows, lane_width)

    compact_keys = land_blocks(got_keys)
    compact_values = land_blocks(got_values)
    merge_bias = math.log(page_len - keep_count)
    bias_row = jnp.where(
        jnp.arange(per_new * block_rows) % block_rows == block_rows - 1, merge_bias, 0.0
    ).astype(jnp.float32)
    home_slots = my_index * new_cap + jnp.arange(new_cap, dtype=jnp.int32)
    new_live = jnp.arange(max_new, dtype=jnp.int32)[None, :] < (request_pages // per_new)[:, None]
    held_at = (new_table[None, :, :] == home_slots[:, None, None]) & new_live[None, :, :]
    group_req = jnp.sum(jnp.where(held_at, request_ids[None, :, None], 0), axis=(1, 2))
    group_live = jnp.any(held_at, axis=(1, 2))
    my_query = lax.dynamic_index_in_dim(queries, my_index, 0, keepdims=False)
    topk_slots = my_query.shape[0]
    own_score = jnp.einsum(
        "khd,hd->kh",
        my_query.reshape(topk_slots, head_count, HD),
        new_keys.reshape(head_count, HD),
        preferred_element_type=jnp.float32,
    ) * (1.0 / math.sqrt(HD))
    selected, scores, request_peak = local_scores(
        compact_keys, group_req, group_live, queries, bias_row
    )
    is_mine = (request_ids == my_index)[:, None, None]
    request_peak = jnp.where(
        is_mine, jnp.maximum(request_peak, own_score[None, :, :]), request_peak
    )
    global_peak = lax.pmax(request_peak, "pages")
    request_num, request_den = local_sums(selected, scores, compact_values, global_peak, group_live)
    my_num, my_den = (
        lax.psum_scatter(request_num, "pages", scatter_dimension=0, tiled=True),
        lax.psum_scatter(request_den, "pages", scatter_dimension=0, tiled=True),
    )
    my_peak = lax.dynamic_index_in_dim(global_peak, my_index, 0, keepdims=False)
    own_prob = jnp.exp(own_score - my_peak)
    own_rounded = lax.optimization_barrier(own_prob.astype(jnp.bfloat16)).astype(jnp.float32)
    numerator = (
        my_num[0].reshape(topk_slots, head_count, HD)
        + own_rounded[:, :, None]
        * new_values.reshape(head_count, HD).astype(jnp.float32)[None, :, :]
    )
    denominator = my_den[0] + own_prob
    my_experts = lax.dynamic_index_in_dim(expert_ids, my_index, 0, keepdims=False)
    chosen = jnp.take(router_logits[0], my_experts)
    gate_weights = jax.nn.softmax(chosen)
    weighted = (
        (gate_weights[:, None, None] * (numerator / denominator[:, :, None]))
        .astype(jnp.bfloat16)
        .reshape(1, topk_slots, lane_width)
    )
    column_blocks = devices // EXPERTS
    my_expert = my_index // column_blocks
    weight_block = out_weight[0]
    match_mask = (expert_ids == my_expert).astype(jnp.bfloat16)
    contrib = jnp.einsum(
        "rkc,rk,co->ro",
        lax.all_gather(weighted, "pages", axis=0, tiled=True),
        match_mask,
        weight_block,
        preferred_element_type=jnp.float32,
    )
    block_cols = contrib.shape[1]
    model_width = block_cols * column_blocks
    full_rows = jnp.zeros((requests, model_width), jnp.float32)
    full_rows = lax.dynamic_update_slice(
        full_rows, contrib, (jnp.zeros((), jnp.int32), my_index % column_blocks * block_cols)
    )
    spread = full_rows.reshape(requests * shard_count, model_width // shard_count)
    mixed = lax.psum_scatter(spread, ("pages", "expert"), scatter_dimension=0, tiled=True).astype(
        jnp.bfloat16
    )
    return (compact_keys, compact_values, mixed)


def solution(mesh):
    in_specs = (
        P("pages", None, "expert"),
        P("pages", None, "expert"),
        P("pages", None),
        P("pages", None),
        P(),
        P(),
        P(),
        P(None, None, "expert"),
        P("pages", "expert"),
        P("pages", "expert"),
        P(),
        P("pages", None),
        P("pages", "expert", None),
    )
    out_specs = (P("pages", None, "expert"), P("pages", None, "expert"), P("pages", "expert"))
    return jax.shard_map(shards, mesh=mesh, in_specs=in_specs, out_specs=out_specs, check_vma=False)
```

profile of v0, /device:TPU:1, one launch (start us, length us, event | category | flops | bytes accessed | tf_op | source)
XLA Modules:
  0.0 820.6 jit_solution(7523858380768102113)
XLA Ops:
  7.2 0.8 iota_compare_fusion.4
  8.0 0.9 select_reduce_fusion.1
  9.0 1.3 gather_fusion
  10.6 0.7 copy.104
  11.3 13.2 %all-to-all-start = ((s32[64,1,1]{2,1,0:T(1,128)}), s32[64,1,1]{2,1,0:T(1,128)S(1)}, u32[]{:S(2)}, u32[]{:S(2)}) async-start(s32[64,1,1]{2,1,0:T(1,128)} %copy.104), calls=%async_computation | async-start | bytes 65536 | tf_op jit(solution)/shard_map/all_to_all | solution.py:139
  24.5 0.8 fusion.22
  25.3 1.0 convolution_convert_fusion.1
  26.3 0.8 fusion.50
  27.1 0.2 fusion.48
  27.4 0.3 fusion.46
  27.8 0.8 convert_bitcast_fusion.1
  28.6 2.5 copy.107
  31.1 2.6 all-to-all-done
  33.7 7.8 all-to-all-start.1
  41.6 1.5 convolution_convert_fusion
  43.2 0.8 convert_bitcast_fusion
  44.0 2.5 copy.112
  46.6 46.2 %all-to-all-done.1 = bf16[64,1,32,512]{3,2,1,0:T(8,128)(2,1)S(1)} async-done(((bf16[64,1,32,512]{3,2,1,0:T(8,128)(2,1)}), bf16[64,1,32,512]{3,2,1,0:T(8,128)(2,1)S(1)}, u32[]{:S(2)}, u32[]{:S(2)}) %all-to-all-start.1) | async-done | bytes 2097184 | tf_op jit(solution)/shard_map/all_to_all | solution.py:137
  92.8 6.0 all-to-all-start.2
  98.8 0.2 all-reduce.6.cloned.1.call-start
  99.1 0.2 fusion.43
  99.3 0.2 select_reduce_fusion.3
  99.9 0.2 dynamic-slice_reduce_fusion.1
  100.3 0.6 dynamic-slice
  100.9 0.6 gather_fusion.1
  101.6 0.6 fusion.79
  102.2 1.2 fusion.77
  103.4 1.3 broadcast_divide_fusion
  104.7 1.2 reduce
  106.0 2.3 fusion.6
  108.3 0.3 copy.109
  108.7 0.5 fusion.80
  109.5 153.3 %pmax.7 = f32[64,2,4]{0,2,1:T(4,128)S(1)} all-reduce(f32[64,2,4]{0,2,1:T(4,128)S(1)} %maximum_select_fusion), channel_id=1, replica_groups=mesh['pages'=64,'expert'=4] {'pages'}, use_global_device_ids=true, to_apply=%region_12.13 | all-reduce | flops 512 | bytes 4096 | tf_op jit(solution)/shard_map/pmax | solution.py:176
  263.0 4.0 fusion.9
  267.0 0.3 copy.114
  267.4 0.2 fusion.78
  267.7 0.2 fusion.54
  268.0 242.0 %all-reduce.1 = f32[64,2,4]{2,1,0:T(2,128)S(1)} all-reduce(f32[64,2,4]{2,1,0:T(2,128)S(1)} %copy.126), channel_id=3, replica_groups=mesh['pages'=64,'expert'=4] {'pages'}, use_global_device_ids=true, to_apply=%region_15.16.clone | all-reduce | flops 512 | bytes 4096
  510.2 0.3 convolution_bitcast_fusion
  510.5 0.3 fusion.27
  510.9 0.9 copy.124
  511.8 0.7 fusion.76
  512.6 173.4 %all-reduce.6.cloned.1.call-done = f32[64,2,512]{2,1,0:T(2,128)} async-done(((f32[64,2,512]{2,1,0:T(2,128)}), f32[64,2,512]{2,1,0:T(2,128)}) %all-reduce.6.cloned.1.call-update) | async-done | bytes 262160
  686.0 1.4 multiply_convert_fusion
  687.4 47.0 %all_gather.3 = bf16[64,2,512]{2,1,0:T(2,128)(2,1)S(1)} all-gather(bf16[1,2,512]{2,1,0:T(2,128)(2,1)S(1)} %multiply_convert_fusion), channel_id=1, replica_groups=mesh['pages'=64,'expert'=4] {'pages'}, dimensions={0}, use_global_device_ids=true | all-gather | bytes 133120 | tf_op jit(solution)/shard_map/all_gather | solution.py:205
  734.5 0.3 fusion.81
  735.1 78.0 %all-reduce.7 = bf16[256,512]{1,0:T(8,128)(2,1)S(1)} all-reduce(f32[256,512]{1,0:T(8,128)S(1)} %reshape.410), channel_id=4, replica_groups=mesh['pages'=64,'expert'=4] {'pages','expert'}, use_global_device_ids=true, to_apply=%region_16.17.clone | all-reduce | flops 131072 | bytes 786432
  813.1 0.6 dynamic-slice_convert_fusion
  (76 shorter events, 2.9 us)
Async XLA Ops:
  7.2 18.1 %copy-start = (bf16[8,128,512]{2,1,0:T(8,128)(2,1)S(1)}, bf16[8,128,512]{2,1,0:T(8,128)(2,1)}, u32[]{:S(2)}) copy-start(bf16[8,128,512]{2,1,0:T(8,128)(2,1)} %param.13) | copy-start | bytes 3145732
  7.2 20.2 %copy-start.3 = (bf16[8,128,512]{2,1,0:T(8,128)(2,1)S(1)}, bf16[8,128,512]{2,1,0:T(8,128)(2,1)}, u32[]{:S(2)}) copy-start(bf16[8,128,512]{2,1,0:T(8,128)(2,1)} %param.14) | copy-start | bytes 3145732
  11.3 22.4 %all-to-all-start = ((s32[64,1,1]{2,1,0:T(1,128)}), s32[64,1,1]{2,1,0:T(1,128)S(1)}, u32[]{:S(2)}, u32[]{:S(2)}) async-start(s32[64,1,1]{2,1,0:T(1,128)} %copy.104), calls=%async_computation | async-start | bytes 65536 | tf_op jit(solution)/shard_map/all_to_all | solution.py:139
  31.1 10.5 %copy-start.8 = (s32[8,31]{1,0:T(8,128)S(1)}, s32[8,31]{1,0:T(8,128)}, u32[]{:S(2)}) copy-start(s32[8,31]{1,0:T(8,128)} %param.15) | copy-start | bytes 2980
  33.7 59.1 %all-to-all-start.1 = ((bf16[64,1,32,512]{3,2,1,0:T(8,128)(2,1)}), bf16[64,1,32,512]{3,2,1,0:T(8,128)(2,1)S(1)}, u32[]{:S(2)}, u32[]{:S(2)}) async-start(bf16[64,1,32,512]{3,2,1,0:T(8,128)(2,1)} %copy.107), calls=%async_computation.1 | async-start | bytes 4194304 | tf_op jit(solution)/shard_map/all_to_all | solution.py:137
  46.5 52.5 %copy-start.11 = (s32[64]{0:T(128)S(1)}, s32[64]{0:T(128)}, u32[]{:S(2)}) copy-start(s32[64]{0:T(128)} %param.17) | copy-start | bytes 772
  46.5 52.6 %copy-start.2 = (s32[64,3]{0,1:T(4,128)S(1)}, s32[64,3]{0,1:T(4,128)}, u32[]{:S(2)}) copy-start(s32[64,3]{0,1:T(4,128)} %param.19) | copy-start | bytes 2308
  46.5 53.0 %copy-start.7 = (bf16[64,2,512]{2,1,0:T(2,128)(2,1)S(1)}, bf16[64,2,512]{2,1,0:T(2,128)(2,1)}, u32[]{:S(2)}) copy-start(bf16[64,2,512]{2,1,0:T(2,128)(2,1)} %param.20) | copy-start | bytes 393220
  46.5 53.2 %copy-start.12 = (bf16[1,512]{1,0:T(2,128)(2,1)S(1)}, bf16[1,512]{1,0:T(2,128)(2,1)}, u32[]{:S(2)}) copy-start(bf16[1,512]{1,0:T(2,128)(2,1)} %param.21) | copy-start | bytes 3076
  46.5 53.4 %copy-start.9 = (s32[64,2]{0,1:T(2,128)S(1)}, s32[64,2]{0,1:T(2,128)}, u32[]{:S(2)}) copy-start(s32[64,2]{0,1:T(2,128)} %param.23) | copy-start | bytes 1540
  46.5 53.6 %copy-start.10 = (bf16[1,512]{1,0:T(2,128)(2,1)S(1)}, bf16[1,512]{1,0:T(2,128)(2,1)}, u32[]{:S(2)}) copy-start(bf16[1,512]{1,0:T(2,128)(2,1)} %param.22) | copy-start | bytes 3076
  46.5 53.8 %copy-start.13 = (u32[256]{0:T(256)S(1)}, u32[256]{0:T(256)}, u32[]{:S(2)}) copy-start(u32[256]{0:T(256)} %constant.168) | copy-start | bytes 3076
  46.6 54.4 %copy-start.1 = (f32[1,8]{1,0:T(1,128)S(1)}, f32[1,8]{1,0:T(1,128)}, u32[]{:S(2)}) copy-start(f32[1,8]{1,0:T(1,128)} %param.24) | copy-start | bytes 100
  92.8 170.3 %all-to-all-start.2 = ((bf16[64,1,32,512]{3,2,1,0:T(8,128)(2,1)}), bf16[64,1,32,512]{3,2,1,0:T(8,128)(2,1)}, u32[]{:S(2)}, u32[]{:S(2)}) async-start(bf16[64,1,32,512]{3,2,1,0:T(8,128)(2,1)} %copy.112), calls=%async_computation.2 | async-start | bytes 4194304 | tf_op jit(solution)/shard_map/all_to_all | solution.py:138
  98.8 587.3 %all-reduce.6.cloned.1.call-start = ((), (), s32[]{:S(2)}) async-start(), calls=%async_computation.3 | async-start | bytes 524288
  108.6 158.4 %copy-start.4 = (bf16[16,32,512]{2,1,0:T(8,128)(2,1)}, bf16[16,32,512]{2,1,0:T(8,128)(2,1)S(1)}, u32[]{:S(2)}) copy-start(bf16[16,32,512]{2,1,0:T(8,128)(2,1)S(1)} %copy.109) | copy-start | bytes 1572868
  267.3 467.5 %copy-start.5 = (bf16[16,32,512]{2,1,0:T(8,128)(2,1)}, bf16[16,32,512]{2,1,0:T(8,128)(2,1)S(1)}, u32[]{:S(2)}) copy-start(bf16[16,32,512]{2,1,0:T(8,128)(2,1)S(1)} %copy.114) | copy-start | bytes 1572868
  510.1 224.7 %copy-start.6 = (bf16[1,512,256]{2,1,0:T(8,128)(2,1)S(1)}, bf16[1,512,256]{2,1,0:T(8,128)(2,1)}, u32[]{:S(2)}) copy-start(bf16[1,512,256]{2,1,0:T(8,128)(2,1)} %param.25) | copy-start | bytes 786436
Sparse Core Ops, SparseCore 0:
  511.9 174.0 all-reduce.5
where the time goes:
time: 821 us
  blocking collectives  520 us (63%)
  waiting for transfers between devices  222 us (27%)
  starting transfers between devices  27.2 us (3%)
  between operations  14.5 us (2%)
  matrix products  13.1 us (2%)
  local copies, waits for them, and re-layouts  12 us (1%)
  other arithmetic  11.1 us (1%)
    unnamed x2, blocking collectives  320 us
    unnamed x2, waiting for transfers between devices  173 us
    pmax x1, blocking collectives, shards(): global_peak = lax.pmax(request_peak, 'pages')  153 us
    all_gather x1, blocking collectives, shards(): lax.all_gather(weighted, 'pages', axis=0, tiled=True)  47 us
    all_to_all x1, waiting for transfers between devices, shards(): lax.all_to_all(pack_blocks(key_blocks), 'pages', split_axis=0, concat_axi...  46.2 us
  transfers between devices with their start and end apart: 4, of which 3 were waited for; matrix products, arithmetic and copies ran while one was open for 3% of the time, Pallas kernels for 0%

commit v1 on v0

v1 whole, which is shorter than its diff:
```python
import math

import jax
import jax.numpy as jnp
from jax import lax
from jax.experimental import pallas as pl
from jax.experimental.pallas import tpu as pltpu
from jax.sharding import PartitionSpec as P

HD = 128
EXPERTS = 8
NEGATIVE = -1e30
F32 = jnp.float32
BF16 = jnp.bfloat16
VMEM = pl.BlockSpec(memory_space=pltpu.VMEM)
SMEM = pl.BlockSpec(memory_space=pltpu.SMEM)
NT = (((1,), (1,)), ((), ()))


def iota(shape, dim):
    return lax.broadcasted_iota(jnp.int32, shape, dim)


def dot(a, b):
    return jnp.dot(a, b, preferred_element_type=F32)


def source_kernel(
    my_ref, table_ref, keep_ref, drop_ref, k_ref, v_ref, q_ref, nk_ref, nv_ref, out_ref, kb, vb, acc
):
    my = my_ref[0]
    slots, page_len, width = k_ref.shape
    rows = keep_ref.shape[0]
    heads = width // HD
    topk = q_ref.shape[0]
    reqs = q_ref.shape[1]
    lane = iota((rows, page_len), 1)
    last = iota((rows, page_len), 0) == rows - 1
    for g in range(slots):
        onehot = jnp.where(keep_ref[:, g : g + 1] == lane, 1.0, 0.0)
        kept = jnp.max(onehot, axis=0, keepdims=True)
        coef = jnp.where(kept > 0.0, 0.0, drop_ref[g : g + 1, :].astype(F32))
        total = jnp.sum(coef, axis=1, keepdims=True)
        mat = jnp.where(last, coef, onehot).astype(BF16)
        denom = jnp.where(last[:, 0:1], total, 1.0)
        kb[g * rows : (g + 1) * rows, :] = (dot(mat, k_ref[g]) / denom).astype(BF16)
        vb[g * rows : (g + 1) * rows, :] = (dot(mat, v_ref[g]) / denom).astype(BF16)
    n = slots * rows
    to = iota((n, n), 0)
    fro = iota((n, n), 1)
    perm = jnp.where((to % slots == fro // rows) & (to // slots == fro % rows), 1.0, 0.0).astype(BF16)
    for base, blocks in ((0, kb), (rows, vb)):
        spread = dot(perm, blocks[...])
        for t in range(heads):
            out_ref[base : base + rows, t * slots : (t + 1) * slots, :] = (
                spread[:, t * HD : (t + 1) * HD].reshape(rows, slots, HD).astype(BF16)
            )
    ent = 2 * slots
    pad = table_ref.shape[1]
    ent_row = iota((ent, pad), 0)
    req_lane = iota((ent, pad), 1)
    sel = jnp.where((ent_row == slots) & (req_lane == my), 1.0, 0.0)
    for g in range(slots):
        hit = jnp.where(table_ref[...] == my * slots + g, 1.0, 0.0)
        sel = jnp.where(ent_row == g, jnp.max(hit, axis=0, keepdims=True), sel)
    sel_b = sel.astype(BF16)
    same = lax.dot_general(sel_b, sel_b, NT, preferred_element_type=F32)
    q_lane = iota((ent, width), 1) // HD
    pieces = []
    for k in range(topk):
        group_query = dot(sel_b[:, :reqs], q_ref[k])
        for h in range(heads):
            pieces.append(jnp.where(q_lane == h, group_query, 0.0))
    queries = jnp.concatenate(pieces, axis=0)
    kh = topk * heads
    scale = 1.0 / math.sqrt(HD)
    scores = lax.dot_general(queries.astype(BF16), kb[...], NT, preferred_element_type=F32) * scale
    col = iota((kh * ent, n), 1)
    scores = scores + jnp.where(col % rows == rows - 1, math.log(page_len - rows + 1), 0.0)
    of_page = jnp.where(iota((ent, n), 1) // rows == iota((ent, n), 0), 1.0, 0.0).astype(BF16)
    shared = dot(same.astype(BF16), of_page)
    mask = jnp.concatenate([shared] * kh, axis=0) > 0.5
    scores = jnp.where(mask, scores, NEGATIVE)
    is_own = iota((kh * ent, 1), 0) % ent == slots
    own = jnp.sum(queries * nk_ref[...].astype(F32), axis=1, keepdims=True) * scale
    own = jnp.where(is_own, own, NEGATIVE)
    peak = jnp.maximum(jnp.max(scores, axis=1, keepdims=True), own)
    shift = peak.astype(BF16).astype(F32)
    probs = jnp.where(mask, jnp.exp(scores - shift), 0.0)
    own_prob = jnp.where(is_own, jnp.exp(own - shift), 0.0)
    den = jnp.sum(probs, axis=1, keepdims=True) + own_prob
    num = dot(probs.astype(BF16), vb[...])
    num = num + own_prob.astype(BF16).astype(F32) * nv_ref[...].astype(F32)
    high = den.astype(BF16).astype(F32)
    stat_lane = iota((kh * ent, HD), 1)
    stats = jnp.where(stat_lane == 0, shift, jnp.where(stat_lane == 1, high, den - high))
    parts = [
        num[j * ent : (j + 1) * ent, (j % heads) * HD : (j % heads + 1) * HD] for j in range(kh)
    ] + [stats[j * ent : (j + 1) * ent, :] for j in range(kh)]
    entries = jnp.concatenate(parts, axis=1).astype(BF16)
    er = iota((ent, ent), 0)
    ec = iota((ent, ent), 1)
    before = jnp.sum(jnp.where((ec < er) | (ec == slots), same, 0.0), axis=1, keepdims=True)
    first = (ent_row == slots) | ((ent_row < slots) & (before < 0.5))
    pick = jnp.where(first, sel, 0.0).T[:reqs, :].astype(BF16)
    placed = dot(pick, entries)
    for j in range(2 * kh):
        acc[:, j, :] = placed[:, j * HD : (j + 1) * HD]
    out_ref[:, heads * slots :, :] = acc[...].astype(BF16)


def home_kernel(my_ref, ids_ref, logit_ref, got_ref, out_ref):
    my = my_ref[0]
    kh = got_ref.shape[1] // 2
    heads = kh // ids_ref.shape[0]
    got = got_ref[...].astype(F32)
    num = got[:, :kh, :]
    shift = got[:, kh:, 0:1]
    den = got[:, kh:, 1:2] + got[:, kh:, 2:3]
    live = den > 0.0
    peak = jnp.max(jnp.where(live, shift, NEGATIVE), axis=0, keepdims=True)
    factor = jnp.where(live, jnp.exp(shift - peak), 0.0)
    total = jnp.sum(factor * den, axis=0)
    value = jnp.sum(factor * num, axis=0) / total
    mine = iota(ids_ref.shape, 1) == my
    ids = jnp.sum(jnp.where(mine, ids_ref[...], 0), axis=1, keepdims=True)
    logits = jnp.sum(
        jnp.where(iota((ids.shape[0], EXPERTS), 1) == ids, logit_ref[...], 0.0), axis=1, keepdims=True
    )
    terms = jnp.exp(logits - jnp.max(logits, axis=0, keepdims=True))
    gate = terms / jnp.sum(terms, axis=0, keepdims=True)
    columns = out_ref.shape[0] // EXPERTS
    for e in range(EXPERTS):
        row = jnp.zeros((heads, HD), F32)
        for k in range(ids.shape[0]):
            weighted = gate[k : k + 1, :] * value[k * heads : (k + 1) * heads, :]
            row = jnp.where(ids[k : k + 1, :] == e, weighted, row)
        out_ref[e * columns : (e + 1) * columns] = jnp.broadcast_to(
            row[None], (columns, heads, HD)
        ).astype(BF16)


def relay_kernel(source_ref, low_ref, high_ref, out_ref):
    devices, per, _ = low_ref.shape
    slots = per // 2
    held = devices * slots
    tiles = []
    for ref in (low_ref, high_ref):
        for t in range(2):
            rows = ref[:, t * slots : (t + 1) * slots, :].astype(F32)
            tiles.append(rows.reshape(held, HD).astype(BF16))
    table = jnp.concatenate(tiles, axis=1)
    local = out_ref.shape[1]
    step = 16
    for c in range(0, devices, step):
        source = source_ref[c * local : (c + step) * local, :]
        pick = jnp.where(source == iota((step * local, held), 1), 1.0, 0.0).astype(BF16)
        out_ref[c : c + step] = dot(pick, table).reshape(step, local, table.shape[1]).astype(BF16)


def land_kernel(got_ref, k_ref, v_ref):
    total, local, width = got_ref.shape
    rows = total // 2
    n = rows * local
    to = iota((n, n), 0)
    fro = iota((n, n), 1)
    perm = jnp.where((to // rows == fro % local) & (to % rows == fro // local), 1.0, 0.0).astype(BF16)
    for base, ref in ((0, k_ref), (rows, v_ref)):
        flat = got_ref[base : base + rows].reshape(n, width)
        ref[...] = dot(perm, flat).reshape(ref.shape).astype(BF16)


def project_kernel(got_ref, w_ref, out_ref, acc):
    reqs, heads, _ = got_ref.shape
    acc[...] = got_ref[...].astype(F32)
    total = dot(acc[:, 0, :].astype(BF16), w_ref[0, 0:HD, :])
    for h in range(1, heads):
        total = total + dot(acc[:, h, :].astype(BF16), w_ref[0, h * HD : (h + 1) * HD, :])
    for c in range(out_ref.shape[1]):
        out_ref[:, c, :] = total[:, c * HD : (c + 1) * HD]


def shards(
    old_keys,
    old_values,
    keep_lists,
    drop_weights,
    request_pages,
    page_table,
    new_table,
    queries,
    new_keys,
    new_values,
    expert_ids,
    router_logits,
    out_weight,
):
    devices = lax.axis_size("pages")
    shard_count = lax.axis_size("expert")
    my = lax.axis_index("pages").astype(jnp.int32).reshape(1)
    slots, page_len, width = old_keys.shape
    rows = keep_lists.shape[1] + 1
    per_new = page_len // rows
    requests, max_pages = page_table.shape
    max_new = new_table.shape[1]
    new_cap = 2 * (slots // per_new)
    local = new_cap * per_new
    heads = width // HD
    topk = queries.shape[1]
    kh = topk * heads
    chunk = heads * slots + 2 * kh

    logical = jnp.arange(max_pages, dtype=jnp.int32)
    live_table = jnp.where(logical[:, None] < request_pages[None, :], page_table.T, -1)
    live_table = jnp.pad(live_table, ((0, 4), (0, 128 - requests)), constant_values=-1)
    keep_columns = jnp.pad(keep_lists.T, ((0, 1), (0, 0)), constant_values=-1)
    by_choice = queries.transpose(1, 0, 2)

    outbox = pl.pallas_call(
        source_kernel,
        out_shape=jax.ShapeDtypeStruct((devices, chunk, HD), BF16),
        in_specs=[SMEM] + [VMEM] * 8,
        out_specs=VMEM,
        scratch_shapes=[
            pltpu.VMEM((slots * rows, width), BF16),
            pltpu.VMEM((slots * rows, width), BF16),
            pltpu.VMEM((requests, 2 * kh, HD), F32),
        ],
        name="source",
    )(my, live_table, keep_columns, drop_weights, old_keys, old_values, by_choice, new_keys, new_values)
    inbox = lax.all_to_all(outbox, "pages", split_axis=0, concat_axis=0, tiled=True)

    part = 2 * kh
    weighted = pl.pallas_call(
        home_kernel,
        grid=(1,),
        out_shape=jax.ShapeDtypeStruct((devices, heads, HD), BF16),
        in_specs=[
            SMEM,
            VMEM,
            VMEM,
            pl.BlockSpec((devices, part, HD), lambda i: (0, heads * slots // part, 0)),
        ],
        out_specs=VMEM,
        name="home",
    )(my, expert_ids.T, router_logits, inbox)
    spread = lax.all_to_all(weighted, "pages", split_axis=0, concat_axis=0, tiled=True)

    new_live = jnp.arange(max_new, dtype=jnp.int32)[None, :] < (request_pages // per_new)[:, None]
    filled = jnp.where(new_live, new_table, -1).reshape(1, -1)
    fills = filled == jnp.arange(devices * new_cap, dtype=jnp.int32)[:, None]
    pages = page_table.reshape(-1, per_new) + 1
    source = (
        jnp.sum(jnp.where(fills[:, :, None], pages[None, :, :], 0), axis=1) - 1
    ).reshape(-1, 1)
    routed = pl.pallas_call(
        relay_kernel,
        grid=(1,),
        out_shape=jax.ShapeDtypeStruct((devices, local, width), BF16),
        in_specs=[
            VMEM,
            pl.BlockSpec((devices, 2 * slots, HD), lambda i: (0, 0, 0)),
            pl.BlockSpec((devices, 2 * slots, HD), lambda i: (0, 1, 0)),
        ],
        out_specs=VMEM,
        name="relay",
    )(source, inbox, inbox)

    block_cols = out_weight.shape[2]
    contrib = pl.pallas_call(
        project_kernel,
        out_shape=jax.ShapeDtypeStruct((requests, block_cols // HD, HD), F32),
        in_specs=[VMEM, VMEM],
        out_specs=VMEM,
        scratch_shapes=[pltpu.VMEM((requests, heads, HD), F32)],
        name="project",
    )(spread, out_weight)
    blocks = devices // EXPERTS
    per = blocks // shard_count
    moves = []
    for e in range(EXPERTS):
        for c in range(blocks):
            for s in range(shard_count):
                target = e * blocks + (c % per) * shard_count + s
                moves.append(((e * blocks + c) * shard_count + s, target * shard_count + c // per))
    contrib = lax.ppermute(contrib, ("pages", "expert"), moves)
    parts = lax.all_to_all(contrib, "pages", split_axis=0, concat_axis=0, tiled=True)
    mixed = jnp.sum(parts.reshape(EXPERTS, per, shard_count, block_cols // HD, HD), axis=(0, 2))
    mixed = mixed.reshape(1, -1).astype(BF16)

    landed = lax.all_to_all(routed, "pages", split_axis=0, concat_axis=0, tiled=True)
    new_page = jax.ShapeDtypeStruct((new_cap, per_new * rows, width), BF16)
    compact_keys, compact_values = pl.pallas_call(
        land_kernel,
        out_shape=(new_page, new_page),
        in_specs=[VMEM],
        out_specs=(VMEM, VMEM),
        name="land",
    )(landed)
    return (compact_keys, compact_values, mixed)


def solution(mesh):
    in_specs = (
        P("pages", None, "expert"),
        P("pages", None, "expert"),
        P("pages", None),
        P("pages", None),
        P(),
        P(),
        P(),
        P(None, None, "expert"),
        P("pages", "expert"),
        P("pages", "expert"),
        P(),
        P("pages", None),
        P("pages", "expert", None),
    )
    out_specs = (P("pages", None, "expert"), P("pages", None, "expert"), P("pages", "expert"))
    return jax.shard_map(shards, mesh=mesh, in_specs=in_specs, out_specs=out_specs, check_vma=False)
```

time: 821 us -> 129 us (0.16)
  blocking collectives: 520 us -> 0 us
  waiting for transfers between devices: 222 us -> 68.1 us
  Pallas kernels: 0 us -> 13.8 us
  between operations: 14.5 us -> 0.76 us
  matrix products: 13.1 us -> 0 us
  other arithmetic: 11.1 us -> 0.35 us
    unnamed x2 -> x0, blocking collectives: 320 us -> none
    unnamed x2 -> x0, waiting for transfers between devices: 173 us -> none
    pmax x1 -> x0, blocking collectives: 153 us -> none  [shards(): global_peak = lax.pmax(request_peak, 'pages')]
    all_gather x1 -> x0, blocking collectives: 47 us -> none  [shards(): lax.all_gather(weighted, 'pages', axis=0, tiled=True)]
    all_to_all x3 -> x4, waiting for transfers between devices: 48.8 us -> 65.2 us  [the longest x1 27.9 us: shards(): lax.all_to_all(routed, 'pages', split_axis=0, concat_axis=0, tiled=True)]
    pallas_call x0 -> x5, Pallas kernels: none -> 13.8 us  [the longest x1 4.07 us: shards(): pl.pallas_call(source_kernel, out_shape=jax.ShapeDtypeStruct((devices, ch...]
    dot_general x17 -> x0, matrix products: 13.1 us -> none  [the longest x2 6.29 us: land_blocks(): jnp.einsum('qp,pec->qec', landing, flat_rows, preferred_element_type=jnp....]
    all_to_all x3 -> x4, starting transfers between devices: 27 us -> 32.6 us  [the longest x1 13.2 us: shards(): lax.all_to_all(outbox, 'pages', split_axis=0, concat_axis=0, tiled=True)]
  transfers between devices with their start and end apart: 4 -> 5, of which waited for: 3 -> 5; matrix products, arithmetic and copies ran while one was open for 3% -> 2% of each run, Pallas kernels for 0% -> 2%
where the time goes in v1:
time: 129 us; the launch traced here: 128 us
  waiting for transfers between devices  68.1 us (53%)
  starting transfers between devices  35.4 us (27%)
  Pallas kernels  13.8 us (11%)
  local copies, waits for them, and re-layouts  9.43 us (7%)
    all_to_all x1, waiting for transfers between devices, shards(): lax.all_to_all(routed, 'pages', split_axis=0, concat_axis=0, tiled=True)  27.9 us
    all_to_all x1, waiting for transfers between devices, shards(): lax.all_to_all(outbox, 'pages', split_axis=0, concat_axis=0, tiled=True)  21.9 us
    all_to_all x1, starting transfers between devices, shards(): lax.all_to_all(outbox, 'pages', split_axis=0, concat_axis=0, tiled=True)  13.2 us
    all_to_all x1, waiting for transfers between devices, shards(): lax.all_to_all(weighted, 'pages', split_axis=0, concat_axis=0, tiled=True)  9.68 us
    all_to_all x1, starting transfers between devices, shards(): lax.all_to_all(contrib, 'pages', split_axis=0, concat_axis=0, tiled=True)  8.59 us
    all_to_all x1, starting transfers between devices, shards(): lax.all_to_all(weighted, 'pages', split_axis=0, concat_axis=0, tiled=True)  6.19 us
    unnamed x16, local copies, waits for them, and re-layouts  6.03 us
    all_to_all x1, waiting for transfers between devices, shards(): lax.all_to_all(contrib, 'pages', split_axis=0, concat_axis=0, tiled=True)  5.67 us
  transfers between devices with their start and end apart: 5, of which 5 were waited for; matrix products, arithmetic and copies ran while one was open for 2% of the time, Pallas kernels for 2%

profile of v1, /device:TPU:1, one launch (start us, length us, event | category | flops | bytes accessed | tf_op | source)
XLA Modules:
  0.0 127.8 jit_solution(17723828296831487613)
XLA Ops:
  0.6 0.0 copy-start.4
  0.6 0.7 copy-done.4
  1.3 0.0 copy-start.3
  1.3 0.0 copy-start.6
  1.3 0.1 copy.27
  1.4 0.6 copy-done.3
  2.0 0.0 copy-done.6
  2.0 0.6 pad.8.table_ref
  2.6 0.6 pad.9.keep_ref
  3.2 1.6 %copy.31 = bf16[64,2,512]{2,0,1:T(8,128)(2,1)} copy(bf16[64,2,512]{2,1,0:T(2,128)(2,1)} %param.20) | data formatting | bytes 262144 | tf_op args[7]
  4.8 4.1 %source.1 = bf16[64,48,128]{2,1,0:T(8,128)(2,1)} custom-call(s32[1]{0:T(128)} %bitcast.my_ref, s32[16,128]{1,0:T(8,128)} %pad.8.table_ref, s32[32,8]{1,0:T(8,128)} %pad.9.keep_ref, s32[8,128]{1,0:T(8,128)} %drop_ref.1, bf16[8,128,512]{2,1,0:T(8,128)(2,1)} %k_ref.1, bf16[8,128,512]{2,1,0:T(8,128)(2,1)} %v_ref.1, bf16[2,64,512]{2,1,0:T(8,128)(2,1)} %bitcast.9, ...), custom_call_target="tpu_custom_call" | custom-call | tf_op jit(solution)/shard_map/source/pallas_call | solution.py:219
  8.9 13.2 %all-to-all-start = ((bf16[64,48,128]{2,1,0:T(8,128)(2,1)}), bf16[64,48,128]{2,1,0:T(8,128)(2,1)S(1)}, u32[]{:S(2)}, u32[]{:S(2)}) async-start(bf16[64,48,128]{2,1,0:T(8,128)(2,1)} %source.1), calls=%async_computation | async-start | bytes 1572864 | tf_op jit(solution)/shard_map/all_to_all | solution.py:231
  22.0 0.0 copy-start.5
  22.1 0.1 copy.24
  22.2 0.6 copy-done.5
  22.7 0.1 copy.23
  22.8 0.1 eq.19
  23.0 0.1 add.29
  23.1 0.1 copy.25
  23.1 21.9 %all-to-all-done.low_ref.high_ref.got_ref = bf16[64,48,128]{2,1,0:T(8,128)(2,1)S(1)} async-done(((bf16[64,48,128]{2,1,0:T(8,128)(2,1)}), bf16[64,48,128]{2,1,0:T(8,128)(2,1)S(1)}, u32[]{:S(2)}, u32[]{:S(2)}) %all-to-all-start) | async-done | bytes 786464 | tf_op jit(solution)/shard_map/all_to_all | solution.py:231
  45.0 0.0 copy-start
  45.0 0.9 copy-done
  45.9 2.1 %home.1 = bf16[64,4,128]{2,1,0:T(4,128)(2,1)} custom-call(s32[1]{0:T(128)} %bitcast.my_ref, s32[2,64]{1,0:T(2,128)} %bitcast.12, f32[1,8]{1,0:T(1,128)} %logit_ref.1, bf16[64,48,128]{2,1,0:T(8,128)(2,1)} %copy-done), custom_call_target="tpu_custom_call" | custom-call | tf_op jit(solution)/shard_map/home/pallas_call | solution.py:234
  48.0 6.2 %all-to-all-start.2 = ((bf16[64,4,128]{2,1,0:T(4,128)(2,1)}), bf16[64,4,128]{2,1,0:T(4,128)(2,1)S(1)}, u32[]{:S(2)}, u32[]{:S(2)}) async-start(bf16[64,4,128]{2,1,0:T(4,128)(2,1)} %home.1), calls=%async_computation.2 | async-start | bytes 131072 | tf_op jit(solution)/shard_map/all_to_all | solution.py:247
  54.2 0.1 iota_compare_fusion
  54.3 9.7 %all-to-all-done.2.got_ref = bf16[64,4,128]{2,1,0:T(4,128)(2,1)S(1)} async-done(((bf16[64,4,128]{2,1,0:T(4,128)(2,1)}), bf16[64,4,128]{2,1,0:T(4,128)(2,1)S(1)}, u32[]{:S(2)}, u32[]{:S(2)}) %all-to-all-start.2) | async-done | bytes 65568 | tf_op jit(solution)/shard_map/all_to_all | solution.py:247
  64.0 0.0 copy-start.2
  64.0 0.6 copy-done.2
  64.7 1.9 %project.1 = f32[64,2,128]{2,1,0:T(2,128)} custom-call(bf16[64,4,128]{2,1,0:T(4,128)(2,1)} %copy-done.2, bf16[1,512,256]{2,1,0:T(8,128)(2,1)} %w_ref.1), custom_call_target="tpu_custom_call" | custom-call | tf_op jit(solution)/shard_map/project/pallas_call | solution.py:270
  66.6 2.8 %collective-permute-start = (f32[64,2,128]{2,1,0:T(2,128)}, f32[64,2,128]{2,1,0:T(2,128)}, u32[]{:S(2)}, u32[]{:S(2)}) collective-permute-start(f32[64,2,128]{2,1,0:T(2,128)} %project.1), channel_id=1, source_target_pairs={{0,0},{1,4},{2,8},{3,12},{4,16},{5,20},{6,24},{7,28},{8,1},{9,5},{... | collective-permute-start | bytes 196616 | tf_op jit(solution)/shard_map/ppermute | solution.py:286
  69.4 0.2 select_reduce_fusion
  69.6 2.9 %collective-permute-done = f32[64,2,128]{2,1,0:T(2,128)} collective-permute-done((f32[64,2,128]{2,1,0:T(2,128)}, f32[64,2,128]{2,1,0:T(2,128)}, u32[]{:S(2)}, u32[]{:S(2)}) %collective-permute-start) | collective-permute-done | bytes 65568 | tf_op jit(solution)/shard_map/ppermute | solution.py:286
  72.5 8.6 %all-to-all-start.3 = ((f32[64,2,128]{2,1,0:T(2,128)}), f32[64,2,128]{2,1,0:T(2,128)S(1)}, u32[]{:S(2)}, u32[]{:S(2)}) async-start(f32[64,2,128]{2,1,0:T(2,128)} %collective-permute-done), calls=%async_computation.3 | async-start | bytes 131072 | tf_op jit(solution)/shard_map/all_to_all | solution.py:287
  81.1 0.1 copy.26
  81.2 1.0 sub.15.source_ref
  82.2 3.0 %relay.1 = bf16[64,16,512]{2,1,0:T(8,128)(2,1)} custom-call(s32[1024,1]{1,0:T(8,128)} %sub.15.source_ref, bf16[64,48,128]{2,1,0:T(8,128)(2,1)} %copy-done, bf16[64,48,128]{2,1,0:T(8,128)(2,1)} %copy-done), custom_call_target="tpu_custom_call" | custom-call | tf_op jit(solution)/shard_map/relay/pallas_call | solution.py:256
  85.2 5.7 %all-to-all-done.3 = f32[64,2,128]{2,1,0:T(2,128)S(1)} async-done(((f32[64,2,128]{2,1,0:T(2,128)}), f32[64,2,128]{2,1,0:T(2,128)S(1)}, u32[]{:S(2)}, u32[]{:S(2)}) %all-to-all-start.3) | async-done | bytes 65568 | tf_op jit(solution)/shard_map/all_to_all | solution.py:287
  90.8 4.6 %all-to-all-start.1 = ((bf16[64,16,512]{2,1,0:T(8,128)(2,1)}), bf16[64,16,512]{2,1,0:T(8,128)(2,1)S(1)}, u32[]{:S(2)}, u32[]{:S(2)}) async-start(bf16[64,16,512]{2,1,0:T(8,128)(2,1)} %relay.1), calls=%async_computation.1 | async-start | bytes 2097152 | tf_op jit(solution)/shard_map/all_to_all | solution.py:291
  95.6 0.6 convert_element_type.15
  96.1 27.9 %all-to-all-done.1.got_ref = bf16[64,16,512]{2,1,0:T(8,128)(2,1)S(1)} async-done(((bf16[64,16,512]{2,1,0:T(8,128)(2,1)}), bf16[64,16,512]{2,1,0:T(8,128)(2,1)S(1)}, u32[]{:S(2)}, u32[]{:S(2)}) %all-to-all-start.1) | async-done | bytes 1048608 | tf_op jit(solution)/shard_map/all_to_all | solution.py:291
  124.1 0.0 copy-start.1
  124.1 1.0 copy-done.1
  125.0 2.7 %land.1 = (bf16[4,128,512]{2,1,0:T(8,128)(2,1)}, bf16[4,128,512]{2,1,0:T(8,128)(2,1)}) custom-call(bf16[64,16,512]{2,1,0:T(8,128)(2,1)} %copy-done.1), custom_call_target="tpu_custom_call" | custom-call | tf_op jit(solution)/shard_map/land/pallas_call | solution.py:293
  (6 shorter events, 0.1 us)
Async XLA Ops:
  0.6 0.7 copy-start.4
  1.3 0.7 copy-start.3
  1.3 0.7 copy-start.6
  8.9 36.1 %all-to-all-start = ((bf16[64,48,128]{2,1,0:T(8,128)(2,1)}), bf16[64,48,128]{2,1,0:T(8,128)(2,1)S(1)}, u32[]{:S(2)}, u32[]{:S(2)}) async-start(bf16[64,48,128]{2,1,0:T(8,128)(2,1)} %source.1), calls=%async_computation | async-start | bytes 1572864 | tf_op jit(solution)/shard_map/all_to_all | solution.py:231
  22.0 0.7 copy-start.5
  45.0 0.9 copy-start
  48.0 16.0 %all-to-all-start.2 = ((bf16[64,4,128]{2,1,0:T(4,128)(2,1)}), bf16[64,4,128]{2,1,0:T(4,128)(2,1)S(1)}, u32[]{:S(2)}, u32[]{:S(2)}) async-start(bf16[64,4,128]{2,1,0:T(4,128)(2,1)} %home.1), calls=%async_computation.2 | async-start | bytes 131072 | tf_op jit(solution)/shard_map/all_to_all | solution.py:247
  64.0 0.6 copy-start.2
  66.6 5.9 %collective-permute-start = (f32[64,2,128]{2,1,0:T(2,128)}, f32[64,2,128]{2,1,0:T(2,128)}, u32[]{:S(2)}, u32[]{:S(2)}) collective-permute-start(f32[64,2,128]{2,1,0:T(2,128)} %project.1), channel_id=1, source_target_pairs={{0,0},{1,4},{2,8},{3,12},{4,16},{5,20},{6,24},{7,28},{8,1},{9,5},{... | collective-permute-start | bytes 196616 | tf_op jit(solution)/shard_map/ppermute | solution.py:286
  72.5 18.4 %all-to-all-start.3 = ((f32[64,2,128]{2,1,0:T(2,128)}), f32[64,2,128]{2,1,0:T(2,128)S(1)}, u32[]{:S(2)}, u32[]{:S(2)}) async-start(f32[64,2,128]{2,1,0:T(2,128)} %collective-permute-done), calls=%async_computation.3 | async-start | bytes 131072 | tf_op jit(solution)/shard_map/all_to_all | solution.py:287
  90.8 33.2 %all-to-all-start.1 = ((bf16[64,16,512]{2,1,0:T(8,128)(2,1)}), bf16[64,16,512]{2,1,0:T(8,128)(2,1)S(1)}, u32[]{:S(2)}, u32[]{:S(2)}) async-start(bf16[64,16,512]{2,1,0:T(8,128)(2,1)} %relay.1), calls=%async_computation.1 | async-start | bytes 2097152 | tf_op jit(solution)/shard_map/all_to_all | solution.py:291
  124.1 1.0 copy-start.1

commit v2 on v1

v2 whole, which is shorter than its diff:
```python
import math

import jax
import jax.numpy as jnp
from jax import lax
from jax.experimental import pallas as pl
from jax.experimental.pallas import tpu as pltpu
from jax.sharding import PartitionSpec as P

HD = 128
EXPERTS = 8
NEGATIVE = -1e30
F32 = jnp.float32
BF16 = jnp.bfloat16
VMEM = pl.BlockSpec(memory_space=pltpu.VMEM)
SMEM = pl.BlockSpec(memory_space=pltpu.SMEM)
NT = (((1,), (1,)), ((), ()))


def iota(shape, dim):
    return lax.broadcasted_iota(jnp.int32, shape, dim)


def dot(a, b):
    return jnp.dot(a, b, preferred_element_type=F32)


def source_kernel(
    my_ref,
    table_ref,
    count_ref,
    ids_ref,
    keep_ref,
    drop_ref,
    k_ref,
    v_ref,
    q_ref,
    nk_ref,
    nv_ref,
    logit_ref,
    out_ref,
    kb,
    vb,
    keep_rows,
    q_rows,
):
    my = my_ref[0]
    slots, page_len, width = k_ref.shape
    keep_count = keep_ref.shape[1]
    rows = keep_count + 1
    heads = width // HD
    reqs, topk, _ = q_ref.shape
    keep_rows[...] = jnp.full(keep_rows.shape, -1.0, F32)
    keep_rows[:, 0:keep_count] = keep_ref[...].astype(F32)
    keep_columns = keep_rows[...].T[0:rows, :].astype(jnp.int32)
    q_rows[...] = q_ref[...].astype(F32)
    lane = iota((rows, page_len), 1)
    last = iota((rows, page_len), 0) == rows - 1
    for g in range(slots):
        onehot = jnp.where(keep_columns[:, g : g + 1] == lane, 1.0, 0.0)
        kept = jnp.max(onehot, axis=0, keepdims=True)
        coef = jnp.where(kept > 0.0, 0.0, drop_ref[g : g + 1, :].astype(F32))
        total = jnp.sum(coef, axis=1, keepdims=True)
        mat = jnp.where(last, coef, onehot).astype(BF16)
        denom = jnp.where(last[:, 0:1], total, 1.0)
        kb[g * rows : (g + 1) * rows, :] = (dot(mat, k_ref[g]) / denom).astype(BF16)
        vb[g * rows : (g + 1) * rows, :] = (dot(mat, v_ref[g]) / denom).astype(BF16)
    n = slots * rows
    to = iota((n, n), 0)
    fro = iota((n, n), 1)
    perm = jnp.where((to % slots == fro // rows) & (to // slots == fro % rows), 1.0, 0.0).astype(BF16)
    for base, blocks in ((0, kb), (rows, vb)):
        spread = dot(perm, blocks[...])
        for t in range(heads):
            out_ref[base : base + rows, t * slots : (t + 1) * slots, :] = (
                spread[:, t * HD : (t + 1) * HD].reshape(rows, slots, HD).astype(BF16)
            )
    ent = 2 * slots
    ent_row = iota((ent, reqs), 0)
    req_lane = iota((ent, reqs), 1)
    sel = jnp.where((ent_row == slots) & (req_lane == my), 1.0, 0.0)
    in_use = iota(table_ref.shape, 0) < count_ref[...]
    table = jnp.where(in_use, table_ref[...], -1)
    for g in range(slots):
        hit = jnp.where(table == my * slots + g, 1.0, 0.0)
        sel = jnp.where(ent_row == g, jnp.max(hit, axis=0, keepdims=True), sel)
    sel_b = sel.astype(BF16)
    same = lax.dot_general(sel_b, sel_b, NT, preferred_element_type=F32)
    q_lane = iota((ent, width), 1) // HD
    pieces = []
    for k in range(topk):
        group_query = dot(sel_b, q_rows[:, k, :].astype(BF16))
        for h in range(heads):
            pieces.append(jnp.where(q_lane == h, group_query, 0.0))
    queries = jnp.concatenate(pieces, axis=0)
    kh = topk * heads
    scale = 1.0 / math.sqrt(HD)
    scores = lax.dot_general(queries.astype(BF16), kb[...], NT, preferred_element_type=F32) * scale
    col = iota((kh * ent, n), 1)
    scores = scores + jnp.where(col % rows == rows - 1, math.log(page_len - rows + 1), 0.0)
    of_page = jnp.where(iota((ent, n), 1) // rows == iota((ent, n), 0), 1.0, 0.0).astype(BF16)
    shared = dot(same.astype(BF16), of_page)
    mask = jnp.concatenate([shared] * kh, axis=0) > 0.5
    scores = jnp.where(mask, scores, NEGATIVE)
    is_own = iota((kh * ent, 1), 0) % ent == slots
    own = jnp.sum(queries * nk_ref[...].astype(F32), axis=1, keepdims=True) * scale
    own = jnp.where(is_own, own, NEGATIVE)
    peak = jnp.maximum(jnp.max(scores, axis=1, keepdims=True), own)
    shift = peak.astype(BF16).astype(F32)
    probs = jnp.where(mask, jnp.exp(scores - shift), 0.0)
    own_prob = jnp.where(is_own, jnp.exp(own - shift), 0.0)
    den = jnp.sum(probs, axis=1, keepdims=True) + own_prob
    num = dot(probs.astype(BF16), vb[...])
    num = num + own_prob.astype(BF16).astype(F32) * nv_ref[...].astype(F32)
    high = den.astype(BF16).astype(F32)
    low = den - high
    er = iota((ent, ent), 0)
    ec = iota((ent, ent), 1)
    before = jnp.sum(jnp.where((ec < er) | (ec == slots), same, 0.0), axis=1, keepdims=True)
    row = ent_row[:, 0:1]
    first = (row == slots) | ((row < slots) & (before < 0.5))
    request = jnp.sum(jnp.where(sel > 0.5, req_lane.astype(F32), 0.0), axis=1, keepdims=True)
    expert = [
        jnp.sum(jnp.where(sel > 0.5, ids_ref[k : k + 1, :].astype(F32), 0.0), axis=1, keepdims=True)
        for k in range(topk)
    ]
    expert_lane = iota((1, EXPERTS), 1).astype(F32)
    logit = [
        jnp.sum(
            jnp.where(expert_lane == expert[k][slots : slots + 1, :], logit_ref[...], 0.0),
            axis=1,
            keepdims=True,
        )
        for k in range(topk)
    ]
    top = logit[0]
    for k in range(1, topk):
        top = jnp.maximum(top, logit[k])
    terms = [jnp.exp(logit[k] - top) for k in range(topk)]
    term_sum = terms[0]
    for k in range(1, topk):
        term_sum = term_sum + terms[k]
    stat_lane = iota((ent, HD), 1)
    by_choice = []
    for k in range(topk):
        gate = jnp.where(row == slots, terms[k] / term_sum, 0.0)
        gate_high = gate.astype(BF16).astype(F32)
        stats = jnp.where(stat_lane == 3 * heads, gate_high, 0.0)
        stats = jnp.where(stat_lane == 3 * heads + 1, gate - gate_high, stats)
        stats = jnp.where(stat_lane == 3 * heads + 2, request, stats)
        lanes = []
        for h in range(heads):
            at = slice((k * heads + h) * ent, (k * heads + h + 1) * ent)
            lanes.append(num[at, h * HD : (h + 1) * HD])
            for i, stat in enumerate((shift, high, low)):
                stats = jnp.where(stat_lane == 3 * h + i, stat[at, :], stats)
        by_choice.append(jnp.concatenate(lanes + [stats], axis=1))
    parts = []
    for e in range(EXPERTS):
        part = jnp.zeros(by_choice[0].shape, F32)
        for k in range(topk):
            part = jnp.where(first & (expert[k] == e), by_choice[k], part)
        parts.append(part)
    entries = jnp.concatenate(parts, axis=0).astype(BF16)
    columns = out_ref.shape[0] // EXPERTS
    cut = width // columns
    at = iota((width + HD, columns * HD), 1)
    l = at % HD
    j = at // HD
    head_stat = width + (j * cut // HD) * 3 + l - cut
    rest_stat = width + 3 * heads + l - cut - 3
    origin = jnp.where(l < cut, j * cut + l, jnp.where(l < cut + 3, head_stat, rest_stat))
    origin = jnp.where(l < cut + 6, origin, -1)
    choose = jnp.where(iota(at.shape, 0) == origin, 1.0, 0.0).astype(BF16)
    sent = dot(entries, choose).astype(BF16)
    for e in range(EXPERTS):
        for j in range(columns):
            out_ref[e * columns + j, heads * slots :, :] = sent[
                e * ent : (e + 1) * ent, j * HD : (j + 1) * HD
            ]


def expert_kernel(at_ref, got_ref, *refs):
    columns = got_ref.shape[0] // EXPERTS
    w_refs, out_refs, (stack,) = refs[:columns], refs[columns:-1], refs[-1:]
    j = at_ref[0]
    s = at_ref[1]
    reqs, ent, _ = got_ref.shape
    cut = w_refs[0].shape[0]
    for d in range(columns):
        stack[d] = w_refs[d][...]
    v = got_ref[...].astype(F32).reshape(reqs * ent, HD)
    lane = iota(v.shape, 1)
    shift = v[:, cut : cut + 1]
    den = v[:, cut + 1 : cut + 2] + v[:, cut + 2 : cut + 3]
    request = v[:, cut + 5 : cut + 6]
    live = den > 0.0
    owns = (request == lane.astype(F32)) & live
    peak = jnp.max(jnp.where(owns, shift, NEGATIVE), axis=0, keepdims=True)
    peak = jnp.sum(jnp.where(owns, peak, 0.0), axis=1, keepdims=True)
    factor = jnp.where(live, jnp.exp(shift - peak), 0.0)
    scaled = jnp.where((lane < cut + 3), v * factor, v)
    high = scaled.astype(BF16)
    low = (scaled - high.astype(F32)).astype(BF16)
    pick = jnp.where(owns, 1.0, 0.0).astype(BF16)
    TN = (((0,), (0,)), ((), ()))
    x = lax.dot_general(pick, high, TN, preferred_element_type=F32)
    x = x + lax.dot_general(pick, low, TN, preferred_element_type=F32)
    x = x[:reqs]
    den = x[:, cut + 1 : cut + 2] + x[:, cut + 2 : cut + 3]
    gate = x[:, cut + 3 : cut + 4] + x[:, cut + 4 : cut + 5]
    some = den > 0.0
    weighted = jnp.where(some, gate * (x / jnp.where(some, den, 1.0)), 0.0)[:, :cut].astype(BF16)
    per = columns // len(out_refs)
    for t, out_ref in enumerate(out_refs):
        for i in range(per):
            c = lax.rem(s + t, len(out_refs)) * per + i
            out_ref[i] = dot(weighted, stack[c ^ j]).astype(out_ref.dtype)


def gather_kernel(*refs):
    out_ref = refs[-1]
    per = refs[0].shape[0]
    tiles = out_ref.shape[1] // per
    for i in range(per):
        total = refs[0][i].astype(F32)
        for ref in refs[1:-1]:
            total = total + ref[i].astype(F32)
        for t in range(tiles):
            out_ref[:, i * tiles + t, :] = total[:, t * HD : (t + 1) * HD]


def route_kernel(new_ref, table_ref, count_ref, out_ref):
    max_new = new_ref.shape[0]
    per_new = table_ref.shape[0] // max_new
    shape = (out_ref.shape[0], new_ref.shape[1])
    slot = iota(shape, 0) // per_new
    quarter = iota(shape, 0) % per_new
    found = jnp.zeros(shape, jnp.int32)
    for i in range(max_new):
        filled = jnp.where(i * per_new < count_ref[...], new_ref[i : i + 1, :], -1)
        page = jnp.zeros(shape, jnp.int32)
        for w in range(per_new):
            page = jnp.where(quarter == w, table_ref[i * per_new + w : i * per_new + w + 1, :] + 1, page)
        found = jnp.where(filled == slot, page, found)
    out_ref[...] = jnp.sum(found, axis=1, keepdims=True) - 1


def relay_kernel(source_ref, low_ref, high_ref, out_ref):
    devices, per, _ = low_ref.shape
    slots = per // 2
    held = devices * slots
    tiles = []
    for ref in (low_ref, high_ref):
        for t in range(2):
            rows = ref[:, t * slots : (t + 1) * slots, :].astype(F32)
            tiles.append(rows.reshape(held, HD).astype(BF16))
    table = jnp.concatenate(tiles, axis=1)
    local = out_ref.shape[1]
    step = 16
    for c in range(0, devices, step):
        source = source_ref[c * local : (c + step) * local, :]
        pick = jnp.where(source == iota((step * local, held), 1), 1.0, 0.0).astype(BF16)
        out_ref[c : c + step] = dot(pick, table).reshape(step, local, table.shape[1]).astype(BF16)


def land_kernel(got_ref, k_ref, v_ref):
    total, local, width = got_ref.shape
    rows = total // 2
    n = rows * local
    to = iota((n, n), 0)
    fro = iota((n, n), 1)
    perm = jnp.where((to // rows == fro % local) & (to % rows == fro // local), 1.0, 0.0).astype(BF16)
    for base, ref in ((0, k_ref), (rows, v_ref)):
        flat = got_ref[base : base + rows].reshape(n, width)
        ref[...] = dot(perm, flat).reshape(ref.shape).astype(BF16)


def shards(
    old_keys,
    old_values,
    keep_lists,
    drop_weights,
    request_pages,
    page_table,
    new_table,
    queries,
    new_keys,
    new_values,
    expert_ids,
    router_logits,
    out_weight,
):
    devices = lax.axis_size("pages")
    shard_count = lax.axis_size("expert")
    my = lax.axis_index("pages").astype(jnp.int32)
    shard = lax.axis_index("expert").astype(jnp.int32)
    slots, page_len, width = old_keys.shape
    rows = keep_lists.shape[1] + 1
    per_new = page_len // rows
    requests, max_pages = page_table.shape
    new_cap = 2 * (slots // per_new)
    local = new_cap * per_new
    heads = width // HD
    topk = queries.shape[1]
    ent = 2 * slots
    chunk = heads * slots + ent
    columns = devices // EXPERTS
    cut = width // columns
    place = lax.rem(my, columns)
    table = page_table.T
    counts = request_pages.reshape(1, -1)

    outbox = pl.pallas_call(
        source_kernel,
        out_shape=jax.ShapeDtypeStruct((devices, chunk, HD), BF16),
        in_specs=[SMEM] + [VMEM] * 11,
        out_specs=VMEM,
        scratch_shapes=[
            pltpu.VMEM((slots * rows, width), BF16),
            pltpu.VMEM((slots * rows, width), BF16),
            pltpu.VMEM((slots, HD), F32),
            pltpu.VMEM((requests, topk, width), F32),
        ],
        name="source",
    )(
        my.reshape(1),
        table,
        counts,
        expert_ids.T,
        keep_lists,
        drop_weights,
        old_keys,
        old_values,
        queries,
        new_keys,
        new_values,
        router_logits,
    )
    inbox = lax.all_to_all(outbox, "pages", split_axis=0, concat_axis=0, tiled=True)

    weight, _ = lax.optimization_barrier((out_weight[0], outbox))
    weight_rows = []
    for d in range(columns):
        piece = lax.dynamic_slice_in_dim(weight, (place ^ d) * cut, cut, 0)
        if d:
            swap = [(p, p // columns * columns + (p % columns ^ d)) for p in range(devices)]
            piece = lax.ppermute(piece, "pages", swap)
        weight_rows.append(piece)
    table, weight_rows = lax.optimization_barrier((table, weight_rows))

    source = pl.pallas_call(
        route_kernel,
        out_shape=jax.ShapeDtypeStruct((devices * local, 1), jnp.int32),
        in_specs=[VMEM] * 3,
        out_specs=VMEM,
        name="route",
    )(new_table.T, table, counts)
    routed = pl.pallas_call(
        relay_kernel,
        grid=(1,),
        out_shape=jax.ShapeDtypeStruct((devices, local, width), BF16),
        in_specs=[
            VMEM,
            pl.BlockSpec((devices, 2 * slots, HD), lambda i: (0, 0, 0)),
            pl.BlockSpec((devices, 2 * slots, HD), lambda i: (0, 1, 0)),
        ],
        out_specs=VMEM,
        name="relay",
    )(source, inbox, inbox)
    landed = lax.all_to_all(routed, "pages", split_axis=0, concat_axis=0, tiled=True)

    inbox, _ = lax.optimization_barrier((inbox, routed))
    per = columns // shard_count
    block_cols = out_weight.shape[2]
    contribs = pl.pallas_call(
        expert_kernel,
        grid=(1,),
        out_shape=[jax.ShapeDtypeStruct((per, requests, block_cols), BF16)] * shard_count,
        in_specs=[
            SMEM,
            pl.BlockSpec((devices, ent, HD), lambda i: (0, heads * slots // ent, 0)),
        ]
        + [VMEM] * columns,
        out_specs=[VMEM] * shard_count,
        scratch_shapes=[pltpu.VMEM((columns, cut, block_cols), BF16)],
        name="expert",
    )(jnp.stack([place, shard]), inbox, *weight_rows)
    moved = [contribs[0]]
    for t in range(1, shard_count):
        moved.append(
            lax.ppermute(contribs[t], "expert", [(i, (i + t) % shard_count) for i in range(shard_count)])
        )
    summed = pl.pallas_call(
        gather_kernel,
        out_shape=jax.ShapeDtypeStruct((requests, per * block_cols // HD, HD), F32),
        in_specs=[VMEM] * shard_count,
        out_specs=VMEM,
        name="gather",
    )(*moved)
    summed, landed = lax.optimization_barrier((summed, landed))
    parts = lax.all_to_all(summed, "pages", split_axis=0, concat_axis=0, tiled=True)
    mixed = jnp.sum(parts, axis=0).reshape(1, -1).astype(BF16)

    new_page = jax.ShapeDtypeStruct((new_cap, per_new * rows, width), BF16)
    compact_keys, compact_values = pl.pallas_call(
        land_kernel,
        out_shape=(new_page, new_page),
        in_specs=[VMEM],
        out_specs=(VMEM, VMEM),
        name="land",
    )(landed)
    return (compact_keys, compact_values, mixed)


def solution(mesh):
    in_specs = (
        P("pages", None, "expert"),
        P("pages", None, "expert"),
        P("pages", None),
        P("pages", None),
        P(),
        P(),
        P(),
        P(None, None, "expert"),
        P("pages", "expert"),
        P("pages", "expert"),
        P(),
        P("pages", None),
        P("pages", "expert", None),
    )
    out_specs = (P("pages", None, "expert"), P("pages", None, "expert"), P("pages", "expert"))
    return jax.shard_map(shards, mesh=mesh, in_specs=in_specs, out_specs=out_specs, check_vma=False)
```

time: 129 us -> 106 us (0.82)
  waiting for transfers between devices: 68.1 us -> 40.1 us
  starting transfers between devices: 35.4 us -> 43.5 us
  local copies, waits for them, and re-layouts: 9.43 us -> 2.75 us
  Pallas kernels: 13.8 us -> 17.3 us
    all_to_all x1, waiting for transfers between devices: 21.9 us -> 0.01 us  [shards(): lax.all_to_all(outbox, 'pages', split_axis=0, concat_axis=0, tiled=True)]
    ppermute x1 -> x10, waiting for transfers between devices: 2.9 us -> 17.5 us  [the longest x7 15 us: shards(): piece = lax.ppermute(piece, 'pages', swap)]
    all_to_all x1, waiting for transfers between devices: 27.9 us -> 15 us  [shards(): lax.all_to_all(routed, 'pages', split_axis=0, concat_axis=0, tiled=True)]
    ppermute x1 -> x10, starting transfers between devices: 2.8 us -> 15 us  [the longest x7 10.2 us: shards(): piece = lax.ppermute(piece, 'pages', swap)]
    all_to_all x2 -> x1, starting transfers between devices: 14.8 us -> 6.19 us  [shards(): lax.all_to_all(summed, 'pages', split_axis=0, concat_axis=0, tiled=True)]
    all_to_all x2 -> x1, waiting for transfers between devices: 15.4 us -> 7.62 us  [shards(): lax.all_to_all(summed, 'pages', split_axis=0, concat_axis=0, tiled=True)]
    all_to_all x1, starting transfers between devices: 4.65 us -> 9.03 us  [shards(): lax.all_to_all(routed, 'pages', split_axis=0, concat_axis=0, tiled=True)]
    unnamed x16 -> x27, local copies, waits for them, and re-layouts: 6.03 us -> 2.12 us
  transfers between devices with their start and end apart: 5 -> 13, of which waited for: 5 -> 7; matrix products, arithmetic and copies ran while one was open for 2% -> 1% of each run, Pallas kernels for 2% -> 9%
where the time goes in v2:
time: 106 us; the launch traced here: 105 us
  starting transfers between devices  43.5 us (41%)
  waiting for transfers between devices  40.1 us (38%)
  Pallas kernels  17.3 us (16%)
  local copies, waits for them, and re-layouts  2.75 us (3%)
    all_to_all x1, waiting for transfers between devices, shards(): lax.all_to_all(routed, 'pages', split_axis=0, concat_axis=0, tiled=True)  15 us
    ppermute x7, waiting for transfers between devices, shards(): piece = lax.ppermute(piece, 'pages', swap)  15 us
    all_to_all x1, starting transfers between devices, shards(): lax.all_to_all(outbox, 'pages', split_axis=0, concat_axis=0, tiled=True)  13.3 us
    ppermute x7, starting transfers between devices, shards(): piece = lax.ppermute(piece, 'pages', swap)  10.2 us
    all_to_all x1, starting transfers between devices, shards(): lax.all_to_all(routed, 'pages', split_axis=0, concat_axis=0, tiled=True)  9.03 us
    all_to_all x1, waiting for transfers between devices, shards(): lax.all_to_all(summed, 'pages', split_axis=0, concat_axis=0, tiled=True)  7.62 us
    all_to_all x1, starting transfers between devices, shards(): lax.all_to_all(summed, 'pages', split_axis=0, concat_axis=0, tiled=True)  6.19 us
    ppermute x3, starting transfers between devices, shards(): lax.ppermute(contribs[t], 'expert', [(i, (i + t) % shard_count) for i in...  4.81 us
  transfers between devices with their start and end apart: 13, of which 7 were waited for; matrix products, arithmetic and copies ran while one was open for 1% of the time, Pallas kernels for 9%

profile of v2, /device:TPU:1, one launch (start us, length us, event | category | flops | bytes accessed | tf_op | source)
XLA Modules:
  0.0 105.2 jit_solution(15640594100362416465)
XLA Ops:
  0.6 4.4 %source.1 = bf16[64,48,128]{2,1,0:T(8,128)(2,1)} custom-call(s32[1]{0:T(128)} %bitcast.2.my_ref, s32[12,64]{1,0:T(8,128)} %bitcast.16, s32[1,64]{1,0:T(1,128)} %bitcast.20, s32[2,64]{1,0:T(2,128)} %bitcast.23, s32[8,31]{1,0:T(8,128)} %keep_ref.1, s32[8,128]{1,0:T(8,128)} %drop_ref.1, bf16[8,128,512]{2,1,0:T(8,128)(2,1)} %k_ref.1, ...), custom_call_target="tpu_custom_call" | custom-call | tf_op jit(solution)/shard_map/source/pallas_call | solution.py:314
  5.0 13.3 %all-to-all-start = ((bf16[64,48,128]{2,1,0:T(8,128)(2,1)}), bf16[64,48,128]{2,1,0:T(8,128)(2,1)S(1)}, u32[]{:S(2)}, u32[]{:S(2)}) async-start(bf16[64,48,128]{2,1,0:T(8,128)(2,1)} %source.1), calls=%async_computation | async-start | bytes 1572864 | tf_op jit(solution)/shard_map/all_to_all | solution.py:340
  18.4 0.0 copy-done.2
  18.4 0.6 constant_dynamic-slice_fusion
  19.0 3.4 %collective-permute-start.6 = (bf16[64,256]{1,0:T(8,128)(2,1)S(1)}, bf16[64,256]{1,0:T(8,128)(2,1)S(1)}, u32[]{:S(2)}, u32[]{:S(2)}) collective-permute-start(bf16[64,256]{1,0:T(8,128)(2,1)S(1)} %get-tuple-element.41), channel_id=1, source_target_pairs={{0,28},{4,24},{8,20},{12,16},{16,12},{20,8},{24,4},{28,0},{32,60},... | collective-permute-start | bytes 98312 | tf_op jit(solution)/shard_map/ppermute | solution.py:348
  22.5 0.2 collective-permute-start.5
  22.6 0.7 collective-permute-start.4
  23.4 1.9 %collective-permute-start.3 = (bf16[64,256]{1,0:T(8,128)(2,1)S(1)}, bf16[64,256]{1,0:T(8,128)(2,1)S(1)}, u32[]{:S(2)}, u32[]{:S(2)}) collective-permute-start(bf16[64,256]{1,0:T(8,128)(2,1)S(1)} %get-tuple-element.44), channel_id=1, source_target_pairs={{0,16},{4,20},{8,24},{12,28},{16,0},{20,4},{24,8},{28,12},{32,48},... | collective-permute-start | bytes 98312 | tf_op jit(solution)/shard_map/ppermute | solution.py:348
  25.2 1.4 %collective-permute-start.2 = (bf16[64,256]{1,0:T(8,128)(2,1)S(1)}, bf16[64,256]{1,0:T(8,128)(2,1)S(1)}, u32[]{:S(2)}, u32[]{:S(2)}) collective-permute-start(bf16[64,256]{1,0:T(8,128)(2,1)S(1)} %get-tuple-element.45), channel_id=1, source_target_pairs={{0,12},{4,8},{8,4},{12,0},{16,28},{20,24},{24,20},{28,16},{32,44},... | collective-permute-start | bytes 98312 | tf_op jit(solution)/shard_map/ppermute | solution.py:348
  26.6 13.3 %collective-permute-done.6.refs_7_ = bf16[64,256]{1,0:T(8,128)(2,1)S(1)} collective-permute-done((bf16[64,256]{1,0:T(8,128)(2,1)S(1)}, bf16[64,256]{1,0:T(8,128)(2,1)S(1)}, u32[]{:S(2)}, u32[]{:S(2)}) %collective-permute-start.6) | collective-permute-done | bytes 32800 | tf_op jit(solution)/shard_map/ppermute | solution.py:348
  39.9 2.6 %collective-permute-start.1 = (bf16[64,256]{1,0:T(8,128)(2,1)S(1)}, bf16[64,256]{1,0:T(8,128)(2,1)S(1)}, u32[]{:S(2)}, u32[]{:S(2)}) collective-permute-start(bf16[64,256]{1,0:T(8,128)(2,1)S(1)} %get-tuple-element.46), channel_id=1, source_target_pairs={{0,8},{4,12},{8,0},{12,4},{16,24},{20,28},{24,16},{28,20},{32,40},... | collective-permute-start | bytes 98312 | tf_op jit(solution)/shard_map/ppermute | solution.py:348
  42.5 0.0 collective-permute-done.5.refs_6_
  42.5 0.0 collective-permute-start
  42.5 1.0 collective-permute-done.4.refs_5_
  43.5 0.0 collective-permute-done.3.refs_4_
  43.5 0.0 collective-permute-done.2.refs_3_
  43.5 0.0 copy-start.10
  43.6 0.7 collective-permute-done.1.refs_2_
  44.2 0.0 collective-permute-done.refs_1_
  44.2 2.2 %route.1.source_ref = s32[1024,1]{1,0:T(8,128)} custom-call(s32[3,64]{1,0:T(4,128)} %bitcast.19, s32[12,64]{1,0:T(8,128)} %bitcast.17, s32[1,64]{1,0:T(1,128)} %bitcast.21), custom_call_target="tpu_custom_call" | custom-call | tf_op jit(solution)/shard_map/route/pallas_call | solution.py:352
  46.4 0.0 copy-done.6
  46.4 0.0 copy-done.7
  46.4 0.0 copy-done.8
  46.4 0.0 copy-done.9
  46.4 0.0 copy-done.10
  46.4 0.0 copy-done.11
  46.5 0.0 all-to-all-done.low_ref.high_ref.got_ref
  46.5 0.9 copy-done
  47.4 3.0 %relay.1 = bf16[64,16,512]{2,1,0:T(8,128)(2,1)} custom-call(s32[1024,1]{1,0:T(8,128)} %route.1.source_ref, bf16[64,48,128]{2,1,0:T(8,128)(2,1)} %copy-done, bf16[64,48,128]{2,1,0:T(8,128)(2,1)} %copy-done), custom_call_target="tpu_custom_call" | custom-call | tf_op jit(solution)/shard_map/relay/pallas_call | solution.py:359
  50.4 9.0 %all-to-all-start.1 = ((bf16[64,16,512]{2,1,0:T(8,128)(2,1)}), bf16[64,16,512]{2,1,0:T(8,128)(2,1)S(1)}, u32[]{:S(2)}, u32[]{:S(2)}) async-start(bf16[64,16,512]{2,1,0:T(8,128)(2,1)} %relay.1), calls=%async_computation.1 | async-start | bytes 2097152 | tf_op jit(solution)/shard_map/all_to_all | solution.py:371
  59.4 0.7 pad_add_fusion.at_ref
  60.1 3.3 %expert.1 = (bf16[2,64,256]{2,1,0:T(8,128)(2,1)}, bf16[2,64,256]{2,1,0:T(8,128)(2,1)}, bf16[2,64,256]{2,1,0:T(8,128)(2,1)}, bf16[2,64,256]{2,1,0:T(8,128)(2,1)}) custom-call(s32[2]{0:T(128)} %pad_add_fusion.at_ref, bf16[64,48,128]{2,1,0:T(8,128)(2,1)} %copy-done, bf16[64,256]{1,0:T(8,128)(2,1)} %get-tuple-element.25.refs_0_, bf16[64,256]{1,0:T(8,128)(2,1)} %copy-done.12, ...), custom_call_target="tpu_custom_call" | custom-call | tf_op jit(solution)/shard_map/expert/pallas_call | solution.py:376
  63.3 1.2 %collective-permute-start.7 = (bf16[2,64,256]{2,1,0:T(8,128)(2,1)}, bf16[2,64,256]{2,1,0:T(8,128)(2,1)S(1)}, u32[]{:S(2)}, u32[]{:S(2)}) collective-permute-start(bf16[2,64,256]{2,1,0:T(8,128)(2,1)} %get-tuple-element.34), channel_id=1, source_target_pairs={{0,1},{1,2},{2,3},{3,0},{4,5},{5,6},{6,7},{7,4},{8,9},{9,10},{10,1... | collective-permute-start | bytes 196616 | tf_op jit(solution)/shard_map/ppermute | solution.py:392
  64.5 2.5 %collective-permute-start.8 = (bf16[2,64,256]{2,1,0:T(8,128)(2,1)}, bf16[2,64,256]{2,1,0:T(8,128)(2,1)S(1)}, u32[]{:S(2)}, u32[]{:S(2)}) collective-permute-start(bf16[2,64,256]{2,1,0:T(8,128)(2,1)} %get-tuple-element.35), channel_id=1, source_target_pairs={{0,2},{1,3},{2,0},{3,1},{4,6},{5,7},{6,4},{7,5},{8,10},{9,11},{10,... | collective-permute-start | bytes 196616 | tf_op jit(solution)/shard_map/ppermute | solution.py:392
  67.0 1.1 %collective-permute-start.9 = (bf16[2,64,256]{2,1,0:T(8,128)(2,1)}, bf16[2,64,256]{2,1,0:T(8,128)(2,1)S(1)}, u32[]{:S(2)}, u32[]{:S(2)}) collective-permute-start(bf16[2,64,256]{2,1,0:T(8,128)(2,1)} %get-tuple-element.36), channel_id=1, source_target_pairs={{0,3},{1,0},{2,1},{3,2},{4,7},{5,4},{6,5},{7,6},{8,11},{9,8},{10,9... | collective-permute-start | bytes 196616 | tf_op jit(solution)/shard_map/ppermute | solution.py:392
  68.1 0.0 collective-permute-done.7.refs_1_
  68.2 2.2 %collective-permute-done.8.refs_2_ = bf16[2,64,256]{2,1,0:T(8,128)(2,1)S(1)} collective-permute-done((bf16[2,64,256]{2,1,0:T(8,128)(2,1)}, bf16[2,64,256]{2,1,0:T(8,128)(2,1)S(1)}, u32[]{:S(2)}, u32[]{:S(2)}) %collective-permute-start.8) | collective-permute-done | bytes 65568 | tf_op jit(solution)/shard_map/ppermute | solution.py:392
  70.4 0.3 collective-permute-done.9.refs_3_
  70.6 0.3 copy-done.4
  71.0 0.3 copy-done.5
  71.3 1.7 %gather.1 = f32[64,4,128]{2,1,0:T(4,128)} custom-call(bf16[2,64,256]{2,1,0:T(8,128)(2,1)} %get-tuple-element.33.refs_0_, bf16[2,64,256]{2,1,0:T(8,128)(2,1)} %copy-done.3, bf16[2,64,256]{2,1,0:T(8,128)(2,1)} %copy-done.4, bf16[2,64,256]{2,1,0:T(8,128)(2,1)} %copy-done.5), custom_call_target="tpu_custom_call" | custom-call | tf_op jit(solution)/shard_map/gather/pallas_call | solution.py:394
  72.9 15.0 %all-to-all-done.1.got_ref = bf16[64,16,512]{2,1,0:T(8,128)(2,1)S(1)} async-done(((bf16[64,16,512]{2,1,0:T(8,128)(2,1)}), bf16[64,16,512]{2,1,0:T(8,128)(2,1)S(1)}, u32[]{:S(2)}, u32[]{:S(2)}) %all-to-all-start.1) | async-done | bytes 1048608 | tf_op jit(solution)/shard_map/all_to_all | solution.py:371
  88.0 6.2 %all-to-all-start.2 = ((f32[64,4,128]{2,1,0:T(4,128)}), f32[64,4,128]{2,1,0:T(4,128)S(1)}, u32[]{:S(2)}, u32[]{:S(2)}) async-start(f32[64,4,128]{2,1,0:T(4,128)} %gather.1), calls=%async_computation.2 | async-start | bytes 262144 | tf_op jit(solution)/shard_map/all_to_all | solution.py:402
  94.2 0.0 copy-done.1
  94.2 2.7 %land.1 = (bf16[4,128,512]{2,1,0:T(8,128)(2,1)}, bf16[4,128,512]{2,1,0:T(8,128)(2,1)}) custom-call(bf16[64,16,512]{2,1,0:T(8,128)(2,1)} %copy-done.1), custom_call_target="tpu_custom_call" | custom-call | tf_op jit(solution)/shard_map/land/pallas_call | solution.py:406
  96.9 7.6 %all-to-all-done.2 = f32[64,4,128]{2,1,0:T(4,128)S(1)} async-done(((f32[64,4,128]{2,1,0:T(4,128)}), f32[64,4,128]{2,1,0:T(4,128)S(1)}, u32[]{:S(2)}, u32[]{:S(2)}) %all-to-all-start.2) | async-done | bytes 131104 | tf_op jit(solution)/shard_map/all_to_all | solution.py:402
  104.5 0.1 reduce_sum.9
  104.6 0.6 copy.18
  (14 shorter events, 0.0 us)
Async XLA Ops:
  5.0 13.3 %copy-start.2 = (bf16[1,512,256]{2,1,0:T(8,128)(2,1)S(1)}, bf16[1,512,256]{2,1,0:T(8,128)(2,1)}, u32[]{:S(2)}) copy-start(bf16[1,512,256]{2,1,0:T(8,128)(2,1)} %param.25) | copy-start | bytes 786436
  5.0 41.4 %all-to-all-start = ((bf16[64,48,128]{2,1,0:T(8,128)(2,1)}), bf16[64,48,128]{2,1,0:T(8,128)(2,1)S(1)}, u32[]{:S(2)}, u32[]{:S(2)}) async-start(bf16[64,48,128]{2,1,0:T(8,128)(2,1)} %source.1), calls=%async_computation | async-start | bytes 1572864 | tf_op jit(solution)/shard_map/all_to_all | solution.py:340
  19.0 20.9 %collective-permute-start.6 = (bf16[64,256]{1,0:T(8,128)(2,1)S(1)}, bf16[64,256]{1,0:T(8,128)(2,1)S(1)}, u32[]{:S(2)}, u32[]{:S(2)}) collective-permute-start(bf16[64,256]{1,0:T(8,128)(2,1)S(1)} %get-tuple-element.41), channel_id=1, source_target_pairs={{0,28},{4,24},{8,20},{12,16},{16,12},{20,8},{24,4},{28,0},{32,60},... | collective-permute-start | bytes 98312 | tf_op jit(solution)/shard_map/ppermute | solution.py:348
  22.5 20.0 %collective-permute-start.5 = (bf16[64,256]{1,0:T(8,128)(2,1)S(1)}, bf16[64,256]{1,0:T(8,128)(2,1)S(1)}, u32[]{:S(2)}, u32[]{:S(2)}) collective-permute-start(bf16[64,256]{1,0:T(8,128)(2,1)S(1)} %get-tuple-element.42), channel_id=1, source_target_pairs={{0,24},{4,28},{8,16},{12,20},{16,8},{20,12},{24,0},{28,4},{32,56},... | collective-permute-start | bytes 98312 | tf_op jit(solution)/shard_map/ppermute | solution.py:348
  22.6 20.9 %collective-permute-start.4 = (bf16[64,256]{1,0:T(8,128)(2,1)S(1)}, bf16[64,256]{1,0:T(8,128)(2,1)S(1)}, u32[]{:S(2)}, u32[]{:S(2)}) collective-permute-start(bf16[64,256]{1,0:T(8,128)(2,1)S(1)} %get-tuple-element.43), channel_id=1, source_target_pairs={{0,20},{4,16},{8,28},{12,24},{16,4},{20,0},{24,12},{28,8},{32,52},... | collective-permute-start | bytes 98312 | tf_op jit(solution)/shard_map/ppermute | solution.py:348
  23.4 20.2 %collective-permute-start.3 = (bf16[64,256]{1,0:T(8,128)(2,1)S(1)}, bf16[64,256]{1,0:T(8,128)(2,1)S(1)}, u32[]{:S(2)}, u32[]{:S(2)}) collective-permute-start(bf16[64,256]{1,0:T(8,128)(2,1)S(1)} %get-tuple-element.44), channel_id=1, source_target_pairs={{0,16},{4,20},{8,24},{12,28},{16,0},{20,4},{24,8},{28,12},{32,48},... | collective-permute-start | bytes 98312 | tf_op jit(solution)/shard_map/ppermute | solution.py:348
  25.2 18.3 %collective-permute-start.2 = (bf16[64,256]{1,0:T(8,128)(2,1)S(1)}, bf16[64,256]{1,0:T(8,128)(2,1)S(1)}, u32[]{:S(2)}, u32[]{:S(2)}) collective-permute-start(bf16[64,256]{1,0:T(8,128)(2,1)S(1)} %get-tuple-element.45), channel_id=1, source_target_pairs={{0,12},{4,8},{8,4},{12,0},{16,28},{20,24},{24,20},{28,16},{32,44},... | collective-permute-start | bytes 98312 | tf_op jit(solution)/shard_map/ppermute | solution.py:348
  39.9 6.5 %copy-start.6 = (bf16[64,256]{1,0:T(8,128)(2,1)}, bf16[64,256]{1,0:T(8,128)(2,1)S(1)}, u32[]{:S(2)}) copy-start(bf16[64,256]{1,0:T(8,128)(2,1)S(1)} %collective-permute-done.6.refs_7_) | copy-start | bytes 98308
  39.9 4.3 %collective-permute-start.1 = (bf16[64,256]{1,0:T(8,128)(2,1)S(1)}, bf16[64,256]{1,0:T(8,128)(2,1)S(1)}, u32[]{:S(2)}, u32[]{:S(2)}) collective-permute-start(bf16[64,256]{1,0:T(8,128)(2,1)S(1)} %get-tuple-element.46), channel_id=1, source_target_pairs={{0,8},{4,12},{8,0},{12,4},{16,24},{20,28},{24,16},{28,20},{32,40},... | collective-permute-start | bytes 98312 | tf_op jit(solution)/shard_map/ppermute | solution.py:348
  42.5 3.9 %copy-start.7 = (bf16[64,256]{1,0:T(8,128)(2,1)}, bf16[64,256]{1,0:T(8,128)(2,1)S(1)}, u32[]{:S(2)}) copy-start(bf16[64,256]{1,0:T(8,128)(2,1)S(1)} %collective-permute-done.5.refs_6_) | copy-start | bytes 98308
  42.5 1.7 %collective-permute-start = (bf16[64,256]{1,0:T(8,128)(2,1)S(1)}, bf16[64,256]{1,0:T(8,128)(2,1)S(1)}, u32[]{:S(2)}, u32[]{:S(2)}) collective-permute-start(bf16[64,256]{1,0:T(8,128)(2,1)S(1)} %get-tuple-element.47), channel_id=1, source_target_pairs={{0,4},{4,0},{8,12},{12,8},{16,20},{20,16},{24,28},{28,24},{32,36},... | collective-permute-start | bytes 98312 | tf_op jit(solution)/shard_map/ppermute | solution.py:348
  43.5 2.9 %copy-start.8 = (bf16[64,256]{1,0:T(8,128)(2,1)}, bf16[64,256]{1,0:T(8,128)(2,1)S(1)}, u32[]{:S(2)}) copy-start(bf16[64,256]{1,0:T(8,128)(2,1)S(1)} %collective-permute-done.4.refs_5_) | copy-start | bytes 98308
  43.5 2.9 %copy-start.9 = (bf16[64,256]{1,0:T(8,128)(2,1)}, bf16[64,256]{1,0:T(8,128)(2,1)S(1)}, u32[]{:S(2)}) copy-start(bf16[64,256]{1,0:T(8,128)(2,1)S(1)} %collective-permute-done.3.refs_4_) | copy-start | bytes 98308
  43.5 2.9 %copy-start.10 = (bf16[64,256]{1,0:T(8,128)(2,1)}, bf16[64,256]{1,0:T(8,128)(2,1)S(1)}, u32[]{:S(2)}) copy-start(bf16[64,256]{1,0:T(8,128)(2,1)S(1)} %collective-permute-done.2.refs_3_) | copy-start | bytes 98308
  44.2 2.2 %copy-start.11 = (bf16[64,256]{1,0:T(8,128)(2,1)}, bf16[64,256]{1,0:T(8,128)(2,1)S(1)}, u32[]{:S(2)}) copy-start(bf16[64,256]{1,0:T(8,128)(2,1)S(1)} %collective-permute-done.1.refs_2_) | copy-start | bytes 98308
  44.2 2.2 %copy-start.12 = (bf16[64,256]{1,0:T(8,128)(2,1)}, bf16[64,256]{1,0:T(8,128)(2,1)S(1)}, u32[]{:S(2)}) copy-start(bf16[64,256]{1,0:T(8,128)(2,1)S(1)} %collective-permute-done.refs_1_) | copy-start | bytes 98308
  46.5 0.9 copy-start
  50.4 37.6 %all-to-all-start.1 = ((bf16[64,16,512]{2,1,0:T(8,128)(2,1)}), bf16[64,16,512]{2,1,0:T(8,128)(2,1)S(1)}, u32[]{:S(2)}, u32[]{:S(2)}) async-start(bf16[64,16,512]{2,1,0:T(8,128)(2,1)} %relay.1), calls=%async_computation.1 | async-start | bytes 2097152 | tf_op jit(solution)/shard_map/all_to_all | solution.py:371
  63.3 4.8 %collective-permute-start.7 = (bf16[2,64,256]{2,1,0:T(8,128)(2,1)}, bf16[2,64,256]{2,1,0:T(8,128)(2,1)S(1)}, u32[]{:S(2)}, u32[]{:S(2)}) collective-permute-start(bf16[2,64,256]{2,1,0:T(8,128)(2,1)} %get-tuple-element.34), channel_id=1, source_target_pairs={{0,1},{1,2},{2,3},{3,0},{4,5},{5,6},{6,7},{7,4},{8,9},{9,10},{10,1... | collective-permute-start | bytes 196616 | tf_op jit(solution)/shard_map/ppermute | solution.py:392
  64.5 5.8 %collective-permute-start.8 = (bf16[2,64,256]{2,1,0:T(8,128)(2,1)}, bf16[2,64,256]{2,1,0:T(8,128)(2,1)S(1)}, u32[]{:S(2)}, u32[]{:S(2)}) collective-permute-start(bf16[2,64,256]{2,1,0:T(8,128)(2,1)} %get-tuple-element.35), channel_id=1, source_target_pairs={{0,2},{1,3},{2,0},{3,1},{4,6},{5,7},{6,4},{7,5},{8,10},{9,11},{10,... | collective-permute-start | bytes 196616 | tf_op jit(solution)/shard_map/ppermute | solution.py:392
  67.0 3.6 %collective-permute-start.9 = (bf16[2,64,256]{2,1,0:T(8,128)(2,1)}, bf16[2,64,256]{2,1,0:T(8,128)(2,1)S(1)}, u32[]{:S(2)}, u32[]{:S(2)}) collective-permute-start(bf16[2,64,256]{2,1,0:T(8,128)(2,1)} %get-tuple-element.36), channel_id=1, source_target_pairs={{0,3},{1,0},{2,1},{3,2},{4,7},{5,4},{6,5},{7,6},{8,11},{9,8},{10,9... | collective-permute-start | bytes 196616 | tf_op jit(solution)/shard_map/ppermute | solution.py:392
  68.2 2.5 %copy-start.3 = (bf16[2,64,256]{2,1,0:T(8,128)(2,1)}, bf16[2,64,256]{2,1,0:T(8,128)(2,1)S(1)}, u32[]{:S(2)}) copy-start(bf16[2,64,256]{2,1,0:T(8,128)(2,1)S(1)} %collective-permute-done.7.refs_1_) | copy-start | bytes 196612
  70.4 0.6 copy-start.4
  70.6 0.6 copy-start.5
  88.0 6.2 %copy-start.1 = (bf16[64,16,512]{2,1,0:T(8,128)(2,1)}, bf16[64,16,512]{2,1,0:T(8,128)(2,1)S(1)}, u32[]{:S(2)}) copy-start(bf16[64,16,512]{2,1,0:T(8,128)(2,1)S(1)} %all-to-all-done.1.got_ref) | copy-start | bytes 3145732
  88.0 16.6 %all-to-all-start.2 = ((f32[64,4,128]{2,1,0:T(4,128)}), f32[64,4,128]{2,1,0:T(4,128)S(1)}, u32[]{:S(2)}, u32[]{:S(2)}) async-start(f32[64,4,128]{2,1,0:T(4,128)} %gather.1), calls=%async_computation.2 | async-start | bytes 262144 | tf_op jit(solution)/shard_map/all_to_all | solution.py:402

commit v3 on v2

--- a/solution.py
+++ b/solution.py
@@ -39,6 +39,7 @@
     nv_ref,
     logit_ref,
     out_ref,
+    part_ref,
     kb,
     vb,
     keep_rows,
@@ -175,9 +176,7 @@
     sent = dot(entries, choose).astype(BF16)
     for e in range(EXPERTS):
         for j in range(columns):
-            out_ref[e * columns + j, heads * slots :, :] = sent[
-                e * ent : (e + 1) * ent, j * HD : (j + 1) * HD
-            ]
+            part_ref[e * columns + j] = sent[e * ent : (e + 1) * ent, j * HD : (j + 1) * HD]
 
 
 def expert_kernel(at_ref, got_ref, *refs):
@@ -218,18 +217,6 @@
             out_ref[i] = dot(weighted, stack[c ^ j]).astype(out_ref.dtype)
 
 
-def gather_kernel(*refs):
-    out_ref = refs[-1]
-    per = refs[0].shape[0]
-    tiles = out_ref.shape[1] // per
-    for i in range(per):
-        total = refs[0][i].astype(F32)
-        for ref in refs[1:-1]:
-            total = total + ref[i].astype(F32)
-        for t in range(tiles):
-            out_ref[:, i * tiles + t, :] = total[:, t * HD : (t + 1) * HD]
-
-
 def route_kernel(new_ref, table_ref, count_ref, out_ref):
     max_new = new_ref.shape[0]
     per_new = table_ref.shape[0] // max_new
@@ -246,34 +233,67 @@
     out_ref[...] = jnp.sum(found, axis=1, keepdims=True) - 1
 
 
-def relay_kernel(source_ref, low_ref, high_ref, out_ref):
-    devices, per, _ = low_ref.shape
-    slots = per // 2
+def relay_kernel(source_ref, rows_ref, *refs):
+    sum_refs, (out_ref, terms) = refs[:-2], refs[-2:]
+    devices, lines, _ = rows_ref.shape
+    terms_at = out_ref.shape[1] - terms.shape[1]
+    half = terms.shape[1] // 2
+    per = sum_refs[0].shape[0]
+    for i in range(per):
+        total = sum_refs[0][i].astype(F32)
+        for ref in sum_refs[1:]:
+            total = total + ref[i].astype(F32)
+        for t in range(half // per):
+            part = total[:, t * HD : (t + 1) * HD]
+            high = part.astype(BF16).astype(F32)
+            terms[:, i * (half // per) + t, :] = high
+            terms[:, half + i * (half // per) + t, :] = part - high
+    out_ref[:, terms_at:, :] = terms[...].astype(BF16)
+    tiles = 4
+    slots = lines // tiles
     held = devices * slots
-    tiles = []
-    for ref in (low_ref, high_ref):
-        for t in range(2):
-            rows = ref[:, t * slots : (t + 1) * slots, :].astype(F32)
-            tiles.append(rows.reshape(held, HD).astype(BF16))
-    table = jnp.concatenate(tiles, axis=1)
-    local = out_ref.shape[1]
+    local = terms_at // tiles
+    table = jnp.concatenate(
+        [
+            rows_ref[:, t * slots : (t + 1) * slots, :].astype(F32).reshape(held, HD).astype(BF16)
+            for t in range(tiles)
+        ],
+        axis=1,
+    )
     step = 16
     for c in range(0, devices, step):
         source = source_ref[c * local : (c + step) * local, :]
         pick = jnp.where(source == iota((step * local, held), 1), 1.0, 0.0).astype(BF16)
-        out_ref[c : c + step] = dot(pick, table).reshape(step, local, table.shape[1]).astype(BF16)
-
-
-def land_kernel(got_ref, k_ref, v_ref):
-    total, local, width = got_ref.shape
+        rows = dot(pick, table)
+        for t in range(tiles):
+            out_ref[c : c + step, t * local : (t + 1) * local, :] = (
+                rows[:, t * HD : (t + 1) * HD].reshape(step, local, HD).astype(BF16)
+            )
+
+
+def land_kernel(got_ref, k_ref, v_ref, mixed_ref):
+    total = got_ref.shape[0]
+    tiles = k_ref.shape[2] // HD
+    terms_at = got_ref.shape[1] - 2 * tiles
+    local = terms_at // tiles
     rows = total // 2
     n = rows * local
     to = iota((n, n), 0)
     fro = iota((n, n), 1)
     perm = jnp.where((to // rows == fro % local) & (to % rows == fro // local), 1.0, 0.0).astype(BF16)
     for base, ref in ((0, k_ref), (rows, v_ref)):
-        flat = got_ref[base : base + rows].reshape(n, width)
+        flat = jnp.concatenate(
+            [
+                got_ref[base : base + rows, t * local : (t + 1) * local, :].reshape(n, HD)
+                for t in range(tiles)
+            ],
+            axis=1,
+        )
         ref[...] = dot(perm, flat).reshape(ref.shape).astype(BF16)
+    terms = jnp.sum(got_ref[:, terms_at:, :].astype(F32), axis=0)
+    mixed = (terms[:tiles] + terms[tiles:]).astype(BF16)
+    for t in range(tiles):
+        mixed_ref[:, t * HD : (t + 1) * HD] = mixed[t : t + 1, :]
 
 
 def shards(
@@ -304,18 +324,20 @@
     heads = width // HD
     topk = queries.shape[1]
     ent = 2 * slots
-    chunk = heads * slots + ent
     columns = devices // EXPERTS
     cut = width // columns
     place = lax.rem(my, columns)
     table = page_table.T
     counts = request_pages.reshape(1, -1)
 
-    outbox = pl.pallas_call(
+    row_outbox, part_outbox = pl.pallas_call(
         source_kernel,
-        out_shape=jax.ShapeDtypeStruct((devices, chunk, HD), BF16),
+        out_shape=(
+            jax.ShapeDtypeStruct((devices, heads * slots, HD), BF16),
+            jax.ShapeDtypeStruct((devices, ent, HD), BF16),
+        ),
         in_specs=[SMEM] + [VMEM] * 11,
-        out_specs=VMEM,
+        out_specs=(VMEM, VMEM),
         scratch_shapes=[
             pltpu.VMEM((slots * rows, width), BF16),
             pltpu.VMEM((slots * rows, width), BF16),
@@ -337,9 +359,9 @@
         new_values,
         router_logits,
     )
-    inbox = lax.all_to_all(outbox, "pages", split_axis=0, concat_axis=0, tiled=True)
-
-    weight, _ = lax.optimization_barrier((out_weight[0], outbox))
+    part_inbox = lax.all_to_all(part_outbox, "pages", split_axis=0, concat_axis=0, tiled=True)
+
+    weight, _ = lax.optimization_barrier((out_weight[0], part_outbox))
     weight_rows = []
     for d in range(columns):
         piece = lax.dynamic_slice_in_dim(weight, (place ^ d) * cut, cut, 0)
@@ -347,7 +369,10 @@
             swap = [(p, p // columns * columns + (p % columns ^ d)) for p in range(devices)]
             piece = lax.ppermute(piece, "pages", swap)
         weight_rows.append(piece)
-    table, weight_rows = lax.optimization_barrier((table, weight_rows))
+    row_outbox, part_inbox, weight_rows = lax.optimization_barrier(
+        (row_outbox, part_inbox, weight_rows)
+    )
+    row_inbox = lax.all_to_all(row_outbox, "pages", split_axis=0, concat_axis=0, tiled=True)
 
     source = pl.pallas_call(
         route_kernel,
@@ -356,61 +381,39 @@
         out_specs=VMEM,
         name="route",
     )(new_table.T, table, counts)
-    routed = pl.pallas_call(
-        relay_kernel,
-        grid=(1,),
-        out_shape=jax.ShapeDtypeStruct((devices, local, width), BF16),
-        in_specs=[
-            VMEM,
-            pl.BlockSpec((devices, 2 * slots, HD), lambda i: (0, 0, 0)),
-            pl.BlockSpec((devices, 2 * slots, HD), lambda i: (0, 1, 0)),
-        ],
-        out_specs=VMEM,
-        name="relay",
-    )(source, inbox, inbox)
-    landed = lax.all_to_all(routed, "pages", split_axis=0, concat_axis=0, tiled=True)
-
-    inbox, _ = lax.optimization_barrier((inbox, routed))
     per = columns // shard_count
     block_cols = out_weight.shape[2]
     contribs = pl.pallas_call(
         expert_kernel,
-        grid=(1,),
         out_shape=[jax.ShapeDtypeStruct((per, requests, block_cols), BF16)] * shard_count,
-        in_specs=[
-            SMEM,
-            pl.BlockSpec((devices, ent, HD), lambda i: (0, heads * slots // ent, 0)),
-        ]
-        + [VMEM] * columns,
+        in_specs=[SMEM] + [VMEM] * (1 + columns),
         out_specs=[VMEM] * shard_count,
         scratch_shapes=[pltpu.VMEM((columns, cut, block_cols), BF16)],
         name="expert",
-    )(jnp.stack([place, shard]), inbox, *weight_rows)
+    )(jnp.stack([place, shard]), part_inbox, *weight_rows)
     moved = [contribs[0]]
     for t in range(1, shard_count):
         moved.append(
             lax.ppermute(contribs[t], "expert", [(i, (i + t) % shard_count) for i in range(shard_count)])
         )
-    summed = pl.pallas_call(
-        gather_kernel,
-        out_shape=jax.ShapeDtypeStruct((requests, per * block_cols // HD, HD), F32),
-        in_specs=[VMEM] * shard_count,
+    terms = 2 * per * block_cols // HD
+    routed = pl.pallas_call(
+        relay_kernel,
+        out_shape=jax.ShapeDtypeStruct((devices, heads * local + terms, HD), BF16),
+        in_specs=[VMEM] * (2 + shard_count),
         out_specs=VMEM,
-        name="gather",
-    )(*moved)
-    summed, landed = lax.optimization_barrier((summed, landed))
-    parts = lax.all_to_all(summed, "pages", split_axis=0, concat_axis=0, tiled=True)
-    mixed = jnp.sum(parts, axis=0).reshape(1, -1).astype(BF16)
-
+        scratch_shapes=[pltpu.VMEM((requests, terms, HD), F32)],
+        name="relay",
+    )(source, row_inbox, *moved)
+    landed = lax.all_to_all(routed, "pages", split_axis=0, concat_axis=0, tiled=True)
     new_page = jax.ShapeDtypeStruct((new_cap, per_new * rows, width), BF16)
-    compact_keys, compact_values = pl.pallas_call(
+    return pl.pallas_call(
         land_kernel,
-        out_shape=(new_page, new_page),
+        out_shape=(new_page, new_page, jax.ShapeDtypeStruct((1, width), BF16)),
         in_specs=[VMEM],
-        out_specs=(VMEM, VMEM),
+        out_specs=(VMEM, VMEM, VMEM),
         name="land",
     )(landed)
-    return (compact_keys, compact_values, mixed)
 
 
 def solution(mesh):

time: 106 us -> 104 us (0.981)
  blocking collectives: 0 us -> 37.7 us
  waiting for transfers between devices: 40.1 us -> 9.09 us
  starting transfers between devices: 43.5 us -> 38.1 us
  Pallas kernels: 17.3 us -> 15.8 us
  local copies, waits for them, and re-layouts: 2.75 us -> 1.47 us
    all_to_all x0 -> x1, blocking collectives: none -> 37.7 us  [shards(): lax.all_to_all(routed, 'pages', split_axis=0, concat_axis=0, tiled=True)]
    all_to_all x3 -> x2, waiting for transfers between devices: 22.6 us -> 5.96 us  [the longest x1 5.95 us: shards(): lax.all_to_all(row_outbox, 'pages', split_axis=0, concat_axis=0, tiled=True)]
    ppermute x7, waiting for transfers between devices: 15 us -> 2.81 us  [shards(): piece = lax.ppermute(piece, 'pages', swap)]
    all_to_all x3 -> x2, starting transfers between devices: 28.5 us -> 22.1 us  [the longest x1 13.1 us: shards(): lax.all_to_all(part_outbox, 'pages', split_axis=0, concat_axis=0, tiled=T...]
    ppermute x3, waiting for transfers between devices: 2.49 us -> 0.33 us  [shards(): lax.ppermute(contribs[t], 'expert', [(i, (i + t) % shard_count) for i in...]
    pallas_call x5 -> x4, Pallas kernels: 15.1 us -> 13.6 us  [the longest x1 4.24 us: shards(): pl.pallas_call(source_kernel, out_shape=(jax.ShapeDtypeStruct((devices, h...]
    unnamed x27 -> x26, local copies, waits for them, and re-layouts: 2.12 us -> 0.83 us
  transfers between devices with their start and end apart: 13 -> 12, of which waited for: 7 -> 5; matrix products, arithmetic and copies ran while one was open for 1% -> 1% of each run, Pallas kernels for 9% -> 5%
where the time goes in v3:
time: 104 us
  starting transfers between devices  38.1 us (37%)
  blocking collectives  37.7 us (36%)
  Pallas kernels  15.8 us (15%)
  waiting for transfers between devices  9.09 us (9%)
  local copies, waits for them, and re-layouts  1.47 us (1%)
    all_to_all x1, blocking collectives, shards(): lax.all_to_all(routed, 'pages', split_axis=0, concat_axis=0, tiled=True)  37.7 us
    all_to_all x1, starting transfers between devices, shards(): lax.all_to_all(part_outbox, 'pages', split_axis=0, concat_axis=0, tiled=T...  13.1 us
    ppermute x7, starting transfers between devices, shards(): piece = lax.ppermute(piece, 'pages', swap)  11.1 us
    all_to_all x1, starting transfers between devices, shards(): lax.all_to_all(row_outbox, 'pages', split_axis=0, concat_axis=0, tiled=True)  9 us
    all_to_all x1, waiting for transfers between devices, shards(): lax.all_to_all(row_outbox, 'pages', split_axis=0, concat_axis=0, tiled=True)  5.95 us
    ppermute x3, starting transfers between devices, shards(): lax.ppermute(contribs[t], 'expert', [(i, (i + t) % shard_count) for i in...  4.82 us
    pallas_call x1, Pallas kernels, shards(): pl.pallas_call(source_kernel, out_shape=(jax.ShapeDtypeStruct((devices, h...  4.24 us
    pallas_call x1, Pallas kernels, shards(): pl.pallas_call(expert_kernel, out_shape=[jax.ShapeDtypeStruct((per, reque...  3.35 us
  transfers between devices with their start and end apart: 12, of which 5 were waited for; matrix products, arithmetic and copies ran while one was open for 1% of the time, Pallas kernels for 5%

profile of v3, /device:TPU:1, one launch (start us, length us, event | category | flops | bytes accessed | tf_op | source)
XLA Modules:
  0.0 103.6 jit_solution(6870028200716326806)
XLA Ops:
  0.6 0.0 copy-start.2
  0.6 4.2 %source.1 = (bf16[64,32,128]{2,1,0:T(8,128)(2,1)}, bf16[64,16,128]{2,1,0:T(8,128)(2,1)}) custom-call(s32[1]{0:T(128)} %bitcast.3.my_ref, s32[12,64]{1,0:T(8,128)} %bitcast.9, s32[1,64]{1,0:T(1,128)} %bitcast.12, s32[2,64]{1,0:T(2,128)} %bitcast.14, s32[8,31]{1,0:T(8,128)} %keep_ref.1, s32[8,128]{1,0:T(8,128)} %drop_ref.1, bf16[8,128,512]{2,1,0:T(8,128)(2,1)} %k_ref.1, ...), custom_call_target="tpu_custom_call" | custom-call | tf_op jit(solution)/shard_map/source/pallas_call | solution.py:333
  4.9 13.1 %all-to-all-start = ((bf16[64,16,128]{2,1,0:T(8,128)(2,1)}), bf16[64,16,128]{2,1,0:T(8,128)(2,1)S(1)}, u32[]{:S(2)}, u32[]{:S(2)}) async-start(bf16[64,16,128]{2,1,0:T(8,128)(2,1)} %get-tuple-element.21), calls=%async_computation | async-start | bytes 524288 | tf_op jit(solution)/shard_map/all_to_all | solution.py:362
  18.1 0.0 copy-done.2
  18.1 0.6 constant_dynamic-slice_fusion
  18.7 3.4 %collective-permute-start.6 = (bf16[64,256]{1,0:T(8,128)(2,1)S(1)}, bf16[64,256]{1,0:T(8,128)(2,1)S(1)}, u32[]{:S(2)}, u32[]{:S(2)}) collective-permute-start(bf16[64,256]{1,0:T(8,128)(2,1)S(1)} %get-tuple-element.37), channel_id=1, source_target_pairs={{0,28},{4,24},{8,20},{12,16},{16,12},{20,8},{24,4},{28,0},{32,60},... | collective-permute-start | bytes 98312 | tf_op jit(solution)/shard_map/ppermute | solution.py:370
  22.2 0.2 collective-permute-start.5
  22.4 0.7 collective-permute-start.4
  23.1 1.9 %collective-permute-start.3 = (bf16[64,256]{1,0:T(8,128)(2,1)S(1)}, bf16[64,256]{1,0:T(8,128)(2,1)S(1)}, u32[]{:S(2)}, u32[]{:S(2)}) collective-permute-start(bf16[64,256]{1,0:T(8,128)(2,1)S(1)} %get-tuple-element.40), channel_id=1, source_target_pairs={{0,16},{4,20},{8,24},{12,28},{16,0},{20,4},{24,8},{28,12},{32,48},... | collective-permute-start | bytes 98312 | tf_op jit(solution)/shard_map/ppermute | solution.py:370
  24.9 1.4 %collective-permute-start.2 = (bf16[64,256]{1,0:T(8,128)(2,1)S(1)}, bf16[64,256]{1,0:T(8,128)(2,1)S(1)}, u32[]{:S(2)}, u32[]{:S(2)}) collective-permute-start(bf16[64,256]{1,0:T(8,128)(2,1)S(1)} %get-tuple-element.41), channel_id=1, source_target_pairs={{0,12},{4,8},{8,4},{12,0},{16,28},{20,24},{24,20},{28,16},{32,44},... | collective-permute-start | bytes 98312 | tf_op jit(solution)/shard_map/ppermute | solution.py:370
  26.4 1.3 %collective-permute-done.6.refs_7_ = bf16[64,256]{1,0:T(8,128)(2,1)S(1)} collective-permute-done((bf16[64,256]{1,0:T(8,128)(2,1)S(1)}, bf16[64,256]{1,0:T(8,128)(2,1)S(1)}, u32[]{:S(2)}, u32[]{:S(2)}) %collective-permute-start.6) | collective-permute-done | bytes 32800 | tf_op jit(solution)/shard_map/ppermute | solution.py:370
  27.7 3.5 %collective-permute-start.1 = (bf16[64,256]{1,0:T(8,128)(2,1)S(1)}, bf16[64,256]{1,0:T(8,128)(2,1)S(1)}, u32[]{:S(2)}, u32[]{:S(2)}) collective-permute-start(bf16[64,256]{1,0:T(8,128)(2,1)S(1)} %get-tuple-element.42), channel_id=1, source_target_pairs={{0,8},{4,12},{8,0},{12,4},{16,24},{20,28},{24,16},{28,20},{32,40},... | collective-permute-start | bytes 98312 | tf_op jit(solution)/shard_map/ppermute | solution.py:370
  31.2 0.0 collective-permute-done.5.refs_6_
  31.2 0.0 collective-permute-start
  31.2 0.8 collective-permute-done.4.refs_5_
  32.0 0.0 collective-permute-done.3.refs_4_
  32.0 0.0 collective-permute-done.2.refs_3_
  32.0 0.0 copy-start.10
  32.0 0.7 collective-permute-done.1.refs_2_
  32.7 0.0 collective-permute-done.refs_1_
  32.7 0.0 all-to-all-done.got_ref
  32.7 0.0 copy-start.1
  32.7 9.0 %all-to-all-start.1 = ((bf16[64,32,128]{2,1,0:T(8,128)(2,1)}), bf16[64,32,128]{2,1,0:T(8,128)(2,1)S(1)}, u32[]{:S(2)}, u32[]{:S(2)}) async-start(bf16[64,32,128]{2,1,0:T(8,128)(2,1)} %get-tuple-element.23), calls=%async_computation.1 | async-start | bytes 1048576 | tf_op jit(solution)/shard_map/all_to_all | solution.py:375
  41.7 0.6 pad_add_fusion.at_ref
  42.4 0.0 copy-done.6
  42.4 0.0 copy-done.7
  42.4 0.0 copy-done.8
  42.4 0.0 copy-done.9
  42.4 0.0 copy-done.10
  42.4 0.0 copy-done.11
  42.4 0.0 copy-done.12
  42.4 0.0 copy-done.1
  42.4 3.4 %expert.1 = (bf16[2,64,256]{2,1,0:T(8,128)(2,1)}, bf16[2,64,256]{2,1,0:T(8,128)(2,1)}, bf16[2,64,256]{2,1,0:T(8,128)(2,1)}, bf16[2,64,256]{2,1,0:T(8,128)(2,1)}) custom-call(s32[2]{0:T(128)} %pad_add_fusion.at_ref, bf16[64,16,128]{2,1,0:T(8,128)(2,1)} %copy-done.1, bf16[64,256]{1,0:T(8,128)(2,1)} %get-tuple-element.25.refs_0_, bf16[64,256]{1,0:T(8,128)(2,1)} %copy-done.12, ...), custom_call_target="tpu_custom_call" | custom-call | tf_op jit(solution)/shard_map/expert/pallas_call | solution.py:386
  45.8 1.2 %collective-permute-start.7 = (bf16[2,64,256]{2,1,0:T(8,128)(2,1)}, bf16[2,64,256]{2,1,0:T(8,128)(2,1)S(1)}, u32[]{:S(2)}, u32[]{:S(2)}) collective-permute-start(bf16[2,64,256]{2,1,0:T(8,128)(2,1)} %get-tuple-element.34), channel_id=1, source_target_pairs={{0,1},{1,2},{2,3},{3,0},{4,5},{5,6},{6,7},{7,4},{8,9},{9,10},{10,1... | collective-permute-start | bytes 196616 | tf_op jit(solution)/shard_map/ppermute | solution.py:397
  47.0 2.4 %collective-permute-start.8 = (bf16[2,64,256]{2,1,0:T(8,128)(2,1)}, bf16[2,64,256]{2,1,0:T(8,128)(2,1)S(1)}, u32[]{:S(2)}, u32[]{:S(2)}) collective-permute-start(bf16[2,64,256]{2,1,0:T(8,128)(2,1)} %get-tuple-element.35), channel_id=1, source_target_pairs={{0,2},{1,3},{2,0},{3,1},{4,6},{5,7},{6,4},{7,5},{8,10},{9,11},{10,... | collective-permute-start | bytes 196616 | tf_op jit(solution)/shard_map/ppermute | solution.py:397
  49.5 1.2 %collective-permute-start.9 = (bf16[2,64,256]{2,1,0:T(8,128)(2,1)}, bf16[2,64,256]{2,1,0:T(8,128)(2,1)S(1)}, u32[]{:S(2)}, u32[]{:S(2)}) collective-permute-start(bf16[2,64,256]{2,1,0:T(8,128)(2,1)} %get-tuple-element.36), channel_id=1, source_target_pairs={{0,3},{1,0},{2,1},{3,2},{4,7},{5,4},{6,5},{7,6},{8,11},{9,8},{10,9... | collective-permute-start | bytes 196616 | tf_op jit(solution)/shard_map/ppermute | solution.py:397
  50.6 2.2 %route.1.source_ref = s32[1024,1]{1,0:T(8,128)} custom-call(s32[3,64]{1,0:T(4,128)} %bitcast.11, s32[12,64]{1,0:T(8,128)} %bitcast.10, s32[1,64]{1,0:T(1,128)} %bitcast.13), custom_call_target="tpu_custom_call" | custom-call | tf_op jit(solution)/shard_map/route/pallas_call | solution.py:377
  52.8 0.0 collective-permute-done.7.refs_1_
  52.8 0.0 collective-permute-done.8.refs_2_
  52.8 0.3 collective-permute-done.9.refs_3_
  53.1 6.0 %all-to-all-done.1.rows_ref = bf16[64,32,128]{2,1,0:T(8,128)(2,1)S(1)} async-done(((bf16[64,32,128]{2,1,0:T(8,128)(2,1)}), bf16[64,32,128]{2,1,0:T(8,128)(2,1)S(1)}, u32[]{:S(2)}, u32[]{:S(2)}) %all-to-all-start.1) | async-done | bytes 524320 | tf_op jit(solution)/shard_map/all_to_all | solution.py:375
  59.1 0.0 copy-done.3
  59.1 0.0 copy-done.4
  59.1 0.0 copy-done.5
  59.1 0.8 copy-done
  59.9 3.2 %relay.1 = bf16[64,72,128]{2,1,0:T(8,128)(2,1)} custom-call(s32[1024,1]{1,0:T(8,128)} %route.1.source_ref, bf16[64,32,128]{2,1,0:T(8,128)(2,1)} %copy-done, bf16[2,64,256]{2,1,0:T(8,128)(2,1)} %get-tuple-element.33.refs_0_, bf16[2,64,256]{2,1,0:T(8,128)(2,1)} %copy-done.3, bf16[2,64,256]{2,1,0:T(8,128)(2,1)} %copy-done.4, bf16[2,64,256]{2,1,0:T(8,128)(2,1)} %copy-done.5), custom_call_target="tpu_custom_call" | custom-call | tf_op jit(solution)/shard_map/relay/pallas_call | solution.py:400
  63.1 37.7 %all_to_all.15.got_ref = bf16[64,72,128]{2,1,0:T(8,128)(2,1)} all-to-all(bf16[64,72,128]{2,1,0:T(8,128)(2,1)} %relay.1), channel_id=1, replica_groups=mesh['pages'=64,'expert'=4] {'pages'}, dimensions={0} | all-to-all | bytes 2359296 | tf_op jit(solution)/shard_map/all_to_all | solution.py:408
  100.8 2.8 %land.1 = (bf16[4,128,512]{2,1,0:T(8,128)(2,1)}, bf16[4,128,512]{2,1,0:T(8,128)(2,1)}, bf16[1,512]{1,0:T(2,128)(2,1)}) custom-call(bf16[64,72,128]{2,1,0:T(8,128)(2,1)} %all_to_all.15.got_ref), custom_call_target="tpu_custom_call" | custom-call | tf_op jit(solution)/shard_map/land/pallas_call | solution.py:410
  (10 shorter events, 0.0 us)
Async XLA Ops:
  0.6 17.5 %copy-start.2 = (bf16[1,512,256]{2,1,0:T(8,128)(2,1)S(1)}, bf16[1,512,256]{2,1,0:T(8,128)(2,1)}, u32[]{:S(2)}) copy-start(bf16[1,512,256]{2,1,0:T(8,128)(2,1)} %param.25) | copy-start | bytes 786436
  4.9 27.8 %all-to-all-start = ((bf16[64,16,128]{2,1,0:T(8,128)(2,1)}), bf16[64,16,128]{2,1,0:T(8,128)(2,1)S(1)}, u32[]{:S(2)}, u32[]{:S(2)}) async-start(bf16[64,16,128]{2,1,0:T(8,128)(2,1)} %get-tuple-element.21), calls=%async_computation | async-start | bytes 524288 | tf_op jit(solution)/shard_map/all_to_all | solution.py:362
  18.7 8.9 %collective-permute-start.6 = (bf16[64,256]{1,0:T(8,128)(2,1)S(1)}, bf16[64,256]{1,0:T(8,128)(2,1)S(1)}, u32[]{:S(2)}, u32[]{:S(2)}) collective-permute-start(bf16[64,256]{1,0:T(8,128)(2,1)S(1)} %get-tuple-element.37), channel_id=1, source_target_pairs={{0,28},{4,24},{8,20},{12,16},{16,12},{20,8},{24,4},{28,0},{32,60},... | collective-permute-start | bytes 98312 | tf_op jit(solution)/shard_map/ppermute | solution.py:370
  22.2 9.0 %collective-permute-start.5 = (bf16[64,256]{1,0:T(8,128)(2,1)S(1)}, bf16[64,256]{1,0:T(8,128)(2,1)S(1)}, u32[]{:S(2)}, u32[]{:S(2)}) collective-permute-start(bf16[64,256]{1,0:T(8,128)(2,1)S(1)} %get-tuple-element.38), channel_id=1, source_target_pairs={{0,24},{4,28},{8,16},{12,20},{16,8},{20,12},{24,0},{28,4},{32,56},... | collective-permute-start | bytes 98312 | tf_op jit(solution)/shard_map/ppermute | solution.py:370
  22.4 9.7 %collective-permute-start.4 = (bf16[64,256]{1,0:T(8,128)(2,1)S(1)}, bf16[64,256]{1,0:T(8,128)(2,1)S(1)}, u32[]{:S(2)}, u32[]{:S(2)}) collective-permute-start(bf16[64,256]{1,0:T(8,128)(2,1)S(1)} %get-tuple-element.39), channel_id=1, source_target_pairs={{0,20},{4,16},{8,28},{12,24},{16,4},{20,0},{24,12},{28,8},{32,52},... | collective-permute-start | bytes 98312 | tf_op jit(solution)/shard_map/ppermute | solution.py:370
  23.1 8.9 %collective-permute-start.3 = (bf16[64,256]{1,0:T(8,128)(2,1)S(1)}, bf16[64,256]{1,0:T(8,128)(2,1)S(1)}, u32[]{:S(2)}, u32[]{:S(2)}) collective-permute-start(bf16[64,256]{1,0:T(8,128)(2,1)S(1)} %get-tuple-element.40), channel_id=1, source_target_pairs={{0,16},{4,20},{8,24},{12,28},{16,0},{20,4},{24,8},{28,12},{32,48},... | collective-permute-start | bytes 98312 | tf_op jit(solution)/shard_map/ppermute | solution.py:370
  24.9 7.1 %collective-permute-start.2 = (bf16[64,256]{1,0:T(8,128)(2,1)S(1)}, bf16[64,256]{1,0:T(8,128)(2,1)S(1)}, u32[]{:S(2)}, u32[]{:S(2)}) collective-permute-start(bf16[64,256]{1,0:T(8,128)(2,1)S(1)} %get-tuple-element.41), channel_id=1, source_target_pairs={{0,12},{4,8},{8,4},{12,0},{16,28},{20,24},{24,20},{28,16},{32,44},... | collective-permute-start | bytes 98312 | tf_op jit(solution)/shard_map/ppermute | solution.py:370
  27.7 14.7 %copy-start.6 = (bf16[64,256]{1,0:T(8,128)(2,1)}, bf16[64,256]{1,0:T(8,128)(2,1)S(1)}, u32[]{:S(2)}) copy-start(bf16[64,256]{1,0:T(8,128)(2,1)S(1)} %collective-permute-done.6.refs_7_) | copy-start | bytes 98308
  27.7 5.1 %collective-permute-start.1 = (bf16[64,256]{1,0:T(8,128)(2,1)S(1)}, bf16[64,256]{1,0:T(8,128)(2,1)S(1)}, u32[]{:S(2)}, u32[]{:S(2)}) collective-permute-start(bf16[64,256]{1,0:T(8,128)(2,1)S(1)} %get-tuple-element.42), channel_id=1, source_target_pairs={{0,8},{4,12},{8,0},{12,4},{16,24},{20,28},{24,16},{28,20},{32,40},... | collective-permute-start | bytes 98312 | tf_op jit(solution)/shard_map/ppermute | solution.py:370
  31.2 11.2 %copy-start.7 = (bf16[64,256]{1,0:T(8,128)(2,1)}, bf16[64,256]{1,0:T(8,128)(2,1)S(1)}, u32[]{:S(2)}) copy-start(bf16[64,256]{1,0:T(8,128)(2,1)S(1)} %collective-permute-done.5.refs_6_) | copy-start | bytes 98308
  31.2 1.5 %collective-permute-start = (bf16[64,256]{1,0:T(8,128)(2,1)S(1)}, bf16[64,256]{1,0:T(8,128)(2,1)S(1)}, u32[]{:S(2)}, u32[]{:S(2)}) collective-permute-start(bf16[64,256]{1,0:T(8,128)(2,1)S(1)} %get-tuple-element.43), channel_id=1, source_target_pairs={{0,4},{4,0},{8,12},{12,8},{16,20},{20,16},{24,28},{28,24},{32,36},... | collective-permute-start | bytes 98312 | tf_op jit(solution)/shard_map/ppermute | solution.py:370
  32.0 10.4 %copy-start.8 = (bf16[64,256]{1,0:T(8,128)(2,1)}, bf16[64,256]{1,0:T(8,128)(2,1)S(1)}, u32[]{:S(2)}) copy-start(bf16[64,256]{1,0:T(8,128)(2,1)S(1)} %collective-permute-done.4.refs_5_) | copy-start | bytes 98308
  32.0 10.4 %copy-start.9 = (bf16[64,256]{1,0:T(8,128)(2,1)}, bf16[64,256]{1,0:T(8,128)(2,1)S(1)}, u32[]{:S(2)}) copy-start(bf16[64,256]{1,0:T(8,128)(2,1)S(1)} %collective-permute-done.3.refs_4_) | copy-start | bytes 98308
  32.0 10.4 %copy-start.10 = (bf16[64,256]{1,0:T(8,128)(2,1)}, bf16[64,256]{1,0:T(8,128)(2,1)S(1)}, u32[]{:S(2)}) copy-start(bf16[64,256]{1,0:T(8,128)(2,1)S(1)} %collective-permute-done.2.refs_3_) | copy-start | bytes 98308
  32.7 9.7 %copy-start.11 = (bf16[64,256]{1,0:T(8,128)(2,1)}, bf16[64,256]{1,0:T(8,128)(2,1)S(1)}, u32[]{:S(2)}) copy-start(bf16[64,256]{1,0:T(8,128)(2,1)S(1)} %collective-permute-done.1.refs_2_) | copy-start | bytes 98308
  32.7 9.7 %copy-start.12 = (bf16[64,256]{1,0:T(8,128)(2,1)}, bf16[64,256]{1,0:T(8,128)(2,1)S(1)}, u32[]{:S(2)}) copy-start(bf16[64,256]{1,0:T(8,128)(2,1)S(1)} %collective-permute-done.refs_1_) | copy-start | bytes 98308
  32.7 9.7 %copy-start.1 = (bf16[64,16,128]{2,1,0:T(8,128)(2,1)}, bf16[64,16,128]{2,1,0:T(8,128)(2,1)S(1)}, u32[]{:S(2)}) copy-start(bf16[64,16,128]{2,1,0:T(8,128)(2,1)S(1)} %all-to-all-done.got_ref) | copy-start | bytes 786436
  32.7 26.3 %all-to-all-start.1 = ((bf16[64,32,128]{2,1,0:T(8,128)(2,1)}), bf16[64,32,128]{2,1,0:T(8,128)(2,1)S(1)}, u32[]{:S(2)}, u32[]{:S(2)}) async-start(bf16[64,32,128]{2,1,0:T(8,128)(2,1)} %get-tuple-element.23), calls=%async_computation.1 | async-start | bytes 1048576 | tf_op jit(solution)/shard_map/all_to_all | solution.py:375
  45.8 7.0 %collective-permute-start.7 = (bf16[2,64,256]{2,1,0:T(8,128)(2,1)}, bf16[2,64,256]{2,1,0:T(8,128)(2,1)S(1)}, u32[]{:S(2)}, u32[]{:S(2)}) collective-permute-start(bf16[2,64,256]{2,1,0:T(8,128)(2,1)} %get-tuple-element.34), channel_id=1, source_target_pairs={{0,1},{1,2},{2,3},{3,0},{4,5},{5,6},{6,7},{7,4},{8,9},{9,10},{10,1... | collective-permute-start | bytes 196616 | tf_op jit(solution)/shard_map/ppermute | solution.py:397
  47.0 5.8 %collective-permute-start.8 = (bf16[2,64,256]{2,1,0:T(8,128)(2,1)}, bf16[2,64,256]{2,1,0:T(8,128)(2,1)S(1)}, u32[]{:S(2)}, u32[]{:S(2)}) collective-permute-start(bf16[2,64,256]{2,1,0:T(8,128)(2,1)} %get-tuple-element.35), channel_id=1, source_target_pairs={{0,2},{1,3},{2,0},{3,1},{4,6},{5,7},{6,4},{7,5},{8,10},{9,11},{10,... | collective-permute-start | bytes 196616 | tf_op jit(solution)/shard_map/ppermute | solution.py:397
  49.5 3.6 %collective-permute-start.9 = (bf16[2,64,256]{2,1,0:T(8,128)(2,1)}, bf16[2,64,256]{2,1,0:T(8,128)(2,1)S(1)}, u32[]{:S(2)}, u32[]{:S(2)}) collective-permute-start(bf16[2,64,256]{2,1,0:T(8,128)(2,1)} %get-tuple-element.36), channel_id=1, source_target_pairs={{0,3},{1,0},{2,1},{3,2},{4,7},{5,4},{6,5},{7,6},{8,11},{9,8},{10,9... | collective-permute-start | bytes 196616 | tf_op jit(solution)/shard_map/ppermute | solution.py:397
  52.8 6.3 %copy-start.3 = (bf16[2,64,256]{2,1,0:T(8,128)(2,1)}, bf16[2,64,256]{2,1,0:T(8,128)(2,1)S(1)}, u32[]{:S(2)}) copy-start(bf16[2,64,256]{2,1,0:T(8,128)(2,1)S(1)} %collective-permute-done.7.refs_1_) | copy-start | bytes 196612
  52.8 6.3 %copy-start.4 = (bf16[2,64,256]{2,1,0:T(8,128)(2,1)}, bf16[2,64,256]{2,1,0:T(8,128)(2,1)S(1)}, u32[]{:S(2)}) copy-start(bf16[2,64,256]{2,1,0:T(8,128)(2,1)S(1)} %collective-permute-done.8.refs_2_) | copy-start | bytes 196612
  53.1 6.0 %copy-start.5 = (bf16[2,64,256]{2,1,0:T(8,128)(2,1)}, bf16[2,64,256]{2,1,0:T(8,128)(2,1)S(1)}, u32[]{:S(2)}) copy-start(bf16[2,64,256]{2,1,0:T(8,128)(2,1)S(1)} %collective-permute-done.9.refs_3_) | copy-start | bytes 196612
  59.1 0.8 copy-start

commit v4 on v3

--- a/solution.py
+++ b/solution.py
@@ -38,7 +38,6 @@
     nk_ref,
     nv_ref,
     logit_ref,
-    out_ref,
     part_ref,
     kb,
     vb,
@@ -67,15 +66,6 @@
         kb[g * rows : (g + 1) * rows, :] = (dot(mat, k_ref[g]) / denom).astype(BF16)
         vb[g * rows : (g + 1) * rows, :] = (dot(mat, v_ref[g]) / denom).astype(BF16)
     n = slots * rows
-    to = iota((n, n), 0)
-    fro = iota((n, n), 1)
-    perm = jnp.where((to % slots == fro // rows) & (to // slots == fro % rows), 1.0, 0.0).astype(BF16)
-    for base, blocks in ((0, kb), (rows, vb)):
-        spread = dot(perm, blocks[...])
-        for t in range(heads):
-            out_ref[base : base + rows, t * slots : (t + 1) * slots, :] = (
-                spread[:, t * HD : (t + 1) * HD].reshape(rows, slots, HD).astype(BF16)
-            )
     ent = 2 * slots
     ent_row = iota((ent, reqs), 0)
     req_lane = iota((ent, reqs), 1)
@@ -163,58 +153,100 @@
             part = jnp.where(first & (expert[k] == e), by_choice[k], part)
         parts.append(part)
     entries = jnp.concatenate(parts, axis=0).astype(BF16)
-    columns = out_ref.shape[0] // EXPERTS
-    cut = width // columns
-    at = iota((width + HD, columns * HD), 1)
-    l = at % HD
-    j = at // HD
-    head_stat = width + (j * cut // HD) * 3 + l - cut
-    rest_stat = width + 3 * heads + l - cut - 3
-    origin = jnp.where(l < cut, j * cut + l, jnp.where(l < cut + 3, head_stat, rest_stat))
-    origin = jnp.where(l < cut + 6, origin, -1)
-    choose = jnp.where(iota(at.shape, 0) == origin, 1.0, 0.0).astype(BF16)
-    sent = dot(entries, choose).astype(BF16)
-    for e in range(EXPERTS):
-        for j in range(columns):
-            part_ref[e * columns + j] = sent[e * ent : (e + 1) * ent, j * HD : (j + 1) * HD]
-
-
-def expert_kernel(at_ref, got_ref, *refs):
-    columns = got_ref.shape[0] // EXPERTS
-    w_refs, out_refs, (stack,) = refs[:columns], refs[columns:-1], refs[-1:]
-    j = at_ref[0]
-    s = at_ref[1]
-    reqs, ent, _ = got_ref.shape
-    cut = w_refs[0].shape[0]
-    for d in range(columns):
-        stack[d] = w_refs[d][...]
-    v = got_ref[...].astype(F32).reshape(reqs * ent, HD)
-    lane = iota(v.shape, 1)
-    shift = v[:, cut : cut + 1]
-    den = v[:, cut + 1 : cut + 2] + v[:, cut + 2 : cut + 3]
-    request = v[:, cut + 5 : cut + 6]
-    live = den > 0.0
-    owns = (request == lane.astype(F32)) & live
-    peak = jnp.max(jnp.where(owns, shift, NEGATIVE), axis=0, keepdims=True)
-    peak = jnp.sum(jnp.where(owns, peak, 0.0), axis=1, keepdims=True)
-    factor = jnp.where(live, jnp.exp(shift - peak), 0.0)
-    scaled = jnp.where((lane < cut + 3), v * factor, v)
+    devices, lines, _ = part_ref.shape
+    columns = devices // EXPERTS
+    to = iota((EXPERTS * lines, EXPERTS * ent), 0)
+    fro = iota((EXPERTS * lines, EXPERTS * ent), 1)
+    alike = to // lines == fro // ent
+    line = to % lines
+    entry = fro % ent
+    one = jnp.where(alike & (line == entry) & (entry <= slots), 1.0, 0.0).astype(BF16)
+    two_line = jnp.where(entry == slots, slots + 1, 2 * slots + entry)
+    two = jnp.where(alike & (line == two_line) & (entry <= slots), 1.0, 0.0).astype(BF16)
+    flat = jnp.where(alike & (line == slots + 2), 1.0, 0.0).astype(BF16)
+    for c in range(2):
+        base = c * 2 * HD
+        lane_out = iota((HD, HD), 1)
+        item = lane_out % 9
+        origin = jnp.where(item < 6, 6 * c + item, 3 * heads + item - 6)
+        copy = jnp.where(iota((HD, HD), 0) == origin, 1.0, 0.0).astype(BF16)
+        stats = dot(entries[:, width:], copy)
+        mine = iota(stats.shape, 1) // 9 == iota(stats.shape, 0) % ent
+        stats = jnp.where(mine, stats, 0.0).astype(BF16)
+        sent = dot(one, entries[:, base : base + HD]) + dot(two, entries[:, base + HD : base + 2 * HD])
+        sent = (sent + dot(flat, stats)).astype(BF16)
+        for e in range(EXPERTS):
+            for z in range(columns // 2):
+                part_ref[e * columns + 2 * z + c] = sent[e * lines : (e + 1) * lines, :]
+
+
+def spread_kernel(kb_ref, vb_ref, out_ref):
+    n, width = kb_ref.shape
+    rows = out_ref.shape[0] // 2
+    slots = n // rows
+    to = iota((n, n), 0)
+    fro = iota((n, n), 1)
+    perm = jnp.where((to % slots == fro // rows) & (to // slots == fro % rows), 1.0, 0.0).astype(BF16)
+    for base, blocks in ((0, kb_ref), (rows, vb_ref)):
+        spread = dot(perm, blocks[...])
+        for t in range(width // HD):
+            out_ref[base : base + rows, t * slots : (t + 1) * slots, :] = (
+                spread[:, t * HD : (t + 1) * HD].reshape(rows, slots, HD).astype(BF16)
+            )
+
+
+def expert_kernel(core_ref, got_ref, w_ref, pair_ref, out_ref, scr):
+    core = core_ref[0]
+    reqs, lines, _ = got_ref.shape
+    slots = lines // 3
+    scr[...] = got_ref[...].astype(F32)
+    stats = scr[:, slots + 2, :]
+    lane = iota((reqs, HD), 1).astype(F32)
+    picks = []
+    peaks = [jnp.full((1, HD), NEGATIVE, F32) for _ in range(2)]
+    for g in range(slots + 1):
+        request = stats[:, 9 * g + 8 : 9 * g + 9]
+        live = stats[:, 9 * g + 1 : 9 * g + 2] > 0.0
+        pick = (request == lane) & live
+        picks.append((pick, live))
+        for i in range(2):
+            shift = stats[:, 9 * g + 3 * i : 9 * g + 3 * i + 1]
+            peaks[i] = jnp.maximum(
+                peaks[i], jnp.max(jnp.where(pick, shift, NEGATIVE), axis=0, keepdims=True)
+            )
+    whole = []
+    for g in range(slots + 1):
+        pick, live = picks[g]
+        lanes = []
+        sums = jnp.where(lane == 2.0, stats[:, 9 * g + 6 : 9 * g + 7] + stats[:, 9 * g + 7 : 9 * g + 8], 0.0)
+        for i in range(2):
+            at = 9 * g + 3 * i
+            peak = jnp.sum(jnp.where(pick, peaks[i], 0.0), axis=1, keepdims=True)
+            factor = jnp.where(live, jnp.exp(stats[:, at : at + 1] - peak), 0.0)
+            line = g if i == 0 else (2 * slots + g if g < slots else slots + 1)
+            lanes.append(scr[:, line, :] * factor)
+            den = stats[:, at + 1 : at + 2] + stats[:, at + 2 : at + 3]
+            sums = jnp.where(lane == float(i), den * factor, sums)
+        whole.append(jnp.concatenate(lanes + [sums], axis=1))
+    pick = jnp.concatenate([jnp.where(p, 1.0, 0.0) for p, _ in picks], axis=0).astype(BF16)
+    scaled = jnp.concatenate(whole, axis=0)
     high = scaled.astype(BF16)
     low = (scaled - high.astype(F32)).astype(BF16)
-    pick = jnp.where(owns, 1.0, 0.0).astype(BF16)
     TN = (((0,), (0,)), ((), ()))
     x = lax.dot_general(pick, high, TN, preferred_element_type=F32)
     x = x + lax.dot_general(pick, low, TN, preferred_element_type=F32)
     x = x[:reqs]
-    den = x[:, cut + 1 : cut + 2] + x[:, cut + 2 : cut + 3]
-    gate = x[:, cut + 3 : cut + 4] + x[:, cut + 4 : cut + 5]
-    some = den > 0.0
-    weighted = jnp.where(some, gate * (x / jnp.where(some, den, 1.0)), 0.0)[:, :cut].astype(BF16)
-    per = columns // len(out_refs)
-    for t, out_ref in enumerate(out_refs):
-        for i in range(per):
-            c = lax.rem(s + t, len(out_refs)) * per + i
-            out_ref[i] = dot(weighted, stack[c ^ j]).astype(out_ref.dtype)
+    gate = x[:, 2 * HD + 2 : 2 * HD + 3]
+    halves = []
+    for i in range(2):
+        den = x[:, 2 * HD + i : 2 * HD + i + 1]
+        some = den > 0.0
+        value = x[:, i * HD : (i + 1) * HD] / jnp.where(some, den, 1.0)
+        halves.append(jnp.where(some, gate * value, 0.0))
+    weighted = jnp.concatenate(halves, axis=1).astype(BF16)
+    depth = weighted.shape[1]
+    out_ref[core] = dot(weighted, w_ref[0, pl.ds(core * depth, depth), :])
+    out_ref[1 - core] = dot(weighted, pair_ref[...])
 
 
 def route_kernel(new_ref, table_ref, count_ref, out_ref):
@@ -233,18 +265,14 @@
     out_ref[...] = jnp.sum(found, axis=1, keepdims=True) - 1
 
 
-def relay_kernel(source_ref, rows_ref, *refs):
-    sum_refs, (out_ref, terms) = refs[:-2], refs[-2:]
+def relay_kernel(source_ref, rows_ref, sum_ref, out_ref, terms):
     devices, lines, _ = rows_ref.shape
     terms_at = out_ref.shape[1] - terms.shape[1]
     half = terms.shape[1] // 2
-    per = sum_refs[0].shape[0]
+    per = sum_ref.shape[0]
     for i in range(per):
-        total = sum_refs[0][i].astype(F32)
-        for ref in sum_refs[1:]:
-            total = total + ref[i].astype(F32)
         for t in range(half // per):
-            part = total[:, t * HD : (t + 1) * HD]
+            part = sum_ref[i, :, t * HD : (t + 1) * HD]
             high = part.astype(BF16).astype(F32)
             terms[:, i * (half // per) + t, :] = high
             terms[:, half + i * (half // per) + t, :] = part - high
@@ -314,7 +342,6 @@
     devices = lax.axis_size("pages")
     shard_count = lax.axis_size("expert")
     my = lax.axis_index("pages").astype(jnp.int32)
-    shard = lax.axis_index("expert").astype(jnp.int32)
     slots, page_len, width = old_keys.shape
     rows = keep_lists.shape[1] + 1
     per_new = page_len // rows
@@ -323,24 +350,22 @@
     local = new_cap * per_new
     heads = width // HD
     topk = queries.shape[1]
-    ent = 2 * slots
+    lines = 3 * slots
     columns = devices // EXPERTS
-    cut = width // columns
-    place = lax.rem(my, columns)
+    core = lax.rem(my, 2)
     table = page_table.T
     counts = request_pages.reshape(1, -1)
 
-    row_outbox, part_outbox = pl.pallas_call(
+    part_outbox, key_blocks, value_blocks = pl.pallas_call(
         source_kernel,
         out_shape=(
-            jax.ShapeDtypeStruct((devices, heads * slots, HD), BF16),
-            jax.ShapeDtypeStruct((devices, ent, HD), BF16),
+            jax.ShapeDtypeStruct((devices, lines, HD), BF16),
+            jax.ShapeDtypeStruct((slots * rows, width), BF16),
+            jax.ShapeDtypeStruct((slots * rows, width), BF16),
         ),
         in_specs=[SMEM] + [VMEM] * 11,
-        out_specs=(VMEM, VMEM),
+        out_specs=(VMEM, VMEM, VMEM),
         scratch_shapes=[
-            pltpu.VMEM((slots * rows, width), BF16),
-            pltpu.VMEM((slots * rows, width), BF16),
             pltpu.VMEM((slots, HD), F32),
             pltpu.VMEM((requests, topk, width), F32),
         ],
@@ -362,18 +387,19 @@
     part_inbox = lax.all_to_all(part_outbox, "pages", split_axis=0, concat_axis=0, tiled=True)
 
     weight, _ = lax.optimization_barrier((out_weight[0], part_outbox))
-    weight_rows = []
-    for d in range(columns):
-        piece = lax.dynamic_slice_in_dim(weight, (place ^ d) * cut, cut, 0)
-        if d:
-            swap = [(p, p // columns * columns + (p % columns ^ d)) for p in range(devices)]
-            piece = lax.ppermute(piece, "pages", swap)
-        weight_rows.append(piece)
-    row_outbox, part_inbox, weight_rows = lax.optimization_barrier(
-        (row_outbox, part_inbox, weight_rows)
+    depth = width // 2
+    pair_weight = lax.ppermute(
+        lax.dynamic_slice_in_dim(weight, (1 - core) * depth, depth, 0),
+        "pages",
+        [(p, p ^ 1) for p in range(devices)],
     )
-    row_inbox = lax.all_to_all(row_outbox, "pages", split_axis=0, concat_axis=0, tiled=True)
-
+    row_outbox = pl.pallas_call(
+        spread_kernel,
+        out_shape=jax.ShapeDtypeStruct((devices, heads * slots, HD), BF16),
+        in_specs=[VMEM, VMEM],
+        out_specs=VMEM,
+        name="spread",
+    )(key_blocks, value_blocks)
     source = pl.pallas_call(
         route_kernel,
         out_shape=jax.ShapeDtypeStruct((devices * local, 1), jnp.int32),
@@ -381,30 +407,38 @@
         out_specs=VMEM,
         name="route",
     )(new_table.T, table, counts)
-    per = columns // shard_count
+    row_outbox, part_inbox, pair_weight, source = lax.optimization_barrier(
+        (row_outbox, part_inbox, pair_weight, source)
+    )
+    row_inbox = lax.all_to_all(row_outbox, "pages", split_axis=0, concat_axis=0, tiled=True)
+
     block_cols = out_weight.shape[2]
-    contribs = pl.pallas_call(
+    contrib = pl.pallas_call(
         expert_kernel,
-        out_shape=[jax.ShapeDtypeStruct((per, requests, block_cols), BF16)] * shard_count,
-        in_specs=[SMEM] + [VMEM] * (1 + columns),
-        out_specs=[VMEM] * shard_count,
-        scratch_shapes=[pltpu.VMEM((columns, cut, block_cols), BF16)],
+        out_shape=jax.ShapeDtypeStruct((2, requests, block_cols), F32),
+        in_specs=[SMEM] + [VMEM] * 3,
+        out_specs=VMEM,
+        scratch_shapes=[pltpu.VMEM((requests, lines, HD), F32)],
         name="expert",
-    )(jnp.stack([place, shard]), part_inbox, *weight_rows)
-    moved = [contribs[0]]
-    for t in range(1, shard_count):
-        moved.append(
-            lax.ppermute(contribs[t], "expert", [(i, (i + t) % shard_count) for i in range(shard_count)])
-        )
-    terms = 2 * per * block_cols // HD
+    )(core.reshape(1), part_inbox, out_weight, pair_weight)
+    moves = []
+    for e in range(EXPERTS):
+        for z in range(columns // 2):
+            for c in range(2):
+                for s in range(shard_count):
+                    here = e * columns + 2 * z + c
+                    there = e * columns + 2 * s + c
+                    moves.append((here * shard_count + s, there * shard_count + z))
+    moved = lax.ppermute(contrib, ("pages", "expert"), moves)
+    terms = 2 * 2 * block_cols // HD
     routed = pl.pallas_call(
         relay_kernel,
         out_shape=jax.ShapeDtypeStruct((devices, heads * local + terms, HD), BF16),
-        in_specs=[VMEM] * (2 + shard_count),
+        in_specs=[VMEM] * 3,
         out_specs=VMEM,
         scratch_shapes=[pltpu.VMEM((requests, terms, HD), F32)],
         name="relay",
-    )(source, row_inbox, *moved)
+    )(source, row_inbox, moved)
     landed = lax.all_to_all(routed, "pages", split_axis=0, concat_axis=0, tiled=True)
     new_page = jax.ShapeDtypeStruct((new_cap, per_new * rows, width), BF16)
     return pl.pallas_call(

time: 104 us -> 109 us (1.048)
  starting transfers between devices: 38.1 us -> 21.5 us
  waiting for transfers between devices: 9.09 us -> 18.1 us
  blocking collectives: 37.7 us -> 45 us
  Pallas kernels: 15.8 us -> 21.5 us
    ppermute x10 -> x2, starting transfers between devices: 15.9 us -> 2.09 us  [the longest x1 1.55 us: shards(): moved = lax.ppermute(contrib, ('pages', 'expert'), moves)]
    all_to_all x1, waiting for transfers between devices: 0.01 us -> 9.74 us  [shards(): lax.all_to_all(part_outbox, 'pages', split_axis=0, concat_axis=0, tiled=T...]
    all_to_all x1, blocking collectives: 37.7 us -> 45 us  [shards(): lax.all_to_all(routed, 'pages', split_axis=0, concat_axis=0, tiled=True)]
    pallas_call x2 -> x3, Pallas kernels: 7.59 us -> 13.4 us  [the longest x1 7.42 us: shards(): pl.pallas_call(expert_kernel, out_shape=jax.ShapeDtypeStruct((2, requests...]
    ppermute x10 -> x2, waiting for transfers between devices: 3.13 us -> 0.01 us  [the longest x1 0.01 us: shards(): lax.ppermute(lax.dynamic_slice_in_dim(weight, (1 - core) * depth, depth,...]
    all_to_all x1, starting transfers between devices: 9 us -> 6.21 us  [shards(): lax.all_to_all(row_outbox, 'pages', split_axis=0, concat_axis=0, tiled=True)]
    all_to_all x1, waiting for transfers between devices: 5.95 us -> 8.33 us  [shards(): lax.all_to_all(row_outbox, 'pages', split_axis=0, concat_axis=0, tiled=True)]
  transfers between devices with their start and end apart: 12 -> 4, of which waited for: 5 -> 2; matrix products, arithmetic and copies ran while one was open for 1% -> 0% of each run, Pallas kernels for 5% -> 11%
where the time goes in v4:
time: 109 us; the launch traced here: 108 us
  blocking collectives  45 us (41%)
  Pallas kernels  21.5 us (20%)
  starting transfers between devices  21.5 us (20%)
  waiting for transfers between devices  18.1 us (17%)
    all_to_all x1, blocking collectives, shards(): lax.all_to_all(routed, 'pages', split_axis=0, concat_axis=0, tiled=True)  45 us
    all_to_all x1, starting transfers between devices, shards(): lax.all_to_all(part_outbox, 'pages', split_axis=0, concat_axis=0, tiled=T...  13.2 us
    all_to_all x1, waiting for transfers between devices, shards(): lax.all_to_all(part_outbox, 'pages', split_axis=0, concat_axis=0, tiled=T...  9.74 us
    all_to_all x1, waiting for transfers between devices, shards(): lax.all_to_all(row_outbox, 'pages', split_axis=0, concat_axis=0, tiled=True)  8.33 us
    pallas_call x1, Pallas kernels, shards(): pl.pallas_call(expert_kernel, out_shape=jax.ShapeDtypeStruct((2, requests...  7.42 us
    all_to_all x1, starting transfers between devices, shards(): lax.all_to_all(row_outbox, 'pages', split_axis=0, concat_axis=0, tiled=True)  6.21 us
    pallas_call x1, Pallas kernels, shards(): pl.pallas_call(source_kernel, out_shape=(jax.ShapeDtypeStruct((devices, l...  3.88 us
    pallas_call x1, Pallas kernels, shards(): pl.pallas_call(relay_kernel, out_shape=jax.ShapeDtypeStruct((devices, hea...  3.17 us
  transfers between devices with their start and end apart: 4, of which 2 were waited for; matrix products, arithmetic and copies ran while one was open for 0% of the time, Pallas kernels for 11%

profile of v4, /device:TPU:1, one launch (start us, length us, event | category | flops | bytes accessed | tf_op | source)
XLA Modules:
  0.0 107.6 jit_solution(17981559856287058213)
XLA Ops:
  0.6 0.0 copy-start.2
  0.6 3.9 %source.1 = (bf16[64,24,128]{2,1,0:T(8,128)(2,1)}, bf16[256,512]{1,0:T(8,128)(2,1)}, bf16[256,512]{1,0:T(8,128)(2,1)}) custom-call(s32[1]{0:T(128)} %bitcast.my_ref, s32[12,64]{1,0:T(8,128)} %bitcast.8, s32[1,64]{1,0:T(1,128)} %bitcast.11, s32[2,64]{1,0:T(2,128)} %bitcast.13, s32[8,31]{1,0:T(8,128)} %keep_ref.1, s32[8,128]{1,0:T(8,128)} %drop_ref.1, ...), custom_call_target="tpu_custom_call" | custom-call | tf_op jit(solution)/shard_map/source/pallas_call | solution.py:359
  4.5 13.2 %all-to-all-start = ((bf16[64,24,128]{2,1,0:T(8,128)(2,1)}), bf16[64,24,128]{2,1,0:T(8,128)(2,1)S(1)}, u32[]{:S(2)}, u32[]{:S(2)}) async-start(bf16[64,24,128]{2,1,0:T(8,128)(2,1)} %get-tuple-element.13), calls=%async_computation | async-start | bytes 786432 | tf_op jit(solution)/shard_map/all_to_all | solution.py:387
  17.7 0.0 copy-done.2
  17.7 0.5 collective-permute-start
  18.3 2.2 %route.1.source_ref = s32[1024,1]{1,0:T(8,128)} custom-call(s32[3,64]{1,0:T(4,128)} %bitcast.10, s32[12,64]{1,0:T(8,128)} %bitcast.9, s32[1,64]{1,0:T(1,128)} %bitcast.12), custom_call_target="tpu_custom_call" | custom-call | tf_op jit(solution)/shard_map/route/pallas_call | solution.py:403
  20.4 2.1 %spread.1 = bf16[64,32,128]{2,1,0:T(8,128)(2,1)} custom-call(bf16[256,512]{1,0:T(8,128)(2,1)} %get-tuple-element.11.kb_ref, bf16[256,512]{1,0:T(8,128)(2,1)} %get-tuple-element.12.vb_ref), custom_call_target="tpu_custom_call" | custom-call | tf_op jit(solution)/shard_map/spread/pallas_call | solution.py:396
  22.6 0.0 collective-permute-done.pair_ref
  22.6 0.0 copy-start.3
  22.6 9.7 %all-to-all-done.got_ref = bf16[64,24,128]{2,1,0:T(8,128)(2,1)S(1)} async-done(((bf16[64,24,128]{2,1,0:T(8,128)(2,1)}), bf16[64,24,128]{2,1,0:T(8,128)(2,1)S(1)}, u32[]{:S(2)}, u32[]{:S(2)}) %all-to-all-start) | async-done | bytes 393248 | tf_op jit(solution)/shard_map/all_to_all | solution.py:387
  32.3 0.0 copy-start.1
  32.3 6.2 %all-to-all-start.1 = ((bf16[64,32,128]{2,1,0:T(8,128)(2,1)}), bf16[64,32,128]{2,1,0:T(8,128)(2,1)S(1)}, u32[]{:S(2)}, u32[]{:S(2)}) async-start(bf16[64,32,128]{2,1,0:T(8,128)(2,1)} %spread.1), calls=%async_computation.1 | async-start | bytes 1048576 | tf_op jit(solution)/shard_map/all_to_all | solution.py:413
  38.5 0.0 copy-done.3
  38.5 0.0 copy-done.1
  38.5 7.4 %expert.1 = f32[2,64,256]{2,1,0:T(8,128)} custom-call(s32[1]{0:T(128)} %bitcast.6.core_ref, bf16[64,24,128]{2,1,0:T(8,128)(2,1)} %copy-done.1, bf16[1,512,256]{2,1,0:T(8,128)(2,1)} %w_ref.1, bf16[256,256]{1,0:T(8,128)(2,1)} %copy-done.3), custom_call_target="tpu_custom_call" | custom-call | tf_op jit(solution)/shard_map/expert/pallas_call | solution.py:416
  46.0 1.6 %collective-permute-start.1 = (f32[2,64,256]{2,1,0:T(8,128)}, f32[2,64,256]{2,1,0:T(8,128)S(1)}, u32[]{:S(2)}, u32[]{:S(2)}) collective-permute-start(f32[2,64,256]{2,1,0:T(8,128)} %expert.1), channel_id=1, source_target_pairs={{0,0},{1,8},{2,16},{3,24},{4,4},{5,12},{6,20},{7,28},{8,1},{9,9},{... | collective-permute-start | bytes 393224 | tf_op jit(solution)/shard_map/ppermute | solution.py:432
  47.5 0.0 collective-permute-done.1.sum_ref
  47.5 0.0 copy-start.4
  47.5 8.3 %all-to-all-done.1.rows_ref = bf16[64,32,128]{2,1,0:T(8,128)(2,1)S(1)} async-done(((bf16[64,32,128]{2,1,0:T(8,128)(2,1)}), bf16[64,32,128]{2,1,0:T(8,128)(2,1)S(1)}, u32[]{:S(2)}, u32[]{:S(2)}) %all-to-all-start.1) | async-done | bytes 524320 | tf_op jit(solution)/shard_map/all_to_all | solution.py:413
  55.8 0.0 copy-done.4
  55.8 0.0 copy-start
  55.8 0.8 copy-done
  56.6 3.2 %relay.1 = bf16[64,72,128]{2,1,0:T(8,128)(2,1)} custom-call(s32[1024,1]{1,0:T(8,128)} %route.1.source_ref, bf16[64,32,128]{2,1,0:T(8,128)(2,1)} %copy-done, f32[2,64,256]{2,1,0:T(8,128)} %copy-done.4), custom_call_target="tpu_custom_call" | custom-call | tf_op jit(solution)/shard_map/relay/pallas_call | solution.py:434
  59.8 45.0 %all_to_all.15.got_ref = bf16[64,72,128]{2,1,0:T(8,128)(2,1)} all-to-all(bf16[64,72,128]{2,1,0:T(8,128)(2,1)} %relay.1), channel_id=1, replica_groups=mesh['pages'=64,'expert'=4] {'pages'}, dimensions={0} | all-to-all | bytes 2359296 | tf_op jit(solution)/shard_map/all_to_all | solution.py:442
  104.8 2.8 %land.1 = (bf16[4,128,512]{2,1,0:T(8,128)(2,1)}, bf16[4,128,512]{2,1,0:T(8,128)(2,1)}, bf16[1,512]{1,0:T(2,128)(2,1)}) custom-call(bf16[64,72,128]{2,1,0:T(8,128)(2,1)} %all_to_all.15.got_ref), custom_call_target="tpu_custom_call" | custom-call | tf_op jit(solution)/shard_map/land/pallas_call | solution.py:444
  (1 shorter events, 0.0 us)
Async XLA Ops:
  0.6 17.1 %copy-start.2 = (bf16[1,512,256]{2,1,0:T(8,128)(2,1)S(1)}, bf16[1,512,256]{2,1,0:T(8,128)(2,1)}, u32[]{:S(2)}) copy-start(bf16[1,512,256]{2,1,0:T(8,128)(2,1)} %w_ref.1) | copy-start | bytes 786436
  4.5 27.8 %all-to-all-start = ((bf16[64,24,128]{2,1,0:T(8,128)(2,1)}), bf16[64,24,128]{2,1,0:T(8,128)(2,1)S(1)}, u32[]{:S(2)}, u32[]{:S(2)}) async-start(bf16[64,24,128]{2,1,0:T(8,128)(2,1)} %get-tuple-element.13), calls=%async_computation | async-start | bytes 786432 | tf_op jit(solution)/shard_map/all_to_all | solution.py:387
  17.7 4.8 %collective-permute-start = (bf16[256,256]{1,0:T(8,128)(2,1)S(1)}, bf16[256,256]{1,0:T(8,128)(2,1)S(1)}, u32[]{:S(2)}, u32[]{:S(2)}) collective-permute-start(bf16[256,256]{1,0:T(8,128)(2,1)S(1)} %constant_dynamic-slice_fusion), channel_id=1, source_target_pairs={{0,4},{4,0},{8,12},{12,8},{16,20},{20,16},{24,28},{28,24},{32,36},... | collective-permute-start | bytes 393224 | tf_op jit(solution)/shard_map/ppermute | solution.py:391
  22.6 16.0 %copy-start.3 = (bf16[256,256]{1,0:T(8,128)(2,1)}, bf16[256,256]{1,0:T(8,128)(2,1)S(1)}, u32[]{:S(2)}) copy-start(bf16[256,256]{1,0:T(8,128)(2,1)S(1)} %collective-permute-done.pair_ref) | copy-start | bytes 393220
  32.3 6.2 %copy-start.1 = (bf16[64,24,128]{2,1,0:T(8,128)(2,1)}, bf16[64,24,128]{2,1,0:T(8,128)(2,1)S(1)}, u32[]{:S(2)}) copy-start(bf16[64,24,128]{2,1,0:T(8,128)(2,1)S(1)} %all-to-all-done.got_ref) | copy-start | bytes 1179652
  32.3 23.5 %all-to-all-start.1 = ((bf16[64,32,128]{2,1,0:T(8,128)(2,1)}), bf16[64,32,128]{2,1,0:T(8,128)(2,1)S(1)}, u32[]{:S(2)}, u32[]{:S(2)}) async-start(bf16[64,32,128]{2,1,0:T(8,128)(2,1)} %spread.1), calls=%async_computation.1 | async-start | bytes 1048576 | tf_op jit(solution)/shard_map/all_to_all | solution.py:413
  46.0 1.6 %collective-permute-start.1 = (f32[2,64,256]{2,1,0:T(8,128)}, f32[2,64,256]{2,1,0:T(8,128)S(1)}, u32[]{:S(2)}, u32[]{:S(2)}) collective-permute-start(f32[2,64,256]{2,1,0:T(8,128)} %expert.1), channel_id=1, source_target_pairs={{0,0},{1,8},{2,16},{3,24},{4,4},{5,12},{6,20},{7,28},{8,1},{9,9},{... | collective-permute-start | bytes 393224 | tf_op jit(solution)/shard_map/ppermute | solution.py:432
  47.5 8.3 %copy-start.4 = (f32[2,64,256]{2,1,0:T(8,128)}, f32[2,64,256]{2,1,0:T(8,128)S(1)}, u32[]{:S(2)}) copy-start(f32[2,64,256]{2,1,0:T(8,128)S(1)} %collective-permute-done.1.sum_ref) | copy-start | bytes 393220
  55.8 0.8 copy-start

commit v5 on v4

--- a/solution.py
+++ b/solution.py
@@ -38,7 +38,7 @@
     nk_ref,
     nv_ref,
     logit_ref,
-    part_ref,
+    out_ref,
     kb,
     vb,
     keep_rows,
@@ -153,7 +153,8 @@
             part = jnp.where(first & (expert[k] == e), by_choice[k], part)
         parts.append(part)
     entries = jnp.concatenate(parts, axis=0).astype(BF16)
-    devices, lines, _ = part_ref.shape
+    devices = out_ref.shape[0]
+    lines = out_ref.shape[1] - heads * slots
     columns = devices // EXPERTS
     to = iota((EXPERTS * lines, EXPERTS * ent), 0)
     fro = iota((EXPERTS * lines, EXPERTS * ent), 1)
@@ -177,20 +178,15 @@
         sent = (sent + dot(flat, stats)).astype(BF16)
         for e in range(EXPERTS):
             for z in range(columns // 2):
-                part_ref[e * columns + 2 * z + c] = sent[e * lines : (e + 1) * lines, :]
-
-
-def spread_kernel(kb_ref, vb_ref, out_ref):
-    n, width = kb_ref.shape
-    rows = out_ref.shape[0] // 2
-    slots = n // rows
+                out_ref[e * columns + 2 * z + c, 0:lines, :] = sent[e * lines : (e + 1) * lines, :]
     to = iota((n, n), 0)
     fro = iota((n, n), 1)
     perm = jnp.where((to % slots == fro // rows) & (to // slots == fro % rows), 1.0, 0.0).astype(BF16)
-    for base, blocks in ((0, kb_ref), (rows, vb_ref)):
+    for base, blocks in ((0, kb), (rows, vb)):
         spread = dot(perm, blocks[...])
-        for t in range(width // HD):
-            out_ref[base : base + rows, t * slots : (t + 1) * slots, :] = (
+        for t in range(heads):
+            at = slice(lines + t * slots, lines + (t + 1) * slots)
+            out_ref[base : base + rows, at, :] = (
                 spread[:, t * HD : (t + 1) * HD].reshape(rows, slots, HD).astype(BF16)
             )
 
@@ -201,52 +197,49 @@
     slots = lines // 3
     scr[...] = got_ref[...].astype(F32)
     stats = scr[:, slots + 2, :]
-    lane = iota((reqs, HD), 1).astype(F32)
-    picks = []
-    peaks = [jnp.full((1, HD), NEGATIVE, F32) for _ in range(2)]
-    for g in range(slots + 1):
-        request = stats[:, 9 * g + 8 : 9 * g + 9]
-        live = stats[:, 9 * g + 1 : 9 * g + 2] > 0.0
-        pick = (request == lane) & live
-        picks.append((pick, live))
-        for i in range(2):
-            shift = stats[:, 9 * g + 3 * i : 9 * g + 3 * i + 1]
-            peaks[i] = jnp.maximum(
-                peaks[i], jnp.max(jnp.where(pick, shift, NEGATIVE), axis=0, keepdims=True)
-            )
-    whole = []
-    for g in range(slots + 1):
-        pick, live = picks[g]
-        lanes = []
-        sums = jnp.where(lane == 2.0, stats[:, 9 * g + 6 : 9 * g + 7] + stats[:, 9 * g + 7 : 9 * g + 8], 0.0)
-        for i in range(2):
-            at = 9 * g + 3 * i
-            peak = jnp.sum(jnp.where(pick, peaks[i], 0.0), axis=1, keepdims=True)
-            factor = jnp.where(live, jnp.exp(stats[:, at : at + 1] - peak), 0.0)
-            line = g if i == 0 else (2 * slots + g if g < slots else slots + 1)
-            lanes.append(scr[:, line, :] * factor)
-            den = stats[:, at + 1 : at + 2] + stats[:, at + 2 : at + 3]
-            sums = jnp.where(lane == float(i), den * factor, sums)
-        whole.append(jnp.concatenate(lanes + [sums], axis=1))
-    pick = jnp.concatenate([jnp.where(p, 1.0, 0.0) for p, _ in picks], axis=0).astype(BF16)
-    scaled = jnp.concatenate(whole, axis=0)
-    high = scaled.astype(BF16)
-    low = (scaled - high.astype(F32)).astype(BF16)
-    TN = (((0,), (0,)), ((), ()))
-    x = lax.dot_general(pick, high, TN, preferred_element_type=F32)
-    x = x + lax.dot_general(pick, low, TN, preferred_element_type=F32)
-    x = x[:reqs]
-    gate = x[:, 2 * HD + 2 : 2 * HD + 3]
+    stats = jnp.concatenate([stats, stats], axis=0).T
+    left = iota((1, 2 * reqs), 1) < reqs
+    target = iota((reqs, 2 * reqs), 0).astype(F32)
+
+    def item(g, i):
+        first = stats[9 * g + i : 9 * g + i + 1, :]
+        if g == slots:
+            return jnp.where(left, first, 0.0)
+        return jnp.where(left, first, stats[9 * g + 9 + i : 9 * g + 10 + i, :])
+
+    groups = range(0, slots + 1, 2)
+    picks = [(item(g, 8) == target) & (item(g, 1) > 0.0) for g in groups]
+    gate = jnp.zeros(target.shape, F32)
+    for g, pick in zip(groups, picks):
+        gate = gate + jnp.where(pick, item(g, 6) + item(g, 7), 0.0)
+    gate = jnp.sum(gate, axis=1, keepdims=True)
     halves = []
     for i in range(2):
-        den = x[:, 2 * HD + i : 2 * HD + i + 1]
+        peak = jnp.full(target.shape, NEGATIVE, F32)
+        for g, pick in zip(groups, picks):
+            peak = jnp.maximum(peak, jnp.where(pick, item(g, 3 * i), NEGATIVE))
+        peak = jnp.max(peak, axis=1, keepdims=True)
+        den = jnp.zeros(target.shape, F32)
+        num = jnp.zeros((2 * reqs, HD), F32)
+        for g, pick in zip(groups, picks):
+            factor = jnp.where(pick, jnp.exp(item(g, 3 * i) - peak), 0.0)
+            den = den + factor * (item(g, 3 * i + 1) + item(g, 3 * i + 2))
+            high = factor.astype(BF16)
+            low = (factor - high.astype(F32)).astype(BF16)
+            entries = []
+            for entry in (g, min(g + 1, slots)):
+                line = entry if i == 0 else (2 * slots + entry if entry < slots else slots + 1)
+                entries.append(scr[:, line, :])
+            entries = jnp.concatenate(entries, axis=0).astype(BF16)
+            num = num + dot(jnp.concatenate([high, low], axis=0), entries)
+        den = jnp.sum(den, axis=1, keepdims=True)
         some = den > 0.0
-        value = x[:, i * HD : (i + 1) * HD] / jnp.where(some, den, 1.0)
+        value = (num[:reqs] + num[reqs:]) / jnp.where(some, den, 1.0)
         halves.append(jnp.where(some, gate * value, 0.0))
     weighted = jnp.concatenate(halves, axis=1).astype(BF16)
     depth = weighted.shape[1]
-    out_ref[core] = dot(weighted, w_ref[0, pl.ds(core * depth, depth), :])
-    out_ref[1 - core] = dot(weighted, pair_ref[...])
+    out_ref[core] = dot(weighted, w_ref[0, pl.ds(core * depth, depth), :]).astype(BF16)
+    out_ref[1 - core] = dot(weighted, pair_ref[...]).astype(BF16)
 
 
 def route_kernel(new_ref, table_ref, count_ref, out_ref):
@@ -265,28 +258,14 @@
     out_ref[...] = jnp.sum(found, axis=1, keepdims=True) - 1
 
 
-def relay_kernel(source_ref, rows_ref, sum_ref, out_ref, terms):
-    devices, lines, _ = rows_ref.shape
-    terms_at = out_ref.shape[1] - terms.shape[1]
-    half = terms.shape[1] // 2
-    per = sum_ref.shape[0]
-    for i in range(per):
-        for t in range(half // per):
-            part = sum_ref[i, :, t * HD : (t + 1) * HD]
-            high = part.astype(BF16).astype(F32)
-            terms[:, i * (half // per) + t, :] = high
-            terms[:, half + i * (half // per) + t, :] = part - high
-    out_ref[:, terms_at:, :] = terms[...].astype(BF16)
-    tiles = 4
-    slots = lines // tiles
+def relay_kernel(source_ref, *refs):
+    row_refs, out_ref = refs[:-1], refs[-1]
+    tiles = len(row_refs)
+    devices, slots, _ = row_refs[0].shape
     held = devices * slots
-    local = terms_at // tiles
+    local = source_ref.shape[0] // devices
     table = jnp.concatenate(
-        [
-            rows_ref[:, t * slots : (t + 1) * slots, :].astype(F32).reshape(held, HD).astype(BF16)
-            for t in range(tiles)
-        ],
-        axis=1,
+        [ref[...].astype(F32).reshape(held, HD).astype(BF16) for ref in row_refs], axis=1
     )
     step = 16
     for c in range(0, devices, step):
@@ -299,10 +278,20 @@
             )
 
 
+def append_kernel(routed_ref, sum_ref, out_ref, terms):
+    del routed_ref
+    terms[...] = jnp.zeros(terms.shape, F32)
+    per, _, cols = sum_ref.shape
+    for i in range(per):
+        for t in range(cols // HD):
+            terms[:, i * (cols // HD) + t, :] = sum_ref[i, :, t * HD : (t + 1) * HD].astype(F32)
+    out_ref[...] = terms[...].astype(BF16)
+
+
 def land_kernel(got_ref, k_ref, v_ref, mixed_ref):
     total = got_ref.shape[0]
     tiles = k_ref.shape[2] // HD
-    terms_at = got_ref.shape[1] - 2 * tiles
+    terms_at = got_ref.shape[1] // (4 * tiles) * (4 * tiles)
     local = terms_at // tiles
     rows = total // 2
     n = rows * local
@@ -319,7 +308,7 @@
         )
         ref[...] = dot(perm, flat).reshape(ref.shape).astype(BF16)
     terms = jnp.sum(got_ref[:, terms_at:, :].astype(F32), axis=0)
-    mixed = (terms[:tiles] + terms[tiles:]).astype(BF16)
+    mixed = terms[:tiles].astype(BF16)
     for t in range(tiles):
         mixed_ref[:, t * HD : (t + 1) * HD] = mixed[t : t + 1, :]
 
@@ -356,16 +345,14 @@
     table = page_table.T
     counts = request_pages.reshape(1, -1)
 
-    part_outbox, key_blocks, value_blocks = pl.pallas_call(
+    outbox = pl.pallas_call(
         source_kernel,
-        out_shape=(
-            jax.ShapeDtypeStruct((devices, lines, HD), BF16),
-            jax.ShapeDtypeStruct((slots * rows, width), BF16),
-            jax.ShapeDtypeStruct((slots * rows, width), BF16),
-        ),
+        out_shape=jax.ShapeDtypeStruct((devices, lines + heads * slots, HD), BF16),
         in_specs=[SMEM] + [VMEM] * 11,
-        out_specs=(VMEM, VMEM, VMEM),
+        out_specs=VMEM,
         scratch_shapes=[
+            pltpu.VMEM((slots * rows, width), BF16),
+            pltpu.VMEM((slots * rows, width), BF16),
             pltpu.VMEM((slots, HD), F32),
             pltpu.VMEM((requests, topk, width), F32),
         ],
@@ -384,22 +371,15 @@
         new_values,
         router_logits,
     )
-    part_inbox = lax.all_to_all(part_outbox, "pages", split_axis=0, concat_axis=0, tiled=True)
-
-    weight, _ = lax.optimization_barrier((out_weight[0], part_outbox))
+    inbox = lax.all_to_all(outbox, "pages", split_axis=0, concat_axis=0, tiled=True)
+
+    weight, _ = lax.optimization_barrier((out_weight[0], outbox))
     depth = width // 2
     pair_weight = lax.ppermute(
         lax.dynamic_slice_in_dim(weight, (1 - core) * depth, depth, 0),
         "pages",
         [(p, p ^ 1) for p in range(devices)],
     )
-    row_outbox = pl.pallas_call(
-        spread_kernel,
-        out_shape=jax.ShapeDtypeStruct((devices, heads * slots, HD), BF16),
-        in_specs=[VMEM, VMEM],
-        out_specs=VMEM,
-        name="spread",
-    )(key_blocks, value_blocks)
     source = pl.pallas_call(
         route_kernel,
         out_shape=jax.ShapeDtypeStruct((devices * local, 1), jnp.int32),
@@ -407,20 +387,18 @@
         out_specs=VMEM,
         name="route",
     )(new_table.T, table, counts)
-    row_outbox, part_inbox, pair_weight, source = lax.optimization_barrier(
-        (row_outbox, part_inbox, pair_weight, source)
-    )
-    row_inbox = lax.all_to_all(row_outbox, "pages", split_axis=0, concat_axis=0, tiled=True)
+    inbox, pair_weight, source = lax.optimization_barrier((inbox, pair_weight, source))
 
     block_cols = out_weight.shape[2]
     contrib = pl.pallas_call(
         expert_kernel,
-        out_shape=jax.ShapeDtypeStruct((2, requests, block_cols), F32),
-        in_specs=[SMEM] + [VMEM] * 3,
+        grid=(1,),
+        out_shape=jax.ShapeDtypeStruct((2, requests, block_cols), BF16),
+        in_specs=[SMEM, pl.BlockSpec((devices, lines, HD), lambda i: (0, 0, 0)), VMEM, VMEM],
         out_specs=VMEM,
         scratch_shapes=[pltpu.VMEM((requests, lines, HD), F32)],
         name="expert",
-    )(core.reshape(1), part_inbox, out_weight, pair_weight)
+    )(core.reshape(1), inbox, out_weight, pair_weight)
     moves = []
     for e in range(EXPERTS):
         for z in range(columns // 2):
@@ -430,15 +408,31 @@
                     there = e * columns + 2 * s + c
                     moves.append((here * shard_count + s, there * shard_count + z))
     moved = lax.ppermute(contrib, ("pages", "expert"), moves)
-    terms = 2 * 2 * block_cols // HD
+
+    source, _ = lax.optimization_barrier((source, contrib))
+    chunk = heads * local + slots
     routed = pl.pallas_call(
         relay_kernel,
-        out_shape=jax.ShapeDtypeStruct((devices, heads * local + terms, HD), BF16),
-        in_specs=[VMEM] * 3,
+        grid=(1,),
+        out_shape=jax.ShapeDtypeStruct((devices, chunk, HD), BF16),
+        in_specs=[VMEM]
+        + [
+            pl.BlockSpec((devices, slots, HD), lambda i, t=t: (0, lines // slots + t, 0))
+            for t in range(heads)
+        ],
         out_specs=VMEM,
-        scratch_shapes=[pltpu.VMEM((requests, terms, HD), F32)],
         name="relay",
-    )(source, row_inbox, moved)
+    )(source, *[inbox] * heads)
+    routed = pl.pallas_call(
+        append_kernel,
+        grid=(1,),
+        out_shape=jax.ShapeDtypeStruct((devices, chunk, HD), BF16),
+        in_specs=[pl.BlockSpec(memory_space=pl.ANY), VMEM],
+        out_specs=pl.BlockSpec((devices, slots, HD), lambda i: (0, heads * local // slots, 0)),
+        scratch_shapes=[pltpu.VMEM((requests, slots, HD), F32)],
+        input_output_aliases={0: 0},
+        name="append",
+    )(routed, moved)
     landed = lax.all_to_all(routed, "pages", split_axis=0, concat_axis=0, tiled=True)
     new_page = jax.ShapeDtypeStruct((new_cap, per_new * rows, width), BF16)
     return pl.pallas_call(

time: 109 us -> 101 us (0.927); the launches traced: 108 us -> 101 us
  starting transfers between devices: 21.5 us -> 15.3 us
  Pallas kernels: 21.5 us -> 16.5 us
  waiting for transfers between devices: 18.1 us -> 23 us
  blocking collectives: 45 us -> 43.6 us
    all_to_all x2 -> x1, starting transfers between devices: 19.4 us -> 13.3 us  [shards(): lax.all_to_all(outbox, 'pages', split_axis=0, concat_axis=0, tiled=True)]
    pallas_call x4, Pallas kernels: 16.6 us -> 11.6 us  [the longest x1 4.23 us: shards(): pl.pallas_call(source_kernel, out_shape=jax.ShapeDtypeStruct((devices, li...]
    all_to_all x2 -> x1, waiting for transfers between devices: 18.1 us -> 23 us  [shards(): lax.all_to_all(outbox, 'pages', split_axis=0, concat_axis=0, tiled=True)]
    all_to_all x1, blocking collectives: 45 us -> 43.6 us  [shards(): lax.all_to_all(routed, 'pages', split_axis=0, concat_axis=0, tiled=True)]
  transfers between devices with their start and end apart: 4 -> 3, of which waited for: 2 -> 1; matrix products, arithmetic and copies ran while one was open for 0% -> 0% of each run, Pallas kernels for 11% -> 5%
where the time goes in v5:
time: 101 us
  blocking collectives  43.6 us (43%)
  waiting for transfers between devices  23 us (23%)
  Pallas kernels  16.5 us (16%)
  starting transfers between devices  15.3 us (15%)
  local copies, waits for them, and re-layouts  1.62 us (2%)
    all_to_all x1, blocking collectives, shards(): lax.all_to_all(routed, 'pages', split_axis=0, concat_axis=0, tiled=True)  43.6 us
    all_to_all x1, waiting for transfers between devices, shards(): lax.all_to_all(outbox, 'pages', split_axis=0, concat_axis=0, tiled=True)  23 us
    all_to_all x1, starting transfers between devices, shards(): lax.all_to_all(outbox, 'pages', split_axis=0, concat_axis=0, tiled=True)  13.3 us
    pallas_call x1, Pallas kernels, shards(): pl.pallas_call(source_kernel, out_shape=jax.ShapeDtypeStruct((devices, li...  4.23 us
    pallas_call x1, Pallas kernels, shards(): pl.pallas_call(relay_kernel, grid=(1,), out_shape=jax.ShapeDtypeStruct((d...  3.08 us
    pallas_call x1, Pallas kernels, shards(): pl.pallas_call(land_kernel, out_shape=(new_page, new_page, jax.ShapeDtype...  2.78 us
    pallas_call x1, Pallas kernels, shards(): pl.pallas_call(expert_kernel, grid=(1,), out_shape=jax.ShapeDtypeStruct((...  2.68 us
    pallas_call x1, Pallas kernels, shards(): pl.pallas_call(route_kernel, out_shape=jax.ShapeDtypeStruct((devices * lo...  2.16 us
  transfers between devices with their start and end apart: 3, of which 1 were waited for; matrix products, arithmetic and copies ran while one was open for 0% of the time, Pallas kernels for 5%

profile of v5, /device:TPU:1, one launch (start us, length us, event | category | flops | bytes accessed | tf_op | source)
XLA Modules:
  0.0 100.8 jit_solution(6290632023361517627)
XLA Ops:
  0.6 4.2 %source.1 = bf16[64,56,128]{2,1,0:T(8,128)(2,1)} custom-call(s32[1]{0:T(128)} %bitcast.my_ref, s32[12,64]{1,0:T(8,128)} %bitcast.8, s32[1,64]{1,0:T(1,128)} %bitcast.11, s32[2,64]{1,0:T(2,128)} %bitcast.13, s32[8,31]{1,0:T(8,128)} %keep_ref.1, s32[8,128]{1,0:T(8,128)} %drop_ref.1, bf16[8,128,512]{2,1,0:T(8,128)(2,1)} %k_ref.1, bf16[8,128,512]{2,1,0:T(8,128)(2,1)} %v_ref.1, ...), custom_call_target="tpu_custom_call" | custom-call | tf_op jit(solution)/shard_map/source/pallas_call | solution.py:348
  4.9 0.0 copy-start.1
  4.9 13.3 %all-to-all-start = ((bf16[64,56,128]{2,1,0:T(8,128)(2,1)}), bf16[64,56,128]{2,1,0:T(8,128)(2,1)S(1)}, u32[]{:S(2)}, u32[]{:S(2)}) async-start(bf16[64,56,128]{2,1,0:T(8,128)(2,1)} %source.1), calls=%async_computation | async-start | bytes 1835008 | tf_op jit(solution)/shard_map/all_to_all | solution.py:374
  18.2 0.0 copy-done.1
  18.2 0.5 collective-permute-start
  18.8 2.2 %route.1.source_ref = s32[1024,1]{1,0:T(8,128)} custom-call(s32[3,64]{1,0:T(4,128)} %bitcast.10, s32[12,64]{1,0:T(8,128)} %bitcast.9, s32[1,64]{1,0:T(1,128)} %bitcast.12), custom_call_target="tpu_custom_call" | custom-call | tf_op jit(solution)/shard_map/route/pallas_call | solution.py:383
  20.9 0.0 collective-permute-done.pair_ref
  20.9 0.0 copy-start.2
  20.9 23.0 %all-to-all-done.got_ref.refs_0_.refs_1_.refs_2_.refs_3_ = bf16[64,56,128]{2,1,0:T(8,128)(2,1)S(1)} async-done(((bf16[64,56,128]{2,1,0:T(8,128)(2,1)}), bf16[64,56,128]{2,1,0:T(8,128)(2,1)S(1)}, u32[]{:S(2)}, u32[]{:S(2)}) %all-to-all-start) | async-done | bytes 917536 | tf_op jit(solution)/shard_map/all_to_all | solution.py:374
  43.9 0.0 copy-start
  43.9 0.0 copy-done.2
  43.9 1.0 copy-done
  44.9 2.7 %expert.1 = bf16[2,64,256]{2,1,0:T(8,128)(2,1)} custom-call(s32[1]{0:T(128)} %bitcast.6.core_ref, bf16[64,56,128]{2,1,0:T(8,128)(2,1)} %copy-done, bf16[1,512,256]{2,1,0:T(8,128)(2,1)} %w_ref.1, bf16[256,256]{1,0:T(8,128)(2,1)} %copy-done.2), custom_call_target="tpu_custom_call" | custom-call | tf_op jit(solution)/shard_map/expert/pallas_call | solution.py:393
  47.6 1.5 %collective-permute-start.1 = (bf16[2,64,256]{2,1,0:T(8,128)(2,1)}, bf16[2,64,256]{2,1,0:T(8,128)(2,1)S(1)}, u32[]{:S(2)}, u32[]{:S(2)}) collective-permute-start(bf16[2,64,256]{2,1,0:T(8,128)(2,1)} %expert.1), channel_id=1, source_target_pairs={{0,0},{1,8},{2,16},{3,24},{4,4},{5,12},{6,20},{7,28},{8,1},{9,9},{... | collective-permute-start | bytes 196616 | tf_op jit(solution)/shard_map/ppermute | solution.py:410
  49.1 3.1 %relay.1.routed_ref = bf16[64,72,128]{2,1,0:T(8,128)(2,1)} custom-call(s32[1024,1]{1,0:T(8,128)} %route.1.source_ref, bf16[64,56,128]{2,1,0:T(8,128)(2,1)} %copy-done, bf16[64,56,128]{2,1,0:T(8,128)(2,1)} %copy-done, bf16[64,56,128]{2,1,0:T(8,128)(2,1)} %copy-done, bf16[64,56,128]{2,1,0:T(8,128)(2,1)} %copy-done), custom_call_target="tpu_custom_call" | custom-call | tf_op jit(solution)/shard_map/relay/pallas_call | solution.py:414
  52.1 0.0 collective-permute-done.1.sum_ref
  52.1 0.0 copy-start.3
  52.1 0.6 copy-done.3
  52.8 1.6 %append.1 = bf16[64,72,128]{2,1,0:T(8,128)(2,1)} custom-call(bf16[64,72,128]{2,1,0:T(8,128)(2,1)} %relay.1.routed_ref, bf16[2,64,256]{2,1,0:T(8,128)(2,1)} %copy-done.3), custom_call_target="tpu_custom_call", output_to_operand_aliasing={{}: (0, {})} | custom-call | tf_op jit(solution)/shard_map/append/pallas_call | solution.py:426
  54.4 43.6 %all_to_all.10.got_ref = bf16[64,72,128]{2,1,0:T(8,128)(2,1)} all-to-all(bf16[64,72,128]{2,1,0:T(8,128)(2,1)} %append.1), channel_id=1, replica_groups=mesh['pages'=64,'expert'=4] {'pages'}, dimensions={0} | all-to-all | bytes 2359296 | tf_op jit(solution)/shard_map/all_to_all | solution.py:436
  98.0 2.8 %land.1 = (bf16[4,128,512]{2,1,0:T(8,128)(2,1)}, bf16[4,128,512]{2,1,0:T(8,128)(2,1)}, bf16[1,512]{1,0:T(2,128)(2,1)}) custom-call(bf16[64,72,128]{2,1,0:T(8,128)(2,1)} %all_to_all.10.got_ref), custom_call_target="tpu_custom_call" | custom-call | tf_op jit(solution)/shard_map/land/pallas_call | solution.py:438
  (1 shorter events, 0.0 us)
Async XLA Ops:
  4.9 13.3 %copy-start.1 = (bf16[1,512,256]{2,1,0:T(8,128)(2,1)S(1)}, bf16[1,512,256]{2,1,0:T(8,128)(2,1)}, u32[]{:S(2)}) copy-start(bf16[1,512,256]{2,1,0:T(8,128)(2,1)} %w_ref.1) | copy-start | bytes 786436
  4.9 39.0 %all-to-all-start = ((bf16[64,56,128]{2,1,0:T(8,128)(2,1)}), bf16[64,56,128]{2,1,0:T(8,128)(2,1)S(1)}, u32[]{:S(2)}, u32[]{:S(2)}) async-start(bf16[64,56,128]{2,1,0:T(8,128)(2,1)} %source.1), calls=%async_computation | async-start | bytes 1835008 | tf_op jit(solution)/shard_map/all_to_all | solution.py:374
  18.2 2.7 %collective-permute-start = (bf16[256,256]{1,0:T(8,128)(2,1)S(1)}, bf16[256,256]{1,0:T(8,128)(2,1)S(1)}, u32[]{:S(2)}, u32[]{:S(2)}) collective-permute-start(bf16[256,256]{1,0:T(8,128)(2,1)S(1)} %constant_dynamic-slice_fusion), channel_id=1, source_target_pairs={{0,4},{4,0},{8,12},{12,8},{16,20},{20,16},{24,28},{28,24},{32,36},... | collective-permute-start | bytes 393224 | tf_op jit(solution)/shard_map/ppermute | solution.py:378
  20.9 23.0 %copy-start.2 = (bf16[256,256]{1,0:T(8,128)(2,1)}, bf16[256,256]{1,0:T(8,128)(2,1)S(1)}, u32[]{:S(2)}) copy-start(bf16[256,256]{1,0:T(8,128)(2,1)S(1)} %collective-permute-done.pair_ref) | copy-start | bytes 393220
  43.9 1.0 copy-start
  47.6 4.6 %collective-permute-start.1 = (bf16[2,64,256]{2,1,0:T(8,128)(2,1)}, bf16[2,64,256]{2,1,0:T(8,128)(2,1)S(1)}, u32[]{:S(2)}, u32[]{:S(2)}) collective-permute-start(bf16[2,64,256]{2,1,0:T(8,128)(2,1)} %expert.1), channel_id=1, source_target_pairs={{0,0},{1,8},{2,16},{3,24},{4,4},{5,12},{6,20},{7,28},{8,1},{9,9},{... | collective-permute-start | bytes 196616 | tf_op jit(solution)/shard_map/ppermute | solution.py:410
  52.1 0.6 copy-start.3

commit v6 on v5

--- a/solution.py
+++ b/solution.py
@@ -152,33 +152,26 @@
         for k in range(topk):
             part = jnp.where(first & (expert[k] == e), by_choice[k], part)
         parts.append(part)
-    entries = jnp.concatenate(parts, axis=0).astype(BF16)
+    entries = jnp.concatenate(parts, axis=0)
+    stats = entries[:, width:].astype(BF16)
     devices = out_ref.shape[0]
     lines = out_ref.shape[1] - heads * slots
     columns = devices // EXPERTS
     to = iota((EXPERTS * lines, EXPERTS * ent), 0)
     fro = iota((EXPERTS * lines, EXPERTS * ent), 1)
-    alike = to // lines == fro // ent
-    line = to % lines
-    entry = fro % ent
-    one = jnp.where(alike & (line == entry) & (entry <= slots), 1.0, 0.0).astype(BF16)
-    two_line = jnp.where(entry == slots, slots + 1, 2 * slots + entry)
-    two = jnp.where(alike & (line == two_line) & (entry <= slots), 1.0, 0.0).astype(BF16)
-    flat = jnp.where(alike & (line == slots + 2), 1.0, 0.0).astype(BF16)
-    for c in range(2):
-        base = c * 2 * HD
-        lane_out = iota((HD, HD), 1)
-        item = lane_out % 9
-        origin = jnp.where(item < 6, 6 * c + item, 3 * heads + item - 6)
-        copy = jnp.where(iota((HD, HD), 0) == origin, 1.0, 0.0).astype(BF16)
-        stats = dot(entries[:, width:], copy)
-        mine = iota(stats.shape, 1) // 9 == iota(stats.shape, 0) % ent
-        stats = jnp.where(mine, stats, 0.0).astype(BF16)
-        sent = dot(one, entries[:, base : base + HD]) + dot(two, entries[:, base + HD : base + 2 * HD])
-        sent = (sent + dot(flat, stats)).astype(BF16)
+    flat = (to // lines == fro // ent) & (to % lines == slots + 1)
+    flat = jnp.where(flat, 1.0, 0.0).astype(BF16)
+    square = iota((HD, HD), 0)
+    item = iota((HD, HD), 1) % 6
+    mine = iota((EXPERTS * ent, HD), 1) // 6 == iota((EXPERTS * ent, HD), 0) % ent
+    for h in range(heads):
+        origin = jnp.where(item < 3, 3 * h + item, 3 * heads + item - 3)
+        spread = dot(stats, jnp.where(square == origin, 1.0, 0.0).astype(BF16))
+        line = dot(flat, jnp.where(mine, spread, 0.0).astype(BF16))
+        sent = (entries[:, h * HD : (h + 1) * HD] + line).astype(BF16)
         for e in range(EXPERTS):
-            for z in range(columns // 2):
-                out_ref[e * columns + 2 * z + c, 0:lines, :] = sent[e * lines : (e + 1) * lines, :]
+            for z in range(columns // heads):
+                out_ref[e * columns + z * heads + h, 0:lines, :] = sent[e * lines : (e + 1) * lines, :]
     to = iota((n, n), 0)
     fro = iota((n, n), 1)
     perm = jnp.where((to % slots == fro // rows) & (to // slots == fro % rows), 1.0, 0.0).astype(BF16)
@@ -191,55 +184,76 @@
             )
 
 
-def expert_kernel(core_ref, got_ref, w_ref, pair_ref, out_ref, scr):
-    core = core_ref[0]
-    reqs, lines, _ = got_ref.shape
-    slots = lines // 3
-    scr[...] = got_ref[...].astype(F32)
-    stats = scr[:, slots + 2, :]
+def middle_kernel(head_ref, got_ref, pick_ref, *refs):
+    w_refs, (out_ref, scr, terms, stack) = refs[:-4], refs[-4:]
+    heads = len(w_refs)
+    head = head_ref[0]
+    reqs, lines, _ = scr.shape
+    slots = lines // 2
+    depth = stack.shape[1]
+    stack[0] = w_refs[0][0, pl.ds(head * depth, depth), :]
+    for d in range(1, heads):
+        stack[d] = w_refs[d][...]
+    scr[...] = got_ref[:, 0:lines, :].astype(F32)
+    stats = scr[:, slots + 1, :]
     stats = jnp.concatenate([stats, stats], axis=0).T
     left = iota((1, 2 * reqs), 1) < reqs
     target = iota((reqs, 2 * reqs), 0).astype(F32)
 
     def item(g, i):
-        first = stats[9 * g + i : 9 * g + i + 1, :]
+        first = stats[6 * g + i : 6 * g + i + 1, :]
         if g == slots:
             return jnp.where(left, first, 0.0)
-        return jnp.where(left, first, stats[9 * g + 9 + i : 9 * g + 10 + i, :])
+        return jnp.where(left, first, stats[6 * g + 6 + i : 6 * g + 7 + i, :])
 
     groups = range(0, slots + 1, 2)
-    picks = [(item(g, 8) == target) & (item(g, 1) > 0.0) for g in groups]
+    picks = [(item(g, 5) == target) & (item(g, 1) > 0.0) for g in groups]
     gate = jnp.zeros(target.shape, F32)
+    peak = jnp.full(target.shape, NEGATIVE, F32)
     for g, pick in zip(groups, picks):
-        gate = gate + jnp.where(pick, item(g, 6) + item(g, 7), 0.0)
+        gate = gate + jnp.where(pick, item(g, 3) + item(g, 4), 0.0)
+        peak = jnp.maximum(peak, jnp.where(pick, item(g, 0), NEGATIVE))
     gate = jnp.sum(gate, axis=1, keepdims=True)
-    halves = []
-    for i in range(2):
-        peak = jnp.full(target.shape, NEGATIVE, F32)
-        for g, pick in zip(groups, picks):
-            peak = jnp.maximum(peak, jnp.where(pick, item(g, 3 * i), NEGATIVE))
-        peak = jnp.max(peak, axis=1, keepdims=True)
-        den = jnp.zeros(target.shape, F32)
-        num = jnp.zeros((2 * reqs, HD), F32)
-        for g, pick in zip(groups, picks):
-            factor = jnp.where(pick, jnp.exp(item(g, 3 * i) - peak), 0.0)
-            den = den + factor * (item(g, 3 * i + 1) + item(g, 3 * i + 2))
-            high = factor.astype(BF16)
-            low = (factor - high.astype(F32)).astype(BF16)
-            entries = []
-            for entry in (g, min(g + 1, slots)):
-                line = entry if i == 0 else (2 * slots + entry if entry < slots else slots + 1)
-                entries.append(scr[:, line, :])
-            entries = jnp.concatenate(entries, axis=0).astype(BF16)
-            num = num + dot(jnp.concatenate([high, low], axis=0), entries)
-        den = jnp.sum(den, axis=1, keepdims=True)
-        some = den > 0.0
-        value = (num[:reqs] + num[reqs:]) / jnp.where(some, den, 1.0)
-        halves.append(jnp.where(some, gate * value, 0.0))
-    weighted = jnp.concatenate(halves, axis=1).astype(BF16)
-    depth = weighted.shape[1]
-    out_ref[core] = dot(weighted, w_ref[0, pl.ds(core * depth, depth), :]).astype(BF16)
-    out_ref[1 - core] = dot(weighted, pair_ref[...]).astype(BF16)
+    peak = jnp.max(peak, axis=1, keepdims=True)
+    den = jnp.zeros(target.shape, F32)
+    num = jnp.zeros((2 * reqs, HD), F32)
+    for g, pick in zip(groups, picks):
+        factor = jnp.where(pick, jnp.exp(item(g, 0) - peak), 0.0)
+        den = den + factor * (item(g, 1) + item(g, 2))
+        high = factor.astype(BF16)
+        low = (factor - high.astype(F32)).astype(BF16)
+        entries = jnp.concatenate([scr[:, g, :], scr[:, min(g + 1, slots), :]], axis=0).astype(BF16)
+        num = num + dot(jnp.concatenate([high, low], axis=0), entries)
+    den = jnp.sum(den, axis=1, keepdims=True)
+    some = den > 0.0
+    value = (num[:reqs] + num[reqs:]) / jnp.where(some, den, 1.0)
+    weighted = jnp.where(some, gate * value, 0.0).astype(BF16)
+    tiles = stack.shape[2] // HD
+    for b in range(heads):
+        part = dot(weighted, stack[b ^ head])
+        for t in range(tiles):
+            terms[:, b * tiles + t, :] = part[:, t * HD : (t + 1) * HD]
+    terms_at = out_ref.shape[1] - heads * tiles
+    out_ref[:, terms_at:, :] = terms[...].astype(BF16)
+    held = reqs * slots
+    local = pick_ref.shape[0] // reqs
+    table = jnp.concatenate(
+        [
+            got_ref[:, lines + t * slots : lines + (t + 1) * slots, :]
+            .astype(F32)
+            .reshape(held, HD)
+            .astype(BF16)
+            for t in range(terms_at // local)
+        ],
+        axis=1,
+    )
+    step = 16
+    for c in range(0, reqs, step):
+        rows = dot(pick_ref[c * local : (c + step) * local, :], table)
+        for t in range(terms_at // local):
+            out_ref[c : c + step, t * local : (t + 1) * local, :] = (
+                rows[:, t * HD : (t + 1) * HD].reshape(step, local, HD).astype(BF16)
+            )
 
 
 def route_kernel(new_ref, table_ref, count_ref, out_ref):
@@ -255,46 +269,45 @@
         for w in range(per_new):
             page = jnp.where(quarter == w, table_ref[i * per_new + w : i * per_new + w + 1, :] + 1, page)
         found = jnp.where(filled == slot, page, found)
-    out_ref[...] = jnp.sum(found, axis=1, keepdims=True) - 1
-
-
-def relay_kernel(source_ref, *refs):
-    row_refs, out_ref = refs[:-1], refs[-1]
-    tiles = len(row_refs)
-    devices, slots, _ = row_refs[0].shape
-    held = devices * slots
-    local = source_ref.shape[0] // devices
-    table = jnp.concatenate(
-        [ref[...].astype(F32).reshape(held, HD).astype(BF16) for ref in row_refs], axis=1
-    )
-    step = 16
-    for c in range(0, devices, step):
-        source = source_ref[c * local : (c + step) * local, :]
-        pick = jnp.where(source == iota((step * local, held), 1), 1.0, 0.0).astype(BF16)
-        rows = dot(pick, table)
-        for t in range(tiles):
-            out_ref[c : c + step, t * local : (t + 1) * local, :] = (
-                rows[:, t * HD : (t + 1) * HD].reshape(step, local, HD).astype(BF16)
-            )
-
-
-def append_kernel(routed_ref, sum_ref, out_ref, terms):
-    del routed_ref
-    terms[...] = jnp.zeros(terms.shape, F32)
-    per, _, cols = sum_ref.shape
-    for i in range(per):
-        for t in range(cols // HD):
-            terms[:, i * (cols // HD) + t, :] = sum_ref[i, :, t * HD : (t + 1) * HD].astype(F32)
-    out_ref[...] = terms[...].astype(BF16)
-
-
-def land_kernel(got_ref, k_ref, v_ref, mixed_ref):
+    source = jnp.sum(found, axis=1, keepdims=True) - 1
+    out_ref[...] = jnp.where(source == iota(out_ref.shape, 1), 1.0, 0.0).astype(BF16)
+
+
+def sum_kernel(shard_ref, got_ref, *refs):
+    out_refs, (quarters,) = refs[:-1], refs[-1:]
+    s = shard_ref[0]
+    count = len(out_refs)
+    heads = count
+    columns = got_ref.shape[0] // EXPERTS
+    got = got_ref[...].astype(F32)
+    per = got.shape[1] // 2
+    for z in range(columns // heads):
+        total = jnp.zeros(got.shape[1:], F32)
+        for e in range(EXPERTS):
+            at = e * columns + z * heads
+            total = total + jnp.sum(got[at : at + heads], axis=0)
+        for i in range(2):
+            quarters[2 * z + i] = total[i * per : (i + 1) * per]
+    for t, out_ref in enumerate(out_refs):
+        out_ref[...] = quarters[lax.rem(s + t, count)]
+
+
+def final_kernel(*refs):
+    out_ref = refs[-1]
+    total = refs[0][...]
+    for ref in refs[1:-1]:
+        total = total + ref[...]
+    mixed = total.astype(BF16)
+    for t in range(mixed.shape[0]):
+        out_ref[:, t * HD : (t + 1) * HD] = mixed[t : t + 1, :]
+
+
+def land_kernel(got_ref, k_ref, v_ref):
     total = got_ref.shape[0]
     tiles = k_ref.shape[2] // HD
-    terms_at = got_ref.shape[1] // (4 * tiles) * (4 * tiles)
-    local = terms_at // tiles
     rows = total // 2
-    n = rows * local
+    n = k_ref.shape[0] * k_ref.shape[1]
+    local = n // rows
     to = iota((n, n), 0)
     fro = iota((n, n), 1)
     perm = jnp.where((to // rows == fro % local) & (to % rows == fro // local), 1.0, 0.0).astype(BF16)
@@ -307,10 +320,6 @@
             axis=1,
         )
         ref[...] = dot(perm, flat).reshape(ref.shape).astype(BF16)
-    terms = jnp.sum(got_ref[:, terms_at:, :].astype(F32), axis=0)
-    mixed = terms[:tiles].astype(BF16)
-    for t in range(tiles):
-        mixed_ref[:, t * HD : (t + 1) * HD] = mixed[t : t + 1, :]
 
 
 def shards(
@@ -339,9 +348,10 @@
     local = new_cap * per_new
     heads = width // HD
     topk = queries.shape[1]
-    lines = 3 * slots
+    lines = 2 * slots
     columns = devices // EXPERTS
-    core = lax.rem(my, 2)
+    head = lax.rem(my, heads)
+    shard = lax.axis_index("expert").astype(jnp.int32).reshape(1)
     table = page_table.T
     counts = request_pages.reshape(1, -1)
 
@@ -374,74 +384,75 @@
     inbox = lax.all_to_all(outbox, "pages", split_axis=0, concat_axis=0, tiled=True)
 
     weight, _ = lax.optimization_barrier((out_weight[0], outbox))
-    depth = width // 2
-    pair_weight = lax.ppermute(
-        lax.dynamic_slice_in_dim(weight, (1 - core) * depth, depth, 0),
-        "pages",
-        [(p, p ^ 1) for p in range(devices)],
-    )
-    source = pl.pallas_call(
+    weights = [out_weight]
+    for d in range(1, heads):
+        weights.append(
+            lax.ppermute(
+                lax.dynamic_slice_in_dim(weight, (head ^ d) * HD, HD, 0),
+                "pages",
+                [(p, p ^ d) for p in range(devices)],
+            )
+        )
+    pick = pl.pallas_call(
         route_kernel,
-        out_shape=jax.ShapeDtypeStruct((devices * local, 1), jnp.int32),
+        out_shape=jax.ShapeDtypeStruct((devices * local, devices * slots), BF16),
         in_specs=[VMEM] * 3,
         out_specs=VMEM,
         name="route",
     )(new_table.T, table, counts)
-    inbox, pair_weight, source = lax.optimization_barrier((inbox, pair_weight, source))
+    inbox, pick, weights = lax.optimization_barrier((inbox, pick, weights))
 
     block_cols = out_weight.shape[2]
-    contrib = pl.pallas_call(
-        expert_kernel,
+    terms = heads * block_cols // HD
+    routed = pl.pallas_call(
+        middle_kernel,
+        out_shape=jax.ShapeDtypeStruct((devices, heads * local + terms, HD), BF16),
+        in_specs=[SMEM] + [VMEM] * (2 + heads),
+        out_specs=VMEM,
+        scratch_shapes=[
+            pltpu.VMEM((requests, lines, HD), F32),
+            pltpu.VMEM((requests, terms, HD), F32),
+            pltpu.VMEM((heads, HD, block_cols), BF16),
+        ],
+        name="middle",
+    )(head.reshape(1), inbox, pick, *weights)
+    landed = lax.all_to_all(routed, "pages", split_axis=0, concat_axis=0, tiled=True)
+
+    quarter = jax.ShapeDtypeStruct((width // HD, HD), F32)
+    quarters = pl.pallas_call(
+        sum_kernel,
         grid=(1,),
-        out_shape=jax.ShapeDtypeStruct((2, requests, block_cols), BF16),
-        in_specs=[SMEM, pl.BlockSpec((devices, lines, HD), lambda i: (0, 0, 0)), VMEM, VMEM],
-        out_specs=VMEM,
-        scratch_shapes=[pltpu.VMEM((requests, lines, HD), F32)],
-        name="expert",
-    )(core.reshape(1), inbox, out_weight, pair_weight)
-    moves = []
-    for e in range(EXPERTS):
-        for z in range(columns // 2):
-            for c in range(2):
-                for s in range(shard_count):
-                    here = e * columns + 2 * z + c
-                    there = e * columns + 2 * s + c
-                    moves.append((here * shard_count + s, there * shard_count + z))
-    moved = lax.ppermute(contrib, ("pages", "expert"), moves)
-
-    source, _ = lax.optimization_barrier((source, contrib))
-    chunk = heads * local + slots
-    routed = pl.pallas_call(
-        relay_kernel,
-        grid=(1,),
-        out_shape=jax.ShapeDtypeStruct((devices, chunk, HD), BF16),
-        in_specs=[VMEM]
-        + [
-            pl.BlockSpec((devices, slots, HD), lambda i, t=t: (0, lines // slots + t, 0))
-            for t in range(heads)
+        out_shape=[quarter] * shard_count,
+        in_specs=[
+            SMEM,
+            pl.BlockSpec((devices, terms, HD), lambda i: (0, heads * local // terms, 0)),
         ],
-        out_specs=VMEM,
-        name="relay",
-    )(source, *[inbox] * heads)
-    routed = pl.pallas_call(
-        append_kernel,
-        grid=(1,),
-        out_shape=jax.ShapeDtypeStruct((devices, chunk, HD), BF16),
-        in_specs=[pl.BlockSpec(memory_space=pl.ANY), VMEM],
-        out_specs=pl.BlockSpec((devices, slots, HD), lambda i: (0, heads * local // slots, 0)),
-        scratch_shapes=[pltpu.VMEM((requests, slots, HD), F32)],
-        input_output_aliases={0: 0},
-        name="append",
-    )(routed, moved)
-    landed = lax.all_to_all(routed, "pages", split_axis=0, concat_axis=0, tiled=True)
+        out_specs=[VMEM] * shard_count,
+        scratch_shapes=[pltpu.VMEM((shard_count, width // HD, HD), F32)],
+        name="sum",
+    )(shard, landed)
+    landed, quarters = lax.optimization_barrier((landed, quarters))
+    moved = [quarters[0]]
+    for t in range(1, shard_count):
+        moved.append(
+            lax.ppermute(quarters[t], "expert", [(i, (i + t) % shard_count) for i in range(shard_count)])
+        )
     new_page = jax.ShapeDtypeStruct((new_cap, per_new * rows, width), BF16)
-    return pl.pallas_call(
+    compact_keys, compact_values = pl.pallas_call(
         land_kernel,
-        out_shape=(new_page, new_page, jax.ShapeDtypeStruct((1, width), BF16)),
+        out_shape=(new_page, new_page),
         in_specs=[VMEM],
-        out_specs=(VMEM, VMEM, VMEM),
+        out_specs=(VMEM, VMEM),
         name="land",
     )(landed)
+    mixed = pl.pallas_call(
+        final_kernel,
+        out_shape=jax.ShapeDtypeStruct((1, width), BF16),
+        in_specs=[VMEM] * shard_count,
+        out_specs=VMEM,
+        name="final",
+    )(*moved)
+    return (compact_keys, compact_values, mixed)
 
 
 def solution(mesh):

time: 101 us -> 99 us (0.980)
  blocking collectives: 43.6 us -> 0 us
  waiting for transfers between devices: 23 us -> 49.8 us
  starting transfers between devices: 15.3 us -> 28.6 us
  local copies, waits for them, and re-layouts: 1.62 us -> 3.09 us
    all_to_all x1 -> x0, blocking collectives: 43.6 us -> none  [shards(): lax.all_to_all(routed, 'pages', split_axis=0, concat_axis=0, tiled=True)]
    all_to_all x0 -> x1, waiting for transfers between devices: none -> 31.4 us  [shards(): lax.all_to_all(routed, 'pages', split_axis=0, concat_axis=0, tiled=True)]
    all_to_all x1, waiting for transfers between devices: 23 us -> 1.55 us  [shards(): lax.all_to_all(outbox, 'pages', split_axis=0, concat_axis=0, tiled=True)]
    ppermute x2 -> x6, waiting for transfers between devices: 0.01 us -> 16.9 us  [the longest x3 16.9 us: shards(): lax.ppermute(lax.dynamic_slice_in_dim(weight, (head ^ d) * HD, HD, 0), 'p...]
    all_to_all x0 -> x1, starting transfers between devices: none -> 8.23 us  [shards(): lax.all_to_all(routed, 'pages', split_axis=0, concat_axis=0, tiled=True)]
    ppermute x2 -> x6, starting transfers between devices: 2.03 us -> 7.05 us  [the longest x3 4.82 us: shards(): lax.ppermute(quarters[t], 'expert', [(i, (i + t) % shard_count) for i in...]
    unnamed x8 -> x18, local copies, waits for them, and re-layouts: 1.61 us -> 3.06 us
  transfers between devices with their start and end apart: 3 -> 8, of which waited for: 1 -> 4; matrix products, arithmetic and copies ran while one was open for 0% -> 0% of each run, Pallas kernels for 5% -> 5%
where the time goes in v6:
time: 99 us; the launch traced here: 98.6 us
  waiting for transfers between devices  49.8 us (50%)
  starting transfers between devices  28.6 us (29%)
  Pallas kernels  16.3 us (16%)
  local copies, waits for them, and re-layouts  3.09 us (3%)
    all_to_all x1, waiting for transfers between devices, shards(): lax.all_to_all(routed, 'pages', split_axis=0, concat_axis=0, tiled=True)  31.4 us
    ppermute x3, waiting for transfers between devices, shards(): lax.ppermute(lax.dynamic_slice_in_dim(weight, (head ^ d) * HD, HD, 0), 'p...  16.9 us
    all_to_all x1, starting transfers between devices, shards(): lax.all_to_all(outbox, 'pages', split_axis=0, concat_axis=0, tiled=True)  13.3 us
    all_to_all x1, starting transfers between devices, shards(): lax.all_to_all(routed, 'pages', split_axis=0, concat_axis=0, tiled=True)  8.23 us
    ppermute x3, starting transfers between devices, shards(): lax.ppermute(quarters[t], 'expert', [(i, (i + t) % shard_count) for i in...  4.82 us
    pallas_call x1, Pallas kernels, shards(): pl.pallas_call(source_kernel, out_shape=jax.ShapeDtypeStruct((devices, li...  4.33 us
    pallas_call x1, Pallas kernels, shards(): pl.pallas_call(middle_kernel, out_shape=jax.ShapeDtypeStruct((devices, he...  3.97 us
    unnamed x18, local copies, waits for them, and re-layouts  3.06 us
  transfers between devices with their start and end apart: 8, of which 4 were waited for; matrix products, arithmetic and copies ran while one was open for 0% of the time, Pallas kernels for 5%

profile of v6, /device:TPU:1, one launch (start us, length us, event | category | flops | bytes accessed | tf_op | source)
XLA Modules:
  0.0 98.6 jit_solution(14781353554029259148)
XLA Ops:
  0.6 4.3 %source.1 = bf16[64,48,128]{2,1,0:T(8,128)(2,1)} custom-call(s32[1]{0:T(128)} %bitcast.1.my_ref, s32[12,64]{1,0:T(8,128)} %bitcast.9, s32[1,64]{1,0:T(1,128)} %bitcast.12, s32[2,64]{1,0:T(2,128)} %bitcast.14, s32[8,31]{1,0:T(8,128)} %keep_ref.1, s32[8,128]{1,0:T(8,128)} %drop_ref.1, bf16[8,128,512]{2,1,0:T(8,128)(2,1)} %k_ref.1, bf16[8,128,512]{2,1,0:T(8,128)(2,1)} %v_ref.1, ...), custom_call_target="tpu_custom_call" | custom-call | tf_op jit(solution)/shard_map/source/pallas_call | solution.py:358
  5.0 0.0 copy-start.2
  5.0 13.3 %all-to-all-start = ((bf16[64,48,128]{2,1,0:T(8,128)(2,1)}), bf16[64,48,128]{2,1,0:T(8,128)(2,1)S(1)}, u32[]{:S(2)}, u32[]{:S(2)}) async-start(bf16[64,48,128]{2,1,0:T(8,128)(2,1)} %source.1), calls=%async_computation | async-start | bytes 1572864 | tf_op jit(solution)/shard_map/all_to_all | solution.py:384
  18.3 0.0 copy-done.2
  18.3 1.7 %collective-permute-start.2 = (bf16[128,256]{1,0:T(8,128)(2,1)S(1)}, bf16[128,256]{1,0:T(8,128)(2,1)S(1)}, u32[]{:S(2)}, u32[]{:S(2)}) collective-permute-start(bf16[128,256]{1,0:T(8,128)(2,1)S(1)} %get-tuple-element.39), channel_id=1, source_target_pairs={{0,12},{4,8},{8,4},{12,0},{16,28},{20,24},{24,20},{28,16},{32,44},... | collective-permute-start | bytes 196616 | tf_op jit(solution)/shard_map/ppermute | solution.py:390
  20.0 0.2 collective-permute-start.1
  20.2 0.3 collective-permute-start
  20.6 2.4 %route.1.pick_ref = bf16[1024,512]{1,0:T(8,128)(2,1)} custom-call(s32[3,64]{1,0:T(4,128)} %bitcast.11, s32[12,64]{1,0:T(8,128)} %bitcast.10, s32[1,64]{1,0:T(1,128)} %bitcast.13), custom_call_target="tpu_custom_call" | custom-call | tf_op jit(solution)/shard_map/route/pallas_call | solution.py:396
  23.0 16.5 %collective-permute-done.2.refs_3_ = bf16[128,256]{1,0:T(8,128)(2,1)S(1)} collective-permute-done((bf16[128,256]{1,0:T(8,128)(2,1)S(1)}, bf16[128,256]{1,0:T(8,128)(2,1)S(1)}, u32[]{:S(2)}, u32[]{:S(2)}) %collective-permute-start.2) | collective-permute-done | bytes 65568 | tf_op jit(solution)/shard_map/ppermute | solution.py:390
  39.5 0.0 copy-start.3
  39.5 0.5 collective-permute-done.1.refs_2_
  39.9 0.0 copy-start.4
  39.9 0.0 collective-permute-done.refs_1_
  39.9 0.0 copy-start.5
  39.9 1.5 %all-to-all-done.got_ref = bf16[64,48,128]{2,1,0:T(8,128)(2,1)S(1)} async-done(((bf16[64,48,128]{2,1,0:T(8,128)(2,1)}), bf16[64,48,128]{2,1,0:T(8,128)(2,1)S(1)}, u32[]{:S(2)}, u32[]{:S(2)}) %all-to-all-start) | async-done | bytes 786464 | tf_op jit(solution)/shard_map/all_to_all | solution.py:384
  41.5 0.0 copy-start.1
  41.5 0.0 copy-done.3
  41.5 0.0 copy-done.4
  41.5 0.0 copy-done.5
  41.5 0.9 copy-done.1
  42.4 4.0 %middle.1 = bf16[64,72,128]{2,1,0:T(8,128)(2,1)} custom-call(s32[1]{0:T(128)} %bitcast.head_ref, bf16[64,48,128]{2,1,0:T(8,128)(2,1)} %copy-done.1, bf16[1024,512]{1,0:T(8,128)(2,1)} %route.1.pick_ref, bf16[1,512,256]{2,1,0:T(8,128)(2,1)} %refs_0_, bf16[128,256]{1,0:T(8,128)(2,1)} %copy-done.5, bf16[128,256]{1,0:T(8,128)(2,1)} %copy-done.4, ...), custom_call_target="tpu_custom_call" | custom-call | tf_op jit(solution)/shard_map/middle/pallas_call | solution.py:407
  46.3 8.2 %all-to-all-start.1 = ((bf16[64,72,128]{2,1,0:T(8,128)(2,1)}), bf16[64,72,128]{2,1,0:T(8,128)(2,1)S(1)}, u32[]{:S(2)}, u32[]{:S(2)}) async-start(bf16[64,72,128]{2,1,0:T(8,128)(2,1)} %middle.1), calls=%async_computation.1 | async-start | bytes 2359296 | tf_op jit(solution)/shard_map/all_to_all | solution.py:419
  54.6 31.4 %all-to-all-done.1.got_ref = bf16[64,72,128]{2,1,0:T(8,128)(2,1)S(1)} async-done(((bf16[64,72,128]{2,1,0:T(8,128)(2,1)}), bf16[64,72,128]{2,1,0:T(8,128)(2,1)S(1)}, u32[]{:S(2)}, u32[]{:S(2)}) %all-to-all-start.1) | async-done | bytes 1179680 | tf_op jit(solution)/shard_map/all_to_all | solution.py:419
  85.9 0.0 copy-start
  85.9 1.0 %copy-done = bf16[64,72,128]{2,1,0:T(8,128)(2,1)} copy-done((bf16[64,72,128]{2,1,0:T(8,128)(2,1)}, bf16[64,72,128]{2,1,0:T(8,128)(2,1)S(1)}, u32[]{:S(2)}) %copy-start) | copy-done | bytes 1179672
  87.0 1.5 %sum.1 = (f32[4,128]{1,0:T(4,128)}, f32[4,128]{1,0:T(4,128)}, f32[4,128]{1,0:T(4,128)}, f32[4,128]{1,0:T(4,128)}) custom-call(s32[1]{0:T(128)} %bitcast.7.shard_ref, bf16[64,72,128]{2,1,0:T(8,128)(2,1)} %copy-done), custom_call_target="tpu_custom_call" | custom-call | tf_op jit(solution)/shard_map/sum/pallas_call | solution.py:422
  88.5 1.2 %collective-permute-start.3 = (f32[4,128]{1,0:T(4,128)}, f32[4,128]{1,0:T(4,128)S(1)}, u32[]{:S(2)}, u32[]{:S(2)}) collective-permute-start(f32[4,128]{1,0:T(4,128)} %get-tuple-element.36), channel_id=1, source_target_pairs={{0,1},{1,2},{2,3},{3,0},{4,5},{5,6},{6,7},{7,4},{8,9},{9,10},{10,1... | collective-permute-start | bytes 6152 | tf_op jit(solution)/shard_map/ppermute | solution.py:438
  89.7 2.5 %collective-permute-start.4 = (f32[4,128]{1,0:T(4,128)}, f32[4,128]{1,0:T(4,128)S(1)}, u32[]{:S(2)}, u32[]{:S(2)}) collective-permute-start(f32[4,128]{1,0:T(4,128)} %get-tuple-element.37), channel_id=1, source_target_pairs={{0,2},{1,3},{2,0},{3,1},{4,6},{5,7},{6,4},{7,5},{8,10},{9,11},{10,... | collective-permute-start | bytes 6152 | tf_op jit(solution)/shard_map/ppermute | solution.py:438
  92.2 1.2 %collective-permute-start.5 = (f32[4,128]{1,0:T(4,128)}, f32[4,128]{1,0:T(4,128)S(1)}, u32[]{:S(2)}, u32[]{:S(2)}) collective-permute-start(f32[4,128]{1,0:T(4,128)} %get-tuple-element.38), channel_id=1, source_target_pairs={{0,3},{1,0},{2,1},{3,2},{4,7},{5,4},{6,5},{7,6},{8,11},{9,8},{10,9... | collective-permute-start | bytes 6152 | tf_op jit(solution)/shard_map/ppermute | solution.py:438
  93.3 2.8 %land.1 = (bf16[4,128,512]{2,1,0:T(8,128)(2,1)}, bf16[4,128,512]{2,1,0:T(8,128)(2,1)}) custom-call(bf16[64,72,128]{2,1,0:T(8,128)(2,1)} %copy-done), custom_call_target="tpu_custom_call" | custom-call | tf_op jit(solution)/shard_map/land/pallas_call | solution.py:441
  96.1 0.0 collective-permute-done.3.refs_1_
  96.1 0.0 copy-start.6
  96.1 0.0 collective-permute-done.4.refs_2_
  96.1 0.0 copy-start.7
  96.1 0.0 collective-permute-done.5.refs_3_
  96.2 0.5 copy-done.6
  96.7 0.0 copy-done.7
  96.7 0.0 copy-start.8
  96.7 0.6 copy-done.8
  97.3 1.3 %final.1 = bf16[1,512]{1,0:T(2,128)(2,1)} custom-call(f32[4,128]{1,0:T(4,128)} %get-tuple-element.35.refs_0_, f32[4,128]{1,0:T(4,128)} %copy-done.6, f32[4,128]{1,0:T(4,128)} %copy-done.7, f32[4,128]{1,0:T(4,128)} %copy-done.8), custom_call_target="tpu_custom_call" | custom-call | tf_op jit(solution)/shard_map/final/pallas_call | solution.py:448
  (1 shorter events, 0.0 us)
Async XLA Ops:
  5.0 13.3 %copy-start.2 = (bf16[1,512,256]{2,1,0:T(8,128)(2,1)S(1)}, bf16[1,512,256]{2,1,0:T(8,128)(2,1)}, u32[]{:S(2)}) copy-start(bf16[1,512,256]{2,1,0:T(8,128)(2,1)} %refs_0_) | copy-start | bytes 786436
  5.0 36.5 %all-to-all-start = ((bf16[64,48,128]{2,1,0:T(8,128)(2,1)}), bf16[64,48,128]{2,1,0:T(8,128)(2,1)S(1)}, u32[]{:S(2)}, u32[]{:S(2)}) async-start(bf16[64,48,128]{2,1,0:T(8,128)(2,1)} %source.1), calls=%async_computation | async-start | bytes 1572864 | tf_op jit(solution)/shard_map/all_to_all | solution.py:384
  18.3 21.1 %collective-permute-start.2 = (bf16[128,256]{1,0:T(8,128)(2,1)S(1)}, bf16[128,256]{1,0:T(8,128)(2,1)S(1)}, u32[]{:S(2)}, u32[]{:S(2)}) collective-permute-start(bf16[128,256]{1,0:T(8,128)(2,1)S(1)} %get-tuple-element.39), channel_id=1, source_target_pairs={{0,12},{4,8},{8,4},{12,0},{16,28},{20,24},{24,20},{28,16},{32,44},... | collective-permute-start | bytes 196616 | tf_op jit(solution)/shard_map/ppermute | solution.py:390
  20.0 19.9 %collective-permute-start.1 = (bf16[128,256]{1,0:T(8,128)(2,1)S(1)}, bf16[128,256]{1,0:T(8,128)(2,1)S(1)}, u32[]{:S(2)}, u32[]{:S(2)}) collective-permute-start(bf16[128,256]{1,0:T(8,128)(2,1)S(1)} %get-tuple-element.40), channel_id=1, source_target_pairs={{0,8},{4,12},{8,0},{12,4},{16,24},{20,28},{24,16},{28,20},{32,40},... | collective-permute-start | bytes 196616 | tf_op jit(solution)/shard_map/ppermute | solution.py:390
  20.2 19.7 %collective-permute-start = (bf16[128,256]{1,0:T(8,128)(2,1)S(1)}, bf16[128,256]{1,0:T(8,128)(2,1)S(1)}, u32[]{:S(2)}, u32[]{:S(2)}) collective-permute-start(bf16[128,256]{1,0:T(8,128)(2,1)S(1)} %get-tuple-element.41), channel_id=1, source_target_pairs={{0,4},{4,0},{8,12},{12,8},{16,20},{20,16},{24,28},{28,24},{32,36},... | collective-permute-start | bytes 196616 | tf_op jit(solution)/shard_map/ppermute | solution.py:390
  39.5 2.0 %copy-start.3 = (bf16[128,256]{1,0:T(8,128)(2,1)}, bf16[128,256]{1,0:T(8,128)(2,1)S(1)}, u32[]{:S(2)}) copy-start(bf16[128,256]{1,0:T(8,128)(2,1)S(1)} %collective-permute-done.2.refs_3_) | copy-start | bytes 196612
  39.9 1.6 %copy-start.4 = (bf16[128,256]{1,0:T(8,128)(2,1)}, bf16[128,256]{1,0:T(8,128)(2,1)S(1)}, u32[]{:S(2)}) copy-start(bf16[128,256]{1,0:T(8,128)(2,1)S(1)} %collective-permute-done.1.refs_2_) | copy-start | bytes 196612
  39.9 1.6 %copy-start.5 = (bf16[128,256]{1,0:T(8,128)(2,1)}, bf16[128,256]{1,0:T(8,128)(2,1)S(1)}, u32[]{:S(2)}) copy-start(bf16[128,256]{1,0:T(8,128)(2,1)S(1)} %collective-permute-done.refs_1_) | copy-start | bytes 196612
  41.5 0.9 copy-start.1
  46.3 39.6 %all-to-all-start.1 = ((bf16[64,72,128]{2,1,0:T(8,128)(2,1)}), bf16[64,72,128]{2,1,0:T(8,128)(2,1)S(1)}, u32[]{:S(2)}, u32[]{:S(2)}) async-start(bf16[64,72,128]{2,1,0:T(8,128)(2,1)} %middle.1), calls=%async_computation.1 | async-start | bytes 2359296 | tf_op jit(solution)/shard_map/all_to_all | solution.py:419
  85.9 1.0 %copy-start = (bf16[64,72,128]{2,1,0:T(8,128)(2,1)}, bf16[64,72,128]{2,1,0:T(8,128)(2,1)S(1)}, u32[]{:S(2)}) copy-start(bf16[64,72,128]{2,1,0:T(8,128)(2,1)S(1)} %all-to-all-done.1.got_ref) | copy-start | bytes 3538948
  88.5 7.6 %collective-permute-start.3 = (f32[4,128]{1,0:T(4,128)}, f32[4,128]{1,0:T(4,128)S(1)}, u32[]{:S(2)}, u32[]{:S(2)}) collective-permute-start(f32[4,128]{1,0:T(4,128)} %get-tuple-element.36), channel_id=1, source_target_pairs={{0,1},{1,2},{2,3},{3,0},{4,5},{5,6},{6,7},{7,4},{8,9},{9,10},{10,1... | collective-permute-start | bytes 6152 | tf_op jit(solution)/shard_map/ppermute | solution.py:438
  89.7 6.4 %collective-permute-start.4 = (f32[4,128]{1,0:T(4,128)}, f32[4,128]{1,0:T(4,128)S(1)}, u32[]{:S(2)}, u32[]{:S(2)}) collective-permute-start(f32[4,128]{1,0:T(4,128)} %get-tuple-element.37), channel_id=1, source_target_pairs={{0,2},{1,3},{2,0},{3,1},{4,6},{5,7},{6,4},{7,5},{8,10},{9,11},{10,... | collective-permute-start | bytes 6152 | tf_op jit(solution)/shard_map/ppermute | solution.py:438
  92.2 4.0 %collective-permute-start.5 = (f32[4,128]{1,0:T(4,128)}, f32[4,128]{1,0:T(4,128)S(1)}, u32[]{:S(2)}, u32[]{:S(2)}) collective-permute-start(f32[4,128]{1,0:T(4,128)} %get-tuple-element.38), channel_id=1, source_target_pairs={{0,3},{1,0},{2,1},{3,2},{4,7},{5,4},{6,5},{7,6},{8,11},{9,8},{10,9... | collective-permute-start | bytes 6152 | tf_op jit(solution)/shard_map/ppermute | solution.py:438
  96.1 0.6 copy-start.6
  96.1 0.6 copy-start.7
  96.7 0.6 copy-start.8

commit v7 on v6

--- a/solution.py
+++ b/solution.py
@@ -14,6 +14,8 @@
 BF16 = jnp.bfloat16
 VMEM = pl.BlockSpec(memory_space=pltpu.VMEM)
 SMEM = pl.BlockSpec(memory_space=pltpu.SMEM)
+ANY = pl.BlockSpec(memory_space=pl.ANY)
+PARAMS = pltpu.CompilerParams(vmem_limit_bytes=28 << 20)
 NT = (((1,), (1,)), ((), ()))
 
 
@@ -32,20 +34,35 @@
     ids_ref,
     keep_ref,
     drop_ref,
-    k_ref,
-    v_ref,
+    k_hbm,
+    v_hbm,
     q_ref,
     nk_ref,
     nv_ref,
     logit_ref,
-    out_ref,
+    out_hbm,
     kb,
     vb,
     keep_rows,
     q_rows,
+    k_ref,
+    v_ref,
+    out_ref,
+    sems,
+    out_sem,
 ):
     my = my_ref[0]
     slots, page_len, width = k_ref.shape
+    loads = []
+    for g in range(slots):
+        loads.append(
+            (
+                pltpu.make_async_copy(k_hbm.at[g], k_ref.at[g], sems.at[2 * g]),
+                pltpu.make_async_copy(v_hbm.at[g], v_ref.at[g], sems.at[2 * g + 1]),
+            )
+        )
+        for load in loads[g]:
+            load.start()
     keep_count = keep_ref.shape[1]
     rows = keep_count + 1
     heads = width // HD
@@ -63,6 +80,8 @@
         total = jnp.sum(coef, axis=1, keepdims=True)
         mat = jnp.where(last, coef, onehot).astype(BF16)
         denom = jnp.where(last[:, 0:1], total, 1.0)
+        for load in loads[g]:
+            load.wait()
         kb[g * rows : (g + 1) * rows, :] = (dot(mat, k_ref[g]) / denom).astype(BF16)
         vb[g * rows : (g + 1) * rows, :] = (dot(mat, v_ref[g]) / denom).astype(BF16)
     n = slots * rows
@@ -182,19 +201,33 @@
             out_ref[base : base + rows, at, :] = (
                 spread[:, t * HD : (t + 1) * HD].reshape(rows, slots, HD).astype(BF16)
             )
-
-
-def middle_kernel(head_ref, got_ref, pick_ref, *refs):
-    w_refs, (out_ref, scr, terms, stack) = refs[:-4], refs[-4:]
+    store = pltpu.make_async_copy(out_ref, out_hbm, out_sem)
+    store.start()
+    store.wait()
+
+
+def middle_kernel(head_ref, got_hbm, pick_hbm, *refs):
+    w_refs, (out_hbm, scr, terms, stack, parts, got_ref, pick_ref, out_ref, sems, out_sems) = (
+        refs[:-10],
+        refs[-10:],
+    )
     heads = len(w_refs)
     head = head_ref[0]
     reqs, lines, _ = scr.shape
     slots = lines // 2
     depth = stack.shape[1]
-    stack[0] = w_refs[0][0, pl.ds(head * depth, depth), :]
+    loads = [pltpu.make_async_copy(got_hbm.at[:, 0:lines, :], parts, sems.at[0])]
+    loads.append(
+        pltpu.make_async_copy(w_refs[0].at[0, pl.ds(head * depth, depth), :], stack.at[0], sems.at[1])
+    )
     for d in range(1, heads):
-        stack[d] = w_refs[d][...]
-    scr[...] = got_ref[:, 0:lines, :].astype(F32)
+        loads.append(pltpu.make_async_copy(w_refs[d], stack.at[d], sems.at[1 + d]))
+    loads.append(pltpu.make_async_copy(got_hbm.at[:, lines:, :], got_ref, sems.at[heads + 1]))
+    loads.append(pltpu.make_async_copy(pick_hbm, pick_ref, sems.at[heads + 2]))
+    for load in loads:
+        load.start()
+    loads[0].wait()
+    scr[...] = parts[...].astype(F32)
     stats = scr[:, slots + 1, :]
     stats = jnp.concatenate([stats, stats], axis=0).T
     left = iota((1, 2 * reqs), 1) < reqs
@@ -229,6 +262,8 @@
     value = (num[:reqs] + num[reqs:]) / jnp.where(some, den, 1.0)
     weighted = jnp.where(some, gate * value, 0.0).astype(BF16)
     tiles = stack.shape[2] // HD
+    for load in loads[1 : 1 + heads]:
+        load.wait()
     for b in range(heads):
         part = dot(weighted, stack[b ^ head])
         for t in range(tiles):
@@ -237,9 +272,11 @@
     out_ref[:, terms_at:, :] = terms[...].astype(BF16)
     held = reqs * slots
     local = pick_ref.shape[0] // reqs
+    for load in loads[1 + heads :]:
+        load.wait()
     table = jnp.concatenate(
         [
-            got_ref[:, lines + t * slots : lines + (t + 1) * slots, :]
+            got_ref[:, t * slots : (t + 1) * slots, :]
             .astype(F32)
             .reshape(held, HD)
             .astype(BF16)
@@ -248,12 +285,18 @@
         axis=1,
     )
     step = 16
+    stores = []
     for c in range(0, reqs, step):
         rows = dot(pick_ref[c * local : (c + step) * local, :], table)
         for t in range(terms_at // local):
             out_ref[c : c + step, t * local : (t + 1) * local, :] = (
                 rows[:, t * HD : (t + 1) * HD].reshape(step, local, HD).astype(BF16)
             )
+        at = pl.ds(c, step)
+        stores.append(pltpu.make_async_copy(out_ref.at[at], out_hbm.at[at], out_sems.at[c // step]))
+        stores[-1].start()
+    for store in stores:
+        store.wait()
 
 
 def route_kernel(new_ref, table_ref, count_ref, out_ref):
@@ -273,8 +316,12 @@
     out_ref[...] = jnp.where(source == iota(out_ref.shape, 1), 1.0, 0.0).astype(BF16)
 
 
-def sum_kernel(shard_ref, got_ref, *refs):
-    out_refs, (quarters,) = refs[:-1], refs[-1:]
+def sum_kernel(shard_ref, got_hbm, *refs):
+    out_refs, (quarters, got_ref, sem) = refs[:-3], refs[-3:]
+    terms = got_ref.shape[1]
+    load = pltpu.make_async_copy(got_hbm.at[:, got_hbm.shape[1] - terms :, :], got_ref, sem)
+    load.start()
+    load.wait()
     s = shard_ref[0]
     count = len(out_refs)
     heads = count
@@ -289,29 +336,29 @@
         for i in range(2):
             quarters[2 * z + i] = total[i * per : (i + 1) * per]
     for t, out_ref in enumerate(out_refs):
-        out_ref[...] = quarters[lax.rem(s + t, count)]
-
-
-def final_kernel(*refs):
-    out_ref = refs[-1]
-    total = refs[0][...]
-    for ref in refs[1:-1]:
-        total = total + ref[...]
-    mixed = total.astype(BF16)
-    for t in range(mixed.shape[0]):
-        out_ref[:, t * HD : (t + 1) * HD] = mixed[t : t + 1, :]
-
-
-def land_kernel(got_ref, k_ref, v_ref):
+        quarter = quarters[lax.rem(s + t, count)]
+        for i in range(per):
+            out_ref[:, i * HD : (i + 1) * HD] = quarter[i : i + 1, :]
+
+
+def land_kernel(got_hbm, k_hbm, v_hbm, got_ref, k_ref, v_ref, sems, out_sems):
     total = got_ref.shape[0]
     tiles = k_ref.shape[2] // HD
     rows = total // 2
+    loads = []
+    for i in range(2):
+        at = pl.ds(i * rows, rows)
+        loads.append(pltpu.make_async_copy(got_hbm.at[at], got_ref.at[at], sems.at[i]))
+        loads[i].start()
     n = k_ref.shape[0] * k_ref.shape[1]
     local = n // rows
     to = iota((n, n), 0)
     fro = iota((n, n), 1)
     perm = jnp.where((to // rows == fro % local) & (to % rows == fro // local), 1.0, 0.0).astype(BF16)
-    for base, ref in ((0, k_ref), (rows, v_ref)):
+    stores = []
+    for i, (ref, hbm) in enumerate(((k_ref, k_hbm), (v_ref, v_hbm))):
+        base = i * rows
+        loads[i].wait()
         flat = jnp.concatenate(
             [
                 got_ref[base : base + rows, t * local : (t + 1) * local, :].reshape(n, HD)
@@ -320,6 +367,10 @@
             axis=1,
         )
         ref[...] = dot(perm, flat).reshape(ref.shape).astype(BF16)
+        stores.append(pltpu.make_async_copy(ref, hbm, out_sems.at[i]))
+        stores[i].start()
+    for store in stores:
+        store.wait()
 
 
 def shards(
@@ -358,13 +409,18 @@
     outbox = pl.pallas_call(
         source_kernel,
         out_shape=jax.ShapeDtypeStruct((devices, lines + heads * slots, HD), BF16),
-        in_specs=[SMEM] + [VMEM] * 11,
-        out_specs=VMEM,
+        in_specs=[SMEM] + [VMEM] * 5 + [ANY] * 2 + [VMEM] * 4,
+        out_specs=ANY,
         scratch_shapes=[
             pltpu.VMEM((slots * rows, width), BF16),
             pltpu.VMEM((slots * rows, width), BF16),
             pltpu.VMEM((slots, HD), F32),
             pltpu.VMEM((requests, topk, width), F32),
+            pltpu.VMEM((slots, page_len, width), BF16),
+            pltpu.VMEM((slots, page_len, width), BF16),
+            pltpu.VMEM((devices, lines + heads * slots, HD), BF16),
+            pltpu.SemaphoreType.DMA((2 * slots,)),
+            pltpu.SemaphoreType.DMA(()),
         ],
         name="source",
     )(
@@ -383,7 +439,7 @@
     )
     inbox = lax.all_to_all(outbox, "pages", split_axis=0, concat_axis=0, tiled=True)
 
-    weight, _ = lax.optimization_barrier((out_weight[0], outbox))
+    weight = out_weight[0]
     weights = [out_weight]
     for d in range(1, heads):
         weights.append(
@@ -398,6 +454,7 @@
         out_shape=jax.ShapeDtypeStruct((devices * local, devices * slots), BF16),
         in_specs=[VMEM] * 3,
         out_specs=VMEM,
+        compiler_params=PARAMS,
         name="route",
     )(new_table.T, table, counts)
     inbox, pick, weights = lax.optimization_barrier((inbox, pick, weights))
@@ -407,28 +464,35 @@
     routed = pl.pallas_call(
         middle_kernel,
         out_shape=jax.ShapeDtypeStruct((devices, heads * local + terms, HD), BF16),
-        in_specs=[SMEM] + [VMEM] * (2 + heads),
-        out_specs=VMEM,
+        in_specs=[SMEM] + [ANY] * (2 + heads),
+        out_specs=ANY,
         scratch_shapes=[
             pltpu.VMEM((requests, lines, HD), F32),
             pltpu.VMEM((requests, terms, HD), F32),
             pltpu.VMEM((heads, HD, block_cols), BF16),
+            pltpu.VMEM((devices, lines, HD), BF16),
+            pltpu.VMEM((devices, heads * slots, HD), BF16),
+            pltpu.VMEM((devices * local, devices * slots), BF16),
+            pltpu.VMEM((devices, heads * local + terms, HD), BF16),
+            pltpu.SemaphoreType.DMA((heads + 3,)),
+            pltpu.SemaphoreType.DMA((devices // 16,)),
         ],
+        compiler_params=PARAMS,
         name="middle",
     )(head.reshape(1), inbox, pick, *weights)
     landed = lax.all_to_all(routed, "pages", split_axis=0, concat_axis=0, tiled=True)
 
-    quarter = jax.ShapeDtypeStruct((width // HD, HD), F32)
     quarters = pl.pallas_call(
         sum_kernel,
-        grid=(1,),
-        out_shape=[quarter] * shard_count,
-        in_specs=[
-            SMEM,
-            pl.BlockSpec((devices, terms, HD), lambda i: (0, heads * local // terms, 0)),
+        out_shape=[jax.ShapeDtypeStruct((1, width), F32)] * shard_count,
+        in_specs=[SMEM, ANY],
+        out_specs=[VMEM] * shard_count,
+        scratch_shapes=[
+            pltpu.VMEM((shard_count, width // HD, HD), F32),
+            pltpu.VMEM((devices, terms, HD), BF16),
+            pltpu.SemaphoreType.DMA(()),
         ],
-        out_specs=[VMEM] * shard_count,
-        scratch_shapes=[pltpu.VMEM((shard_count, width // HD, HD), F32)],
+        compiler_params=PARAMS,
         name="sum",
     )(shard, landed)
     landed, quarters = lax.optimization_barrier((landed, quarters))
@@ -441,17 +505,19 @@
     compact_keys, compact_values = pl.pallas_call(
         land_kernel,
         out_shape=(new_page, new_page),
-        in_specs=[VMEM],
-        out_specs=(VMEM, VMEM),
+        in_specs=[ANY],
+        out_specs=(ANY, ANY),
+        scratch_shapes=[
+            pltpu.VMEM((devices, heads * local + terms, HD), BF16),
+            pltpu.VMEM(new_page.shape, BF16),
+            pltpu.VMEM(new_page.shape, BF16),
+            pltpu.SemaphoreType.DMA((2,)),
+            pltpu.SemaphoreType.DMA((2,)),
+        ],
+        compiler_params=PARAMS,
         name="land",
     )(landed)
-    mixed = pl.pallas_call(
-        final_kernel,
-        out_shape=jax.ShapeDtypeStruct((1, width), BF16),
-        in_specs=[VMEM] * shard_count,
-        out_specs=VMEM,
-        name="final",
-    )(*moved)
+    mixed = sum(moved[1:], moved[0]).astype(BF16)
     return (compact_keys, compact_values, mixed)
 
 

time: 99 us -> 93.2 us (0.941)
  Pallas kernels: 16.3 us -> 11.3 us
  local copies, waits for them, and re-layouts: 3.09 us -> 0.05 us
  waiting for transfers between devices: 49.8 us -> 51.5 us
    pallas_call x3 -> x2, Pallas kernels: 5.59 us -> 2.09 us  [the longest x1 2.02 us: shards(): pl.pallas_call(land_kernel, out_shape=(new_page, new_page), in_specs=[ANY...]
    unnamed x18 -> x8, local copies, waits for them, and re-layouts: 3.06 us -> 0.03 us
    pallas_call x1, Pallas kernels: 2.45 us -> 0.79 us  [shards(): pl.pallas_call(route_kernel, out_shape=jax.ShapeDtypeStruct((devices * lo...]
    ppermute x3, waiting for transfers between devices: 16.9 us -> 18.6 us  [shards(): lax.ppermute(lax.dynamic_slice_in_dim(weight, (head ^ d) * HD, HD, 0), 'p...]
    pallas_call x1, Pallas kernels: 4.33 us -> 5.57 us  [shards(): pl.pallas_call(source_kernel, out_shape=jax.ShapeDtypeStruct((devices, li...]
    pallas_call x1, Pallas kernels: 3.97 us -> 2.88 us  [shards(): pl.pallas_call(middle_kernel, out_shape=jax.ShapeDtypeStruct((devices, he...]
  transfers between devices with their start and end apart: 8 -> 8, of which waited for: 4 -> 4; matrix products, arithmetic and copies ran while one was open for 0% -> 0% of each run, Pallas kernels for 5% -> 3%
where the time goes in v7:
time: 93.2 us; the launch traced here: 92.9 us
  waiting for transfers between devices  51.5 us (55%)
  starting transfers between devices  28.6 us (31%)
  Pallas kernels  11.3 us (12%)
    all_to_all x1, waiting for transfers between devices, shards(): lax.all_to_all(routed, 'pages', split_axis=0, concat_axis=0, tiled=True)  31.4 us
    ppermute x3, waiting for transfers between devices, shards(): lax.ppermute(lax.dynamic_slice_in_dim(weight, (head ^ d) * HD, HD, 0), 'p...  18.6 us
    all_to_all x1, starting transfers between devices, shards(): lax.all_to_all(outbox, 'pages', split_axis=0, concat_axis=0, tiled=True)  13.3 us
    all_to_all x1, starting transfers between devices, shards(): lax.all_to_all(routed, 'pages', split_axis=0, concat_axis=0, tiled=True)  8.21 us
    pallas_call x1, Pallas kernels, shards(): pl.pallas_call(source_kernel, out_shape=jax.ShapeDtypeStruct((devices, li...  5.57 us
    ppermute x3, starting transfers between devices, shards(): lax.ppermute(quarters[t], 'expert', [(i, (i + t) % shard_count) for i in...  4.89 us
    pallas_call x1, Pallas kernels, shards(): pl.pallas_call(middle_kernel, out_shape=jax.ShapeDtypeStruct((devices, he...  2.88 us
    ppermute x3, starting transfers between devices, shards(): lax.ppermute(lax.dynamic_slice_in_dim(weight, (head ^ d) * HD, HD, 0), 'p...  2.23 us
  transfers between devices with their start and end apart: 8, of which 4 were waited for; matrix products, arithmetic and copies ran while one was open for 0% of the time, Pallas kernels for 3%

profile of v7, /device:TPU:1, one launch (start us, length us, event | category | flops | bytes accessed | tf_op | source)
XLA Modules:
  0.0 92.9 jit_solution(117084496927769665)
XLA Ops:
  0.6 5.6 %source.1 = bf16[64,48,128]{2,1,0:T(8,128)(2,1)} custom-call(s32[1]{0:T(128)} %bitcast.1.my_ref, s32[12,64]{1,0:T(8,128)} %bitcast.13, s32[1,64]{1,0:T(1,128)} %bitcast.16, s32[2,64]{1,0:T(2,128)} %bitcast.18, s32[8,31]{1,0:T(8,128)} %keep_ref.1, s32[8,128]{1,0:T(8,128)} %drop_ref.1, bf16[8,128,512]{2,1,0:T(8,128)(2,1)} %k_hbm.1, ...), custom_call_target="tpu_custom_call" | custom-call | tf_op jit(solution)/shard_map/source/pallas_call | solution.py:409
  6.2 0.0 copy-start
  6.2 0.0 copy-start.1
  6.2 0.0 copy-start.2
  6.3 0.0 copy-start.3
  6.3 13.3 %all-to-all-start = ((bf16[64,48,128]{2,1,0:T(8,128)(2,1)}), bf16[64,48,128]{2,1,0:T(8,128)(2,1)S(1)}, u32[]{:S(2)}, u32[]{:S(2)}) async-start(bf16[64,48,128]{2,1,0:T(8,128)(2,1)} %source.1), calls=%async_computation | async-start | bytes 1572864 | tf_op jit(solution)/shard_map/all_to_all | solution.py:440
  19.6 0.0 copy-done
  19.6 1.7 %collective-permute-start.2 = (bf16[128,256]{1,0:T(8,128)(2,1)S(1)}, bf16[128,256]{1,0:T(8,128)(2,1)S(1)}, u32[]{:S(2)}, u32[]{:S(2)}) collective-permute-start(bf16[128,256]{1,0:T(8,128)(2,1)S(1)} %get-tuple-element.37), channel_id=1, source_target_pairs={{0,12},{4,8},{8,4},{12,0},{16,28},{20,24},{24,20},{28,16},{32,44},... | collective-permute-start | bytes 196616 | tf_op jit(solution)/shard_map/ppermute | solution.py:446
  21.4 0.2 collective-permute-start.1
  21.5 0.3 collective-permute-start
  21.9 0.0 copy-done.1
  21.9 0.0 copy-done.2
  21.9 0.0 copy-done.3
  21.9 0.8 route.1.pick_hbm
  22.7 18.1 %collective-permute-done.2.refs_3_ = bf16[128,256]{1,0:T(8,128)(2,1)S(1)} collective-permute-done((bf16[128,256]{1,0:T(8,128)(2,1)S(1)}, bf16[128,256]{1,0:T(8,128)(2,1)S(1)}, u32[]{:S(2)}, u32[]{:S(2)}) %collective-permute-start.2) | collective-permute-done | bytes 65568 | tf_op jit(solution)/shard_map/ppermute | solution.py:446
  40.8 0.5 collective-permute-done.1.refs_2_
  41.2 0.0 collective-permute-done.refs_1_
  41.2 1.6 %all-to-all-done.got_hbm = bf16[64,48,128]{2,1,0:T(8,128)(2,1)S(1)} async-done(((bf16[64,48,128]{2,1,0:T(8,128)(2,1)}), bf16[64,48,128]{2,1,0:T(8,128)(2,1)S(1)}, u32[]{:S(2)}, u32[]{:S(2)}) %all-to-all-start) | async-done | bytes 786464 | tf_op jit(solution)/shard_map/all_to_all | solution.py:440
  42.8 2.9 %middle.1 = bf16[64,72,128]{2,1,0:T(8,128)(2,1)} custom-call(s32[1]{0:T(128)} %bitcast.head_ref, bf16[64,48,128]{2,1,0:T(8,128)(2,1)S(1)} %all-to-all-done.got_hbm, bf16[1024,512]{1,0:T(8,128)(2,1)S(1)} %route.1.pick_hbm, bf16[1,512,256]{2,1,0:T(8,128)(2,1)S(1)} %copy-done, bf16[128,256]{1,0:T(8,128)(2,1)S(1)} %collective-permute-done.refs_1_, ...), custom_call_target="tpu_custom_call" | custom-call | tf_op jit(solution)/shard_map/middle/pallas_call | solution.py:464
  45.7 8.2 %all-to-all-start.1 = ((bf16[64,72,128]{2,1,0:T(8,128)(2,1)}), bf16[64,72,128]{2,1,0:T(8,128)(2,1)S(1)}, u32[]{:S(2)}, u32[]{:S(2)}) async-start(bf16[64,72,128]{2,1,0:T(8,128)(2,1)} %middle.1), calls=%async_computation.1 | async-start | bytes 2359296 | tf_op jit(solution)/shard_map/all_to_all | solution.py:483
  53.9 31.4 %all-to-all-done.1.got_hbm = bf16[64,72,128]{2,1,0:T(8,128)(2,1)S(1)} async-done(((bf16[64,72,128]{2,1,0:T(8,128)(2,1)}), bf16[64,72,128]{2,1,0:T(8,128)(2,1)S(1)}, u32[]{:S(2)}, u32[]{:S(2)}) %all-to-all-start.1) | async-done | bytes 1179680 | tf_op jit(solution)/shard_map/all_to_all | solution.py:483
  85.3 0.1 sum.1
  85.3 1.3 %collective-permute-start.3 = (f32[1,512]{1,0:T(1,128)S(1)}, f32[1,512]{1,0:T(1,128)S(1)}, u32[]{:S(2)}, u32[]{:S(2)}) collective-permute-start(f32[1,512]{1,0:T(1,128)S(1)} %get-tuple-element.34), channel_id=1, source_target_pairs={{0,1},{1,2},{2,3},{3,0},{4,5},{5,6},{6,7},{7,4},{8,9},{9,10},{10,1... | collective-permute-start | bytes 6152 | tf_op jit(solution)/shard_map/ppermute | solution.py:502
  86.6 2.4 %collective-permute-start.4 = (f32[1,512]{1,0:T(1,128)S(1)}, f32[1,512]{1,0:T(1,128)S(1)}, u32[]{:S(2)}, u32[]{:S(2)}) collective-permute-start(f32[1,512]{1,0:T(1,128)S(1)} %get-tuple-element.35), channel_id=1, source_target_pairs={{0,2},{1,3},{2,0},{3,1},{4,6},{5,7},{6,4},{7,5},{8,10},{9,11},{10,... | collective-permute-start | bytes 6152 | tf_op jit(solution)/shard_map/ppermute | solution.py:502
  89.1 1.2 %collective-permute-start.5 = (f32[1,512]{1,0:T(1,128)S(1)}, f32[1,512]{1,0:T(1,128)S(1)}, u32[]{:S(2)}, u32[]{:S(2)}) collective-permute-start(f32[1,512]{1,0:T(1,128)S(1)} %get-tuple-element.36), channel_id=1, source_target_pairs={{0,3},{1,0},{2,1},{3,2},{4,7},{5,4},{6,5},{7,6},{8,11},{9,8},{10,9... | collective-permute-start | bytes 6152 | tf_op jit(solution)/shard_map/ppermute | solution.py:502
  90.2 2.0 %land.1 = (bf16[4,128,512]{2,1,0:T(8,128)(2,1)}, bf16[4,128,512]{2,1,0:T(8,128)(2,1)}) custom-call(bf16[64,72,128]{2,1,0:T(8,128)(2,1)S(1)} %all-to-all-done.1.got_hbm), custom_call_target="tpu_custom_call" | custom-call | tf_op jit(solution)/shard_map/land/pallas_call | solution.py:505
  92.3 0.0 collective-permute-done.3
  92.3 0.0 collective-permute-done.4
  92.3 0.0 collective-permute-done.5
  92.3 0.6 add_convert_fusion
  (1 shorter events, 0.0 us)
Async XLA Ops:
  6.2 13.4 %copy-start = (bf16[1,512,256]{2,1,0:T(8,128)(2,1)S(1)}, bf16[1,512,256]{2,1,0:T(8,128)(2,1)}, u32[]{:S(2)}) copy-start(bf16[1,512,256]{2,1,0:T(8,128)(2,1)} %refs_0_) | copy-start | bytes 786436
  6.2 15.6 %copy-start.1 = (s32[64,12]{0,1:T(8,128)S(1)}, s32[64,12]{0,1:T(8,128)}, u32[]{:S(2)}) copy-start(s32[64,12]{0,1:T(8,128)} %param.18) | copy-start | bytes 9220
  6.2 15.6 %copy-start.2 = (s32[64,3]{0,1:T(4,128)S(1)}, s32[64,3]{0,1:T(4,128)}, u32[]{:S(2)}) copy-start(s32[64,3]{0,1:T(4,128)} %param.19) | copy-start | bytes 2308
  6.3 15.6 %copy-start.3 = (s32[64]{0:T(128)S(1)}, s32[64]{0:T(128)}, u32[]{:S(2)}) copy-start(s32[64]{0:T(128)} %param.17) | copy-start | bytes 772
  6.3 36.5 %all-to-all-start = ((bf16[64,48,128]{2,1,0:T(8,128)(2,1)}), bf16[64,48,128]{2,1,0:T(8,128)(2,1)S(1)}, u32[]{:S(2)}, u32[]{:S(2)}) async-start(bf16[64,48,128]{2,1,0:T(8,128)(2,1)} %source.1), calls=%async_computation | async-start | bytes 1572864 | tf_op jit(solution)/shard_map/all_to_all | solution.py:440
  19.6 21.1 %collective-permute-start.2 = (bf16[128,256]{1,0:T(8,128)(2,1)S(1)}, bf16[128,256]{1,0:T(8,128)(2,1)S(1)}, u32[]{:S(2)}, u32[]{:S(2)}) collective-permute-start(bf16[128,256]{1,0:T(8,128)(2,1)S(1)} %get-tuple-element.37), channel_id=1, source_target_pairs={{0,12},{4,8},{8,4},{12,0},{16,28},{20,24},{24,20},{28,16},{32,44},... | collective-permute-start | bytes 196616 | tf_op jit(solution)/shard_map/ppermute | solution.py:446
  21.4 19.9 %collective-permute-start.1 = (bf16[128,256]{1,0:T(8,128)(2,1)S(1)}, bf16[128,256]{1,0:T(8,128)(2,1)S(1)}, u32[]{:S(2)}, u32[]{:S(2)}) collective-permute-start(bf16[128,256]{1,0:T(8,128)(2,1)S(1)} %get-tuple-element.38), channel_id=1, source_target_pairs={{0,8},{4,12},{8,0},{12,4},{16,24},{20,28},{24,16},{28,20},{32,40},... | collective-permute-start | bytes 196616 | tf_op jit(solution)/shard_map/ppermute | solution.py:446
  21.5 19.7 %collective-permute-start = (bf16[128,256]{1,0:T(8,128)(2,1)S(1)}, bf16[128,256]{1,0:T(8,128)(2,1)S(1)}, u32[]{:S(2)}, u32[]{:S(2)}) collective-permute-start(bf16[128,256]{1,0:T(8,128)(2,1)S(1)} %get-tuple-element.39), channel_id=1, source_target_pairs={{0,4},{4,0},{8,12},{12,8},{16,20},{20,16},{24,28},{28,24},{32,36},... | collective-permute-start | bytes 196616 | tf_op jit(solution)/shard_map/ppermute | solution.py:446
  45.7 39.6 %all-to-all-start.1 = ((bf16[64,72,128]{2,1,0:T(8,128)(2,1)}), bf16[64,72,128]{2,1,0:T(8,128)(2,1)S(1)}, u32[]{:S(2)}, u32[]{:S(2)}) async-start(bf16[64,72,128]{2,1,0:T(8,128)(2,1)} %middle.1), calls=%async_computation.1 | async-start | bytes 2359296 | tf_op jit(solution)/shard_map/all_to_all | solution.py:483
  85.3 6.9 %collective-permute-start.3 = (f32[1,512]{1,0:T(1,128)S(1)}, f32[1,512]{1,0:T(1,128)S(1)}, u32[]{:S(2)}, u32[]{:S(2)}) collective-permute-start(f32[1,512]{1,0:T(1,128)S(1)} %get-tuple-element.34), channel_id=1, source_target_pairs={{0,1},{1,2},{2,3},{3,0},{4,5},{5,6},{6,7},{7,4},{8,9},{9,10},{10,1... | collective-permute-start | bytes 6152 | tf_op jit(solution)/shard_map/ppermute | solution.py:502
  86.6 5.6 %collective-permute-start.4 = (f32[1,512]{1,0:T(1,128)S(1)}, f32[1,512]{1,0:T(1,128)S(1)}, u32[]{:S(2)}, u32[]{:S(2)}) collective-permute-start(f32[1,512]{1,0:T(1,128)S(1)} %get-tuple-element.35), channel_id=1, source_target_pairs={{0,2},{1,3},{2,0},{3,1},{4,6},{5,7},{6,4},{7,5},{8,10},{9,11},{10,... | collective-permute-start | bytes 6152 | tf_op jit(solution)/shard_map/ppermute | solution.py:502
  89.1 3.2 %collective-permute-start.5 = (f32[1,512]{1,0:T(1,128)S(1)}, f32[1,512]{1,0:T(1,128)S(1)}, u32[]{:S(2)}, u32[]{:S(2)}) collective-permute-start(f32[1,512]{1,0:T(1,128)S(1)} %get-tuple-element.36), channel_id=1, source_target_pairs={{0,3},{1,0},{2,1},{3,2},{4,7},{5,4},{6,5},{7,6},{8,11},{9,8},{10,9... | collective-permute-start | bytes 6152 | tf_op jit(solution)/shard_map/ppermute | solution.py:502

commit v8 on v7

--- a/solution.py
+++ b/solution.py
@@ -34,35 +34,20 @@
     ids_ref,
     keep_ref,
     drop_ref,
-    k_hbm,
-    v_hbm,
+    k_ref,
+    v_ref,
     q_ref,
     nk_ref,
     nv_ref,
     logit_ref,
-    out_hbm,
+    out_ref,
     kb,
     vb,
     keep_rows,
     q_rows,
-    k_ref,
-    v_ref,
-    out_ref,
-    sems,
-    out_sem,
 ):
     my = my_ref[0]
     slots, page_len, width = k_ref.shape
-    loads = []
-    for g in range(slots):
-        loads.append(
-            (
-                pltpu.make_async_copy(k_hbm.at[g], k_ref.at[g], sems.at[2 * g]),
-                pltpu.make_async_copy(v_hbm.at[g], v_ref.at[g], sems.at[2 * g + 1]),
-            )
-        )
-        for load in loads[g]:
-            load.start()
     keep_count = keep_ref.shape[1]
     rows = keep_count + 1
     heads = width // HD
@@ -80,8 +65,6 @@
         total = jnp.sum(coef, axis=1, keepdims=True)
         mat = jnp.where(last, coef, onehot).astype(BF16)
         denom = jnp.where(last[:, 0:1], total, 1.0)
-        for load in loads[g]:
-            load.wait()
         kb[g * rows : (g + 1) * rows, :] = (dot(mat, k_ref[g]) / denom).astype(BF16)
         vb[g * rows : (g + 1) * rows, :] = (dot(mat, v_ref[g]) / denom).astype(BF16)
     n = slots * rows
@@ -201,9 +184,6 @@
             out_ref[base : base + rows, at, :] = (
                 spread[:, t * HD : (t + 1) * HD].reshape(rows, slots, HD).astype(BF16)
             )
-    store = pltpu.make_async_copy(out_ref, out_hbm, out_sem)
-    store.start()
-    store.wait()
 
 
 def middle_kernel(head_ref, got_hbm, pick_hbm, *refs):
@@ -406,21 +386,24 @@
     table = page_table.T
     counts = request_pages.reshape(1, -1)
 
+    pieces = [
+        lax.dynamic_slice_in_dim(out_weight[0], (head ^ d) * HD, HD, 0) for d in range(1, heads)
+    ]
+    table, pieces = lax.optimization_barrier((table, pieces))
+    weights = [
+        lax.ppermute(piece, "pages", [(p, p ^ d) for p in range(devices)])
+        for d, piece in enumerate(pieces, 1)
+    ]
     outbox = pl.pallas_call(
         source_kernel,
         out_shape=jax.ShapeDtypeStruct((devices, lines + heads * slots, HD), BF16),
-        in_specs=[SMEM] + [VMEM] * 5 + [ANY] * 2 + [VMEM] * 4,
-        out_specs=ANY,
+        in_specs=[SMEM] + [VMEM] * 11,
+        out_specs=VMEM,
         scratch_shapes=[
             pltpu.VMEM((slots * rows, width), BF16),
             pltpu.VMEM((slots * rows, width), BF16),
             pltpu.VMEM((slots, HD), F32),
             pltpu.VMEM((requests, topk, width), F32),
-            pltpu.VMEM((slots, page_len, width), BF16),
-            pltpu.VMEM((slots, page_len, width), BF16),
-            pltpu.VMEM((devices, lines + heads * slots, HD), BF16),
-            pltpu.SemaphoreType.DMA((2 * slots,)),
-            pltpu.SemaphoreType.DMA(()),
         ],
         name="source",
     )(
@@ -437,18 +420,9 @@
         new_values,
         router_logits,
     )
+    outbox, weights = lax.optimization_barrier((outbox, weights))
     inbox = lax.all_to_all(outbox, "pages", split_axis=0, concat_axis=0, tiled=True)
 
-    weight = out_weight[0]
-    weights = [out_weight]
-    for d in range(1, heads):
-        weights.append(
-            lax.ppermute(
-                lax.dynamic_slice_in_dim(weight, (head ^ d) * HD, HD, 0),
-                "pages",
-                [(p, p ^ d) for p in range(devices)],
-            )
-        )
     pick = pl.pallas_call(
         route_kernel,
         out_shape=jax.ShapeDtypeStruct((devices * local, devices * slots), BF16),
@@ -457,7 +431,7 @@
         compiler_params=PARAMS,
         name="route",
     )(new_table.T, table, counts)
-    inbox, pick, weights = lax.optimization_barrier((inbox, pick, weights))
+    inbox, pick = lax.optimization_barrier((inbox, pick))
 
     block_cols = out_weight.shape[2]
     terms = heads * block_cols // HD
@@ -479,7 +453,7 @@
         ],
         compiler_params=PARAMS,
         name="middle",
-    )(head.reshape(1), inbox, pick, *weights)
+    )(head.reshape(1), inbox, pick, out_weight, *weights)
     landed = lax.all_to_all(routed, "pages", split_axis=0, concat_axis=0, tiled=True)
 
     quarters = pl.pallas_call(

time: 93.2 us -> 92.7 us (level)
  starting transfers between devices: 28.6 us -> 26.4 us
  waiting for transfers between devices: 51.5 us -> 53.5 us
  Pallas kernels: 11.3 us -> 10.1 us
    all_to_all x1, waiting for transfers between devices: 1.55 us -> 22.2 us  [shards(): lax.all_to_all(outbox, 'pages', split_axis=0, concat_axis=0, tiled=True)]
    ppermute x3, waiting for transfers between devices: 18.6 us -> 0.01 us  [shards(): lax.ppermute(piece, 'pages', [(p, p ^ d) for p in range(devices)])]
    all_to_all x1, starting transfers between devices: 13.3 us -> 10.2 us  [shards(): lax.all_to_all(outbox, 'pages', split_axis=0, concat_axis=0, tiled=True)]
    ppermute x3, starting transfers between devices: 2.23 us -> 5.06 us  [shards(): lax.ppermute(piece, 'pages', [(p, p ^ d) for p in range(devices)])]
    all_to_all x1, starting transfers between devices: 8.21 us -> 6.21 us  [shards(): lax.all_to_all(routed, 'pages', split_axis=0, concat_axis=0, tiled=True)]
    pallas_call x1, Pallas kernels: 5.57 us -> 4.35 us  [shards(): pl.pallas_call(source_kernel, out_shape=jax.ShapeDtypeStruct((devices, li...]
  transfers between devices with their start and end apart: 8 -> 8, of which waited for: 4 -> 2; matrix products, arithmetic and copies ran while one was open for 0% -> 0% of each run, Pallas kernels for 3% -> 8%
where the time goes in v8:
time: 92.7 us; the launch traced here: 92.4 us
  waiting for transfers between devices  53.5 us (58%)
  starting transfers between devices  26.4 us (28%)
  Pallas kernels  10.1 us (11%)
  local copies, waits for them, and re-layouts  0.94 us (1%)
    all_to_all x1, waiting for transfers between devices, shards(): lax.all_to_all(routed, 'pages', split_axis=0, concat_axis=0, tiled=True)  31.4 us
    all_to_all x1, waiting for transfers between devices, shards(): lax.all_to_all(outbox, 'pages', split_axis=0, concat_axis=0, tiled=True)  22.2 us
    all_to_all x1, starting transfers between devices, shards(): lax.all_to_all(outbox, 'pages', split_axis=0, concat_axis=0, tiled=True)  10.2 us
    all_to_all x1, starting transfers between devices, shards(): lax.all_to_all(routed, 'pages', split_axis=0, concat_axis=0, tiled=True)  6.21 us
    ppermute x3, starting transfers between devices, shards(): lax.ppermute(piece, 'pages', [(p, p ^ d) for p in range(devices)])  5.06 us
    ppermute x3, starting transfers between devices, shards(): lax.ppermute(quarters[t], 'expert', [(i, (i + t) % shard_count) for i in...  4.89 us
    pallas_call x1, Pallas kernels, shards(): pl.pallas_call(source_kernel, out_shape=jax.ShapeDtypeStruct((devices, li...  4.35 us
    pallas_call x1, Pallas kernels, shards(): pl.pallas_call(middle_kernel, out_shape=jax.ShapeDtypeStruct((devices, he...  2.88 us
  transfers between devices with their start and end apart: 8, of which 2 were waited for; matrix products, arithmetic and copies ran while one was open for 0% of the time, Pallas kernels for 8%

profile of v8, /device:TPU:1, one launch (start us, length us, event | category | flops | bytes accessed | tf_op | source)
XLA Modules:
  0.0 92.4 jit_solution(16917294939607415992)
XLA Ops:
  0.7 0.9 %dynamic-slice_bitcast_fusion = (bf16[128,256]{1,0:T(8,128)(2,1)S(1)}, bf16[128,256]{1,0:T(8,128)(2,1)S(1)}, bf16[128,256]{1,0:T(8,128)(2,1)S(1)}) fusion(bf16[1,512,256]{2,1,0:T(8,128)(2,1)} %refs_0_.1, s32[]{:T(128)S(6)} %select_n.11, s32[]{:T(128)S(6)} %select_n.10, s32[]{:T(128)S(6)} %select_n.9), kind=kLoop, calls=%fused_computation | loop fusion | bytes 393228 | tf_op jit(solution)/shard_map/dynamic_slice | solution.py:390
  1.6 3.3 %collective-permute-start = (bf16[128,256]{1,0:T(8,128)(2,1)S(1)}, bf16[128,256]{1,0:T(8,128)(2,1)S(1)}, u32[]{:S(2)}, u32[]{:S(2)}) collective-permute-start(bf16[128,256]{1,0:T(8,128)(2,1)S(1)} %get-tuple-element.25), channel_id=1, source_target_pairs={{0,4},{4,0},{8,12},{12,8},{16,20},{20,16},{24,28},{28,24},{32,36},... | collective-permute-start | bytes 196616 | tf_op jit(solution)/shard_map/ppermute | solution.py:394
  4.9 0.0 collective-permute-start.1
  4.9 1.7 %collective-permute-start.2 = (bf16[128,256]{1,0:T(8,128)(2,1)S(1)}, bf16[128,256]{1,0:T(8,128)(2,1)S(1)}, u32[]{:S(2)}, u32[]{:S(2)}) collective-permute-start(bf16[128,256]{1,0:T(8,128)(2,1)S(1)} %get-tuple-element.27), channel_id=1, source_target_pairs={{0,12},{4,8},{8,4},{12,0},{16,28},{20,24},{24,20},{28,16},{32,44},... | collective-permute-start | bytes 196616 | tf_op jit(solution)/shard_map/ppermute | solution.py:394
  6.6 4.4 %source.1 = bf16[64,48,128]{2,1,0:T(8,128)(2,1)} custom-call(s32[1]{0:T(128)} %bitcast.1.my_ref, s32[12,64]{1,0:T(8,128)} %bitcast.13, s32[1,64]{1,0:T(1,128)} %bitcast.16, s32[2,64]{1,0:T(2,128)} %bitcast.18, s32[8,31]{1,0:T(8,128)} %keep_ref.1, s32[8,128]{1,0:T(8,128)} %drop_ref.1, bf16[8,128,512]{2,1,0:T(8,128)(2,1)} %k_ref.1, ...), custom_call_target="tpu_custom_call" | custom-call | tf_op jit(solution)/shard_map/source/pallas_call | solution.py:397
  11.0 0.0 copy-start.1
  11.0 0.0 copy-start.2
  11.0 0.0 copy-start.3
  11.0 0.0 copy-start
  11.0 0.0 collective-permute-done.refs_1_
  11.0 0.0 collective-permute-done.1.refs_2_
  11.0 0.0 collective-permute-done.2.refs_3_
  11.1 10.2 %all-to-all-start = ((bf16[64,48,128]{2,1,0:T(8,128)(2,1)}), bf16[64,48,128]{2,1,0:T(8,128)(2,1)S(1)}, u32[]{:S(2)}, u32[]{:S(2)}) async-start(bf16[64,48,128]{2,1,0:T(8,128)(2,1)} %source.1), calls=%async_computation | async-start | bytes 1572864 | tf_op jit(solution)/shard_map/all_to_all | solution.py:424
  21.3 0.0 copy-done.1
  21.3 0.0 copy-done.2
  21.3 0.0 copy-done.3
  21.3 0.8 route.1.pick_hbm
  22.1 22.2 %all-to-all-done.got_hbm = bf16[64,48,128]{2,1,0:T(8,128)(2,1)S(1)} async-done(((bf16[64,48,128]{2,1,0:T(8,128)(2,1)}), bf16[64,48,128]{2,1,0:T(8,128)(2,1)S(1)}, u32[]{:S(2)}, u32[]{:S(2)}) %all-to-all-start) | async-done | bytes 786464 | tf_op jit(solution)/shard_map/all_to_all | solution.py:424
  44.3 0.0 copy-done
  44.3 2.9 %middle.1 = bf16[64,72,128]{2,1,0:T(8,128)(2,1)} custom-call(s32[1]{0:T(128)} %bitcast.head_ref, bf16[64,48,128]{2,1,0:T(8,128)(2,1)S(1)} %all-to-all-done.got_hbm, bf16[1024,512]{1,0:T(8,128)(2,1)S(1)} %route.1.pick_hbm, bf16[1,512,256]{2,1,0:T(8,128)(2,1)S(1)} %copy-done, bf16[128,256]{1,0:T(8,128)(2,1)S(1)} %collective-permute-done.refs_1_, ...), custom_call_target="tpu_custom_call" | custom-call | tf_op jit(solution)/shard_map/middle/pallas_call | solution.py:438
  47.1 6.2 %all-to-all-start.1 = ((bf16[64,72,128]{2,1,0:T(8,128)(2,1)}), bf16[64,72,128]{2,1,0:T(8,128)(2,1)S(1)}, u32[]{:S(2)}, u32[]{:S(2)}) async-start(bf16[64,72,128]{2,1,0:T(8,128)(2,1)} %middle.1), calls=%async_computation.1 | async-start | bytes 2359296 | tf_op jit(solution)/shard_map/all_to_all | solution.py:457
  53.4 31.4 %all-to-all-done.1.got_hbm = bf16[64,72,128]{2,1,0:T(8,128)(2,1)S(1)} async-done(((bf16[64,72,128]{2,1,0:T(8,128)(2,1)}), bf16[64,72,128]{2,1,0:T(8,128)(2,1)S(1)}, u32[]{:S(2)}, u32[]{:S(2)}) %all-to-all-start.1) | async-done | bytes 1179680 | tf_op jit(solution)/shard_map/all_to_all | solution.py:457
  84.7 0.1 sum.1
  84.8 1.3 %collective-permute-start.3 = (f32[1,512]{1,0:T(1,128)S(1)}, f32[1,512]{1,0:T(1,128)S(1)}, u32[]{:S(2)}, u32[]{:S(2)}) collective-permute-start(f32[1,512]{1,0:T(1,128)S(1)} %get-tuple-element.42), channel_id=1, source_target_pairs={{0,1},{1,2},{2,3},{3,0},{4,5},{5,6},{6,7},{7,4},{8,9},{9,10},{10,1... | collective-permute-start | bytes 6152 | tf_op jit(solution)/shard_map/ppermute | solution.py:476
  86.1 2.5 %collective-permute-start.4 = (f32[1,512]{1,0:T(1,128)S(1)}, f32[1,512]{1,0:T(1,128)S(1)}, u32[]{:S(2)}, u32[]{:S(2)}) collective-permute-start(f32[1,512]{1,0:T(1,128)S(1)} %get-tuple-element.43), channel_id=1, source_target_pairs={{0,2},{1,3},{2,0},{3,1},{4,6},{5,7},{6,4},{7,5},{8,10},{9,11},{10,... | collective-permute-start | bytes 6152 | tf_op jit(solution)/shard_map/ppermute | solution.py:476
  88.5 1.2 %collective-permute-start.5 = (f32[1,512]{1,0:T(1,128)S(1)}, f32[1,512]{1,0:T(1,128)S(1)}, u32[]{:S(2)}, u32[]{:S(2)}) collective-permute-start(f32[1,512]{1,0:T(1,128)S(1)} %get-tuple-element.44), channel_id=1, source_target_pairs={{0,3},{1,0},{2,1},{3,2},{4,7},{5,4},{6,5},{7,6},{8,11},{9,8},{10,9... | collective-permute-start | bytes 6152 | tf_op jit(solution)/shard_map/ppermute | solution.py:476
  89.7 2.0 %land.1 = (bf16[4,128,512]{2,1,0:T(8,128)(2,1)}, bf16[4,128,512]{2,1,0:T(8,128)(2,1)}) custom-call(bf16[64,72,128]{2,1,0:T(8,128)(2,1)S(1)} %all-to-all-done.1.got_hbm), custom_call_target="tpu_custom_call" | custom-call | tf_op jit(solution)/shard_map/land/pallas_call | solution.py:479
  91.7 0.0 collective-permute-done.3
  91.7 0.0 collective-permute-done.4
  91.8 0.0 collective-permute-done.5
  91.8 0.6 add_convert_fusion
Async XLA Ops:
  1.6 9.4 %collective-permute-start = (bf16[128,256]{1,0:T(8,128)(2,1)S(1)}, bf16[128,256]{1,0:T(8,128)(2,1)S(1)}, u32[]{:S(2)}, u32[]{:S(2)}) collective-permute-start(bf16[128,256]{1,0:T(8,128)(2,1)S(1)} %get-tuple-element.25), channel_id=1, source_target_pairs={{0,4},{4,0},{8,12},{12,8},{16,20},{20,16},{24,28},{28,24},{32,36},... | collective-permute-start | bytes 196616 | tf_op jit(solution)/shard_map/ppermute | solution.py:394
  4.9 6.1 %collective-permute-start.1 = (bf16[128,256]{1,0:T(8,128)(2,1)S(1)}, bf16[128,256]{1,0:T(8,128)(2,1)S(1)}, u32[]{:S(2)}, u32[]{:S(2)}) collective-permute-start(bf16[128,256]{1,0:T(8,128)(2,1)S(1)} %get-tuple-element.26), channel_id=1, source_target_pairs={{0,8},{4,12},{8,0},{12,4},{16,24},{20,28},{24,16},{28,20},{32,40},... | collective-permute-start | bytes 196616 | tf_op jit(solution)/shard_map/ppermute | solution.py:394
  4.9 6.1 %collective-permute-start.2 = (bf16[128,256]{1,0:T(8,128)(2,1)S(1)}, bf16[128,256]{1,0:T(8,128)(2,1)S(1)}, u32[]{:S(2)}, u32[]{:S(2)}) collective-permute-start(bf16[128,256]{1,0:T(8,128)(2,1)S(1)} %get-tuple-element.27), channel_id=1, source_target_pairs={{0,12},{4,8},{8,4},{12,0},{16,28},{20,24},{24,20},{28,16},{32,44},... | collective-permute-start | bytes 196616 | tf_op jit(solution)/shard_map/ppermute | solution.py:394
  11.0 10.3 %copy-start.1 = (s32[64,12]{0,1:T(8,128)S(1)}, s32[64,12]{0,1:T(8,128)}, u32[]{:S(2)}) copy-start(s32[64,12]{0,1:T(8,128)} %param.18) | copy-start | bytes 9220
  11.0 10.3 %copy-start.2 = (s32[64,3]{0,1:T(4,128)S(1)}, s32[64,3]{0,1:T(4,128)}, u32[]{:S(2)}) copy-start(s32[64,3]{0,1:T(4,128)} %param.19) | copy-start | bytes 2308
  11.0 10.3 %copy-start.3 = (s32[64]{0:T(128)S(1)}, s32[64]{0:T(128)}, u32[]{:S(2)}) copy-start(s32[64]{0:T(128)} %param.17) | copy-start | bytes 772
  11.0 33.3 %copy-start = (bf16[1,512,256]{2,1,0:T(8,128)(2,1)S(1)}, bf16[1,512,256]{2,1,0:T(8,128)(2,1)}, u32[]{:S(2)}) copy-start(bf16[1,512,256]{2,1,0:T(8,128)(2,1)} %refs_0_.1) | copy-start | bytes 786436
  11.1 33.2 %all-to-all-start = ((bf16[64,48,128]{2,1,0:T(8,128)(2,1)}), bf16[64,48,128]{2,1,0:T(8,128)(2,1)S(1)}, u32[]{:S(2)}, u32[]{:S(2)}) async-start(bf16[64,48,128]{2,1,0:T(8,128)(2,1)} %source.1), calls=%async_computation | async-start | bytes 1572864 | tf_op jit(solution)/shard_map/all_to_all | solution.py:424
  47.1 37.6 %all-to-all-start.1 = ((bf16[64,72,128]{2,1,0:T(8,128)(2,1)}), bf16[64,72,128]{2,1,0:T(8,128)(2,1)S(1)}, u32[]{:S(2)}, u32[]{:S(2)}) async-start(bf16[64,72,128]{2,1,0:T(8,128)(2,1)} %middle.1), calls=%async_computation.1 | async-start | bytes 2359296 | tf_op jit(solution)/shard_map/all_to_all | solution.py:457
  84.8 6.9 %collective-permute-start.3 = (f32[1,512]{1,0:T(1,128)S(1)}, f32[1,512]{1,0:T(1,128)S(1)}, u32[]{:S(2)}, u32[]{:S(2)}) collective-permute-start(f32[1,512]{1,0:T(1,128)S(1)} %get-tuple-element.42), channel_id=1, source_target_pairs={{0,1},{1,2},{2,3},{3,0},{4,5},{5,6},{6,7},{7,4},{8,9},{9,10},{10,1... | collective-permute-start | bytes 6152 | tf_op jit(solution)/shard_map/ppermute | solution.py:476
  86.1 5.7 %collective-permute-start.4 = (f32[1,512]{1,0:T(1,128)S(1)}, f32[1,512]{1,0:T(1,128)S(1)}, u32[]{:S(2)}, u32[]{:S(2)}) collective-permute-start(f32[1,512]{1,0:T(1,128)S(1)} %get-tuple-element.43), channel_id=1, source_target_pairs={{0,2},{1,3},{2,0},{3,1},{4,6},{5,7},{6,4},{7,5},{8,10},{9,11},{10,... | collective-permute-start | bytes 6152 | tf_op jit(solution)/shard_map/ppermute | solution.py:476
  88.5 3.2 %collective-permute-start.5 = (f32[1,512]{1,0:T(1,128)S(1)}, f32[1,512]{1,0:T(1,128)S(1)}, u32[]{:S(2)}, u32[]{:S(2)}) collective-permute-start(f32[1,512]{1,0:T(1,128)S(1)} %get-tuple-element.44), channel_id=1, source_target_pairs={{0,3},{1,0},{2,1},{3,2},{4,7},{5,4},{6,5},{7,6},{8,11},{9,8},{10,9... | collective-permute-start | bytes 6152 | tf_op jit(solution)/shard_map/ppermute | solution.py:476

commit v9 on v8

--- a/solution.py
+++ b/solution.py
@@ -21,6 +21,14 @@
 
 def iota(shape, dim):
     return lax.broadcasted_iota(jnp.int32, shape, dim)
+
+
+def over(x, n):
+    return lax.shift_right_logical(x, n.bit_length() - 1) if n & (n - 1) == 0 else x // n
+
+
+def rest(x, n):
+    return x & (n - 1) if n & (n - 1) == 0 else x % n
 
 
 def dot(a, b):
@@ -64,9 +72,11 @@
         coef = jnp.where(kept > 0.0, 0.0, drop_ref[g : g + 1, :].astype(F32))
         total = jnp.sum(coef, axis=1, keepdims=True)
         mat = jnp.where(last, coef, onehot).astype(BF16)
-        denom = jnp.where(last[:, 0:1], total, 1.0)
-        kb[g * rows : (g + 1) * rows, :] = (dot(mat, k_ref[g]) / denom).astype(BF16)
-        vb[g * rows : (g + 1) * rows, :] = (dot(mat, v_ref[g]) / denom).astype(BF16)
+        denom = jnp.where(last[rows - 8 :, 0:1], total, 1.0)
+        for ref, blocks in ((k_ref, kb), (v_ref, vb)):
+            block = dot(mat, ref[g])
+            block = jnp.concatenate([block[: rows - 8], block[rows - 8 :] / denom], axis=0)
+            blocks[g * rows : (g + 1) * rows, :] = block.astype(BF16)
     n = slots * rows
     ent = 2 * slots
     ent_row = iota((ent, reqs), 0)
@@ -79,7 +89,7 @@
         sel = jnp.where(ent_row == g, jnp.max(hit, axis=0, keepdims=True), sel)
     sel_b = sel.astype(BF16)
     same = lax.dot_general(sel_b, sel_b, NT, preferred_element_type=F32)
-    q_lane = iota((ent, width), 1) // HD
+    q_lane = over(iota((ent, width), 1), HD)
     pieces = []
     for k in range(topk):
         group_query = dot(sel_b, q_rows[:, k, :].astype(BF16))
@@ -90,12 +100,12 @@
     scale = 1.0 / math.sqrt(HD)
     scores = lax.dot_general(queries.astype(BF16), kb[...], NT, preferred_element_type=F32) * scale
     col = iota((kh * ent, n), 1)
-    scores = scores + jnp.where(col % rows == rows - 1, math.log(page_len - rows + 1), 0.0)
-    of_page = jnp.where(iota((ent, n), 1) // rows == iota((ent, n), 0), 1.0, 0.0).astype(BF16)
+    scores = scores + jnp.where(rest(col, rows) == rows - 1, math.log(page_len - rows + 1), 0.0)
+    of_page = jnp.where(over(iota((ent, n), 1), rows) == iota((ent, n), 0), 1.0, 0.0).astype(BF16)
     shared = dot(same.astype(BF16), of_page)
     mask = jnp.concatenate([shared] * kh, axis=0) > 0.5
     scores = jnp.where(mask, scores, NEGATIVE)
-    is_own = iota((kh * ent, 1), 0) % ent == slots
+    is_own = rest(iota((kh * ent, 1), 0), ent) == slots
     own = jnp.sum(queries * nk_ref[...].astype(F32), axis=1, keepdims=True) * scale
     own = jnp.where(is_own, own, NEGATIVE)
     peak = jnp.maximum(jnp.max(scores, axis=1, keepdims=True), own)
@@ -161,11 +171,11 @@
     columns = devices // EXPERTS
     to = iota((EXPERTS * lines, EXPERTS * ent), 0)
     fro = iota((EXPERTS * lines, EXPERTS * ent), 1)
-    flat = (to // lines == fro // ent) & (to % lines == slots + 1)
+    flat = (over(to, lines) == over(fro, ent)) & (rest(to, lines) == slots + 1)
     flat = jnp.where(flat, 1.0, 0.0).astype(BF16)
     square = iota((HD, HD), 0)
     item = iota((HD, HD), 1) % 6
-    mine = iota((EXPERTS * ent, HD), 1) // 6 == iota((EXPERTS * ent, HD), 0) % ent
+    mine = iota((EXPERTS * ent, HD), 1) // 6 == rest(iota((EXPERTS * ent, HD), 0), ent)
     for h in range(heads):
         origin = jnp.where(item < 3, 3 * h + item, 3 * heads + item - 3)
         spread = dot(stats, jnp.where(square == origin, 1.0, 0.0).astype(BF16))
@@ -176,7 +186,7 @@
                 out_ref[e * columns + z * heads + h, 0:lines, :] = sent[e * lines : (e + 1) * lines, :]
     to = iota((n, n), 0)
     fro = iota((n, n), 1)
-    perm = jnp.where((to % slots == fro // rows) & (to // slots == fro % rows), 1.0, 0.0).astype(BF16)
+    perm = jnp.where((rest(to, slots) == over(fro, rows)) & (over(to, slots) == rest(fro, rows)), 1.0, 0.0).astype(BF16)
     for base, blocks in ((0, kb), (rows, vb)):
         spread = dot(perm, blocks[...])
         for t in range(heads):
@@ -283,8 +293,8 @@
     max_new = new_ref.shape[0]
     per_new = table_ref.shape[0] // max_new
     shape = (out_ref.shape[0], new_ref.shape[1])
-    slot = iota(shape, 0) // per_new
-    quarter = iota(shape, 0) % per_new
+    slot = over(iota(shape, 0), per_new)
+    quarter = rest(iota(shape, 0), per_new)
     found = jnp.zeros(shape, jnp.int32)
     for i in range(max_new):
         filled = jnp.where(i * per_new < count_ref[...], new_ref[i : i + 1, :], -1)
@@ -334,7 +344,7 @@
     local = n // rows
     to = iota((n, n), 0)
     fro = iota((n, n), 1)
-    perm = jnp.where((to // rows == fro % local) & (to % rows == fro // local), 1.0, 0.0).astype(BF16)
+    perm = jnp.where((over(to, rows) == rest(fro, local)) & (rest(to, rows) == over(fro, local)), 1.0, 0.0).astype(BF16)
     stores = []
     for i, (ref, hbm) in enumerate(((k_ref, k_hbm), (v_ref, v_hbm))):
         base = i * rows
@@ -386,14 +396,6 @@
     table = page_table.T
     counts = request_pages.reshape(1, -1)
 
-    pieces = [
-        lax.dynamic_slice_in_dim(out_weight[0], (head ^ d) * HD, HD, 0) for d in range(1, heads)
-    ]
-    table, pieces = lax.optimization_barrier((table, pieces))
-    weights = [
-        lax.ppermute(piece, "pages", [(p, p ^ d) for p in range(devices)])
-        for d, piece in enumerate(pieces, 1)
-    ]
     outbox = pl.pallas_call(
         source_kernel,
         out_shape=jax.ShapeDtypeStruct((devices, lines + heads * slots, HD), BF16),
@@ -420,9 +422,14 @@
         new_values,
         router_logits,
     )
-    outbox, weights = lax.optimization_barrier((outbox, weights))
     inbox = lax.all_to_all(outbox, "pages", split_axis=0, concat_axis=0, tiled=True)
 
+    weight, _ = lax.optimization_barrier((out_weight[0], outbox))
+    pieces = [lax.dynamic_slice_in_dim(weight, (head ^ d) * HD, HD, 0) for d in range(1, heads)]
+    weights = [
+        lax.ppermute(piece, "pages", [(p, p ^ d) for p in range(devices)])
+        for d, piece in enumerate(pieces, 1)
+    ]
     pick = pl.pallas_call(
         route_kernel,
         out_shape=jax.ShapeDtypeStruct((devices * local, devices * slots), BF16),
@@ -431,7 +438,7 @@
         compiler_params=PARAMS,
         name="route",
     )(new_table.T, table, counts)
-    inbox, pick = lax.optimization_barrier((inbox, pick))
+    inbox, pick, weights = lax.optimization_barrier((inbox, pick, weights))
 
     block_cols = out_weight.shape[2]
     terms = heads * block_cols // HD

time: 92.7 us -> 91.9 us (level)
  starting transfers between devices: 26.4 us -> 28.6 us
  waiting for transfers between devices: 53.5 us -> 51.5 us
    all_to_all x1, waiting for transfers between devices: 22.2 us -> 1.55 us  [shards(): lax.all_to_all(outbox, 'pages', split_axis=0, concat_axis=0, tiled=True)]
    ppermute x3, waiting for transfers between devices: 0.01 us -> 18.6 us  [shards(): lax.ppermute(piece, 'pages', [(p, p ^ d) for p in range(devices)])]
    all_to_all x1, starting transfers between devices: 10.2 us -> 13.3 us  [shards(): lax.all_to_all(outbox, 'pages', split_axis=0, concat_axis=0, tiled=True)]
    ppermute x3, starting transfers between devices: 5.06 us -> 2.23 us  [shards(): lax.ppermute(piece, 'pages', [(p, p ^ d) for p in range(devices)])]
    all_to_all x1, starting transfers between devices: 6.21 us -> 8.21 us  [shards(): lax.all_to_all(routed, 'pages', split_axis=0, concat_axis=0, tiled=True)]
  transfers between devices with their start and end apart: 8 -> 8, of which waited for: 2 -> 4; matrix products, arithmetic and copies ran while one was open for 0% -> 0% of each run, Pallas kernels for 8% -> 3%
where the time goes in v9:
time: 91.9 us; the launch traced here: 91.6 us
  waiting for transfers between devices  51.5 us (56%)
  starting transfers between devices  28.6 us (31%)
  Pallas kernels  10.1 us (11%)
    all_to_all x1, waiting for transfers between devices, shards(): lax.all_to_all(routed, 'pages', split_axis=0, concat_axis=0, tiled=True)  31.4 us
    ppermute x3, waiting for transfers between devices, shards(): lax.ppermute(piece, 'pages', [(p, p ^ d) for p in range(devices)])  18.6 us
    all_to_all x1, starting transfers between devices, shards(): lax.all_to_all(outbox, 'pages', split_axis=0, concat_axis=0, tiled=True)  13.3 us
    all_to_all x1, starting transfers between devices, shards(): lax.all_to_all(routed, 'pages', split_axis=0, concat_axis=0, tiled=True)  8.21 us
    ppermute x3, starting transfers between devices, shards(): lax.ppermute(quarters[t], 'expert', [(i, (i + t) % shard_count) for i in...  4.89 us
    pallas_call x1, Pallas kernels, shards(): pl.pallas_call(source_kernel, out_shape=jax.ShapeDtypeStruct((devices, li...  4.35 us
    pallas_call x1, Pallas kernels, shards(): pl.pallas_call(middle_kernel, out_shape=jax.ShapeDtypeStruct((devices, he...  2.88 us
    ppermute x3, starting transfers between devices, shards(): lax.ppermute(piece, 'pages', [(p, p ^ d) for p in range(devices)])  2.23 us
  transfers between devices with their start and end apart: 8, of which 4 were waited for; matrix products, arithmetic and copies ran while one was open for 0% of the time, Pallas kernels for 3%

profile of v9, /device:TPU:1, one launch (start us, length us, event | category | flops | bytes accessed | tf_op | source)
XLA Modules:
  0.0 91.6 jit_solution(17266660979624733021)
XLA Ops:
  0.6 4.4 %source.1 = bf16[64,48,128]{2,1,0:T(8,128)(2,1)} custom-call(s32[1]{0:T(128)} %bitcast.1.my_ref, s32[12,64]{1,0:T(8,128)} %bitcast.9, s32[1,64]{1,0:T(1,128)} %bitcast.12, s32[2,64]{1,0:T(2,128)} %bitcast.14, s32[8,31]{1,0:T(8,128)} %keep_ref.1, s32[8,128]{1,0:T(8,128)} %drop_ref.1, bf16[8,128,512]{2,1,0:T(8,128)(2,1)} %k_ref.1, bf16[8,128,512]{2,1,0:T(8,128)(2,1)} %v_ref.1, ...), custom_call_target="tpu_custom_call" | custom-call | tf_op jit(solution)/shard_map/source/pallas_call | solution.py:399
  5.0 0.0 copy-start
  5.0 0.0 copy-start.1
  5.0 0.0 copy-start.2
  5.0 0.0 copy-start.3
  5.0 13.3 %all-to-all-start = ((bf16[64,48,128]{2,1,0:T(8,128)(2,1)}), bf16[64,48,128]{2,1,0:T(8,128)(2,1)S(1)}, u32[]{:S(2)}, u32[]{:S(2)}) async-start(bf16[64,48,128]{2,1,0:T(8,128)(2,1)} %source.1), calls=%async_computation | async-start | bytes 1572864 | tf_op jit(solution)/shard_map/all_to_all | solution.py:425
  18.3 0.0 copy-done
  18.4 1.7 %collective-permute-start.2 = (bf16[128,256]{1,0:T(8,128)(2,1)S(1)}, bf16[128,256]{1,0:T(8,128)(2,1)S(1)}, u32[]{:S(2)}, u32[]{:S(2)}) collective-permute-start(bf16[128,256]{1,0:T(8,128)(2,1)S(1)} %get-tuple-element.37), channel_id=1, source_target_pairs={{0,12},{4,8},{8,4},{12,0},{16,28},{20,24},{24,20},{28,16},{32,44},... | collective-permute-start | bytes 196616 | tf_op jit(solution)/shard_map/ppermute | solution.py:430
  20.1 0.2 collective-permute-start.1
  20.3 0.3 collective-permute-start
  20.6 0.0 copy-done.1
  20.6 0.0 copy-done.2
  20.6 0.0 copy-done.3
  20.6 0.8 route.1.pick_hbm
  21.4 18.1 %collective-permute-done.2.refs_3_ = bf16[128,256]{1,0:T(8,128)(2,1)S(1)} collective-permute-done((bf16[128,256]{1,0:T(8,128)(2,1)S(1)}, bf16[128,256]{1,0:T(8,128)(2,1)S(1)}, u32[]{:S(2)}, u32[]{:S(2)}) %collective-permute-start.2) | collective-permute-done | bytes 65568 | tf_op jit(solution)/shard_map/ppermute | solution.py:430
  39.5 0.5 collective-permute-done.1.refs_2_
  40.0 0.0 collective-permute-done.refs_1_
  40.0 1.6 %all-to-all-done.got_hbm = bf16[64,48,128]{2,1,0:T(8,128)(2,1)S(1)} async-done(((bf16[64,48,128]{2,1,0:T(8,128)(2,1)}), bf16[64,48,128]{2,1,0:T(8,128)(2,1)S(1)}, u32[]{:S(2)}, u32[]{:S(2)}) %all-to-all-start) | async-done | bytes 786464 | tf_op jit(solution)/shard_map/all_to_all | solution.py:425
  41.5 2.9 %middle.1 = bf16[64,72,128]{2,1,0:T(8,128)(2,1)} custom-call(s32[1]{0:T(128)} %bitcast.head_ref, bf16[64,48,128]{2,1,0:T(8,128)(2,1)S(1)} %all-to-all-done.got_hbm, bf16[1024,512]{1,0:T(8,128)(2,1)S(1)} %route.1.pick_hbm, bf16[1,512,256]{2,1,0:T(8,128)(2,1)S(1)} %copy-done, bf16[128,256]{1,0:T(8,128)(2,1)S(1)} %collective-permute-done.refs_1_, ...), custom_call_target="tpu_custom_call" | custom-call | tf_op jit(solution)/shard_map/middle/pallas_call | solution.py:445
  44.4 8.2 %all-to-all-start.1 = ((bf16[64,72,128]{2,1,0:T(8,128)(2,1)}), bf16[64,72,128]{2,1,0:T(8,128)(2,1)S(1)}, u32[]{:S(2)}, u32[]{:S(2)}) async-start(bf16[64,72,128]{2,1,0:T(8,128)(2,1)} %middle.1), calls=%async_computation.1 | async-start | bytes 2359296 | tf_op jit(solution)/shard_map/all_to_all | solution.py:464
  52.6 31.4 %all-to-all-done.1.got_hbm = bf16[64,72,128]{2,1,0:T(8,128)(2,1)S(1)} async-done(((bf16[64,72,128]{2,1,0:T(8,128)(2,1)}), bf16[64,72,128]{2,1,0:T(8,128)(2,1)S(1)}, u32[]{:S(2)}, u32[]{:S(2)}) %all-to-all-start.1) | async-done | bytes 1179680 | tf_op jit(solution)/shard_map/all_to_all | solution.py:464
  84.0 0.1 sum.1
  84.1 1.3 %collective-permute-start.3 = (f32[1,512]{1,0:T(1,128)S(1)}, f32[1,512]{1,0:T(1,128)S(1)}, u32[]{:S(2)}, u32[]{:S(2)}) collective-permute-start(f32[1,512]{1,0:T(1,128)S(1)} %get-tuple-element.34), channel_id=1, source_target_pairs={{0,1},{1,2},{2,3},{3,0},{4,5},{5,6},{6,7},{7,4},{8,9},{9,10},{10,1... | collective-permute-start | bytes 6152 | tf_op jit(solution)/shard_map/ppermute | solution.py:483
  85.4 2.5 %collective-permute-start.4 = (f32[1,512]{1,0:T(1,128)S(1)}, f32[1,512]{1,0:T(1,128)S(1)}, u32[]{:S(2)}, u32[]{:S(2)}) collective-permute-start(f32[1,512]{1,0:T(1,128)S(1)} %get-tuple-element.35), channel_id=1, source_target_pairs={{0,2},{1,3},{2,0},{3,1},{4,6},{5,7},{6,4},{7,5},{8,10},{9,11},{10,... | collective-permute-start | bytes 6152 | tf_op jit(solution)/shard_map/ppermute | solution.py:483
  87.8 1.2 %collective-permute-start.5 = (f32[1,512]{1,0:T(1,128)S(1)}, f32[1,512]{1,0:T(1,128)S(1)}, u32[]{:S(2)}, u32[]{:S(2)}) collective-permute-start(f32[1,512]{1,0:T(1,128)S(1)} %get-tuple-element.36), channel_id=1, source_target_pairs={{0,3},{1,0},{2,1},{3,2},{4,7},{5,4},{6,5},{7,6},{8,11},{9,8},{10,9... | collective-permute-start | bytes 6152 | tf_op jit(solution)/shard_map/ppermute | solution.py:483
  89.0 2.0 %land.1 = (bf16[4,128,512]{2,1,0:T(8,128)(2,1)}, bf16[4,128,512]{2,1,0:T(8,128)(2,1)}) custom-call(bf16[64,72,128]{2,1,0:T(8,128)(2,1)S(1)} %all-to-all-done.1.got_hbm), custom_call_target="tpu_custom_call" | custom-call | tf_op jit(solution)/shard_map/land/pallas_call | solution.py:486
  91.0 0.0 collective-permute-done.3
  91.0 0.0 collective-permute-done.4
  91.0 0.0 collective-permute-done.5
  91.0 0.6 add_convert_fusion
  (1 shorter events, 0.0 us)
Async XLA Ops:
  5.0 13.4 %copy-start = (bf16[1,512,256]{2,1,0:T(8,128)(2,1)S(1)}, bf16[1,512,256]{2,1,0:T(8,128)(2,1)}, u32[]{:S(2)}) copy-start(bf16[1,512,256]{2,1,0:T(8,128)(2,1)} %refs_0_.1) | copy-start | bytes 786436
  5.0 15.6 %copy-start.1 = (s32[64,12]{0,1:T(8,128)S(1)}, s32[64,12]{0,1:T(8,128)}, u32[]{:S(2)}) copy-start(s32[64,12]{0,1:T(8,128)} %param.18) | copy-start | bytes 9220
  5.0 15.6 %copy-start.2 = (s32[64,3]{0,1:T(4,128)S(1)}, s32[64,3]{0,1:T(4,128)}, u32[]{:S(2)}) copy-start(s32[64,3]{0,1:T(4,128)} %param.19) | copy-start | bytes 2308
  5.0 15.6 %copy-start.3 = (s32[64]{0:T(128)S(1)}, s32[64]{0:T(128)}, u32[]{:S(2)}) copy-start(s32[64]{0:T(128)} %param.17) | copy-start | bytes 772
  5.0 36.5 %all-to-all-start = ((bf16[64,48,128]{2,1,0:T(8,128)(2,1)}), bf16[64,48,128]{2,1,0:T(8,128)(2,1)S(1)}, u32[]{:S(2)}, u32[]{:S(2)}) async-start(bf16[64,48,128]{2,1,0:T(8,128)(2,1)} %source.1), calls=%async_computation | async-start | bytes 1572864 | tf_op jit(solution)/shard_map/all_to_all | solution.py:425
  18.4 21.1 %collective-permute-start.2 = (bf16[128,256]{1,0:T(8,128)(2,1)S(1)}, bf16[128,256]{1,0:T(8,128)(2,1)S(1)}, u32[]{:S(2)}, u32[]{:S(2)}) collective-permute-start(bf16[128,256]{1,0:T(8,128)(2,1)S(1)} %get-tuple-element.37), channel_id=1, source_target_pairs={{0,12},{4,8},{8,4},{12,0},{16,28},{20,24},{24,20},{28,16},{32,44},... | collective-permute-start | bytes 196616 | tf_op jit(solution)/shard_map/ppermute | solution.py:430
  20.1 19.9 %collective-permute-start.1 = (bf16[128,256]{1,0:T(8,128)(2,1)S(1)}, bf16[128,256]{1,0:T(8,128)(2,1)S(1)}, u32[]{:S(2)}, u32[]{:S(2)}) collective-permute-start(bf16[128,256]{1,0:T(8,128)(2,1)S(1)} %get-tuple-element.38), channel_id=1, source_target_pairs={{0,8},{4,12},{8,0},{12,4},{16,24},{20,28},{24,16},{28,20},{32,40},... | collective-permute-start | bytes 196616 | tf_op jit(solution)/shard_map/ppermute | solution.py:430
  20.3 19.7 %collective-permute-start = (bf16[128,256]{1,0:T(8,128)(2,1)S(1)}, bf16[128,256]{1,0:T(8,128)(2,1)S(1)}, u32[]{:S(2)}, u32[]{:S(2)}) collective-permute-start(bf16[128,256]{1,0:T(8,128)(2,1)S(1)} %get-tuple-element.39), channel_id=1, source_target_pairs={{0,4},{4,0},{8,12},{12,8},{16,20},{20,16},{24,28},{28,24},{32,36},... | collective-permute-start | bytes 196616 | tf_op jit(solution)/shard_map/ppermute | solution.py:430
  44.4 39.6 %all-to-all-start.1 = ((bf16[64,72,128]{2,1,0:T(8,128)(2,1)}), bf16[64,72,128]{2,1,0:T(8,128)(2,1)S(1)}, u32[]{:S(2)}, u32[]{:S(2)}) async-start(bf16[64,72,128]{2,1,0:T(8,128)(2,1)} %middle.1), calls=%async_computation.1 | async-start | bytes 2359296 | tf_op jit(solution)/shard_map/all_to_all | solution.py:464
  84.1 6.9 %collective-permute-start.3 = (f32[1,512]{1,0:T(1,128)S(1)}, f32[1,512]{1,0:T(1,128)S(1)}, u32[]{:S(2)}, u32[]{:S(2)}) collective-permute-start(f32[1,512]{1,0:T(1,128)S(1)} %get-tuple-element.34), channel_id=1, source_target_pairs={{0,1},{1,2},{2,3},{3,0},{4,5},{5,6},{6,7},{7,4},{8,9},{9,10},{10,1... | collective-permute-start | bytes 6152 | tf_op jit(solution)/shard_map/ppermute | solution.py:483
  85.4 5.6 %collective-permute-start.4 = (f32[1,512]{1,0:T(1,128)S(1)}, f32[1,512]{1,0:T(1,128)S(1)}, u32[]{:S(2)}, u32[]{:S(2)}) collective-permute-start(f32[1,512]{1,0:T(1,128)S(1)} %get-tuple-element.35), channel_id=1, source_target_pairs={{0,2},{1,3},{2,0},{3,1},{4,6},{5,7},{6,4},{7,5},{8,10},{9,11},{10,... | collective-permute-start | bytes 6152 | tf_op jit(solution)/shard_map/ppermute | solution.py:483
  87.8 3.2 %collective-permute-start.5 = (f32[1,512]{1,0:T(1,128)S(1)}, f32[1,512]{1,0:T(1,128)S(1)}, u32[]{:S(2)}, u32[]{:S(2)}) collective-permute-start(f32[1,512]{1,0:T(1,128)S(1)} %get-tuple-element.36), channel_id=1, source_target_pairs={{0,3},{1,0},{2,1},{3,2},{4,7},{5,4},{6,5},{7,6},{8,11},{9,8},{10,9... | collective-permute-start | bytes 6152 | tf_op jit(solution)/shard_map/ppermute | solution.py:483

commit v10 on v9

--- a/solution.py
+++ b/solution.py
@@ -1,3 +1,4 @@
+import functools
 import math
 
 import jax
@@ -196,13 +197,14 @@
             )
 
 
-def middle_kernel(head_ref, got_hbm, pick_hbm, *refs):
-    w_refs, (out_hbm, scr, terms, stack, parts, got_ref, pick_ref, out_ref, sems, out_sems) = (
-        refs[:-10],
-        refs[-10:],
-    )
-    heads = len(w_refs)
-    head = head_ref[0]
+def expert_kernel(at_ref, got_hbm, *refs):
+    scr, halves, stack, parts, sems = refs[-5:]
+    heads = stack.shape[0]
+    w_refs, out_refs = refs[:heads], refs[heads:-5]
+    page = at_ref[0]
+    shard = at_ref[1]
+    head = page & (heads - 1)
+    group = lax.shift_right_logical(page, 2) & 1
     reqs, lines, _ = scr.shape
     slots = lines // 2
     depth = stack.shape[1]
@@ -212,8 +214,6 @@
     )
     for d in range(1, heads):
         loads.append(pltpu.make_async_copy(w_refs[d], stack.at[d], sems.at[1 + d]))
-    loads.append(pltpu.make_async_copy(got_hbm.at[:, lines:, :], got_ref, sems.at[heads + 1]))
-    loads.append(pltpu.make_async_copy(pick_hbm, pick_ref, sems.at[heads + 2]))
     for load in loads:
         load.start()
     loads[0].wait()
@@ -221,7 +221,8 @@
     stats = scr[:, slots + 1, :]
     stats = jnp.concatenate([stats, stats], axis=0).T
     left = iota((1, 2 * reqs), 1) < reqs
-    target = iota((reqs, 2 * reqs), 0).astype(F32)
+    order = iota((reqs, 2 * reqs), 0)
+    target = (rest(order, reqs // 2) * 2 + over(order, reqs // 2)).astype(F32)
 
     def item(g, i):
         first = stats[6 * g + i : 6 * g + i + 1, :]
@@ -251,19 +252,48 @@
     some = den > 0.0
     value = (num[:reqs] + num[reqs:]) / jnp.where(some, den, 1.0)
     weighted = jnp.where(some, gate * value, 0.0).astype(BF16)
-    tiles = stack.shape[2] // HD
-    for load in loads[1 : 1 + heads]:
+    for load in loads[1:]:
         load.wait()
+    cols = stack.shape[2]
     for b in range(heads):
-        part = dot(weighted, stack[b ^ head])
-        for t in range(tiles):
-            terms[:, b * tiles + t, :] = part[:, t * HD : (t + 1) * HD]
-    terms_at = out_ref.shape[1] - heads * tiles
-    out_ref[:, terms_at:, :] = terms[...].astype(BF16)
+        at = slice(b % 2 * cols, (b % 2 + 1) * cols)
+        halves[b // 2, :, at] = dot(weighted, stack[b ^ head])
+    for t, out_ref in enumerate(out_refs):
+        part = halves[(shard + t) & 1]
+        if t == 0:
+            part = jnp.where(lax.shift_right_logical(shard, 1) == group, part, 0.0)
+        out_ref[...] = part.astype(BF16)
+
+
+def stage_kernel(at_ref, *refs, count):
+    in_refs, out_refs, (total,) = refs[: -count - 1], refs[-count - 1 : -1], refs[-1:]
+    value = in_refs[0][...].astype(F32)
+    for ref in in_refs[1:]:
+        value = value + ref[...].astype(F32)
+    total[...] = value
+    rows = value.shape[0] // count
+    for t, out_ref in enumerate(out_refs):
+        at = ((at_ref[0] + t) & (count - 1)) * rows
+        if rows % 8 == 0:
+            at = pl.multiple_of(at, 8)
+        out_ref[...] = total[pl.ds(at, rows), :]
+
+
+def relay_kernel(got_hbm, pick_hbm, out_hbm, got_ref, pick_ref, out_ref, sems, out_sems):
+    reqs, width, _ = got_ref.shape
+    slots = width // 4
+    lines = got_hbm.shape[1] - width
+    loads = [
+        pltpu.make_async_copy(got_hbm.at[:, lines:, :], got_ref, sems.at[0]),
+        pltpu.make_async_copy(pick_hbm, pick_ref, sems.at[1]),
+    ]
+    for load in loads:
+        load.start()
+    for load in loads:
+        load.wait()
+    terms_at = out_ref.shape[1]
     held = reqs * slots
     local = pick_ref.shape[0] // reqs
-    for load in loads[1 + heads :]:
-        load.wait()
     table = jnp.concatenate(
         [
             got_ref[:, t * slots : (t + 1) * slots, :]
@@ -304,31 +334,6 @@
         found = jnp.where(filled == slot, page, found)
     source = jnp.sum(found, axis=1, keepdims=True) - 1
     out_ref[...] = jnp.where(source == iota(out_ref.shape, 1), 1.0, 0.0).astype(BF16)
-
-
-def sum_kernel(shard_ref, got_hbm, *refs):
-    out_refs, (quarters, got_ref, sem) = refs[:-3], refs[-3:]
-    terms = got_ref.shape[1]
-    load = pltpu.make_async_copy(got_hbm.at[:, got_hbm.shape[1] - terms :, :], got_ref, sem)
-    load.start()
-    load.wait()
-    s = shard_ref[0]
-    count = len(out_refs)
-    heads = count
-    columns = got_ref.shape[0] // EXPERTS
-    got = got_ref[...].astype(F32)
-    per = got.shape[1] // 2
-    for z in range(columns // heads):
-        total = jnp.zeros(got.shape[1:], F32)
-        for e in range(EXPERTS):
-            at = e * columns + z * heads
-            total = total + jnp.sum(got[at : at + heads], axis=0)
-        for i in range(2):
-            quarters[2 * z + i] = total[i * per : (i + 1) * per]
-    for t, out_ref in enumerate(out_refs):
-        quarter = quarters[lax.rem(s + t, count)]
-        for i in range(per):
-            out_ref[:, i * HD : (i + 1) * HD] = quarter[i : i + 1, :]
 
 
 def land_kernel(got_hbm, k_hbm, v_hbm, got_ref, k_ref, v_ref, sems, out_sems):
@@ -392,7 +397,7 @@
     lines = 2 * slots
     columns = devices // EXPERTS
     head = lax.rem(my, heads)
-    shard = lax.axis_index("expert").astype(jnp.int32).reshape(1)
+    shard = lax.axis_index("expert").astype(jnp.int32)
     table = page_table.T
     counts = request_pages.reshape(1, -1)
 
@@ -440,48 +445,90 @@
     )(new_table.T, table, counts)
     inbox, pick, weights = lax.optimization_barrier((inbox, pick, weights))
 
-    block_cols = out_weight.shape[2]
-    terms = heads * block_cols // HD
     routed = pl.pallas_call(
-        middle_kernel,
-        out_shape=jax.ShapeDtypeStruct((devices, heads * local + terms, HD), BF16),
-        in_specs=[SMEM] + [ANY] * (2 + heads),
+        relay_kernel,
+        out_shape=jax.ShapeDtypeStruct((devices, heads * local, HD), BF16),
+        in_specs=[ANY, ANY],
         out_specs=ANY,
         scratch_shapes=[
-            pltpu.VMEM((requests, lines, HD), F32),
-            pltpu.VMEM((requests, terms, HD), F32),
-            pltpu.VMEM((heads, HD, block_cols), BF16),
-            pltpu.VMEM((devices, lines, HD), BF16),
             pltpu.VMEM((devices, heads * slots, HD), BF16),
             pltpu.VMEM((devices * local, devices * slots), BF16),
-            pltpu.VMEM((devices, heads * local + terms, HD), BF16),
-            pltpu.SemaphoreType.DMA((heads + 3,)),
+            pltpu.VMEM((devices, heads * local, HD), BF16),
+            pltpu.SemaphoreType.DMA((2,)),
             pltpu.SemaphoreType.DMA((devices // 16,)),
         ],
         compiler_params=PARAMS,
-        name="middle",
-    )(head.reshape(1), inbox, pick, out_weight, *weights)
+        name="relay",
+    )(inbox, pick)
     landed = lax.all_to_all(routed, "pages", split_axis=0, concat_axis=0, tiled=True)
 
-    quarters = pl.pallas_call(
-        sum_kernel,
-        out_shape=[jax.ShapeDtypeStruct((1, width), F32)] * shard_count,
-        in_specs=[SMEM, ANY],
+    inbox, _ = lax.optimization_barrier((inbox, routed))
+    block_cols = out_weight.shape[2]
+    deep = columns
+    tall = devices // (2 * deep)
+    parts = pl.pallas_call(
+        expert_kernel,
+        out_shape=[jax.ShapeDtypeStruct((requests, width), BF16)] * shard_count,
+        in_specs=[SMEM, ANY] + [ANY] * heads,
         out_specs=[VMEM] * shard_count,
         scratch_shapes=[
-            pltpu.VMEM((shard_count, width // HD, HD), F32),
-            pltpu.VMEM((devices, terms, HD), BF16),
-            pltpu.SemaphoreType.DMA(()),
+            pltpu.VMEM((requests, lines, HD), F32),
+            pltpu.VMEM((2, requests, width), F32),
+            pltpu.VMEM((heads, HD, block_cols), BF16),
+            pltpu.VMEM((devices, lines, HD), BF16),
+            pltpu.SemaphoreType.DMA((heads + 1,)),
         ],
         compiler_params=PARAMS,
-        name="sum",
-    )(shard, landed)
-    landed, quarters = lax.optimization_barrier((landed, quarters))
-    moved = [quarters[0]]
+        name="expert",
+    )(jnp.stack([my, shard]), inbox, out_weight, *weights)
+
+    def holds(p, q):
+        return p // heads % 2 == q // 2
+
+    def stage(arrays, count, place, name):
+        rows, cols = arrays[0].shape
+        return pl.pallas_call(
+            functools.partial(stage_kernel, count=count),
+            out_shape=[jax.ShapeDtypeStruct((rows // count, cols), F32)] * count,
+            in_specs=[SMEM] + [VMEM] * len(arrays),
+            out_specs=[VMEM] * count,
+            scratch_shapes=[pltpu.VMEM((rows, cols), F32)],
+            compiler_params=PARAMS,
+            name=name,
+        )(place.reshape(1), *arrays)
+
+    arrived = [parts[0]]
     for t in range(1, shard_count):
-        moved.append(
-            lax.ppermute(quarters[t], "expert", [(i, (i + t) % shard_count) for i in range(shard_count)])
-        )
+        moves = []
+        for p in range(devices):
+            for s in range(shard_count):
+                q = (s + t) % shard_count
+                if holds(p, q):
+                    moves.append((p * shard_count + s, p * shard_count + q))
+        arrived.append(lax.ppermute(parts[t], ("pages", "expert"), moves))
+
+    def send(arrays, target):
+        result = [arrays[0]]
+        for t in range(1, len(arrays)):
+            moves = [
+                (p * shard_count + q, target(p, t) * shard_count + q)
+                for p in range(devices)
+                for q in range(shard_count)
+                if holds(p, q)
+            ]
+            result.append(lax.ppermute(arrays[t], ("pages", "expert"), moves))
+        return result
+
+    parts = stage(arrived, 2, my & 1, "by_core")
+    arrived = send(parts, lambda p, t: p ^ t)
+    parts = stage(arrived, tall, lax.shift_right_logical(my, 4), "by_y")
+    arrived = send(parts, lambda p, t: (p + 2 * deep * t) % devices)
+    parts = stage(arrived, deep, lax.shift_right_logical(my, 1) & (deep - 1), "by_z")
+    landed, _ = lax.optimization_barrier((landed, parts))
+    arrived = send(
+        parts, lambda p, t: p // (2 * deep) * 2 * deep + (p + 2 * t) % (2 * deep)
+    )
+    mixed = sum(arrived[1:], arrived[0]).astype(BF16)
     new_page = jax.ShapeDtypeStruct((new_cap, per_new * rows, width), BF16)
     compact_keys, compact_values = pl.pallas_call(
         land_kernel,
@@ -489,7 +536,7 @@
         in_specs=[ANY],
         out_specs=(ANY, ANY),
         scratch_shapes=[
-            pltpu.VMEM((devices, heads * local + terms, HD), BF16),
+            pltpu.VMEM((devices, heads * local, HD), BF16),
             pltpu.VMEM(new_page.shape, BF16),
             pltpu.VMEM(new_page.shape, BF16),
             pltpu.SemaphoreType.DMA((2,)),
@@ -498,7 +545,6 @@
         compiler_params=PARAMS,
         name="land",
     )(landed)
-    mixed = sum(moved[1:], moved[0]).astype(BF16)
     return (compact_keys, compact_values, mixed)
 
 

time: 91.9 us -> 110 us (1.20)
  the two profiles are of different devices: /device:TPU:1 before, /device:TPU:2 now
where the time goes in v10:
time: 110 us; the launch traced here: 109 us
  starting transfers between devices  66.2 us (60%)
  waiting for transfers between devices  30.3 us (28%)
  Pallas kernels  10.4 us (9%)
    ppermute x11, starting transfers between devices, send(): result.append(lax.ppermute(arrays[t], ('pages', 'expert'), moves))  36.6 us
    ppermute x3, waiting for transfers between devices, shards(): lax.ppermute(piece, 'pages', [(p, p ^ d) for p in range(devices)])  18.2 us
    all_to_all x1, starting transfers between devices, shards(): lax.all_to_all(outbox, 'pages', split_axis=0, concat_axis=0, tiled=True)  12.2 us
    all_to_all x1, starting transfers between devices, shards(): lax.all_to_all(routed, 'pages', split_axis=0, concat_axis=0, tiled=True)  8.19 us
    ppermute x3, starting transfers between devices, shards(): arrived.append(lax.ppermute(parts[t], ('pages', 'expert'), moves))  7.13 us
    ppermute x11, waiting for transfers between devices, send(): result.append(lax.ppermute(arrays[t], ('pages', 'expert'), moves))  7.09 us
    pallas_call x1, Pallas kernels, shards(): pl.pallas_call(source_kernel, out_shape=jax.ShapeDtypeStruct((devices, li...  4.35 us
    ppermute x3, waiting for transfers between devices, shards(): arrived.append(lax.ppermute(parts[t], ('pages', 'expert'), moves))  3.67 us
  transfers between devices with their start and end apart: 19, of which 8 were waited for; matrix products, arithmetic and copies ran while one was open for 1% of the time, Pallas kernels for 2%

profile of v10, /device:TPU:2, one launch (start us, length us, event | category | flops | bytes accessed | tf_op | source)
XLA Modules:
  0.0 109.0 jit_solution(17961043110582394593)
XLA Ops:
  0.6 4.4 %source.1 = bf16[64,48,128]{2,1,0:T(8,128)(2,1)} custom-call(s32[1]{0:T(128)} %bitcast.my_ref, s32[12,64]{1,0:T(8,128)} %bitcast.11, s32[1,64]{1,0:T(1,128)} %bitcast.14, s32[2,64]{1,0:T(2,128)} %bitcast.16, s32[8,31]{1,0:T(8,128)} %keep_ref.1, s32[8,128]{1,0:T(8,128)} %drop_ref.1, bf16[8,128,512]{2,1,0:T(8,128)(2,1)} %k_ref.1, bf16[8,128,512]{2,1,0:T(8,128)(2,1)} %v_ref.1, ...), custom_call_target="tpu_custom_call" | custom-call | tf_op jit(solution)/shard_map/source/pallas_call | solution.py:404
  5.0 12.2 %all-to-all-start = ((bf16[64,48,128]{2,1,0:T(8,128)(2,1)}), bf16[64,48,128]{2,1,0:T(8,128)(2,1)S(1)}, u32[]{:S(2)}, u32[]{:S(2)}) async-start(bf16[64,48,128]{2,1,0:T(8,128)(2,1)} %source.1), calls=%async_computation | async-start | bytes 1572864 | tf_op jit(solution)/shard_map/all_to_all | solution.py:430
  17.3 0.0 copy-done
  17.3 0.0 copy-start.1
  17.3 0.1 collective-permute-start
  17.5 1.7 %collective-permute-start.1 = (bf16[128,256]{1,0:T(8,128)(2,1)S(1)}, bf16[128,256]{1,0:T(8,128)(2,1)S(1)}, u32[]{:S(2)}, u32[]{:S(2)}) collective-permute-start(bf16[128,256]{1,0:T(8,128)(2,1)S(1)} %get-tuple-element.60), channel_id=1, source_target_pairs={{0,8},{4,12},{8,0},{12,4},{16,24},{20,28},{24,16},{28,20},{32,40},... | collective-permute-start | bytes 196616 | tf_op jit(solution)/shard_map/ppermute | solution.py:435
  19.1 0.2 collective-permute-start.2
  19.3 0.5 copy-done.3
  19.8 0.8 route.1.pick_hbm
  20.6 0.0 collective-permute-done.refs_1_
  20.6 17.8 %collective-permute-done.1.refs_2_ = bf16[128,256]{1,0:T(8,128)(2,1)S(1)} collective-permute-done((bf16[128,256]{1,0:T(8,128)(2,1)S(1)}, bf16[128,256]{1,0:T(8,128)(2,1)S(1)}, u32[]{:S(2)}, u32[]{:S(2)}) %collective-permute-start.1) | collective-permute-done | bytes 65568 | tf_op jit(solution)/shard_map/ppermute | solution.py:435
  38.4 0.5 collective-permute-done.2.refs_3_
  38.8 1.3 %all-to-all-done.got_hbm = bf16[64,48,128]{2,1,0:T(8,128)(2,1)S(1)} async-done(((bf16[64,48,128]{2,1,0:T(8,128)(2,1)}), bf16[64,48,128]{2,1,0:T(8,128)(2,1)S(1)}, u32[]{:S(2)}, u32[]{:S(2)}) %all-to-all-start) | async-done | bytes 786464 | tf_op jit(solution)/shard_map/all_to_all | solution.py:430
  40.2 1.6 %relay.1 = bf16[64,64,128]{2,1,0:T(8,128)(2,1)} custom-call(bf16[64,48,128]{2,1,0:T(8,128)(2,1)S(1)} %all-to-all-done.got_hbm, bf16[1024,512]{1,0:T(8,128)(2,1)S(1)} %route.1.pick_hbm), custom_call_target="tpu_custom_call" | custom-call | tf_op jit(solution)/shard_map/relay/pallas_call | solution.py:448
  41.8 8.2 %all-to-all-start.1 = ((bf16[64,64,128]{2,1,0:T(8,128)(2,1)}), bf16[64,64,128]{2,1,0:T(8,128)(2,1)S(1)}, u32[]{:S(2)}, u32[]{:S(2)}) async-start(bf16[64,64,128]{2,1,0:T(8,128)(2,1)} %relay.1), calls=%async_computation.1 | async-start | bytes 2097152 | tf_op jit(solution)/shard_map/all_to_all | solution.py:463
  50.0 0.1 pad_add_fusion.at_ref
  50.1 1.8 %expert.1 = (bf16[64,512]{1,0:T(8,128)(2,1)S(1)}, bf16[64,512]{1,0:T(8,128)(2,1)S(1)}, bf16[64,512]{1,0:T(8,128)(2,1)S(1)}, bf16[64,512]{1,0:T(8,128)(2,1)S(1)}) custom-call(s32[2]{0:T(128)S(1)} %pad_add_fusion.at_ref, bf16[64,48,128]{2,1,0:T(8,128)(2,1)S(1)} %all-to-all-done.got_hbm, bf16[1,512,256]{2,1,0:T(8,128)(2,1)S(1)} %copy-done, ...), custom_call_target="tpu_custom_call" | custom-call | tf_op jit(solution)/shard_map/expert/pallas_call | solution.py:469
  51.8 1.3 %collective-permute-start.3 = (bf16[64,512]{1,0:T(8,128)(2,1)S(1)}, bf16[64,512]{1,0:T(8,128)(2,1)S(1)}, u32[]{:S(2)}, u32[]{:S(2)}) collective-permute-start(bf16[64,512]{1,0:T(8,128)(2,1)S(1)} %get-tuple-element.39), channel_id=1, source_target_pairs={{0,1},{3,0},{4,5},{7,4},{8,9},{11,8},{12,13},{15,12},{17,18},{18,1... | collective-permute-start | bytes 196616 | tf_op jit(solution)/shard_map/ppermute | solution.py:508
  53.1 1.3 %collective-permute-start.4 = (bf16[64,512]{1,0:T(8,128)(2,1)S(1)}, bf16[64,512]{1,0:T(8,128)(2,1)S(1)}, u32[]{:S(2)}, u32[]{:S(2)}) collective-permute-start(bf16[64,512]{1,0:T(8,128)(2,1)S(1)} %get-tuple-element.40), channel_id=1, source_target_pairs={{2,0},{3,1},{6,4},{7,5},{10,8},{11,9},{14,12},{15,13},{16,18},{17,... | collective-permute-start | bytes 196616 | tf_op jit(solution)/shard_map/ppermute | solution.py:508
  54.4 4.6 %collective-permute-start.5 = (bf16[64,512]{1,0:T(8,128)(2,1)S(1)}, bf16[64,512]{1,0:T(8,128)(2,1)S(1)}, u32[]{:S(2)}, u32[]{:S(2)}) collective-permute-start(bf16[64,512]{1,0:T(8,128)(2,1)S(1)} %get-tuple-element.41), channel_id=1, source_target_pairs={{1,0},{2,1},{5,4},{6,5},{9,8},{10,9},{13,12},{14,13},{16,19},{19,1... | collective-permute-start | bytes 196616 | tf_op jit(solution)/shard_map/ppermute | solution.py:508
  59.0 0.0 collective-permute-done.3.refs_1_
  59.0 1.8 %collective-permute-done.4.refs_2_ = bf16[64,512]{1,0:T(8,128)(2,1)S(1)} collective-permute-done((bf16[64,512]{1,0:T(8,128)(2,1)S(1)}, bf16[64,512]{1,0:T(8,128)(2,1)S(1)}, u32[]{:S(2)}, u32[]{:S(2)}) %collective-permute-start.4) | collective-permute-done | bytes 65568 | tf_op jit(solution)/shard_map/ppermute | solution.py:508
  60.8 1.9 %collective-permute-done.5.refs_3_ = bf16[64,512]{1,0:T(8,128)(2,1)S(1)} collective-permute-done((bf16[64,512]{1,0:T(8,128)(2,1)S(1)}, bf16[64,512]{1,0:T(8,128)(2,1)S(1)}, u32[]{:S(2)}, u32[]{:S(2)}) %collective-permute-start.5) | collective-permute-done | bytes 65568 | tf_op jit(solution)/shard_map/ppermute | solution.py:508
  62.7 1.9 %collective-permute-start.6 = (f32[32,512]{1,0:T(8,128)S(1)}, f32[32,512]{1,0:T(8,128)S(1)}, u32[]{:S(2)}, u32[]{:S(2)}) collective-permute-start(f32[32,512]{1,0:T(8,128)S(1)} %get-tuple-element.43), channel_id=1, source_target_pairs={{0,4},{1,5},{4,0},{5,1},{8,12},{9,13},{12,8},{13,9},{18,22},{19,23... | collective-permute-start | bytes 196616 | tf_op jit(solution)/shard_map/ppermute | solution.py:519
  64.7 1.2 %collective-permute-done.6.refs_1_ = f32[32,512]{1,0:T(8,128)S(1)} collective-permute-done((f32[32,512]{1,0:T(8,128)S(1)}, f32[32,512]{1,0:T(8,128)S(1)}, u32[]{:S(2)}, u32[]{:S(2)}) %collective-permute-start.6) | collective-permute-done | bytes 65568 | tf_op jit(solution)/shard_map/ppermute | solution.py:519
  65.9 3.5 %collective-permute-start.7 = (f32[8,512]{1,0:T(8,128)S(1)}, f32[8,512]{1,0:T(8,128)S(1)}, u32[]{:S(2)}, u32[]{:S(2)}) collective-permute-start(f32[8,512]{1,0:T(8,128)S(1)} %get-tuple-element.45), channel_id=1, source_target_pairs={{0,64},{1,65},{4,68},{5,69},{8,72},{9,73},{12,76},{13,77},{18,82},... | collective-permute-start | bytes 49160 | tf_op jit(solution)/shard_map/ppermute | solution.py:519
  69.4 4.8 %collective-permute-start.8 = (f32[8,512]{1,0:T(8,128)S(1)}, f32[8,512]{1,0:T(8,128)S(1)}, u32[]{:S(2)}, u32[]{:S(2)}) collective-permute-start(f32[8,512]{1,0:T(8,128)S(1)} %get-tuple-element.46), channel_id=1, source_target_pairs={{0,128},{1,129},{4,132},{5,133},{8,136},{9,137},{12,140},{13,141},... | collective-permute-start | bytes 49160 | tf_op jit(solution)/shard_map/ppermute | solution.py:519
  74.2 3.3 %collective-permute-start.9 = (f32[8,512]{1,0:T(8,128)S(1)}, f32[8,512]{1,0:T(8,128)S(1)}, u32[]{:S(2)}, u32[]{:S(2)}) collective-permute-start(f32[8,512]{1,0:T(8,128)S(1)} %get-tuple-element.47), channel_id=1, source_target_pairs={{0,192},{1,193},{4,196},{5,197},{8,200},{9,201},{12,204},{13,205},... | collective-permute-start | bytes 49160 | tf_op jit(solution)/shard_map/ppermute | solution.py:519
  77.4 0.0 collective-permute-done.7.refs_1_
  77.5 0.0 collective-permute-done.8.refs_2_
  77.5 2.3 %collective-permute-done.9.refs_3_ = f32[8,512]{1,0:T(8,128)S(1)} collective-permute-done((f32[8,512]{1,0:T(8,128)S(1)}, f32[8,512]{1,0:T(8,128)S(1)}, u32[]{:S(2)}, u32[]{:S(2)}) %collective-permute-start.9) | collective-permute-done | bytes 16416 | tf_op jit(solution)/shard_map/ppermute | solution.py:519
  79.8 3.4 %collective-permute-start.10 = (f32[1,512]{1,0:T(1,128)S(1)}, f32[1,512]{1,0:T(1,128)S(1)}, u32[]{:S(2)}, u32[]{:S(2)}) collective-permute-start(f32[1,512]{1,0:T(1,128)S(1)} %get-tuple-element.49), channel_id=1, source_target_pairs={{0,8},{1,9},{4,12},{5,13},{8,16},{9,17},{12,20},{13,21},{18,26},{1... | collective-permute-start | bytes 6152 | tf_op jit(solution)/shard_map/ppermute | solution.py:519
  83.2 1.3 %collective-permute-start.11 = (f32[1,512]{1,0:T(1,128)S(1)}, f32[1,512]{1,0:T(1,128)S(1)}, u32[]{:S(2)}, u32[]{:S(2)}) collective-permute-start(f32[1,512]{1,0:T(1,128)S(1)} %get-tuple-element.50), channel_id=1, source_target_pairs={{0,16},{1,17},{4,20},{5,21},{8,24},{9,25},{12,28},{13,29},{18,34},... | collective-permute-start | bytes 6152 | tf_op jit(solution)/shard_map/ppermute | solution.py:519
  84.5 1.9 %collective-permute-start.12 = (f32[1,512]{1,0:T(1,128)S(1)}, f32[1,512]{1,0:T(1,128)S(1)}, u32[]{:S(2)}, u32[]{:S(2)}) collective-permute-start(f32[1,512]{1,0:T(1,128)S(1)} %get-tuple-element.51), channel_id=1, source_target_pairs={{0,24},{1,25},{4,28},{5,29},{8,32},{9,33},{12,36},{13,37},{18,42},... | collective-permute-start | bytes 6152 | tf_op jit(solution)/shard_map/ppermute | solution.py:519
  86.4 6.4 %collective-permute-start.13 = (f32[1,512]{1,0:T(1,128)S(1)}, f32[1,512]{1,0:T(1,128)S(1)}, u32[]{:S(2)}, u32[]{:S(2)}) collective-permute-start(f32[1,512]{1,0:T(1,128)S(1)} %get-tuple-element.52), channel_id=1, source_target_pairs={{0,32},{1,33},{4,36},{5,37},{8,40},{9,41},{12,44},{13,45},{18,50},... | collective-permute-start | bytes 6152 | tf_op jit(solution)/shard_map/ppermute | solution.py:519
  92.9 6.9 %collective-permute-start.14 = (f32[1,512]{1,0:T(1,128)S(1)}, f32[1,512]{1,0:T(1,128)S(1)}, u32[]{:S(2)}, u32[]{:S(2)}) collective-permute-start(f32[1,512]{1,0:T(1,128)S(1)} %get-tuple-element.53), channel_id=1, source_target_pairs={{0,40},{1,41},{4,44},{5,45},{8,48},{9,49},{12,52},{13,53},{18,58},... | collective-permute-start | bytes 6152 | tf_op jit(solution)/shard_map/ppermute | solution.py:519
  99.8 0.0 collective-permute-done.10
  99.8 1.3 %collective-permute-start.15 = (f32[1,512]{1,0:T(1,128)S(1)}, f32[1,512]{1,0:T(1,128)S(1)}, u32[]{:S(2)}, u32[]{:S(2)}) collective-permute-start(f32[1,512]{1,0:T(1,128)S(1)} %get-tuple-element.54), channel_id=1, source_target_pairs={{0,48},{1,49},{4,52},{5,53},{8,56},{9,57},{12,60},{13,61},{18,2},{... | collective-permute-start | bytes 6152 | tf_op jit(solution)/shard_map/ppermute | solution.py:519
  101.1 0.0 collective-permute-done.11
  101.1 1.9 %collective-permute-start.16 = (f32[1,512]{1,0:T(1,128)S(1)}, f32[1,512]{1,0:T(1,128)S(1)}, u32[]{:S(2)}, u32[]{:S(2)}) collective-permute-start(f32[1,512]{1,0:T(1,128)S(1)} %get-tuple-element.55), channel_id=1, source_target_pairs={{0,56},{1,57},{4,60},{5,61},{8,0},{9,1},{12,4},{13,5},{18,10},{19,... | collective-permute-start | bytes 6152 | tf_op jit(solution)/shard_map/ppermute | solution.py:519
  103.1 0.0 collective-permute-done.12
  103.1 0.0 collective-permute-done.13
  103.1 0.0 collective-permute-done.14
  103.1 0.0 collective-permute-done.15
  103.1 3.5 %collective-permute-done.16 = f32[1,512]{1,0:T(1,128)S(1)} collective-permute-done((f32[1,512]{1,0:T(1,128)S(1)}, f32[1,512]{1,0:T(1,128)S(1)}, u32[]{:S(2)}, u32[]{:S(2)}) %collective-permute-start.16) | collective-permute-done | bytes 2080 | tf_op jit(solution)/shard_map/ppermute | solution.py:519
  106.6 0.6 add_convert_fusion
  107.2 0.0 all-to-all-done.1.got_hbm
  107.2 1.8 %land.1 = (bf16[4,128,512]{2,1,0:T(8,128)(2,1)}, bf16[4,128,512]{2,1,0:T(8,128)(2,1)}) custom-call(bf16[64,64,128]{2,1,0:T(8,128)(2,1)S(1)} %all-to-all-done.1.got_hbm), custom_call_target="tpu_custom_call" | custom-call | tf_op jit(solution)/shard_map/land/pallas_call | solution.py:533
  (9 shorter events, 0.1 us)
Async XLA Ops:
  5.0 12.3 %copy-start = (bf16[1,512,256]{2,1,0:T(8,128)(2,1)S(1)}, bf16[1,512,256]{2,1,0:T(8,128)(2,1)}, u32[]{:S(2)}) copy-start(bf16[1,512,256]{2,1,0:T(8,128)(2,1)} %refs_0_.1) | copy-start | bytes 786436
  5.0 35.2 %all-to-all-start = ((bf16[64,48,128]{2,1,0:T(8,128)(2,1)}), bf16[64,48,128]{2,1,0:T(8,128)(2,1)S(1)}, u32[]{:S(2)}, u32[]{:S(2)}) async-start(bf16[64,48,128]{2,1,0:T(8,128)(2,1)} %source.1), calls=%async_computation | async-start | bytes 1572864 | tf_op jit(solution)/shard_map/all_to_all | solution.py:430
  17.3 2.0 %copy-start.1 = (s32[64,12]{0,1:T(8,128)S(1)}, s32[64,12]{0,1:T(8,128)}, u32[]{:S(2)}) copy-start(s32[64,12]{0,1:T(8,128)} %param.18) | copy-start | bytes 9220
  17.3 3.3 %collective-permute-start = (bf16[128,256]{1,0:T(8,128)(2,1)S(1)}, bf16[128,256]{1,0:T(8,128)(2,1)S(1)}, u32[]{:S(2)}, u32[]{:S(2)}) collective-permute-start(bf16[128,256]{1,0:T(8,128)(2,1)S(1)} %get-tuple-element.61), channel_id=1, source_target_pairs={{0,4},{4,0},{8,12},{12,8},{16,20},{20,16},{24,28},{28,24},{32,36},... | collective-permute-start | bytes 196616 | tf_op jit(solution)/shard_map/ppermute | solution.py:435
  17.5 1.8 %copy-start.2 = (s32[64,3]{0,1:T(4,128)S(1)}, s32[64,3]{0,1:T(4,128)}, u32[]{:S(2)}) copy-start(s32[64,3]{0,1:T(4,128)} %param.19) | copy-start | bytes 2308
  17.5 20.9 %collective-permute-start.1 = (bf16[128,256]{1,0:T(8,128)(2,1)S(1)}, bf16[128,256]{1,0:T(8,128)(2,1)S(1)}, u32[]{:S(2)}, u32[]{:S(2)}) collective-permute-start(bf16[128,256]{1,0:T(8,128)(2,1)S(1)} %get-tuple-element.60), channel_id=1, source_target_pairs={{0,8},{4,12},{8,0},{12,4},{16,24},{20,28},{24,16},{28,20},{32,40},... | collective-permute-start | bytes 196616 | tf_op jit(solution)/shard_map/ppermute | solution.py:435
  19.1 0.7 copy-start.3
  19.1 19.7 %collective-permute-start.2 = (bf16[128,256]{1,0:T(8,128)(2,1)S(1)}, bf16[128,256]{1,0:T(8,128)(2,1)S(1)}, u32[]{:S(2)}, u32[]{:S(2)}) collective-permute-start(bf16[128,256]{1,0:T(8,128)(2,1)S(1)} %get-tuple-element.59), channel_id=1, source_target_pairs={{0,12},{4,8},{8,4},{12,0},{16,28},{20,24},{24,20},{28,16},{32,44},... | collective-permute-start | bytes 196616 | tf_op jit(solution)/shard_map/ppermute | solution.py:435
  41.8 65.4 %all-to-all-start.1 = ((bf16[64,64,128]{2,1,0:T(8,128)(2,1)}), bf16[64,64,128]{2,1,0:T(8,128)(2,1)S(1)}, u32[]{:S(2)}, u32[]{:S(2)}) async-start(bf16[64,64,128]{2,1,0:T(8,128)(2,1)} %relay.1), calls=%async_computation.1 | async-start | bytes 2097152 | tf_op jit(solution)/shard_map/all_to_all | solution.py:463
  51.8 7.2 %collective-permute-start.3 = (bf16[64,512]{1,0:T(8,128)(2,1)S(1)}, bf16[64,512]{1,0:T(8,128)(2,1)S(1)}, u32[]{:S(2)}, u32[]{:S(2)}) collective-permute-start(bf16[64,512]{1,0:T(8,128)(2,1)S(1)} %get-tuple-element.39), channel_id=1, source_target_pairs={{0,1},{3,0},{4,5},{7,4},{8,9},{11,8},{12,13},{15,12},{17,18},{18,1... | collective-permute-start | bytes 196616 | tf_op jit(solution)/shard_map/ppermute | solution.py:508
  53.1 7.7 %collective-permute-start.4 = (bf16[64,512]{1,0:T(8,128)(2,1)S(1)}, bf16[64,512]{1,0:T(8,128)(2,1)S(1)}, u32[]{:S(2)}, u32[]{:S(2)}) collective-permute-start(bf16[64,512]{1,0:T(8,128)(2,1)S(1)} %get-tuple-element.40), channel_id=1, source_target_pairs={{2,0},{3,1},{6,4},{7,5},{10,8},{11,9},{14,12},{15,13},{16,18},{17,... | collective-permute-start | bytes 196616 | tf_op jit(solution)/shard_map/ppermute | solution.py:508
  54.4 8.2 %collective-permute-start.5 = (bf16[64,512]{1,0:T(8,128)(2,1)S(1)}, bf16[64,512]{1,0:T(8,128)(2,1)S(1)}, u32[]{:S(2)}, u32[]{:S(2)}) collective-permute-start(bf16[64,512]{1,0:T(8,128)(2,1)S(1)} %get-tuple-element.41), channel_id=1, source_target_pairs={{1,0},{2,1},{5,4},{6,5},{9,8},{10,9},{13,12},{14,13},{16,19},{19,1... | collective-permute-start | bytes 196616 | tf_op jit(solution)/shard_map/ppermute | solution.py:508
  62.7 3.1 %collective-permute-start.6 = (f32[32,512]{1,0:T(8,128)S(1)}, f32[32,512]{1,0:T(8,128)S(1)}, u32[]{:S(2)}, u32[]{:S(2)}) collective-permute-start(f32[32,512]{1,0:T(8,128)S(1)} %get-tuple-element.43), channel_id=1, source_target_pairs={{0,4},{1,5},{4,0},{5,1},{8,12},{9,13},{12,8},{13,9},{18,22},{19,23... | collective-permute-start | bytes 196616 | tf_op jit(solution)/shard_map/ppermute | solution.py:519
  65.9 11.6 %collective-permute-start.7 = (f32[8,512]{1,0:T(8,128)S(1)}, f32[8,512]{1,0:T(8,128)S(1)}, u32[]{:S(2)}, u32[]{:S(2)}) collective-permute-start(f32[8,512]{1,0:T(8,128)S(1)} %get-tuple-element.45), channel_id=1, source_target_pairs={{0,64},{1,65},{4,68},{5,69},{8,72},{9,73},{12,76},{13,77},{18,82},... | collective-permute-start | bytes 49160 | tf_op jit(solution)/shard_map/ppermute | solution.py:519
  69.4 8.1 %collective-permute-start.8 = (f32[8,512]{1,0:T(8,128)S(1)}, f32[8,512]{1,0:T(8,128)S(1)}, u32[]{:S(2)}, u32[]{:S(2)}) collective-permute-start(f32[8,512]{1,0:T(8,128)S(1)} %get-tuple-element.46), channel_id=1, source_target_pairs={{0,128},{1,129},{4,132},{5,133},{8,136},{9,137},{12,140},{13,141},... | collective-permute-start | bytes 49160 | tf_op jit(solution)/shard_map/ppermute | solution.py:519
  74.2 5.6 %collective-permute-start.9 = (f32[8,512]{1,0:T(8,128)S(1)}, f32[8,512]{1,0:T(8,128)S(1)}, u32[]{:S(2)}, u32[]{:S(2)}) collective-permute-start(f32[8,512]{1,0:T(8,128)S(1)} %get-tuple-element.47), channel_id=1, source_target_pairs={{0,192},{1,193},{4,196},{5,197},{8,200},{9,201},{12,204},{13,205},... | collective-permute-start | bytes 49160 | tf_op jit(solution)/shard_map/ppermute | solution.py:519
  79.8 20.0 %collective-permute-start.10 = (f32[1,512]{1,0:T(1,128)S(1)}, f32[1,512]{1,0:T(1,128)S(1)}, u32[]{:S(2)}, u32[]{:S(2)}) collective-permute-start(f32[1,512]{1,0:T(1,128)S(1)} %get-tuple-element.49), channel_id=1, source_target_pairs={{0,8},{1,9},{4,12},{5,13},{8,16},{9,17},{12,20},{13,21},{18,26},{1... | collective-permute-start | bytes 6152 | tf_op jit(solution)/shard_map/ppermute | solution.py:519
  83.2 17.9 %collective-permute-start.11 = (f32[1,512]{1,0:T(1,128)S(1)}, f32[1,512]{1,0:T(1,128)S(1)}, u32[]{:S(2)}, u32[]{:S(2)}) collective-permute-start(f32[1,512]{1,0:T(1,128)S(1)} %get-tuple-element.50), channel_id=1, source_target_pairs={{0,16},{1,17},{4,20},{5,21},{8,24},{9,25},{12,28},{13,29},{18,34},... | collective-permute-start | bytes 6152 | tf_op jit(solution)/shard_map/ppermute | solution.py:519
  84.5 18.6 %collective-permute-start.12 = (f32[1,512]{1,0:T(1,128)S(1)}, f32[1,512]{1,0:T(1,128)S(1)}, u32[]{:S(2)}, u32[]{:S(2)}) collective-permute-start(f32[1,512]{1,0:T(1,128)S(1)} %get-tuple-element.51), channel_id=1, source_target_pairs={{0,24},{1,25},{4,28},{5,29},{8,32},{9,33},{12,36},{13,37},{18,42},... | collective-permute-start | bytes 6152 | tf_op jit(solution)/shard_map/ppermute | solution.py:519
  86.4 16.6 %collective-permute-start.13 = (f32[1,512]{1,0:T(1,128)S(1)}, f32[1,512]{1,0:T(1,128)S(1)}, u32[]{:S(2)}, u32[]{:S(2)}) collective-permute-start(f32[1,512]{1,0:T(1,128)S(1)} %get-tuple-element.52), channel_id=1, source_target_pairs={{0,32},{1,33},{4,36},{5,37},{8,40},{9,41},{12,44},{13,45},{18,50},... | collective-permute-start | bytes 6152 | tf_op jit(solution)/shard_map/ppermute | solution.py:519
  92.9 10.2 %collective-permute-start.14 = (f32[1,512]{1,0:T(1,128)S(1)}, f32[1,512]{1,0:T(1,128)S(1)}, u32[]{:S(2)}, u32[]{:S(2)}) collective-permute-start(f32[1,512]{1,0:T(1,128)S(1)} %get-tuple-element.53), channel_id=1, source_target_pairs={{0,40},{1,41},{4,44},{5,45},{8,48},{9,49},{12,52},{13,53},{18,58},... | collective-permute-start | bytes 6152 | tf_op jit(solution)/shard_map/ppermute | solution.py:519
  99.8 3.3 %collective-permute-start.15 = (f32[1,512]{1,0:T(1,128)S(1)}, f32[1,512]{1,0:T(1,128)S(1)}, u32[]{:S(2)}, u32[]{:S(2)}) collective-permute-start(f32[1,512]{1,0:T(1,128)S(1)} %get-tuple-element.54), channel_id=1, source_target_pairs={{0,48},{1,49},{4,52},{5,53},{8,56},{9,57},{12,60},{13,61},{18,2},{... | collective-permute-start | bytes 6152 | tf_op jit(solution)/shard_map/ppermute | solution.py:519
  101.1 5.5 %collective-permute-start.16 = (f32[1,512]{1,0:T(1,128)S(1)}, f32[1,512]{1,0:T(1,128)S(1)}, u32[]{:S(2)}, u32[]{:S(2)}) collective-permute-start(f32[1,512]{1,0:T(1,128)S(1)} %get-tuple-element.55), channel_id=1, source_target_pairs={{0,56},{1,57},{4,60},{5,61},{8,0},{9,1},{12,4},{13,5},{18,10},{19,... | collective-permute-start | bytes 6152 | tf_op jit(solution)/shard_map/ppermute | solution.py:519

commit v11 on v9

--- a/solution.py
+++ b/solution.py
@@ -1,3 +1,4 @@
+import functools
 import math
 
 import jax
@@ -42,20 +43,33 @@
     ids_ref,
     keep_ref,
     drop_ref,
-    k_ref,
-    v_ref,
+    k_hbm,
+    v_hbm,
     q_ref,
     nk_ref,
     nv_ref,
     logit_ref,
-    out_ref,
+    out_hbm,
     kb,
     vb,
     keep_rows,
     q_rows,
+    k_ref,
+    v_ref,
+    row_ref,
+    part_ref,
+    mats,
+    sems,
 ):
+    loads = [
+        pltpu.make_async_copy(k_hbm, k_ref, sems.at[0]),
+        pltpu.make_async_copy(v_hbm, v_ref, sems.at[1]),
+    ]
+    for load in loads:
+        load.start()
     my = my_ref[0]
     slots, page_len, width = k_ref.shape
+    lines = part_ref.shape[1]
     keep_count = keep_ref.shape[1]
     rows = keep_count + 1
     heads = width // HD
@@ -66,18 +80,32 @@
     q_rows[...] = q_ref[...].astype(F32)
     lane = iota((rows, page_len), 1)
     last = iota((rows, page_len), 0) == rows - 1
+    totals = []
     for g in range(slots):
         onehot = jnp.where(keep_columns[:, g : g + 1] == lane, 1.0, 0.0)
         kept = jnp.max(onehot, axis=0, keepdims=True)
         coef = jnp.where(kept > 0.0, 0.0, drop_ref[g : g + 1, :].astype(F32))
         total = jnp.sum(coef, axis=1, keepdims=True)
-        mat = jnp.where(last, coef, onehot).astype(BF16)
-        denom = jnp.where(last[rows - 8 :, 0:1], total, 1.0)
-        for ref, blocks in ((k_ref, kb), (v_ref, vb)):
-            block = dot(mat, ref[g])
-            block = jnp.concatenate([block[: rows - 8], block[rows - 8 :] / denom], axis=0)
+        mats[g] = jnp.where(last, coef, onehot).astype(BF16)
+        totals.append(jnp.where(last[rows - 8 :, 0:1], total, 1.0))
+    n = slots * rows
+    to = iota((n, n), 0)
+    fro = iota((n, n), 1)
+    perm = (rest(to, slots) == over(fro, rows)) & (over(to, slots) == rest(fro, rows))
+    perm = jnp.where(perm, 1.0, 0.0).astype(BF16)
+    for i, (ref, blocks) in enumerate(((k_ref, kb), (v_ref, vb))):
+        loads[i].wait()
+        for g in range(slots):
+            block = dot(mats[g], ref[g])
+            block = jnp.concatenate([block[: rows - 8], block[rows - 8 :] / totals[g]], axis=0)
             blocks[g * rows : (g + 1) * rows, :] = block.astype(BF16)
-    n = slots * rows
+        spread = dot(perm, blocks[...])
+        for t in range(heads):
+            row_ref[i * rows : (i + 1) * rows, t * slots : (t + 1) * slots, :] = (
+                spread[:, t * HD : (t + 1) * HD].reshape(rows, slots, HD).astype(BF16)
+            )
+    row_store = pltpu.make_async_copy(row_ref, out_hbm.at[:, lines:, :], sems.at[2])
+    row_store.start()
     ent = 2 * slots
     ent_row = iota((ent, reqs), 0)
     req_lane = iota((ent, reqs), 1)
@@ -166,9 +194,7 @@
         parts.append(part)
     entries = jnp.concatenate(parts, axis=0)
     stats = entries[:, width:].astype(BF16)
-    devices = out_ref.shape[0]
-    lines = out_ref.shape[1] - heads * slots
-    columns = devices // EXPERTS
+    columns = part_ref.shape[0] // EXPERTS
     to = iota((EXPERTS * lines, EXPERTS * ent), 0)
     fro = iota((EXPERTS * lines, EXPERTS * ent), 1)
     flat = (over(to, lines) == over(fro, ent)) & (rest(to, lines) == slots + 1)
@@ -183,17 +209,11 @@
         sent = (entries[:, h * HD : (h + 1) * HD] + line).astype(BF16)
         for e in range(EXPERTS):
             for z in range(columns // heads):
-                out_ref[e * columns + z * heads + h, 0:lines, :] = sent[e * lines : (e + 1) * lines, :]
-    to = iota((n, n), 0)
-    fro = iota((n, n), 1)
-    perm = jnp.where((rest(to, slots) == over(fro, rows)) & (over(to, slots) == rest(fro, rows)), 1.0, 0.0).astype(BF16)
-    for base, blocks in ((0, kb), (rows, vb)):
-        spread = dot(perm, blocks[...])
-        for t in range(heads):
-            at = slice(lines + t * slots, lines + (t + 1) * slots)
-            out_ref[base : base + rows, at, :] = (
-                spread[:, t * HD : (t + 1) * HD].reshape(rows, slots, HD).astype(BF16)
-            )
+                part_ref[e * columns + z * heads + h] = sent[e * lines : (e + 1) * lines, :]
+    part_store = pltpu.make_async_copy(part_ref, out_hbm.at[:, 0:lines, :], sems.at[3])
+    part_store.start()
+    row_store.wait()
+    part_store.wait()
 
 
 def middle_kernel(head_ref, got_hbm, pick_hbm, *refs):
@@ -331,36 +351,27 @@
             out_ref[:, i * HD : (i + 1) * HD] = quarter[i : i + 1, :]
 
 
-def land_kernel(got_hbm, k_hbm, v_hbm, got_ref, k_ref, v_ref, sems, out_sems):
-    total = got_ref.shape[0]
-    tiles = k_ref.shape[2] // HD
-    rows = total // 2
-    loads = []
-    for i in range(2):
-        at = pl.ds(i * rows, rows)
-        loads.append(pltpu.make_async_copy(got_hbm.at[at], got_ref.at[at], sems.at[i]))
-        loads[i].start()
-    n = k_ref.shape[0] * k_ref.shape[1]
-    local = n // rows
+def land_kernel(got_hbm, page_hbm, got_ref, page_ref, sems, *, base):
+    rows, width, _ = got_ref.shape
+    tiles = page_ref.shape[2] // HD
+    local = width // tiles
+    n = rows * local
+    load = pltpu.make_async_copy(
+        got_hbm.at[base : base + rows, 0:width, :], got_ref, sems.at[0]
+    )
+    load.start()
     to = iota((n, n), 0)
     fro = iota((n, n), 1)
-    perm = jnp.where((over(to, rows) == rest(fro, local)) & (rest(to, rows) == over(fro, local)), 1.0, 0.0).astype(BF16)
-    stores = []
-    for i, (ref, hbm) in enumerate(((k_ref, k_hbm), (v_ref, v_hbm))):
-        base = i * rows
-        loads[i].wait()
-        flat = jnp.concatenate(
-            [
-                got_ref[base : base + rows, t * local : (t + 1) * local, :].reshape(n, HD)
-                for t in range(tiles)
-            ],
-            axis=1,
-        )
-        ref[...] = dot(perm, flat).reshape(ref.shape).astype(BF16)
-        stores.append(pltpu.make_async_copy(ref, hbm, out_sems.at[i]))
-        stores[i].start()
-    for store in stores:
-        store.wait()
+    perm = (over(to, rows) == rest(fro, local)) & (rest(to, rows) == over(fro, local))
+    perm = jnp.where(perm, 1.0, 0.0).astype(BF16)
+    load.wait()
+    flat = jnp.concatenate(
+        [got_ref[:, t * local : (t + 1) * local, :].reshape(n, HD) for t in range(tiles)], axis=1
+    )
+    page_ref[...] = dot(perm, flat).reshape(page_ref.shape).astype(BF16)
+    store = pltpu.make_async_copy(page_ref, page_hbm, sems.at[1])
+    store.start()
+    store.wait()
 
 
 def shards(
@@ -399,13 +410,19 @@
     outbox = pl.pallas_call(
         source_kernel,
         out_shape=jax.ShapeDtypeStruct((devices, lines + heads * slots, HD), BF16),
-        in_specs=[SMEM] + [VMEM] * 11,
-        out_specs=VMEM,
+        in_specs=[SMEM] + [VMEM] * 5 + [ANY] * 2 + [VMEM] * 4,
+        out_specs=ANY,
         scratch_shapes=[
             pltpu.VMEM((slots * rows, width), BF16),
             pltpu.VMEM((slots * rows, width), BF16),
             pltpu.VMEM((slots, HD), F32),
             pltpu.VMEM((requests, topk, width), F32),
+            pltpu.VMEM((slots, page_len, width), BF16),
+            pltpu.VMEM((slots, page_len, width), BF16),
+            pltpu.VMEM((devices, heads * slots, HD), BF16),
+            pltpu.VMEM((devices, lines, HD), BF16),
+            pltpu.VMEM((slots, rows, page_len), BF16),
+            pltpu.SemaphoreType.DMA((4,)),
         ],
         name="source",
     )(
@@ -476,28 +493,31 @@
         compiler_params=PARAMS,
         name="sum",
     )(shard, landed)
-    landed, quarters = lax.optimization_barrier((landed, quarters))
+    new_page = jax.ShapeDtypeStruct((new_cap, per_new * rows, width), BF16)
+
+    def land(got, base, name):
+        return pl.pallas_call(
+            functools.partial(land_kernel, base=base),
+            out_shape=new_page,
+            in_specs=[ANY],
+            out_specs=ANY,
+            scratch_shapes=[
+                pltpu.VMEM((rows, heads * local, HD), BF16),
+                pltpu.VMEM(new_page.shape, BF16),
+                pltpu.SemaphoreType.DMA((2,)),
+            ],
+            compiler_params=PARAMS,
+            name=name,
+        )(got)
+
+    compact_keys = land(landed, 0, "land_keys")
+    landed, quarters, _ = lax.optimization_barrier((landed, quarters, compact_keys))
     moved = [quarters[0]]
     for t in range(1, shard_count):
         moved.append(
             lax.ppermute(quarters[t], "expert", [(i, (i + t) % shard_count) for i in range(shard_count)])
         )
-    new_page = jax.ShapeDtypeStruct((new_cap, per_new * rows, width), BF16)
-    compact_keys, compact_values = pl.pallas_call(
-        land_kernel,
-        out_shape=(new_page, new_page),
-        in_specs=[ANY],
-        out_specs=(ANY, ANY),
-        scratch_shapes=[
-            pltpu.VMEM((devices, heads * local + terms, HD), BF16),
-            pltpu.VMEM(new_page.shape, BF16),
-            pltpu.VMEM(new_page.shape, BF16),
-            pltpu.SemaphoreType.DMA((2,)),
-            pltpu.SemaphoreType.DMA((2,)),
-        ],
-        compiler_params=PARAMS,
-        name="land",
-    )(landed)
+    compact_values = land(landed, rows, "land_values")
     mixed = sum(moved[1:], moved[0]).astype(BF16)
     return (compact_keys, compact_values, mixed)
 

time: 91.9 us -> 93.2 us (1.014)
  Pallas kernels: 10.1 us -> 11.3 us
    pallas_call x1 -> x2, Pallas kernels: 2 us -> 2.69 us  [land(): pl.pallas_call(functools.partial(land_kernel, base=base), out_shape=new_p...]
  transfers between devices with their start and end apart: 8 -> 8, of which waited for: 4 -> 4; matrix products, arithmetic and copies ran while one was open for 0% -> 0% of each run, Pallas kernels for 3% -> 2%
where the time goes in v11:
time: 93.2 us; the launch traced here: 92.9 us
  waiting for transfers between devices  51.5 us (55%)
  starting transfers between devices  28.6 us (31%)
  Pallas kernels  11.3 us (12%)
    all_to_all x1, waiting for transfers between devices, shards(): lax.all_to_all(routed, 'pages', split_axis=0, concat_axis=0, tiled=True)  31.4 us
    ppermute x3, waiting for transfers between devices, shards(): lax.ppermute(piece, 'pages', [(p, p ^ d) for p in range(devices)])  18.6 us
    all_to_all x1, starting transfers between devices, shards(): lax.all_to_all(outbox, 'pages', split_axis=0, concat_axis=0, tiled=True)  13.3 us
    all_to_all x1, starting transfers between devices, shards(): lax.all_to_all(routed, 'pages', split_axis=0, concat_axis=0, tiled=True)  8.21 us
    pallas_call x1, Pallas kernels, shards(): pl.pallas_call(source_kernel, out_shape=jax.ShapeDtypeStruct((devices, li...  4.91 us
    ppermute x3, starting transfers between devices, shards(): lax.ppermute(quarters[t], 'expert', [(i, (i + t) % shard_count) for i in...  4.89 us
    pallas_call x1, Pallas kernels, shards(): pl.pallas_call(middle_kernel, out_shape=jax.ShapeDtypeStruct((devices, he...  2.86 us
    pallas_call x2, Pallas kernels, land(): pl.pallas_call(functools.partial(land_kernel, base=base), out_shape=new_p...  2.69 us
  transfers between devices with their start and end apart: 8, of which 4 were waited for; matrix products, arithmetic and copies ran while one was open for 0% of the time, Pallas kernels for 2%

profile of v11, /device:TPU:1, one launch (start us, length us, event | category | flops | bytes accessed | tf_op | source)
XLA Modules:
  0.0 92.9 jit_solution(17876332025804388991)
XLA Ops:
  0.6 4.9 %source.1 = bf16[64,48,128]{2,1,0:T(8,128)(2,1)} custom-call(s32[1]{0:T(128)} %bitcast.1.my_ref, s32[12,64]{1,0:T(8,128)} %bitcast.9, s32[1,64]{1,0:T(1,128)} %bitcast.12, s32[2,64]{1,0:T(2,128)} %bitcast.14, s32[8,31]{1,0:T(8,128)} %keep_ref.1, s32[8,128]{1,0:T(8,128)} %drop_ref.1, bf16[8,128,512]{2,1,0:T(8,128)(2,1)} %k_hbm.1, bf16[8,128,512]{2,1,0:T(8,128)(2,1)} %v_hbm.1, ...), custom_call_target="tpu_custom_call" | custom-call | tf_op jit(solution)/shard_map/source/pallas_call | solution.py:410
  5.6 0.0 copy-start
  5.6 0.0 copy-start.1
  5.6 0.0 copy-start.2
  5.6 0.0 copy-start.3
  5.6 13.3 %all-to-all-start = ((bf16[64,48,128]{2,1,0:T(8,128)(2,1)}), bf16[64,48,128]{2,1,0:T(8,128)(2,1)S(1)}, u32[]{:S(2)}, u32[]{:S(2)}) async-start(bf16[64,48,128]{2,1,0:T(8,128)(2,1)} %source.1), calls=%async_computation | async-start | bytes 1572864 | tf_op jit(solution)/shard_map/all_to_all | solution.py:442
  18.9 0.0 copy-done
  19.0 1.7 %collective-permute-start.2 = (bf16[128,256]{1,0:T(8,128)(2,1)S(1)}, bf16[128,256]{1,0:T(8,128)(2,1)S(1)}, u32[]{:S(2)}, u32[]{:S(2)}) collective-permute-start(bf16[128,256]{1,0:T(8,128)(2,1)S(1)} %get-tuple-element.33), channel_id=1, source_target_pairs={{0,12},{4,8},{8,4},{12,0},{16,28},{20,24},{24,20},{28,16},{32,44},... | collective-permute-start | bytes 196616 | tf_op jit(solution)/shard_map/ppermute | solution.py:447
  20.7 0.2 collective-permute-start.1
  20.9 0.3 collective-permute-start
  21.2 0.0 copy-done.1
  21.2 0.0 copy-done.2
  21.2 0.0 copy-done.3
  21.2 0.8 route.1.pick_hbm
  22.0 18.1 %collective-permute-done.2.refs_3_ = bf16[128,256]{1,0:T(8,128)(2,1)S(1)} collective-permute-done((bf16[128,256]{1,0:T(8,128)(2,1)S(1)}, bf16[128,256]{1,0:T(8,128)(2,1)S(1)}, u32[]{:S(2)}, u32[]{:S(2)}) %collective-permute-start.2) | collective-permute-done | bytes 65568 | tf_op jit(solution)/shard_map/ppermute | solution.py:447
  40.1 0.5 collective-permute-done.1.refs_2_
  40.6 0.0 collective-permute-done.refs_1_
  40.6 1.6 %all-to-all-done.got_hbm = bf16[64,48,128]{2,1,0:T(8,128)(2,1)S(1)} async-done(((bf16[64,48,128]{2,1,0:T(8,128)(2,1)}), bf16[64,48,128]{2,1,0:T(8,128)(2,1)S(1)}, u32[]{:S(2)}, u32[]{:S(2)}) %all-to-all-start) | async-done | bytes 786464 | tf_op jit(solution)/shard_map/all_to_all | solution.py:442
  42.1 2.9 %middle.1 = bf16[64,72,128]{2,1,0:T(8,128)(2,1)} custom-call(s32[1]{0:T(128)} %bitcast.head_ref, bf16[64,48,128]{2,1,0:T(8,128)(2,1)S(1)} %all-to-all-done.got_hbm, bf16[1024,512]{1,0:T(8,128)(2,1)S(1)} %route.1.pick_hbm, bf16[1,512,256]{2,1,0:T(8,128)(2,1)S(1)} %copy-done, bf16[128,256]{1,0:T(8,128)(2,1)S(1)} %collective-permute-done.refs_1_, ...), custom_call_target="tpu_custom_call" | custom-call | tf_op jit(solution)/shard_map/middle/pallas_call | solution.py:462
  45.0 8.2 %all-to-all-start.1 = ((bf16[64,72,128]{2,1,0:T(8,128)(2,1)}), bf16[64,72,128]{2,1,0:T(8,128)(2,1)S(1)}, u32[]{:S(2)}, u32[]{:S(2)}) async-start(bf16[64,72,128]{2,1,0:T(8,128)(2,1)} %middle.1), calls=%async_computation.1 | async-start | bytes 2359296 | tf_op jit(solution)/shard_map/all_to_all | solution.py:481
  53.2 31.4 %all-to-all-done.1.got_hbm = bf16[64,72,128]{2,1,0:T(8,128)(2,1)S(1)} async-done(((bf16[64,72,128]{2,1,0:T(8,128)(2,1)}), bf16[64,72,128]{2,1,0:T(8,128)(2,1)S(1)}, u32[]{:S(2)}, u32[]{:S(2)}) %all-to-all-start.1) | async-done | bytes 1179680 | tf_op jit(solution)/shard_map/all_to_all | solution.py:481
  84.6 1.3 %land_keys.1 = bf16[4,128,512]{2,1,0:T(8,128)(2,1)} custom-call(bf16[64,72,128]{2,1,0:T(8,128)(2,1)S(1)} %all-to-all-done.1.got_hbm), custom_call_target="tpu_custom_call" | custom-call | tf_op jit(solution)/shard_map/land_keys/pallas_call | solution.py:499
  85.9 0.1 sum.1
  86.0 1.3 %collective-permute-start.3 = (f32[1,512]{1,0:T(1,128)S(1)}, f32[1,512]{1,0:T(1,128)S(1)}, u32[]{:S(2)}, u32[]{:S(2)}) collective-permute-start(f32[1,512]{1,0:T(1,128)S(1)} %get-tuple-element.30), channel_id=1, source_target_pairs={{0,1},{1,2},{2,3},{3,0},{4,5},{5,6},{6,7},{7,4},{8,9},{9,10},{10,1... | collective-permute-start | bytes 6152 | tf_op jit(solution)/shard_map/ppermute | solution.py:518
  87.3 2.5 %collective-permute-start.4 = (f32[1,512]{1,0:T(1,128)S(1)}, f32[1,512]{1,0:T(1,128)S(1)}, u32[]{:S(2)}, u32[]{:S(2)}) collective-permute-start(f32[1,512]{1,0:T(1,128)S(1)} %get-tuple-element.31), channel_id=1, source_target_pairs={{0,2},{1,3},{2,0},{3,1},{4,6},{5,7},{6,4},{7,5},{8,10},{9,11},{10,... | collective-permute-start | bytes 6152 | tf_op jit(solution)/shard_map/ppermute | solution.py:518
  89.8 1.1 %collective-permute-start.5 = (f32[1,512]{1,0:T(1,128)S(1)}, f32[1,512]{1,0:T(1,128)S(1)}, u32[]{:S(2)}, u32[]{:S(2)}) collective-permute-start(f32[1,512]{1,0:T(1,128)S(1)} %get-tuple-element.32), channel_id=1, source_target_pairs={{0,3},{1,0},{2,1},{3,2},{4,7},{5,4},{6,5},{7,6},{8,11},{9,8},{10,9... | collective-permute-start | bytes 6152 | tf_op jit(solution)/shard_map/ppermute | solution.py:518
  90.9 1.3 %land_values.1 = bf16[4,128,512]{2,1,0:T(8,128)(2,1)} custom-call(bf16[64,72,128]{2,1,0:T(8,128)(2,1)S(1)} %all-to-all-done.1.got_hbm), custom_call_target="tpu_custom_call" | custom-call | tf_op jit(solution)/shard_map/land_values/pallas_call | solution.py:499
  92.3 0.0 collective-permute-done.3
  92.3 0.0 collective-permute-done.4
  92.3 0.0 collective-permute-done.5
  92.3 0.6 add_convert_fusion
  (1 shorter events, 0.0 us)
Async XLA Ops:
  5.6 13.4 %copy-start = (bf16[1,512,256]{2,1,0:T(8,128)(2,1)S(1)}, bf16[1,512,256]{2,1,0:T(8,128)(2,1)}, u32[]{:S(2)}) copy-start(bf16[1,512,256]{2,1,0:T(8,128)(2,1)} %refs_0_.1) | copy-start | bytes 786436
  5.6 15.6 %copy-start.1 = (s32[64,12]{0,1:T(8,128)S(1)}, s32[64,12]{0,1:T(8,128)}, u32[]{:S(2)}) copy-start(s32[64,12]{0,1:T(8,128)} %param.18) | copy-start | bytes 9220
  5.6 15.6 %copy-start.2 = (s32[64,3]{0,1:T(4,128)S(1)}, s32[64,3]{0,1:T(4,128)}, u32[]{:S(2)}) copy-start(s32[64,3]{0,1:T(4,128)} %param.19) | copy-start | bytes 2308
  5.6 15.6 %copy-start.3 = (s32[64]{0:T(128)S(1)}, s32[64]{0:T(128)}, u32[]{:S(2)}) copy-start(s32[64]{0:T(128)} %param.17) | copy-start | bytes 772
  5.6 36.5 %all-to-all-start = ((bf16[64,48,128]{2,1,0:T(8,128)(2,1)}), bf16[64,48,128]{2,1,0:T(8,128)(2,1)S(1)}, u32[]{:S(2)}, u32[]{:S(2)}) async-start(bf16[64,48,128]{2,1,0:T(8,128)(2,1)} %source.1), calls=%async_computation | async-start | bytes 1572864 | tf_op jit(solution)/shard_map/all_to_all | solution.py:442
  19.0 21.1 %collective-permute-start.2 = (bf16[128,256]{1,0:T(8,128)(2,1)S(1)}, bf16[128,256]{1,0:T(8,128)(2,1)S(1)}, u32[]{:S(2)}, u32[]{:S(2)}) collective-permute-start(bf16[128,256]{1,0:T(8,128)(2,1)S(1)} %get-tuple-element.33), channel_id=1, source_target_pairs={{0,12},{4,8},{8,4},{12,0},{16,28},{20,24},{24,20},{28,16},{32,44},... | collective-permute-start | bytes 196616 | tf_op jit(solution)/shard_map/ppermute | solution.py:447
  20.7 19.9 %collective-permute-start.1 = (bf16[128,256]{1,0:T(8,128)(2,1)S(1)}, bf16[128,256]{1,0:T(8,128)(2,1)S(1)}, u32[]{:S(2)}, u32[]{:S(2)}) collective-permute-start(bf16[128,256]{1,0:T(8,128)(2,1)S(1)} %get-tuple-element.34), channel_id=1, source_target_pairs={{0,8},{4,12},{8,0},{12,4},{16,24},{20,28},{24,16},{28,20},{32,40},... | collective-permute-start | bytes 196616 | tf_op jit(solution)/shard_map/ppermute | solution.py:447
  20.9 19.7 %collective-permute-start = (bf16[128,256]{1,0:T(8,128)(2,1)S(1)}, bf16[128,256]{1,0:T(8,128)(2,1)S(1)}, u32[]{:S(2)}, u32[]{:S(2)}) collective-permute-start(bf16[128,256]{1,0:T(8,128)(2,1)S(1)} %get-tuple-element.35), channel_id=1, source_target_pairs={{0,4},{4,0},{8,12},{12,8},{16,20},{20,16},{24,28},{28,24},{32,36},... | collective-permute-start | bytes 196616 | tf_op jit(solution)/shard_map/ppermute | solution.py:447
  45.0 39.6 %all-to-all-start.1 = ((bf16[64,72,128]{2,1,0:T(8,128)(2,1)}), bf16[64,72,128]{2,1,0:T(8,128)(2,1)S(1)}, u32[]{:S(2)}, u32[]{:S(2)}) async-start(bf16[64,72,128]{2,1,0:T(8,128)(2,1)} %middle.1), calls=%async_computation.1 | async-start | bytes 2359296 | tf_op jit(solution)/shard_map/all_to_all | solution.py:481
  86.0 6.2 %collective-permute-start.3 = (f32[1,512]{1,0:T(1,128)S(1)}, f32[1,512]{1,0:T(1,128)S(1)}, u32[]{:S(2)}, u32[]{:S(2)}) collective-permute-start(f32[1,512]{1,0:T(1,128)S(1)} %get-tuple-element.30), channel_id=1, source_target_pairs={{0,1},{1,2},{2,3},{3,0},{4,5},{5,6},{6,7},{7,4},{8,9},{9,10},{10,1... | collective-permute-start | bytes 6152 | tf_op jit(solution)/shard_map/ppermute | solution.py:518
  87.3 5.0 %collective-permute-start.4 = (f32[1,512]{1,0:T(1,128)S(1)}, f32[1,512]{1,0:T(1,128)S(1)}, u32[]{:S(2)}, u32[]{:S(2)}) collective-permute-start(f32[1,512]{1,0:T(1,128)S(1)} %get-tuple-element.31), channel_id=1, source_target_pairs={{0,2},{1,3},{2,0},{3,1},{4,6},{5,7},{6,4},{7,5},{8,10},{9,11},{10,... | collective-permute-start | bytes 6152 | tf_op jit(solution)/shard_map/ppermute | solution.py:518
  89.8 2.5 %collective-permute-start.5 = (f32[1,512]{1,0:T(1,128)S(1)}, f32[1,512]{1,0:T(1,128)S(1)}, u32[]{:S(2)}, u32[]{:S(2)}) collective-permute-start(f32[1,512]{1,0:T(1,128)S(1)} %get-tuple-element.32), channel_id=1, source_target_pairs={{0,3},{1,0},{2,1},{3,2},{4,7},{5,4},{6,5},{7,6},{8,11},{9,8},{10,9... | collective-permute-start | bytes 6152 | tf_op jit(solution)/shard_map/ppermute | solution.py:518

commit v12 on v9

--- a/solution.py
+++ b/solution.py
@@ -1,3 +1,4 @@
+import functools
 import math
 
 import jax
@@ -196,28 +197,17 @@
             )
 
 
-def middle_kernel(head_ref, got_hbm, pick_hbm, *refs):
-    w_refs, (out_hbm, scr, terms, stack, parts, got_ref, pick_ref, out_ref, sems, out_sems) = (
-        refs[:-10],
-        refs[-10:],
-    )
+def middle_kernel(head_ref, got_ref, pick_ref, *refs):
+    w_refs, (out_hbm, scr, terms, stack, out_ref, out_sems) = refs[:-6], refs[-6:]
     heads = len(w_refs)
     head = head_ref[0]
     reqs, lines, _ = scr.shape
     slots = lines // 2
     depth = stack.shape[1]
-    loads = [pltpu.make_async_copy(got_hbm.at[:, 0:lines, :], parts, sems.at[0])]
-    loads.append(
-        pltpu.make_async_copy(w_refs[0].at[0, pl.ds(head * depth, depth), :], stack.at[0], sems.at[1])
-    )
+    stack[0] = w_refs[0][0, pl.ds(head * depth, depth), :]
     for d in range(1, heads):
-        loads.append(pltpu.make_async_copy(w_refs[d], stack.at[d], sems.at[1 + d]))
-    loads.append(pltpu.make_async_copy(got_hbm.at[:, lines:, :], got_ref, sems.at[heads + 1]))
-    loads.append(pltpu.make_async_copy(pick_hbm, pick_ref, sems.at[heads + 2]))
-    for load in loads:
-        load.start()
-    loads[0].wait()
-    scr[...] = parts[...].astype(F32)
+        stack[d] = w_refs[d][...]
+    scr[...] = got_ref[:, 0:lines, :].astype(F32)
     stats = scr[:, slots + 1, :]
     stats = jnp.concatenate([stats, stats], axis=0).T
     left = iota((1, 2 * reqs), 1) < reqs
@@ -252,8 +242,6 @@
     value = (num[:reqs] + num[reqs:]) / jnp.where(some, den, 1.0)
     weighted = jnp.where(some, gate * value, 0.0).astype(BF16)
     tiles = stack.shape[2] // HD
-    for load in loads[1 : 1 + heads]:
-        load.wait()
     for b in range(heads):
         part = dot(weighted, stack[b ^ head])
         for t in range(tiles):
@@ -262,11 +250,9 @@
     out_ref[:, terms_at:, :] = terms[...].astype(BF16)
     held = reqs * slots
     local = pick_ref.shape[0] // reqs
-    for load in loads[1 + heads :]:
-        load.wait()
     table = jnp.concatenate(
         [
-            got_ref[:, t * slots : (t + 1) * slots, :]
+            got_ref[:, lines + t * slots : lines + (t + 1) * slots, :]
             .astype(F32)
             .reshape(held, HD)
             .astype(BF16)
@@ -306,61 +292,48 @@
     out_ref[...] = jnp.where(source == iota(out_ref.shape, 1), 1.0, 0.0).astype(BF16)
 
 
-def sum_kernel(shard_ref, got_hbm, *refs):
-    out_refs, (quarters, got_ref, sem) = refs[:-3], refs[-3:]
-    terms = got_ref.shape[1]
-    load = pltpu.make_async_copy(got_hbm.at[:, got_hbm.shape[1] - terms :, :], got_ref, sem)
-    load.start()
-    load.wait()
-    s = shard_ref[0]
-    count = len(out_refs)
-    heads = count
+def sum_kernel(shard_ref, got_ref, keep_ref, send_ref, quarters, *, lines):
+    mine = lax.shift_right_logical(shard_ref[0], 1)
     columns = got_ref.shape[0] // EXPERTS
-    got = got_ref[...].astype(F32)
-    per = got.shape[1] // 2
-    for z in range(columns // heads):
+    got = got_ref[:, got_ref.shape[1] - lines :, :].astype(F32)
+    heads = columns // 2
+    per = lines // 2
+    for z in range(2):
         total = jnp.zeros(got.shape[1:], F32)
         for e in range(EXPERTS):
             at = e * columns + z * heads
             total = total + jnp.sum(got[at : at + heads], axis=0)
+        quarters[z] = total
+    for ref, half in ((keep_ref, quarters[mine]), (send_ref, quarters[1 - mine])):
         for i in range(2):
-            quarters[2 * z + i] = total[i * per : (i + 1) * per]
-    for t, out_ref in enumerate(out_refs):
-        quarter = quarters[lax.rem(s + t, count)]
-        for i in range(per):
-            out_ref[:, i * HD : (i + 1) * HD] = quarter[i : i + 1, :]
-
-
-def land_kernel(got_hbm, k_hbm, v_hbm, got_ref, k_ref, v_ref, sems, out_sems):
-    total = got_ref.shape[0]
-    tiles = k_ref.shape[2] // HD
-    rows = total // 2
-    loads = []
-    for i in range(2):
-        at = pl.ds(i * rows, rows)
-        loads.append(pltpu.make_async_copy(got_hbm.at[at], got_ref.at[at], sems.at[i]))
-        loads[i].start()
-    n = k_ref.shape[0] * k_ref.shape[1]
+            for t in range(per):
+                ref[i : i + 1, t * HD : (t + 1) * HD] = half[i * per + t : i * per + t + 1, :]
+
+
+def halve_kernel(shard_ref, here_ref, came_ref, keep_ref, send_ref, total):
+    mine = shard_ref[0] & 1
+    total[...] = here_ref[...] + came_ref[...]
+    keep_ref[...] = total[pl.ds(mine, 1), :]
+    send_ref[...] = total[pl.ds(1 - mine, 1), :]
+
+
+def land_kernel(got_ref, page_ref, *, base):
+    tiles = page_ref.shape[2] // HD
+    rows = got_ref.shape[0] // 2
+    n = page_ref.shape[0] * page_ref.shape[1]
     local = n // rows
     to = iota((n, n), 0)
     fro = iota((n, n), 1)
-    perm = jnp.where((over(to, rows) == rest(fro, local)) & (rest(to, rows) == over(fro, local)), 1.0, 0.0).astype(BF16)
-    stores = []
-    for i, (ref, hbm) in enumerate(((k_ref, k_hbm), (v_ref, v_hbm))):
-        base = i * rows
-        loads[i].wait()
-        flat = jnp.concatenate(
-            [
-                got_ref[base : base + rows, t * local : (t + 1) * local, :].reshape(n, HD)
-                for t in range(tiles)
-            ],
-            axis=1,
-        )
-        ref[...] = dot(perm, flat).reshape(ref.shape).astype(BF16)
-        stores.append(pltpu.make_async_copy(ref, hbm, out_sems.at[i]))
-        stores[i].start()
-    for store in stores:
-        store.wait()
+    perm = (over(to, rows) == rest(fro, local)) & (rest(to, rows) == over(fro, local))
+    perm = jnp.where(perm, 1.0, 0.0).astype(BF16)
+    flat = jnp.concatenate(
+        [
+            got_ref[base : base + rows, t * local : (t + 1) * local, :].reshape(n, HD)
+            for t in range(tiles)
+        ],
+        axis=1,
+    )
+    page_ref[...] = dot(perm, flat).reshape(page_ref.shape).astype(BF16)
 
 
 def shards(
@@ -445,17 +418,13 @@
     routed = pl.pallas_call(
         middle_kernel,
         out_shape=jax.ShapeDtypeStruct((devices, heads * local + terms, HD), BF16),
-        in_specs=[SMEM] + [ANY] * (2 + heads),
+        in_specs=[SMEM] + [VMEM] * (2 + heads),
         out_specs=ANY,
         scratch_shapes=[
             pltpu.VMEM((requests, lines, HD), F32),
             pltpu.VMEM((requests, terms, HD), F32),
             pltpu.VMEM((heads, HD, block_cols), BF16),
-            pltpu.VMEM((devices, lines, HD), BF16),
-            pltpu.VMEM((devices, heads * slots, HD), BF16),
-            pltpu.VMEM((devices * local, devices * slots), BF16),
             pltpu.VMEM((devices, heads * local + terms, HD), BF16),
-            pltpu.SemaphoreType.DMA((heads + 3,)),
             pltpu.SemaphoreType.DMA((devices // 16,)),
         ],
         compiler_params=PARAMS,
@@ -463,42 +432,45 @@
     )(head.reshape(1), inbox, pick, out_weight, *weights)
     landed = lax.all_to_all(routed, "pages", split_axis=0, concat_axis=0, tiled=True)
 
-    quarters = pl.pallas_call(
-        sum_kernel,
-        out_shape=[jax.ShapeDtypeStruct((1, width), F32)] * shard_count,
-        in_specs=[SMEM, ANY],
-        out_specs=[VMEM] * shard_count,
-        scratch_shapes=[
-            pltpu.VMEM((shard_count, width // HD, HD), F32),
-            pltpu.VMEM((devices, terms, HD), BF16),
-            pltpu.SemaphoreType.DMA(()),
-        ],
+    def swap(array, bit):
+        return lax.ppermute(array, "expert", [(i, i ^ bit) for i in range(shard_count)])
+
+    def land(got, base, name):
+        return pl.pallas_call(
+            functools.partial(land_kernel, base=base),
+            out_shape=jax.ShapeDtypeStruct((new_cap, per_new * rows, width), BF16),
+            in_specs=[VMEM],
+            out_specs=VMEM,
+            compiler_params=PARAMS,
+            name=name,
+        )(got)
+
+    here, there = pl.pallas_call(
+        functools.partial(sum_kernel, lines=terms),
+        out_shape=[jax.ShapeDtypeStruct((2, width), F32)] * 2,
+        in_specs=[SMEM, VMEM],
+        out_specs=[VMEM] * 2,
+        scratch_shapes=[pltpu.VMEM((2, terms, HD), F32)],
         compiler_params=PARAMS,
         name="sum",
     )(shard, landed)
-    landed, quarters = lax.optimization_barrier((landed, quarters))
-    moved = [quarters[0]]
-    for t in range(1, shard_count):
-        moved.append(
-            lax.ppermute(quarters[t], "expert", [(i, (i + t) % shard_count) for i in range(shard_count)])
-        )
-    new_page = jax.ShapeDtypeStruct((new_cap, per_new * rows, width), BF16)
-    compact_keys, compact_values = pl.pallas_call(
-        land_kernel,
-        out_shape=(new_page, new_page),
-        in_specs=[ANY],
-        out_specs=(ANY, ANY),
-        scratch_shapes=[
-            pltpu.VMEM((devices, heads * local + terms, HD), BF16),
-            pltpu.VMEM(new_page.shape, BF16),
-            pltpu.VMEM(new_page.shape, BF16),
-            pltpu.SemaphoreType.DMA((2,)),
-            pltpu.SemaphoreType.DMA((2,)),
-        ],
+    came = swap(there, 2)
+    landed, _ = lax.optimization_barrier((landed, there))
+    compact_keys = land(landed, 0, "land_keys")
+    came, _ = lax.optimization_barrier((came, compact_keys))
+    here, there = pl.pallas_call(
+        halve_kernel,
+        out_shape=[jax.ShapeDtypeStruct((1, width), F32)] * 2,
+        in_specs=[SMEM, VMEM, VMEM],
+        out_specs=[VMEM] * 2,
+        scratch_shapes=[pltpu.VMEM((2, width), F32)],
         compiler_params=PARAMS,
-        name="land",
-    )(landed)
-    mixed = sum(moved[1:], moved[0]).astype(BF16)
+        name="halve",
+    )(shard, here, came)
+    came = swap(there, 1)
+    landed, _ = lax.optimization_barrier((landed, there))
+    compact_values = land(landed, rows, "land_values")
+    mixed = (here + came).astype(BF16)
     return (compact_keys, compact_values, mixed)
 
 

time: 91.9 us -> 91.5 us (level)
    ppermute x3 -> x2, starting transfers between devices: 4.89 us -> 4.01 us  [swap(): lax.ppermute(array, 'expert', [(i, i ^ bit) for i in range(shard_count)])]
    pallas_call x2 -> x4, Pallas kernels: 2.07 us -> 2.52 us  [the longest x2 2.48 us: land(): pl.pallas_call(functools.partial(land_kernel, base=base), out_shape=jax.S...]
  transfers between devices with their start and end apart: 8 -> 7, of which waited for: 4 -> 5; matrix products, arithmetic and copies ran while one was open for 0% -> 0% of each run, Pallas kernels for 3% -> 4%
where the time goes in v12:
time: 91.5 us; the launch traced here: 90.5 us
  waiting for transfers between devices  51.6 us (56%)
  starting transfers between devices  27.7 us (30%)
  Pallas kernels  9.83 us (11%)
    all_to_all x1, waiting for transfers between devices, shards(): lax.all_to_all(routed, 'pages', split_axis=0, concat_axis=0, tiled=True)  31.4 us
    ppermute x3, waiting for transfers between devices, shards(): lax.ppermute(piece, 'pages', [(p, p ^ d) for p in range(devices)])  18.6 us
    all_to_all x1, starting transfers between devices, shards(): lax.all_to_all(outbox, 'pages', split_axis=0, concat_axis=0, tiled=True)  13.3 us
    all_to_all x1, starting transfers between devices, shards(): lax.all_to_all(routed, 'pages', split_axis=0, concat_axis=0, tiled=True)  8.21 us
    pallas_call x1, Pallas kernels, shards(): pl.pallas_call(source_kernel, out_shape=jax.ShapeDtypeStruct((devices, li...  4.36 us
    ppermute x2, starting transfers between devices, swap(): lax.ppermute(array, 'expert', [(i, i ^ bit) for i in range(shard_count)])  4.01 us
    pallas_call x2, Pallas kernels, land(): pl.pallas_call(functools.partial(land_kernel, base=base), out_shape=jax.S...  2.48 us
    ppermute x3, starting transfers between devices, shards(): lax.ppermute(piece, 'pages', [(p, p ^ d) for p in range(devices)])  2.23 us
  transfers between devices with their start and end apart: 7, of which 5 were waited for; matrix products, arithmetic and copies ran while one was open for 0% of the time, Pallas kernels for 4%

profile of v12, /device:TPU:1, one launch (start us, length us, event | category | flops | bytes accessed | tf_op | source)
XLA Modules:
  0.0 90.5 jit_solution(5536783167675724904)
XLA Ops:
  0.6 4.4 %source.1 = bf16[64,48,128]{2,1,0:T(8,128)(2,1)} custom-call(s32[1]{0:T(128)} %bitcast.1.my_ref, s32[12,64]{1,0:T(8,128)} %bitcast.9, s32[1,64]{1,0:T(1,128)} %bitcast.12, s32[2,64]{1,0:T(2,128)} %bitcast.14, s32[8,31]{1,0:T(8,128)} %keep_ref.1, s32[8,128]{1,0:T(8,128)} %drop_ref.1, bf16[8,128,512]{2,1,0:T(8,128)(2,1)} %k_ref.1, bf16[8,128,512]{2,1,0:T(8,128)(2,1)} %v_ref.1, ...), custom_call_target="tpu_custom_call" | custom-call | tf_op jit(solution)/shard_map/source/pallas_call | solution.py:372
  5.0 0.0 copy-start
  5.0 0.0 copy-start.1
  5.0 0.0 copy-start.2
  5.0 0.0 copy-start.3
  5.0 13.3 %all-to-all-start = ((bf16[64,48,128]{2,1,0:T(8,128)(2,1)}), bf16[64,48,128]{2,1,0:T(8,128)(2,1)S(1)}, u32[]{:S(2)}, u32[]{:S(2)}) async-start(bf16[64,48,128]{2,1,0:T(8,128)(2,1)} %source.1), calls=%async_computation | async-start | bytes 1572864 | tf_op jit(solution)/shard_map/all_to_all | solution.py:398
  18.3 0.0 copy-done
  18.4 1.7 %collective-permute-start.2 = (bf16[128,256]{1,0:T(8,128)(2,1)S(1)}, bf16[128,256]{1,0:T(8,128)(2,1)S(1)}, u32[]{:S(2)}, u32[]{:S(2)}) collective-permute-start(bf16[128,256]{1,0:T(8,128)(2,1)S(1)} %get-tuple-element.29), channel_id=1, source_target_pairs={{0,12},{4,8},{8,4},{12,0},{16,28},{20,24},{24,20},{28,16},{32,44},... | collective-permute-start | bytes 196616 | tf_op jit(solution)/shard_map/ppermute | solution.py:403
  20.1 0.2 collective-permute-start.1
  20.3 0.3 collective-permute-start
  20.6 0.0 copy-done.1
  20.6 0.0 copy-done.2
  20.6 0.0 copy-done.3
  20.6 0.8 route.1.pick_ref
  21.4 18.1 %collective-permute-done.2.refs_3_ = bf16[128,256]{1,0:T(8,128)(2,1)S(1)} collective-permute-done((bf16[128,256]{1,0:T(8,128)(2,1)S(1)}, bf16[128,256]{1,0:T(8,128)(2,1)S(1)}, u32[]{:S(2)}, u32[]{:S(2)}) %collective-permute-start.2) | collective-permute-done | bytes 65568 | tf_op jit(solution)/shard_map/ppermute | solution.py:403
  39.5 0.5 collective-permute-done.1.refs_2_
  40.0 0.0 collective-permute-done.refs_1_
  40.0 1.6 %all-to-all-done.got_ref = bf16[64,48,128]{2,1,0:T(8,128)(2,1)S(1)} async-done(((bf16[64,48,128]{2,1,0:T(8,128)(2,1)}), bf16[64,48,128]{2,1,0:T(8,128)(2,1)S(1)}, u32[]{:S(2)}, u32[]{:S(2)}) %all-to-all-start) | async-done | bytes 786464 | tf_op jit(solution)/shard_map/all_to_all | solution.py:398
  41.5 2.2 %middle.1 = bf16[64,72,128]{2,1,0:T(8,128)(2,1)} custom-call(s32[1]{0:T(128)} %bitcast.head_ref, bf16[64,48,128]{2,1,0:T(8,128)(2,1)S(1)} %all-to-all-done.got_ref, bf16[1024,512]{1,0:T(8,128)(2,1)S(1)} %route.1.pick_ref, bf16[1,512,256]{2,1,0:T(8,128)(2,1)S(1)} %copy-done, bf16[128,256]{1,0:T(8,128)(2,1)S(1)} %collective-permute-done.refs_1_, ...), custom_call_target="tpu_custom_call" | custom-call | tf_op jit(solution)/shard_map/middle/pallas_call | solution.py:418
  43.7 8.2 %all-to-all-start.1 = ((bf16[64,72,128]{2,1,0:T(8,128)(2,1)}), bf16[64,72,128]{2,1,0:T(8,128)(2,1)S(1)}, u32[]{:S(2)}, u32[]{:S(2)}) async-start(bf16[64,72,128]{2,1,0:T(8,128)(2,1)} %middle.1), calls=%async_computation.1 | async-start | bytes 2359296 | tf_op jit(solution)/shard_map/all_to_all | solution.py:433
  51.9 31.4 %all-to-all-done.1.got_ref = bf16[64,72,128]{2,1,0:T(8,128)(2,1)S(1)} async-done(((bf16[64,72,128]{2,1,0:T(8,128)(2,1)}), bf16[64,72,128]{2,1,0:T(8,128)(2,1)S(1)}, u32[]{:S(2)}, u32[]{:S(2)}) %all-to-all-start.1) | async-done | bytes 1179680 | tf_op jit(solution)/shard_map/all_to_all | solution.py:433
  83.3 2.8 %collective-permute-start.3 = (f32[2,512]{1,0:T(2,128)S(1)}, f32[2,512]{1,0:T(2,128)S(1)}, u32[]{:S(2)}, u32[]{:S(2)}) collective-permute-start(f32[2,512]{1,0:T(2,128)S(1)} %get-tuple-element.22), channel_id=1, source_target_pairs={{0,2},{1,3},{2,0},{3,1},{4,6},{5,7},{6,4},{7,5},{8,10},{9,11},{10,... | collective-permute-start | bytes 12296 | tf_op jit(solution)/shard_map/ppermute | solution.py:436
  86.2 1.2 %land_keys.1 = bf16[4,128,512]{2,1,0:T(8,128)(2,1)} custom-call(bf16[64,72,128]{2,1,0:T(8,128)(2,1)S(1)} %all-to-all-done.1.got_ref), custom_call_target="tpu_custom_call" | custom-call | tf_op jit(solution)/shard_map/land_keys/pallas_call | solution.py:439
  87.4 0.0 collective-permute-done.3.came_ref
  87.4 1.2 %collective-permute-start.4 = (f32[1,512]{1,0:T(1,128)S(1)}, f32[1,512]{1,0:T(1,128)S(1)}, u32[]{:S(2)}, u32[]{:S(2)}) collective-permute-start(f32[1,512]{1,0:T(1,128)S(1)} %get-tuple-element.26), channel_id=1, source_target_pairs={{0,1},{1,0},{2,3},{3,2},{4,5},{5,4},{6,7},{7,6},{8,9},{9,8},{10,11... | collective-permute-start | bytes 6152 | tf_op jit(solution)/shard_map/ppermute | solution.py:436
  88.6 1.2 %land_values.1 = bf16[4,128,512]{2,1,0:T(8,128)(2,1)} custom-call(bf16[64,72,128]{2,1,0:T(8,128)(2,1)S(1)} %all-to-all-done.1.got_ref), custom_call_target="tpu_custom_call" | custom-call | tf_op jit(solution)/shard_map/land_values/pallas_call | solution.py:439
  89.8 0.1 collective-permute-done.4
  89.9 0.6 add_convert_fusion
  (3 shorter events, 0.1 us)
Async XLA Ops:
  5.0 13.4 %copy-start = (bf16[1,512,256]{2,1,0:T(8,128)(2,1)S(1)}, bf16[1,512,256]{2,1,0:T(8,128)(2,1)}, u32[]{:S(2)}) copy-start(bf16[1,512,256]{2,1,0:T(8,128)(2,1)} %refs_0_.1) | copy-start | bytes 786436
  5.0 15.6 %copy-start.1 = (s32[64,12]{0,1:T(8,128)S(1)}, s32[64,12]{0,1:T(8,128)}, u32[]{:S(2)}) copy-start(s32[64,12]{0,1:T(8,128)} %param.18) | copy-start | bytes 9220
  5.0 15.6 %copy-start.2 = (s32[64,3]{0,1:T(4,128)S(1)}, s32[64,3]{0,1:T(4,128)}, u32[]{:S(2)}) copy-start(s32[64,3]{0,1:T(4,128)} %param.19) | copy-start | bytes 2308
  5.0 15.6 %copy-start.3 = (s32[64]{0:T(128)S(1)}, s32[64]{0:T(128)}, u32[]{:S(2)}) copy-start(s32[64]{0:T(128)} %param.17) | copy-start | bytes 772
  5.0 36.5 %all-to-all-start = ((bf16[64,48,128]{2,1,0:T(8,128)(2,1)}), bf16[64,48,128]{2,1,0:T(8,128)(2,1)S(1)}, u32[]{:S(2)}, u32[]{:S(2)}) async-start(bf16[64,48,128]{2,1,0:T(8,128)(2,1)} %source.1), calls=%async_computation | async-start | bytes 1572864 | tf_op jit(solution)/shard_map/all_to_all | solution.py:398
  18.4 21.1 %collective-permute-start.2 = (bf16[128,256]{1,0:T(8,128)(2,1)S(1)}, bf16[128,256]{1,0:T(8,128)(2,1)S(1)}, u32[]{:S(2)}, u32[]{:S(2)}) collective-permute-start(bf16[128,256]{1,0:T(8,128)(2,1)S(1)} %get-tuple-element.29), channel_id=1, source_target_pairs={{0,12},{4,8},{8,4},{12,0},{16,28},{20,24},{24,20},{28,16},{32,44},... | collective-permute-start | bytes 196616 | tf_op jit(solution)/shard_map/ppermute | solution.py:403
  20.1 19.9 %collective-permute-start.1 = (bf16[128,256]{1,0:T(8,128)(2,1)S(1)}, bf16[128,256]{1,0:T(8,128)(2,1)S(1)}, u32[]{:S(2)}, u32[]{:S(2)}) collective-permute-start(bf16[128,256]{1,0:T(8,128)(2,1)S(1)} %get-tuple-element.30), channel_id=1, source_target_pairs={{0,8},{4,12},{8,0},{12,4},{16,24},{20,28},{24,16},{28,20},{32,40},... | collective-permute-start | bytes 196616 | tf_op jit(solution)/shard_map/ppermute | solution.py:403
  20.3 19.7 %collective-permute-start = (bf16[128,256]{1,0:T(8,128)(2,1)S(1)}, bf16[128,256]{1,0:T(8,128)(2,1)S(1)}, u32[]{:S(2)}, u32[]{:S(2)}) collective-permute-start(bf16[128,256]{1,0:T(8,128)(2,1)S(1)} %get-tuple-element.31), channel_id=1, source_target_pairs={{0,4},{4,0},{8,12},{12,8},{16,20},{20,16},{24,28},{28,24},{32,36},... | collective-permute-start | bytes 196616 | tf_op jit(solution)/shard_map/ppermute | solution.py:403
  43.7 39.6 %all-to-all-start.1 = ((bf16[64,72,128]{2,1,0:T(8,128)(2,1)}), bf16[64,72,128]{2,1,0:T(8,128)(2,1)S(1)}, u32[]{:S(2)}, u32[]{:S(2)}) async-start(bf16[64,72,128]{2,1,0:T(8,128)(2,1)} %middle.1), calls=%async_computation.1 | async-start | bytes 2359296 | tf_op jit(solution)/shard_map/all_to_all | solution.py:433
  83.3 4.1 %collective-permute-start.3 = (f32[2,512]{1,0:T(2,128)S(1)}, f32[2,512]{1,0:T(2,128)S(1)}, u32[]{:S(2)}, u32[]{:S(2)}) collective-permute-start(f32[2,512]{1,0:T(2,128)S(1)} %get-tuple-element.22), channel_id=1, source_target_pairs={{0,2},{1,3},{2,0},{3,1},{4,6},{5,7},{6,4},{7,5},{8,10},{9,11},{10,... | collective-permute-start | bytes 12296 | tf_op jit(solution)/shard_map/ppermute | solution.py:436
  87.4 2.5 %collective-permute-start.4 = (f32[1,512]{1,0:T(1,128)S(1)}, f32[1,512]{1,0:T(1,128)S(1)}, u32[]{:S(2)}, u32[]{:S(2)}) collective-permute-start(f32[1,512]{1,0:T(1,128)S(1)} %get-tuple-element.26), channel_id=1, source_target_pairs={{0,1},{1,0},{2,3},{3,2},{4,5},{5,4},{6,7},{7,6},{8,9},{9,8},{10,11... | collective-permute-start | bytes 6152 | tf_op jit(solution)/shard_map/ppermute | solution.py:436

commit v13 on v9

--- a/solution.py
+++ b/solution.py
@@ -1,3 +1,4 @@
+import functools
 import math
 
 import jax
@@ -196,28 +197,17 @@
             )
 
 
-def middle_kernel(head_ref, got_hbm, pick_hbm, *refs):
-    w_refs, (out_hbm, scr, terms, stack, parts, got_ref, pick_ref, out_ref, sems, out_sems) = (
-        refs[:-10],
-        refs[-10:],
-    )
+def middle_kernel(head_ref, got_ref, pick_ref, *refs):
+    w_refs, (out_hbm, scr, terms, stack, out_ref, out_sems) = refs[:-6], refs[-6:]
     heads = len(w_refs)
     head = head_ref[0]
     reqs, lines, _ = scr.shape
     slots = lines // 2
     depth = stack.shape[1]
-    loads = [pltpu.make_async_copy(got_hbm.at[:, 0:lines, :], parts, sems.at[0])]
-    loads.append(
-        pltpu.make_async_copy(w_refs[0].at[0, pl.ds(head * depth, depth), :], stack.at[0], sems.at[1])
-    )
+    stack[0] = w_refs[0][0, pl.ds(head * depth, depth), :]
     for d in range(1, heads):
-        loads.append(pltpu.make_async_copy(w_refs[d], stack.at[d], sems.at[1 + d]))
-    loads.append(pltpu.make_async_copy(got_hbm.at[:, lines:, :], got_ref, sems.at[heads + 1]))
-    loads.append(pltpu.make_async_copy(pick_hbm, pick_ref, sems.at[heads + 2]))
-    for load in loads:
-        load.start()
-    loads[0].wait()
-    scr[...] = parts[...].astype(F32)
+        stack[d] = w_refs[d][...]
+    scr[...] = got_ref[:, 0:lines, :].astype(F32)
     stats = scr[:, slots + 1, :]
     stats = jnp.concatenate([stats, stats], axis=0).T
     left = iota((1, 2 * reqs), 1) < reqs
@@ -252,8 +242,6 @@
     value = (num[:reqs] + num[reqs:]) / jnp.where(some, den, 1.0)
     weighted = jnp.where(some, gate * value, 0.0).astype(BF16)
     tiles = stack.shape[2] // HD
-    for load in loads[1 : 1 + heads]:
-        load.wait()
     for b in range(heads):
         part = dot(weighted, stack[b ^ head])
         for t in range(tiles):
@@ -262,11 +250,9 @@
     out_ref[:, terms_at:, :] = terms[...].astype(BF16)
     held = reqs * slots
     local = pick_ref.shape[0] // reqs
-    for load in loads[1 + heads :]:
-        load.wait()
     table = jnp.concatenate(
         [
-            got_ref[:, t * slots : (t + 1) * slots, :]
+            got_ref[:, lines + t * slots : lines + (t + 1) * slots, :]
             .astype(F32)
             .reshape(held, HD)
             .astype(BF16)
@@ -306,19 +292,14 @@
     out_ref[...] = jnp.where(source == iota(out_ref.shape, 1), 1.0, 0.0).astype(BF16)
 
 
-def sum_kernel(shard_ref, got_hbm, *refs):
-    out_refs, (quarters, got_ref, sem) = refs[:-3], refs[-3:]
-    terms = got_ref.shape[1]
-    load = pltpu.make_async_copy(got_hbm.at[:, got_hbm.shape[1] - terms :, :], got_ref, sem)
-    load.start()
-    load.wait()
+def sum_kernel(shard_ref, got_ref, *refs, lines):
+    out_refs, (quarters,) = refs[:-1], refs[-1:]
     s = shard_ref[0]
-    count = len(out_refs)
-    heads = count
     columns = got_ref.shape[0] // EXPERTS
-    got = got_ref[...].astype(F32)
-    per = got.shape[1] // 2
-    for z in range(columns // heads):
+    got = got_ref[:, got_ref.shape[1] - lines :, :].astype(F32)
+    heads = columns // 2
+    per = lines // 2
+    for z in range(2):
         total = jnp.zeros(got.shape[1:], F32)
         for e in range(EXPERTS):
             at = e * columns + z * heads
@@ -326,38 +307,31 @@
         for i in range(2):
             quarters[2 * z + i] = total[i * per : (i + 1) * per]
     for t, out_ref in enumerate(out_refs):
-        quarter = quarters[lax.rem(s + t, count)]
+        quarter = quarters[s ^ t]
         for i in range(per):
             out_ref[:, i * HD : (i + 1) * HD] = quarter[i : i + 1, :]
 
 
-def land_kernel(got_hbm, k_hbm, v_hbm, got_ref, k_ref, v_ref, sems, out_sems):
-    total = got_ref.shape[0]
+def land_kernel(got_ref, k_hbm, v_hbm, k_ref, v_ref, sems):
     tiles = k_ref.shape[2] // HD
-    rows = total // 2
-    loads = []
-    for i in range(2):
-        at = pl.ds(i * rows, rows)
-        loads.append(pltpu.make_async_copy(got_hbm.at[at], got_ref.at[at], sems.at[i]))
-        loads[i].start()
+    rows = got_ref.shape[0] // 2
     n = k_ref.shape[0] * k_ref.shape[1]
     local = n // rows
     to = iota((n, n), 0)
     fro = iota((n, n), 1)
-    perm = jnp.where((over(to, rows) == rest(fro, local)) & (rest(to, rows) == over(fro, local)), 1.0, 0.0).astype(BF16)
+    perm = (over(to, rows) == rest(fro, local)) & (rest(to, rows) == over(fro, local))
+    perm = jnp.where(perm, 1.0, 0.0).astype(BF16)
     stores = []
     for i, (ref, hbm) in enumerate(((k_ref, k_hbm), (v_ref, v_hbm))):
-        base = i * rows
-        loads[i].wait()
         flat = jnp.concatenate(
             [
-                got_ref[base : base + rows, t * local : (t + 1) * local, :].reshape(n, HD)
+                got_ref[i * rows : (i + 1) * rows, t * local : (t + 1) * local, :].reshape(n, HD)
                 for t in range(tiles)
             ],
             axis=1,
         )
         ref[...] = dot(perm, flat).reshape(ref.shape).astype(BF16)
-        stores.append(pltpu.make_async_copy(ref, hbm, out_sems.at[i]))
+        stores.append(pltpu.make_async_copy(ref, hbm, sems.at[i]))
         stores[i].start()
     for store in stores:
         store.wait()
@@ -445,17 +419,13 @@
     routed = pl.pallas_call(
         middle_kernel,
         out_shape=jax.ShapeDtypeStruct((devices, heads * local + terms, HD), BF16),
-        in_specs=[SMEM] + [ANY] * (2 + heads),
+        in_specs=[SMEM] + [VMEM] * (2 + heads),
         out_specs=ANY,
         scratch_shapes=[
             pltpu.VMEM((requests, lines, HD), F32),
             pltpu.VMEM((requests, terms, HD), F32),
             pltpu.VMEM((heads, HD, block_cols), BF16),
-            pltpu.VMEM((devices, lines, HD), BF16),
-            pltpu.VMEM((devices, heads * slots, HD), BF16),
-            pltpu.VMEM((devices * local, devices * slots), BF16),
             pltpu.VMEM((devices, heads * local + terms, HD), BF16),
-            pltpu.SemaphoreType.DMA((heads + 3,)),
             pltpu.SemaphoreType.DMA((devices // 16,)),
         ],
         compiler_params=PARAMS,
@@ -464,35 +434,27 @@
     landed = lax.all_to_all(routed, "pages", split_axis=0, concat_axis=0, tiled=True)
 
     quarters = pl.pallas_call(
-        sum_kernel,
+        functools.partial(sum_kernel, lines=terms),
         out_shape=[jax.ShapeDtypeStruct((1, width), F32)] * shard_count,
-        in_specs=[SMEM, ANY],
+        in_specs=[SMEM, VMEM],
         out_specs=[VMEM] * shard_count,
-        scratch_shapes=[
-            pltpu.VMEM((shard_count, width // HD, HD), F32),
-            pltpu.VMEM((devices, terms, HD), BF16),
-            pltpu.SemaphoreType.DMA(()),
-        ],
+        scratch_shapes=[pltpu.VMEM((shard_count, width // HD, HD), F32)],
         compiler_params=PARAMS,
         name="sum",
     )(shard, landed)
     landed, quarters = lax.optimization_barrier((landed, quarters))
     moved = [quarters[0]]
     for t in range(1, shard_count):
-        moved.append(
-            lax.ppermute(quarters[t], "expert", [(i, (i + t) % shard_count) for i in range(shard_count)])
-        )
+        moved.append(lax.ppermute(quarters[t], "expert", [(i, i ^ t) for i in range(shard_count)]))
     new_page = jax.ShapeDtypeStruct((new_cap, per_new * rows, width), BF16)
     compact_keys, compact_values = pl.pallas_call(
         land_kernel,
         out_shape=(new_page, new_page),
-        in_specs=[ANY],
+        in_specs=[VMEM],
         out_specs=(ANY, ANY),
         scratch_shapes=[
-            pltpu.VMEM((devices, heads * local + terms, HD), BF16),
             pltpu.VMEM(new_page.shape, BF16),
             pltpu.VMEM(new_page.shape, BF16),
-            pltpu.SemaphoreType.DMA((2,)),
             pltpu.SemaphoreType.DMA((2,)),
         ],
         compiler_params=PARAMS,

time: 91.9 us -> 91.6 us (level)
  waiting for transfers between devices: 51.5 us -> 53.4 us
  Pallas kernels: 10.1 us -> 8.87 us
    ppermute x3, waiting for transfers between devices: 0.01 us -> 1.9 us  [shards(): lax.ppermute(quarters[t], 'expert', [(i, i ^ t) for i in range(shard_coun...]
    ppermute x3, starting transfers between devices: 4.89 us -> 3.94 us  [shards(): lax.ppermute(quarters[t], 'expert', [(i, i ^ t) for i in range(shard_coun...]
  transfers between devices with their start and end apart: 8 -> 8, of which waited for: 4 -> 5; matrix products, arithmetic and copies ran while one was open for 0% -> 0% of each run, Pallas kernels for 3% -> 3%
where the time goes in v13:
time: 91.6 us; the launch traced here: 91.3 us
  waiting for transfers between devices  53.4 us (58%)
  starting transfers between devices  27.7 us (30%)
  Pallas kernels  8.87 us (10%)
    all_to_all x1, waiting for transfers between devices, shards(): lax.all_to_all(routed, 'pages', split_axis=0, concat_axis=0, tiled=True)  31.4 us
    ppermute x3, waiting for transfers between devices, shards(): lax.ppermute(piece, 'pages', [(p, p ^ d) for p in range(devices)])  18.6 us
    all_to_all x1, starting transfers between devices, shards(): lax.all_to_all(outbox, 'pages', split_axis=0, concat_axis=0, tiled=True)  13.3 us
    all_to_all x1, starting transfers between devices, shards(): lax.all_to_all(routed, 'pages', split_axis=0, concat_axis=0, tiled=True)  8.21 us
    pallas_call x1, Pallas kernels, shards(): pl.pallas_call(source_kernel, out_shape=jax.ShapeDtypeStruct((devices, li...  4.35 us
    ppermute x3, starting transfers between devices, shards(): lax.ppermute(quarters[t], 'expert', [(i, i ^ t) for i in range(shard_coun...  3.94 us
    ppermute x3, starting transfers between devices, shards(): lax.ppermute(piece, 'pages', [(p, p ^ d) for p in range(devices)])  2.23 us
    pallas_call x1, Pallas kernels, shards(): pl.pallas_call(middle_kernel, out_shape=jax.ShapeDtypeStruct((devices, he...  2.17 us
  transfers between devices with their start and end apart: 8, of which 5 were waited for; matrix products, arithmetic and copies ran while one was open for 0% of the time, Pallas kernels for 3%

profile of v13, /device:TPU:1, one launch (start us, length us, event | category | flops | bytes accessed | tf_op | source)
XLA Modules:
  0.0 91.3 jit_solution(301267820656610241)
XLA Ops:
  0.6 4.4 %source.1 = bf16[64,48,128]{2,1,0:T(8,128)(2,1)} custom-call(s32[1]{0:T(128)} %bitcast.1.my_ref, s32[12,64]{1,0:T(8,128)} %bitcast.9, s32[1,64]{1,0:T(1,128)} %bitcast.12, s32[2,64]{1,0:T(2,128)} %bitcast.14, s32[8,31]{1,0:T(8,128)} %keep_ref.1, s32[8,128]{1,0:T(8,128)} %drop_ref.1, bf16[8,128,512]{2,1,0:T(8,128)(2,1)} %k_ref.1, bf16[8,128,512]{2,1,0:T(8,128)(2,1)} %v_ref.1, ...), custom_call_target="tpu_custom_call" | custom-call | tf_op jit(solution)/shard_map/source/pallas_call | solution.py:373
  5.0 0.0 copy-start
  5.0 0.0 copy-start.1
  5.0 0.0 copy-start.2
  5.0 0.0 copy-start.3
  5.0 13.3 %all-to-all-start = ((bf16[64,48,128]{2,1,0:T(8,128)(2,1)}), bf16[64,48,128]{2,1,0:T(8,128)(2,1)S(1)}, u32[]{:S(2)}, u32[]{:S(2)}) async-start(bf16[64,48,128]{2,1,0:T(8,128)(2,1)} %source.1), calls=%async_computation | async-start | bytes 1572864 | tf_op jit(solution)/shard_map/all_to_all | solution.py:399
  18.3 0.0 copy-done
  18.4 1.7 %collective-permute-start.2 = (bf16[128,256]{1,0:T(8,128)(2,1)S(1)}, bf16[128,256]{1,0:T(8,128)(2,1)S(1)}, u32[]{:S(2)}, u32[]{:S(2)}) collective-permute-start(bf16[128,256]{1,0:T(8,128)(2,1)S(1)} %get-tuple-element.37), channel_id=1, source_target_pairs={{0,12},{4,8},{8,4},{12,0},{16,28},{20,24},{24,20},{28,16},{32,44},... | collective-permute-start | bytes 196616 | tf_op jit(solution)/shard_map/ppermute | solution.py:404
  20.1 0.2 collective-permute-start.1
  20.3 0.3 collective-permute-start
  20.6 0.0 copy-done.1
  20.6 0.0 copy-done.2
  20.6 0.0 copy-done.3
  20.6 0.8 route.1.pick_ref
  21.4 18.1 %collective-permute-done.2.refs_3_ = bf16[128,256]{1,0:T(8,128)(2,1)S(1)} collective-permute-done((bf16[128,256]{1,0:T(8,128)(2,1)S(1)}, bf16[128,256]{1,0:T(8,128)(2,1)S(1)}, u32[]{:S(2)}, u32[]{:S(2)}) %collective-permute-start.2) | collective-permute-done | bytes 65568 | tf_op jit(solution)/shard_map/ppermute | solution.py:404
  39.5 0.5 collective-permute-done.1.refs_2_
  40.0 0.0 collective-permute-done.refs_1_
  40.0 1.6 %all-to-all-done.got_ref = bf16[64,48,128]{2,1,0:T(8,128)(2,1)S(1)} async-done(((bf16[64,48,128]{2,1,0:T(8,128)(2,1)}), bf16[64,48,128]{2,1,0:T(8,128)(2,1)S(1)}, u32[]{:S(2)}, u32[]{:S(2)}) %all-to-all-start) | async-done | bytes 786464 | tf_op jit(solution)/shard_map/all_to_all | solution.py:399
  41.5 2.2 %middle.1 = bf16[64,72,128]{2,1,0:T(8,128)(2,1)} custom-call(s32[1]{0:T(128)} %bitcast.head_ref, bf16[64,48,128]{2,1,0:T(8,128)(2,1)S(1)} %all-to-all-done.got_ref, bf16[1024,512]{1,0:T(8,128)(2,1)S(1)} %route.1.pick_ref, bf16[1,512,256]{2,1,0:T(8,128)(2,1)S(1)} %copy-done, bf16[128,256]{1,0:T(8,128)(2,1)S(1)} %collective-permute-done.refs_1_, ...), custom_call_target="tpu_custom_call" | custom-call | tf_op jit(solution)/shard_map/middle/pallas_call | solution.py:419
  43.7 8.2 %all-to-all-start.1 = ((bf16[64,72,128]{2,1,0:T(8,128)(2,1)}), bf16[64,72,128]{2,1,0:T(8,128)(2,1)S(1)}, u32[]{:S(2)}, u32[]{:S(2)}) async-start(bf16[64,72,128]{2,1,0:T(8,128)(2,1)} %middle.1), calls=%async_computation.1 | async-start | bytes 2359296 | tf_op jit(solution)/shard_map/all_to_all | solution.py:434
  51.9 31.4 %all-to-all-done.1.got_ref = bf16[64,72,128]{2,1,0:T(8,128)(2,1)S(1)} async-done(((bf16[64,72,128]{2,1,0:T(8,128)(2,1)}), bf16[64,72,128]{2,1,0:T(8,128)(2,1)S(1)}, u32[]{:S(2)}, u32[]{:S(2)}) %all-to-all-start.1) | async-done | bytes 1179680 | tf_op jit(solution)/shard_map/all_to_all | solution.py:434
  83.3 1.3 %collective-permute-start.3 = (f32[1,512]{1,0:T(1,128)S(1)}, f32[1,512]{1,0:T(1,128)S(1)}, u32[]{:S(2)}, u32[]{:S(2)}) collective-permute-start(f32[1,512]{1,0:T(1,128)S(1)} %get-tuple-element.34), channel_id=1, source_target_pairs={{0,1},{1,0},{2,3},{3,2},{4,5},{5,4},{6,7},{7,6},{8,9},{9,8},{10,11... | collective-permute-start | bytes 6152 | tf_op jit(solution)/shard_map/ppermute | solution.py:448
  84.6 2.4 %collective-permute-start.4 = (f32[1,512]{1,0:T(1,128)S(1)}, f32[1,512]{1,0:T(1,128)S(1)}, u32[]{:S(2)}, u32[]{:S(2)}) collective-permute-start(f32[1,512]{1,0:T(1,128)S(1)} %get-tuple-element.35), channel_id=1, source_target_pairs={{0,2},{1,3},{2,0},{3,1},{4,6},{5,7},{6,4},{7,5},{8,10},{9,11},{10,... | collective-permute-start | bytes 6152 | tf_op jit(solution)/shard_map/ppermute | solution.py:448
  87.1 0.2 collective-permute-start.5
  87.3 1.5 %land.1 = (bf16[4,128,512]{2,1,0:T(8,128)(2,1)}, bf16[4,128,512]{2,1,0:T(8,128)(2,1)}) custom-call(bf16[64,72,128]{2,1,0:T(8,128)(2,1)S(1)} %all-to-all-done.1.got_ref), custom_call_target="tpu_custom_call" | custom-call | tf_op jit(solution)/shard_map/land/pallas_call | solution.py:450
  88.8 0.0 collective-permute-done.3
  88.8 0.0 collective-permute-done.4
  88.8 1.9 %collective-permute-done.5 = f32[1,512]{1,0:T(1,128)S(1)} collective-permute-done((f32[1,512]{1,0:T(1,128)S(1)}, f32[1,512]{1,0:T(1,128)S(1)}, u32[]{:S(2)}, u32[]{:S(2)}) %collective-permute-start.5) | collective-permute-done | bytes 2080 | tf_op jit(solution)/shard_map/ppermute | solution.py:448
  90.7 0.6 add_convert_fusion
  (2 shorter events, 0.1 us)
Async XLA Ops:
  5.0 13.4 %copy-start = (bf16[1,512,256]{2,1,0:T(8,128)(2,1)S(1)}, bf16[1,512,256]{2,1,0:T(8,128)(2,1)}, u32[]{:S(2)}) copy-start(bf16[1,512,256]{2,1,0:T(8,128)(2,1)} %refs_0_.1) | copy-start | bytes 786436
  5.0 15.6 %copy-start.1 = (s32[64,12]{0,1:T(8,128)S(1)}, s32[64,12]{0,1:T(8,128)}, u32[]{:S(2)}) copy-start(s32[64,12]{0,1:T(8,128)} %param.18) | copy-start | bytes 9220
  5.0 15.6 %copy-start.2 = (s32[64,3]{0,1:T(4,128)S(1)}, s32[64,3]{0,1:T(4,128)}, u32[]{:S(2)}) copy-start(s32[64,3]{0,1:T(4,128)} %param.19) | copy-start | bytes 2308
  5.0 15.6 %copy-start.3 = (s32[64]{0:T(128)S(1)}, s32[64]{0:T(128)}, u32[]{:S(2)}) copy-start(s32[64]{0:T(128)} %param.17) | copy-start | bytes 772
  5.0 36.5 %all-to-all-start = ((bf16[64,48,128]{2,1,0:T(8,128)(2,1)}), bf16[64,48,128]{2,1,0:T(8,128)(2,1)S(1)}, u32[]{:S(2)}, u32[]{:S(2)}) async-start(bf16[64,48,128]{2,1,0:T(8,128)(2,1)} %source.1), calls=%async_computation | async-start | bytes 1572864 | tf_op jit(solution)/shard_map/all_to_all | solution.py:399
  18.4 21.1 %collective-permute-start.2 = (bf16[128,256]{1,0:T(8,128)(2,1)S(1)}, bf16[128,256]{1,0:T(8,128)(2,1)S(1)}, u32[]{:S(2)}, u32[]{:S(2)}) collective-permute-start(bf16[128,256]{1,0:T(8,128)(2,1)S(1)} %get-tuple-element.37), channel_id=1, source_target_pairs={{0,12},{4,8},{8,4},{12,0},{16,28},{20,24},{24,20},{28,16},{32,44},... | collective-permute-start | bytes 196616 | tf_op jit(solution)/shard_map/ppermute | solution.py:404
  20.1 19.9 %collective-permute-start.1 = (bf16[128,256]{1,0:T(8,128)(2,1)S(1)}, bf16[128,256]{1,0:T(8,128)(2,1)S(1)}, u32[]{:S(2)}, u32[]{:S(2)}) collective-permute-start(bf16[128,256]{1,0:T(8,128)(2,1)S(1)} %get-tuple-element.38), channel_id=1, source_target_pairs={{0,8},{4,12},{8,0},{12,4},{16,24},{20,28},{24,16},{28,20},{32,40},... | collective-permute-start | bytes 196616 | tf_op jit(solution)/shard_map/ppermute | solution.py:404
  20.3 19.7 %collective-permute-start = (bf16[128,256]{1,0:T(8,128)(2,1)S(1)}, bf16[128,256]{1,0:T(8,128)(2,1)S(1)}, u32[]{:S(2)}, u32[]{:S(2)}) collective-permute-start(bf16[128,256]{1,0:T(8,128)(2,1)S(1)} %get-tuple-element.39), channel_id=1, source_target_pairs={{0,4},{4,0},{8,12},{12,8},{16,20},{20,16},{24,28},{28,24},{32,36},... | collective-permute-start | bytes 196616 | tf_op jit(solution)/shard_map/ppermute | solution.py:404
  43.7 39.6 %all-to-all-start.1 = ((bf16[64,72,128]{2,1,0:T(8,128)(2,1)}), bf16[64,72,128]{2,1,0:T(8,128)(2,1)S(1)}, u32[]{:S(2)}, u32[]{:S(2)}) async-start(bf16[64,72,128]{2,1,0:T(8,128)(2,1)} %middle.1), calls=%async_computation.1 | async-start | bytes 2359296 | tf_op jit(solution)/shard_map/all_to_all | solution.py:434
  83.3 5.5 %collective-permute-start.3 = (f32[1,512]{1,0:T(1,128)S(1)}, f32[1,512]{1,0:T(1,128)S(1)}, u32[]{:S(2)}, u32[]{:S(2)}) collective-permute-start(f32[1,512]{1,0:T(1,128)S(1)} %get-tuple-element.34), channel_id=1, source_target_pairs={{0,1},{1,0},{2,3},{3,2},{4,5},{5,4},{6,7},{7,6},{8,9},{9,8},{10,11... | collective-permute-start | bytes 6152 | tf_op jit(solution)/shard_map/ppermute | solution.py:448
  84.6 4.2 %collective-permute-start.4 = (f32[1,512]{1,0:T(1,128)S(1)}, f32[1,512]{1,0:T(1,128)S(1)}, u32[]{:S(2)}, u32[]{:S(2)}) collective-permute-start(f32[1,512]{1,0:T(1,128)S(1)} %get-tuple-element.35), channel_id=1, source_target_pairs={{0,2},{1,3},{2,0},{3,1},{4,6},{5,7},{6,4},{7,5},{8,10},{9,11},{10,... | collective-permute-start | bytes 6152 | tf_op jit(solution)/shard_map/ppermute | solution.py:448
  87.1 3.6 %collective-permute-start.5 = (f32[1,512]{1,0:T(1,128)S(1)}, f32[1,512]{1,0:T(1,128)S(1)}, u32[]{:S(2)}, u32[]{:S(2)}) collective-permute-start(f32[1,512]{1,0:T(1,128)S(1)} %get-tuple-element.36), channel_id=1, source_target_pairs={{0,3},{1,2},{2,1},{3,0},{4,7},{5,6},{6,5},{7,4},{8,11},{9,10},{10,... | collective-permute-start | bytes 6152 | tf_op jit(solution)/shard_map/ppermute | solution.py:448

commit v14 on v13

--- a/solution.py
+++ b/solution.py
@@ -197,8 +197,9 @@
             )
 
 
-def middle_kernel(head_ref, got_ref, pick_ref, *refs):
-    w_refs, (out_hbm, scr, terms, stack, out_ref, out_sems) = refs[:-6], refs[-6:]
+def expert_kernel(head_ref, routed_hbm, got_ref, *refs):
+    del routed_hbm
+    w_refs, (out_hbm, scr, terms, stack, out_ref, sem) = refs[:-6], refs[-6:]
     heads = len(w_refs)
     head = head_ref[0]
     reqs, lines, _ = scr.shape
@@ -246,10 +247,20 @@
         part = dot(weighted, stack[b ^ head])
         for t in range(tiles):
             terms[:, b * tiles + t, :] = part[:, t * HD : (t + 1) * HD]
-    terms_at = out_ref.shape[1] - heads * tiles
-    out_ref[:, terms_at:, :] = terms[...].astype(BF16)
-    held = reqs * slots
+    out_ref[...] = terms[...].astype(BF16)
+    terms_at = out_hbm.shape[1] - out_ref.shape[1]
+    store = pltpu.make_async_copy(out_ref, out_hbm.at[:, terms_at:, :], sem)
+    store.start()
+    store.wait()
+
+
+def relay_kernel(got_ref, pick_ref, out_hbm, out_ref, out_sems):
+    reqs = got_ref.shape[0]
+    held = pick_ref.shape[1]
+    slots = held // reqs
+    lines = 2 * slots
     local = pick_ref.shape[0] // reqs
+    terms_at = out_ref.shape[1]
     table = jnp.concatenate(
         [
             got_ref[:, lines + t * slots : lines + (t + 1) * slots, :]
@@ -269,7 +280,11 @@
                 rows[:, t * HD : (t + 1) * HD].reshape(step, local, HD).astype(BF16)
             )
         at = pl.ds(c, step)
-        stores.append(pltpu.make_async_copy(out_ref.at[at], out_hbm.at[at], out_sems.at[c // step]))
+        stores.append(
+            pltpu.make_async_copy(
+                out_ref.at[at], out_hbm.at[at, 0:terms_at, :], out_sems.at[c // step]
+            )
+        )
         stores[-1].start()
     for store in stores:
         store.wait()
@@ -412,25 +427,39 @@
         compiler_params=PARAMS,
         name="route",
     )(new_table.T, table, counts)
-    inbox, pick, weights = lax.optimization_barrier((inbox, pick, weights))
+    inbox, pick = lax.optimization_barrier((inbox, pick))
 
     block_cols = out_weight.shape[2]
     terms = heads * block_cols // HD
+    outgoing = jax.ShapeDtypeStruct((devices, heads * local + terms, HD), BF16)
     routed = pl.pallas_call(
-        middle_kernel,
-        out_shape=jax.ShapeDtypeStruct((devices, heads * local + terms, HD), BF16),
-        in_specs=[SMEM] + [VMEM] * (2 + heads),
+        relay_kernel,
+        out_shape=outgoing,
+        in_specs=[VMEM, VMEM],
+        out_specs=ANY,
+        scratch_shapes=[
+            pltpu.VMEM((devices, heads * local, HD), BF16),
+            pltpu.SemaphoreType.DMA((devices // 16,)),
+        ],
+        compiler_params=PARAMS,
+        name="relay",
+    )(inbox, pick)
+    routed = pl.pallas_call(
+        expert_kernel,
+        out_shape=outgoing,
+        in_specs=[SMEM, ANY] + [VMEM] * (1 + heads),
         out_specs=ANY,
         scratch_shapes=[
             pltpu.VMEM((requests, lines, HD), F32),
             pltpu.VMEM((requests, terms, HD), F32),
             pltpu.VMEM((heads, HD, block_cols), BF16),
-            pltpu.VMEM((devices, heads * local + terms, HD), BF16),
-            pltpu.SemaphoreType.DMA((devices // 16,)),
+            pltpu.VMEM((requests, terms, HD), BF16),
+            pltpu.SemaphoreType.DMA(()),
         ],
+        input_output_aliases={1: 0},
         compiler_params=PARAMS,
-        name="middle",
-    )(head.reshape(1), inbox, pick, out_weight, *weights)
+        name="expert",
+    )(head.reshape(1), routed, inbox, out_weight, *weights)
     landed = lax.all_to_all(routed, "pages", split_axis=0, concat_axis=0, tiled=True)
 
     quarters = pl.pallas_call(

time: 91.6 us -> 91 us (level)
  starting transfers between devices: 27.7 us -> 26.2 us
    all_to_all x1, waiting for transfers between devices: 1.55 us -> 20.1 us  [shards(): lax.all_to_all(outbox, 'pages', split_axis=0, concat_axis=0, tiled=True)]
    ppermute x3, waiting for transfers between devices: 18.6 us -> 0.01 us  [shards(): lax.ppermute(piece, 'pages', [(p, p ^ d) for p in range(devices)])]
    all_to_all x1, starting transfers between devices: 8.21 us -> 6.69 us  [shards(): lax.all_to_all(routed, 'pages', split_axis=0, concat_axis=0, tiled=True)]
    pallas_call x1 -> x2, Pallas kernels: 2.17 us -> 3 us  [the longest x1 1.53 us: shards(): pl.pallas_call(expert_kernel, out_shape=outgoing, in_specs=[SMEM, ANY] +...]
  transfers between devices with their start and end apart: 8 -> 8, of which waited for: 5 -> 3; matrix products, arithmetic and copies ran while one was open for 0% -> 0% of each run, Pallas kernels for 3% -> 4%
where the time goes in v14:
time: 91 us; the launch traced here: 90.7 us
  waiting for transfers between devices  53.4 us (59%)
  starting transfers between devices  26.2 us (29%)
  Pallas kernels  9.71 us (11%)
    all_to_all x1, waiting for transfers between devices, shards(): lax.all_to_all(routed, 'pages', split_axis=0, concat_axis=0, tiled=True)  31.4 us
    all_to_all x1, waiting for transfers between devices, shards(): lax.all_to_all(outbox, 'pages', split_axis=0, concat_axis=0, tiled=True)  20.1 us
    all_to_all x1, starting transfers between devices, shards(): lax.all_to_all(outbox, 'pages', split_axis=0, concat_axis=0, tiled=True)  13.3 us
    all_to_all x1, starting transfers between devices, shards(): lax.all_to_all(routed, 'pages', split_axis=0, concat_axis=0, tiled=True)  6.69 us
    pallas_call x1, Pallas kernels, shards(): pl.pallas_call(source_kernel, out_shape=jax.ShapeDtypeStruct((devices, li...  4.35 us
    ppermute x3, starting transfers between devices, shards(): lax.ppermute(quarters[t], 'expert', [(i, i ^ t) for i in range(shard_coun...  3.94 us
    ppermute x3, starting transfers between devices, shards(): lax.ppermute(piece, 'pages', [(p, p ^ d) for p in range(devices)])  2.23 us
    ppermute x3, waiting for transfers between devices, shards(): lax.ppermute(quarters[t], 'expert', [(i, i ^ t) for i in range(shard_coun...  1.9 us
  transfers between devices with their start and end apart: 8, of which 3 were waited for; matrix products, arithmetic and copies ran while one was open for 0% of the time, Pallas kernels for 4%

profile of v14, /device:TPU:1, one launch (start us, length us, event | category | flops | bytes accessed | tf_op | source)
XLA Modules:
  0.0 90.7 jit_solution(8496061940874153207)
XLA Ops:
  0.6 4.4 %source.1 = bf16[64,48,128]{2,1,0:T(8,128)(2,1)} custom-call(s32[1]{0:T(128)} %bitcast.1.my_ref, s32[12,64]{1,0:T(8,128)} %bitcast.9, s32[1,64]{1,0:T(1,128)} %bitcast.12, s32[2,64]{1,0:T(2,128)} %bitcast.14, s32[8,31]{1,0:T(8,128)} %keep_ref.1, s32[8,128]{1,0:T(8,128)} %drop_ref.1, bf16[8,128,512]{2,1,0:T(8,128)(2,1)} %k_ref.1, bf16[8,128,512]{2,1,0:T(8,128)(2,1)} %v_ref.1, ...), custom_call_target="tpu_custom_call" | custom-call | tf_op jit(solution)/shard_map/source/pallas_call | solution.py:388
  5.0 0.0 copy-start
  5.0 0.0 copy-start.1
  5.0 0.0 copy-start.2
  5.0 0.0 copy-start.3
  5.0 13.3 %all-to-all-start = ((bf16[64,48,128]{2,1,0:T(8,128)(2,1)}), bf16[64,48,128]{2,1,0:T(8,128)(2,1)S(1)}, u32[]{:S(2)}, u32[]{:S(2)}) async-start(bf16[64,48,128]{2,1,0:T(8,128)(2,1)} %source.1), calls=%async_computation | async-start | bytes 1572864 | tf_op jit(solution)/shard_map/all_to_all | solution.py:414
  18.3 0.0 copy-done
  18.4 1.7 %collective-permute-start.2 = (bf16[128,256]{1,0:T(8,128)(2,1)S(1)}, bf16[128,256]{1,0:T(8,128)(2,1)S(1)}, u32[]{:S(2)}, u32[]{:S(2)}) collective-permute-start(bf16[128,256]{1,0:T(8,128)(2,1)S(1)} %get-tuple-element.31), channel_id=1, source_target_pairs={{0,12},{4,8},{8,4},{12,0},{16,28},{20,24},{24,20},{28,16},{32,44},... | collective-permute-start | bytes 196616 | tf_op jit(solution)/shard_map/ppermute | solution.py:419
  20.1 0.2 collective-permute-start.1
  20.3 0.3 collective-permute-start
  20.6 0.0 copy-done.1
  20.6 0.0 copy-done.2
  20.6 0.0 copy-done.3
  20.6 0.8 route.1.pick_ref
  21.4 20.1 %all-to-all-done.got_ref = bf16[64,48,128]{2,1,0:T(8,128)(2,1)S(1)} async-done(((bf16[64,48,128]{2,1,0:T(8,128)(2,1)}), bf16[64,48,128]{2,1,0:T(8,128)(2,1)S(1)}, u32[]{:S(2)}, u32[]{:S(2)}) %all-to-all-start) | async-done | bytes 786464 | tf_op jit(solution)/shard_map/all_to_all | solution.py:414
  41.5 1.5 %relay.1.routed_hbm = bf16[64,72,128]{2,1,0:T(8,128)(2,1)} custom-call(bf16[64,48,128]{2,1,0:T(8,128)(2,1)S(1)} %all-to-all-done.got_ref, bf16[1024,512]{1,0:T(8,128)(2,1)S(1)} %route.1.pick_ref), custom_call_target="tpu_custom_call" | custom-call | tf_op jit(solution)/shard_map/relay/pallas_call | solution.py:435
  43.0 0.0 collective-permute-done.2.refs_3_
  43.0 0.0 collective-permute-done.1.refs_2_
  43.0 0.0 collective-permute-done.refs_1_
  43.0 1.5 %expert.1 = bf16[64,72,128]{2,1,0:T(8,128)(2,1)} custom-call(s32[1]{0:T(128)} %bitcast.head_ref, bf16[64,72,128]{2,1,0:T(8,128)(2,1)} %relay.1.routed_hbm, bf16[64,48,128]{2,1,0:T(8,128)(2,1)S(1)} %all-to-all-done.got_ref, bf16[1,512,256]{2,1,0:T(8,128)(2,1)S(1)} %copy-done, ...), custom_call_target="tpu_custom_call", output_to_operand_aliasing={{}: (1, {})} | custom-call | tf_op jit(solution)/shard_map/expert/pallas_call | solution.py:447
  44.6 6.7 %all-to-all-start.1 = ((bf16[64,72,128]{2,1,0:T(8,128)(2,1)}), bf16[64,72,128]{2,1,0:T(8,128)(2,1)S(1)}, u32[]{:S(2)}, u32[]{:S(2)}) async-start(bf16[64,72,128]{2,1,0:T(8,128)(2,1)} %expert.1), calls=%async_computation.1 | async-start | bytes 2359296 | tf_op jit(solution)/shard_map/all_to_all | solution.py:463
  51.3 31.4 %all-to-all-done.1.got_ref = bf16[64,72,128]{2,1,0:T(8,128)(2,1)S(1)} async-done(((bf16[64,72,128]{2,1,0:T(8,128)(2,1)}), bf16[64,72,128]{2,1,0:T(8,128)(2,1)S(1)}, u32[]{:S(2)}, u32[]{:S(2)}) %all-to-all-start.1) | async-done | bytes 1179680 | tf_op jit(solution)/shard_map/all_to_all | solution.py:463
  82.7 1.3 %collective-permute-start.3 = (f32[1,512]{1,0:T(1,128)S(1)}, f32[1,512]{1,0:T(1,128)S(1)}, u32[]{:S(2)}, u32[]{:S(2)}) collective-permute-start(f32[1,512]{1,0:T(1,128)S(1)} %get-tuple-element.28), channel_id=1, source_target_pairs={{0,1},{1,0},{2,3},{3,2},{4,5},{5,4},{6,7},{7,6},{8,9},{9,8},{10,11... | collective-permute-start | bytes 6152 | tf_op jit(solution)/shard_map/ppermute | solution.py:477
  84.0 2.5 %collective-permute-start.4 = (f32[1,512]{1,0:T(1,128)S(1)}, f32[1,512]{1,0:T(1,128)S(1)}, u32[]{:S(2)}, u32[]{:S(2)}) collective-permute-start(f32[1,512]{1,0:T(1,128)S(1)} %get-tuple-element.29), channel_id=1, source_target_pairs={{0,2},{1,3},{2,0},{3,1},{4,6},{5,7},{6,4},{7,5},{8,10},{9,11},{10,... | collective-permute-start | bytes 6152 | tf_op jit(solution)/shard_map/ppermute | solution.py:477
  86.4 0.2 collective-permute-start.5
  86.6 1.5 %land.1 = (bf16[4,128,512]{2,1,0:T(8,128)(2,1)}, bf16[4,128,512]{2,1,0:T(8,128)(2,1)}) custom-call(bf16[64,72,128]{2,1,0:T(8,128)(2,1)S(1)} %all-to-all-done.1.got_ref), custom_call_target="tpu_custom_call" | custom-call | tf_op jit(solution)/shard_map/land/pallas_call | solution.py:479
  88.2 0.0 collective-permute-done.3
  88.2 0.0 collective-permute-done.4
  88.2 1.9 %collective-permute-done.5 = f32[1,512]{1,0:T(1,128)S(1)} collective-permute-done((f32[1,512]{1,0:T(1,128)S(1)}, f32[1,512]{1,0:T(1,128)S(1)}, u32[]{:S(2)}, u32[]{:S(2)}) %collective-permute-start.5) | collective-permute-done | bytes 2080 | tf_op jit(solution)/shard_map/ppermute | solution.py:477
  90.1 0.6 add_convert_fusion
  (2 shorter events, 0.1 us)
Async XLA Ops:
  5.0 13.4 %copy-start = (bf16[1,512,256]{2,1,0:T(8,128)(2,1)S(1)}, bf16[1,512,256]{2,1,0:T(8,128)(2,1)}, u32[]{:S(2)}) copy-start(bf16[1,512,256]{2,1,0:T(8,128)(2,1)} %refs_0_.1) | copy-start | bytes 786436
  5.0 15.6 %copy-start.1 = (s32[64,12]{0,1:T(8,128)S(1)}, s32[64,12]{0,1:T(8,128)}, u32[]{:S(2)}) copy-start(s32[64,12]{0,1:T(8,128)} %param.18) | copy-start | bytes 9220
  5.0 15.6 %copy-start.2 = (s32[64,3]{0,1:T(4,128)S(1)}, s32[64,3]{0,1:T(4,128)}, u32[]{:S(2)}) copy-start(s32[64,3]{0,1:T(4,128)} %param.19) | copy-start | bytes 2308
  5.0 15.6 %copy-start.3 = (s32[64]{0:T(128)S(1)}, s32[64]{0:T(128)}, u32[]{:S(2)}) copy-start(s32[64]{0:T(128)} %param.17) | copy-start | bytes 772
  5.0 36.5 %all-to-all-start = ((bf16[64,48,128]{2,1,0:T(8,128)(2,1)}), bf16[64,48,128]{2,1,0:T(8,128)(2,1)S(1)}, u32[]{:S(2)}, u32[]{:S(2)}) async-start(bf16[64,48,128]{2,1,0:T(8,128)(2,1)} %source.1), calls=%async_computation | async-start | bytes 1572864 | tf_op jit(solution)/shard_map/all_to_all | solution.py:414
  18.4 24.6 %collective-permute-start.2 = (bf16[128,256]{1,0:T(8,128)(2,1)S(1)}, bf16[128,256]{1,0:T(8,128)(2,1)S(1)}, u32[]{:S(2)}, u32[]{:S(2)}) collective-permute-start(bf16[128,256]{1,0:T(8,128)(2,1)S(1)} %get-tuple-element.31), channel_id=1, source_target_pairs={{0,12},{4,8},{8,4},{12,0},{16,28},{20,24},{24,20},{28,16},{32,44},... | collective-permute-start | bytes 196616 | tf_op jit(solution)/shard_map/ppermute | solution.py:419
  20.1 22.9 %collective-permute-start.1 = (bf16[128,256]{1,0:T(8,128)(2,1)S(1)}, bf16[128,256]{1,0:T(8,128)(2,1)S(1)}, u32[]{:S(2)}, u32[]{:S(2)}) collective-permute-start(bf16[128,256]{1,0:T(8,128)(2,1)S(1)} %get-tuple-element.32), channel_id=1, source_target_pairs={{0,8},{4,12},{8,0},{12,4},{16,24},{20,28},{24,16},{28,20},{32,40},... | collective-permute-start | bytes 196616 | tf_op jit(solution)/shard_map/ppermute | solution.py:419
  20.3 22.8 %collective-permute-start = (bf16[128,256]{1,0:T(8,128)(2,1)S(1)}, bf16[128,256]{1,0:T(8,128)(2,1)S(1)}, u32[]{:S(2)}, u32[]{:S(2)}) collective-permute-start(bf16[128,256]{1,0:T(8,128)(2,1)S(1)} %get-tuple-element.33), channel_id=1, source_target_pairs={{0,4},{4,0},{8,12},{12,8},{16,20},{20,16},{24,28},{28,24},{32,36},... | collective-permute-start | bytes 196616 | tf_op jit(solution)/shard_map/ppermute | solution.py:419
  44.6 38.1 %all-to-all-start.1 = ((bf16[64,72,128]{2,1,0:T(8,128)(2,1)}), bf16[64,72,128]{2,1,0:T(8,128)(2,1)S(1)}, u32[]{:S(2)}, u32[]{:S(2)}) async-start(bf16[64,72,128]{2,1,0:T(8,128)(2,1)} %expert.1), calls=%async_computation.1 | async-start | bytes 2359296 | tf_op jit(solution)/shard_map/all_to_all | solution.py:463
  82.7 5.5 %collective-permute-start.3 = (f32[1,512]{1,0:T(1,128)S(1)}, f32[1,512]{1,0:T(1,128)S(1)}, u32[]{:S(2)}, u32[]{:S(2)}) collective-permute-start(f32[1,512]{1,0:T(1,128)S(1)} %get-tuple-element.28), channel_id=1, source_target_pairs={{0,1},{1,0},{2,3},{3,2},{4,5},{5,4},{6,7},{7,6},{8,9},{9,8},{10,11... | collective-permute-start | bytes 6152 | tf_op jit(solution)/shard_map/ppermute | solution.py:477
  84.0 4.2 %collective-permute-start.4 = (f32[1,512]{1,0:T(1,128)S(1)}, f32[1,512]{1,0:T(1,128)S(1)}, u32[]{:S(2)}, u32[]{:S(2)}) collective-permute-start(f32[1,512]{1,0:T(1,128)S(1)} %get-tuple-element.29), channel_id=1, source_target_pairs={{0,2},{1,3},{2,0},{3,1},{4,6},{5,7},{6,4},{7,5},{8,10},{9,11},{10,... | collective-permute-start | bytes 6152 | tf_op jit(solution)/shard_map/ppermute | solution.py:477
  86.4 3.6 %collective-permute-start.5 = (f32[1,512]{1,0:T(1,128)S(1)}, f32[1,512]{1,0:T(1,128)S(1)}, u32[]{:S(2)}, u32[]{:S(2)}) collective-permute-start(f32[1,512]{1,0:T(1,128)S(1)} %get-tuple-element.30), channel_id=1, source_target_pairs={{0,3},{1,2},{2,1},{3,0},{4,7},{5,6},{6,5},{7,4},{8,11},{9,10},{10,... | collective-permute-start | bytes 6152 | tf_op jit(solution)/shard_map/ppermute | solution.py:477
